TPU v7x, 256 devices: a whole 4x4x8 slice. The times are simulated.
256 devices in a mesh: node: 16 (over z_lo, y), rep: 16 (over x, z_hi, core).
Axes of the slice: x: 4, y: 4, z: 8 (z_hi: 2, z_lo: 4; z = z_hi * 4 + z_lo), core: 2. Of those that a mesh axis runs over, the one named last changes fastest.
Arguments:
- tokens: bfloat16 [32768, 8192], P(('node', 'rep')), may hold values from -24 to 24
- norm_gain: float32 [8192], replicated, may hold values from 0.5 to 1.5
- key_cotangent: bfloat16 [32768, 512], P(('node', 'rep')), may hold values from -6 to 6
- secondary: bfloat16 [8192, 512], P('node'), may hold values from -0.0625 to 0.0625
- master: float32 [8192, 512], P(('node', 'rep')), may hold values from -0.0625 to 0.0625
- moment_first: float32 [4096, 1024], P(('node', 'rep')), may hold values from -0.03314563 to 0.03314563
- moment_second: float32 [4096, 1024], P(('node', 'rep')), may hold values from 7.6293945e-06 to 0.00012207031
- signs: int32 [1024], replicated, may hold values from 0 to 1
Outputs:
- keys: bfloat16 [32768, 512], P(('node', 'rep'))
- token_grad: bfloat16 [32768, 8192], P(('node', 'rep'))
- new_master: float32 [8192, 512], P(('node', 'rep'))
- new_first: float32 [4096, 1024], P(('node', 'rep'))
- new_second: float32 [4096, 1024], P(('node', 'rep'))
- new_secondary: bfloat16 [8192, 512], P('node')
All inputs are finite; a program needn't handle non-finite values.
Results may differ from a plain program's by a relative error of at most 0.0049.
Values may be sent and summed in bfloat16 or wider, within the bound.
No kernel may reach another device: no remote copies, remote signals or barrier semaphores. Data moves between devices by JAX's collectives and lax.ppermute only.
A program may use at most 128 MiB of HBM per device.

v0:
```python
import math

import jax
import jax.numpy as jnp
from jax import lax
from jax.sharding import PartitionSpec as P

PAIR_GAP = 16


norm_eps = 1e-05
adam_eps = 1e-08
beta_first = 0.9
beta_second = 0.95
adam_steps = 10
learn_rate = 0.002
weight_decay = 0.1


def split_up(value, dim, peers):
    dims = value.shape
    blocks = value.reshape(*dims[:dim], peers, dims[dim] // peers, *dims[dim + 1 :])
    return jnp.moveaxis(blocks, dim, 0)


def sent_and_summed(value, axis, dim):
    peers = lax.axis_size(axis)
    blocks = lax.all_to_all(split_up(value, dim, peers), axis, 0, 0, tiled=True)
    return jnp.sum(blocks.astype(jnp.float32), axis=0)


def sent_to_all(value, axis):
    copies = jnp.broadcast_to(value, (lax.axis_size(axis), *value.shape))
    return lax.all_to_all(copies, axis, split_axis=0, concat_axis=0, tiled=True)


def laid_out(blocks, dim):
    blocks = jnp.moveaxis(blocks, 0, dim)
    dims = blocks.shape
    return blocks.reshape(*dims[:dim], dims[dim] * dims[dim + 1], *dims[dim + 2 :])


def gathered_copies(value, axis, dim):
    blocks = sent_to_all(value, axis)
    return laid_out(blocks, dim)


def sylvester(extent):
    position = jnp.arange(extent, dtype=jnp.int32)
    parity = jnp.zeros((extent, extent), jnp.int32)
    for bit_place in range(extent.bit_length() - 1):
        parity = parity + (position[:, None] >> bit_place & 1) * (
            position[None, :] >> bit_place & 1
        )
    return (1 - 2 * (parity % 2)).astype(jnp.float32)


def shards(tokens, norm_gain, key_cotangent, secondary, master, moment_first, moment_second, signs):
    tok_rows, model_width = tokens.shape
    key_width = key_cotangent.shape[1]
    node_count = lax.axis_size("node")
    rep_count = lax.axis_size("rep")
    all_tokens = tok_rows * node_count * rep_count
    had_table = sylvester(key_width)
    sign_rows = (1 - 2 * signs).astype(jnp.float32).reshape(2, key_width)
    floats = tokens.astype(jnp.float32)
    inverse = lax.rsqrt(jnp.mean(floats * floats, axis=-1, keepdims=True) + norm_eps)
    normed = floats * inverse
    hidden = (normed * norm_gain).astype(jnp.bfloat16)
    gathered = lax.all_gather(secondary, "node", axis=0, tiled=True)
    keys = jnp.dot(hidden, gathered, preferred_element_type=jnp.float32).astype(jnp.bfloat16)
    hidden_grad = lax.dot_general(
        key_cotangent, gathered, (((1,), (1,)), ((), ())), preferred_element_type=jnp.float32
    )
    scaled = hidden_grad * norm_gain
    token_grad = (
        inverse * (scaled - normed * jnp.mean(scaled * normed, axis=-1, keepdims=True))
    ).astype(jnp.bfloat16)
    rot_scale = 1.0 / (math.sqrt(2 * key_width) * all_tokens)
    flipped = (key_cotangent[:, None, :] * sign_rows.astype(jnp.bfloat16)).reshape(
        2 * tok_rows, key_width
    )
    rotated = (
        jnp.dot(flipped, had_table.astype(jnp.bfloat16), preferred_element_type=jnp.float32)
        * rot_scale
    )
    rotated = rotated.astype(jnp.bfloat16).reshape(tok_rows, 2, key_width)
    amount = lax.axis_size("node") * (model_width // 2 // node_count)
    grouped = hidden.reshape(tok_rows, amount // PAIR_GAP, 2, PAIR_GAP)
    halves = jnp.einsum("tgaj,tak->agjk", grouped, rotated, preferred_element_type=jnp.float32)
    joined = jnp.concatenate([halves[0] + halves[1], halves[0] - halves[1]], axis=-1)
    partial_sum = lax.psum_scatter(
        joined.reshape(amount, 2 * key_width).astype(jnp.bfloat16),
        "node",
        scatter_dimension=0,
        tiled=True,
    )
    coded = sent_and_summed(partial_sum, "rep", 0)
    new_first = beta_first * moment_first + (1.0 - beta_first) * coded
    new_second = beta_second * moment_second + (1.0 - beta_second) * coded * coded
    first_hat = new_first / (1.0 - beta_first**adam_steps)
    second_hat = new_second / (1.0 - beta_second**adam_steps)
    ratio = first_hat / (jnp.sqrt(second_hat) + adam_eps)
    lower = ratio[:, :key_width]
    upper = ratio[:, key_width:]
    norm_root = math.sqrt(2 * key_width)
    row_even = jnp.dot(lower + upper, had_table) / norm_root * sign_rows[0]
    row_odd = jnp.dot(lower - upper, had_table) / norm_root * sign_rows[1]
    stacked = jnp.stack([row_even, row_odd], axis=1)
    master_rows = master.shape[0]
    update = (
        stacked.reshape(master_rows // (2 * PAIR_GAP), PAIR_GAP, 2, key_width)
        .transpose(0, 2, 1, 3)
        .reshape(master_rows, key_width)
    )
    new_master = master - learn_rate * (update + weight_decay * master)
    new_secondary = gathered_copies(new_master.astype(jnp.bfloat16), "rep", 0)
    return (keys, token_grad, new_master, new_first, new_second, new_secondary)


def solution(mesh):
    return jax.shard_map(
        shards,
        mesh=mesh,
        in_specs=(
            P(("node", "rep"), None),
            P(),
            P(("node", "rep"), None),
            P("node", None),
            P(("node", "rep"), None),
            P(("node", "rep"), None),
            P(("node", "rep"), None),
            P(),
        ),
        out_specs=(
            P(("node", "rep"), None),
            P(("node", "rep"), None),
            P(("node", "rep"), None),
            P(("node", "rep"), None),
            P(("node", "rep"), None),
            P("node", None),
        ),
        check_vma=False,
    )
```

profile of v0, /device:TPU:33, one launch (start us, length us, event | category | flops | bytes accessed | tf_op | source)
XLA Modules:
  0.0 311.2 jit_solution(15563459181511982867)
XLA Ops:
  7.2 0.0 all-gather.2.cloned.1.call-start
  7.2 0.7 all-gather.2.cloned.1.call-update
  7.9 0.0 reduce-scatter.2.cloned.1.call-start
  7.9 0.7 subtract_convert_fusion.1
  8.7 1.2 broadcast_multiply_fusion
  9.8 0.1 mul.382
  10.0 0.0 copy-start
  10.0 0.0 copy-start.2
  10.0 0.0 copy-start.3
  10.0 1.4 fusion.11
  11.5 0.1 reshape.197
  11.6 0.0 copy-done
  11.6 0.5 fusion.8
  12.1 99.8 %all-gather.2.cloned.1.call-done = bf16[8192,512]{1,0:T(8,128)(2,1)} async-done(((bf16[512,512]{1,0:T(8,128)(2,1)}), bf16[8192,512]{1,0:T(8,128)(2,1)}) %all-gather.2.cloned.1.call-update) | async-done | bytes 8388624 | tf_op jit(solution)/shard_map/all_gather | solution.py:70
  111.9 0.0 copy-done.2
  111.9 0.0 copy-done.3
  111.9 0.0 copy-start.1
  111.9 6.5 %fusion.4 = (f32[128]{0:T(128)S(1)}, f32[128,8192]{1,0:T(8,128)S(1)}) fusion(bf16[128,8192]{1,0:T(8,128)(2,1)S(1)} %copy-done, f32[128]{0:T(128)S(1)} %add_rsqrt_fusion, f32[8192]{0:T(1024)S(1)} %copy-done.3, bf16[128,512]{1,0:T(8,128)(2,1)S(1)} %copy-done.2, bf16[8192,512]{1,0:T(8,128)(2,1)} %all-gather.2.cloned.1.call-done), kind=kOutput, calls=%fused_computation.10 | convolution fusion | flops 1078984576 | bytes 14844928 | tf_op jit(solution)/shard_map/dot_general | solution.py:72
  118.3 0.0 copy-done.1
  118.3 2.5 fusion.7
  120.9 2.5 copy.16
  123.4 3.9 %fusion.9 = f32[2,256,16,512]{3,1,2,0:T(8,128)S(1)} fusion(bf16[128,256,2,16]{0,3,2,1:T(8,128)(2,1)} %bitcast.28, bf16[128,2,512,1]{2,1,0,3:T(2,128)(2,1)S(1)} %bitcast.30), kind=kOutput, calls=%fused_computation.15 | convolution fusion | flops 1073741824 | bytes 19136512 | tf_op jit(solution)/shard_map/tgaj,tak->agjk/dot_general | solution.py:90
  127.3 4.1 %add_convert_fusion = (bf16[1,256,16,512]{3,1,2,0:T(8,128)(2,1)}, bf16[1,256,16,512]{3,1,2,0:T(8,128)(2,1)S(1)}) fusion(f32[2,256,16,512]{3,1,2,0:T(8,128)S(1)} %fusion.9), kind=kLoop, calls=%fused_computation.3 | loop fusion | flops 8388608 | bytes 25165824 | tf_op jit(solution)/shard_map/convert.3
  131.4 6.5 %copy.19 = bf16[1,256,16,512]{3,2,1,0:T(8,128)(2,1)} copy(bf16[1,256,16,512]{3,1,2,0:T(8,128)(2,1)} %get-tuple-element.11) | data formatting | bytes 8388608 | tf_op jit(solution)/shard_map/convert.3
  137.9 4.3 %copy.20 = bf16[1,256,16,512]{3,2,1,0:T(8,128)(2,1)} copy(bf16[1,256,16,512]{3,1,2,0:T(8,128)(2,1)S(1)} %get-tuple-element.12) | data formatting | bytes 8388608 | tf_op jit(solution)/shard_map/convert.2
  142.3 7.9 %pad_maximum_fusion = bf16[4096,1024]{1,0:T(8,128)(2,1)} fusion(bf16[4096,512]{1,0:T(8,128)(2,1)} %bitcast.27, bf16[4096,512]{1,0:T(8,128)(2,1)} %bitcast.26), kind=kLoop, calls=%fused_computation.1 | loop fusion | flops 16777216 | bytes 16777216 | tf_op jit(solution)/shard_map/concatenate | solution.py:91
  150.1 0.0 copy-start.5
  150.1 0.0 copy-start.6
  150.1 0.0 reduce-scatter.2.cloned.1.call-update
  150.2 98.5 %reduce-scatter.2.cloned.1.call-done = bf16[256,1024]{1,0:T(8,128)(2,1)} async-done(((bf16[4096,1024]{1,0:T(8,128)(2,1)}), bf16[256,1024]{1,0:T(8,128)(2,1)}) %reduce-scatter.2.cloned.1.call-update) | async-done | bytes 524304 | tf_op jit(solution)/shard_map/reduce_scatter | solution.py:92
  248.7 11.1 %all-to-all-start = ((bf16[16,16,1024]{2,1,0:T(8,128)(2,1)}), bf16[16,16,1024]{2,1,0:T(8,128)(2,1)S(1)}, u32[]{:S(2)}, u32[]{:S(2)}) async-start(bf16[16,16,1024]{2,1,0:T(8,128)(2,1)} %bitcast.31), calls=%async_computation.1 | async-start | bytes 1048576 | tf_op jit(solution)/shard_map/all_to_all | solution.py:28
  259.8 19.8 %all-to-all-done = bf16[16,16,1024]{2,1,0:T(8,128)(2,1)S(1)} async-done(((bf16[16,16,1024]{2,1,0:T(8,128)(2,1)}), bf16[16,16,1024]{2,1,0:T(8,128)(2,1)S(1)}, u32[]{:S(2)}, u32[]{:S(2)}) %all-to-all-start) | async-done | bytes 524320 | tf_op jit(solution)/shard_map/all_to_all | solution.py:28
  279.6 0.1 convert_reduce_fusion
  279.7 0.0 copy-done.5
  279.7 0.0 copy-done.6
  279.7 0.7 add_divide_fusion
  280.4 1.3 fusion.13
  281.7 0.0 copy-start.4
  281.7 1.3 fusion.12
  283.0 0.0 copy-done.4
  283.0 0.6 fusion.42
  283.7 0.8 broadcast_in_dim.2
  284.5 4.1 %all-to-all-start.1 = ((bf16[16,32,512]{2,1,0:T(8,128)(2,1)}), bf16[16,32,512]{2,1,0:T(8,128)(2,1)S(1)}, u32[]{:S(2)}, u32[]{:S(2)}) async-start(bf16[16,32,512]{2,1,0:T(8,128)(2,1)} %broadcast_in_dim.2), calls=%async_computation.2 | async-start | bytes 1048576 | tf_op jit(solution)/shard_map/all_to_all | solution.py:34
  288.6 5.3 %convolution_convert_fusion = bf16[128,512]{1,0:T(8,128)(2,1)} fusion(bf16[128,8192]{1,0:T(8,128)(2,1)S(1)} %get-tuple-element.14, bf16[8192,512]{1,0:T(8,128)(2,1)} %all-gather.2.cloned.1.call-done), kind=kOutput, calls=%fused_computation.22 | convolution fusion | flops 1073807360 | bytes 10616832 | tf_op jit(solution)/shard_map/dot_general | solution.py:71
  293.8 9.7 %all-to-all-done.1 = bf16[16,32,512]{2,1,0:T(8,128)(2,1)S(1)} async-done(((bf16[16,32,512]{2,1,0:T(8,128)(2,1)}), bf16[16,32,512]{2,1,0:T(8,128)(2,1)S(1)}, u32[]{:S(2)}, u32[]{:S(2)}) %all-to-all-start.1) | async-done | bytes 524320 | tf_op jit(solution)/shard_map/all_to_all | solution.py:34
  303.6 0.8 copy.29
  (10 shorter events, 0.1 us)
Async XLA Ops:
  7.2 104.7 %all-gather.2.cloned.1.call-start = ((), (), s32[]{:S(2)}) async-start(), calls=%async_computation.3 | async-start | bytes 8912896 | tf_op jit(solution)/shard_map/all_gather | solution.py:70
  7.9 240.8 %reduce-scatter.2.cloned.1.call-start = ((), (), s32[]{:S(2)}) async-start(), calls=%async_computation.4 | async-start | bytes 8912896 | tf_op jit(solution)/shard_map/reduce_scatter | solution.py:92
  10.0 1.6 copy-start
  10.0 101.9 %copy-start.2 = (bf16[128,512]{1,0:T(8,128)(2,1)S(1)}, bf16[128,512]{1,0:T(8,128)(2,1)}, u32[]{:S(2)}) copy-start(bf16[128,512]{1,0:T(8,128)(2,1)} %param.10) | copy-start | bytes 393220
  10.0 101.8 %copy-start.3 = (f32[8192]{0:T(1024)S(1)}, f32[8192]{0:T(1024)}, u32[]{:S(2)}) copy-start(f32[8192]{0:T(1024)} %param.9) | copy-start | bytes 98308
  111.9 6.5 %copy-start.1 = (bf16[128,8192]{1,0:T(8,128)(2,1)S(1)}, bf16[128,8192]{1,0:T(8,128)(2,1)}, u32[]{:S(2)}) copy-start(bf16[128,8192]{1,0:T(8,128)(2,1)} %param.8) | copy-start | bytes 6291460
  150.1 129.5 %copy-start.5 = (f32[16,1024]{1,0:T(8,128)S(1)}, f32[16,1024]{1,0:T(8,128)}, u32[]{:S(2)}) copy-start(f32[16,1024]{1,0:T(8,128)} %param.13) | copy-start | bytes 196612
  150.1 129.6 %copy-start.6 = (f32[16,1024]{1,0:T(8,128)S(1)}, f32[16,1024]{1,0:T(8,128)}, u32[]{:S(2)}) copy-start(f32[16,1024]{1,0:T(8,128)} %param.14) | copy-start | bytes 196612
  248.7 30.9 %all-to-all-start = ((bf16[16,16,1024]{2,1,0:T(8,128)(2,1)}), bf16[16,16,1024]{2,1,0:T(8,128)(2,1)S(1)}, u32[]{:S(2)}, u32[]{:S(2)}) async-start(bf16[16,16,1024]{2,1,0:T(8,128)(2,1)} %bitcast.31), calls=%async_computation.1 | async-start | bytes 1048576 | tf_op jit(solution)/shard_map/all_to_all | solution.py:28
  281.7 1.3 copy-start.4
  284.5 19.1 %all-to-all-start.1 = ((bf16[16,32,512]{2,1,0:T(8,128)(2,1)}), bf16[16,32,512]{2,1,0:T(8,128)(2,1)S(1)}, u32[]{:S(2)}, u32[]{:S(2)}) async-start(bf16[16,32,512]{2,1,0:T(8,128)(2,1)} %broadcast_in_dim.2), calls=%async_computation.2 | async-start | bytes 1048576 | tf_op jit(solution)/shard_map/all_to_all | solution.py:34
Sparse Core Ops, SparseCore 0:
  9.8 102.0 all-gather.1
  150.3 98.3 reduce-scatter.1
where the time goes:
time: 314 us; the launch traced here: 311 us
  waiting for transfers between devices  229 us (73%)
  matrix products  19.7 us (6%)
  other arithmetic  18.3 us (6%)
  starting transfers between devices  15.2 us (5%)
  local copies, waits for them, and re-layouts  15.2 us (5%)
  between operations  14.2 us (5%)
    all_gather x1, waiting for transfers between devices, shards(): gathered = lax.all_gather(secondary, 'node', axis=0, tiled=True)  99.8 us
    reduce_scatter x1, waiting for transfers between devices, shards(): lax.psum_scatter(joined.reshape(amount, 2 * key_width).astype(jnp.bfloat1...  98.5 us
    all_to_all x1, waiting for transfers between devices, sent_and_summed(): blocks = lax.all_to_all(split_up(value, dim, peers), axis, 0, 0, tiled=True)  19.8 us
    all_to_all x1, starting transfers between devices, sent_and_summed(): blocks = lax.all_to_all(split_up(value, dim, peers), axis, 0, 0, tiled=True)  11.1 us
    another operation x2, local copies, waits for them, and re-layouts  10.8 us
    all_to_all x1, waiting for transfers between devices, sent_to_all(): return lax.all_to_all(copies, axis, split_axis=0, concat_axis=0, tiled=True)  9.74 us
    concatenate x1, other arithmetic, shards(): jnp.concatenate([halves[0] + halves[1], halves[0] - halves[1]], axis=-1)  7.88 us
    dot_general x1, matrix products, shards(): lax.dot_general(key_cotangent, gathered, (((1,), (1,)), ((), ())), prefer...  6.46 us
  transfers between devices with their start and end apart: 4, of which 4 were waited for; matrix products, arithmetic and copies ran while one was open for 3% of the time, Pallas kernels for 0%

commit v1 on v0

v1 whole, which is shorter than its diff:
```python
import functools
import math

import jax
import jax.numpy as jnp
from jax import lax
from jax.experimental import pallas as pl
from jax.experimental.pallas import tpu as pltpu
from jax.sharding import Mesh
from jax.sharding import PartitionSpec as P

PAIR_GAP = 16
norm_eps = 1e-05
adam_eps = 1e-08
beta_first = 0.9
beta_second = 0.95
adam_steps = 10
learn_rate = 0.002
weight_decay = 0.1

AXES = ("zl", "y", "x", "zh", "c")
SIZES = (4, 4, 4, 2, 2)
ZL, Y, X, ZH, C = SIZES
ROWS = 32
VMEM = pl.BlockSpec(memory_space=pltpu.VMEM)
BF16 = jnp.bfloat16
F32 = jnp.float32


def shape(dims, kind):
    return jax.ShapeDtypeStruct(dims, kind)


def kernel_call(body, outs, flops, nbytes, n_in):
    return pl.pallas_call(
        body,
        out_shape=outs,
        in_specs=[VMEM] * n_in,
        out_specs=jax.tree.map(lambda _: VMEM, outs),
        cost_estimate=pl.CostEstimate(flops=flops, bytes_accessed=nbytes, transcendentals=0),
        compiler_params=pltpu.CompilerParams(vmem_limit_bytes=56 << 20),
    )


def norm_kernel(tok_ref, gain_ref, cot_ref, send_ref, inv_ref):
    rows, width = tok_ref.shape
    step = X * ZH * C * ROWS
    acc = jnp.zeros((rows, step), F32)
    for k in range(width // step):
        t = tok_ref[:, k * step : (k + 1) * step].astype(F32)
        acc = acc + t * t
    inv = lax.rsqrt(jnp.sum(acc, axis=-1, keepdims=True) / width + norm_eps)
    inv = jnp.broadcast_to(inv, inv_ref.shape)
    inv_ref[...] = inv
    part = ZH * C * ROWS
    for n in range(ZL * Y):
        for x in range(X):
            cols = slice(n * step + x * part, n * step + (x + 1) * part)
            normed = tok_ref[:, cols].astype(F32) * inv
            send_ref[x, :, n * part : (n + 1) * part] = (normed * gain_ref[:, cols]).astype(BF16)
    for x in range(X):
        send_ref[x, :, ZL * Y * part :] = cot_ref[...]


def grad_kernel(recv_ref, own_ref, sib_ref):
    c = lax.axis_index("c")
    part = ZH * C * ROWS
    cols = ZL * Y * part
    cot = recv_ref[:, cols:]
    for zl in range(ZL):
        block = recv_ref[:, zl * Y * part : (zl + 1) * Y * part]
        grad = lax.dot_general(block, cot, (((0,), (0,)), ((), ())), preferred_element_type=F32)
        for y in range(Y):
            for zh in range(ZH):
                at = y * part + zh * C * ROWS
                first, second = grad[at : at + ROWS], grad[at + ROWS : at + 2 * ROWS]
                to = ((y * ZL + zl) * ZH + zh) * ROWS
                own_ref[to : to + ROWS, :] = jnp.where(c == 0, first, second)
                sib_ref[to : to + ROWS, :] = jnp.where(c == 0, second, first).astype(BF16)


def out_kernel(tok_ref, gain_ref, cot_ref, inv_ref, *refs):
    w_refs, (keys_ref, tg_ref) = refs[:-2], refs[-2:]
    c, zl = lax.axis_index("c"), lax.axis_index("zl")
    rows, width = tok_ref.shape
    step = width // (ZL * Y)
    half = step // 2
    inv = jnp.concatenate([inv_ref[...]] * (half // inv_ref.shape[1]), axis=1)
    cot = cot_ref[...]

    def places():
        for s, off in enumerate((0, 1, 3, 2)):
            for h in range(2):
                for y in range(Y):
                    node = lax.rem(zl + off, ZL) * Y + y
                    core = c if h == 0 else 1 - c
                    at = pl.multiple_of(node * step + core * half, half)
                    yield pl.ds(at, half), w_refs[2 * s + h], slice(y * half, (y + 1) * half)

    keys = jnp.zeros(keys_ref.shape, F32)
    for cols, w_ref, wrows in places():
        normed = tok_ref[:, cols].astype(F32) * inv
        hidden = (normed * gain_ref[:, cols]).astype(BF16)
        keys = keys + jnp.dot(hidden, w_ref[wrows, :], preferred_element_type=F32)
    keys_ref[...] = keys.astype(BF16)
    mean = jnp.sum(cot.astype(F32) * keys, axis=-1, keepdims=True) / width
    for cols, w_ref, wrows in places():
        hidden_grad = lax.dot_general(
            cot, w_ref[wrows, :], (((1,), (1,)), ((), ())), preferred_element_type=F32
        )
        normed = tok_ref[:, cols].astype(F32) * inv
        tg_ref[:, cols] = (inv * (hidden_grad * gain_ref[:, cols] - normed * mean)).astype(BF16)


def hadamard(value, extent=128):
    rows, width = value.shape
    i = lax.broadcasted_iota(jnp.int32, (extent, extent), 0)
    j = lax.broadcasted_iota(jnp.int32, (extent, extent), 1)
    both = i & j
    both = both ^ (both >> 4)
    both = both ^ (both >> 2)
    both = both ^ (both >> 1)
    table = (1 - 2 * (both & 1)).astype(F32).astype(BF16)
    parts = []
    for k in range(width // extent):
        rest = value[:, k * extent : (k + 1) * extent]
        for _ in range(3):
            top = rest.astype(BF16)
            parts.append(top)
            rest = rest - top.astype(F32)
    out = jnp.dot(jnp.concatenate(parts, axis=0), table, preferred_element_type=F32)
    p = []
    for k in range(width // extent):
        at = 3 * k * rows
        p.append((out[at + 2 * rows : at + 3 * rows] + out[at + rows : at + 2 * rows]) + out[at : at + rows])
    s, t, u, v = p[0] + p[1], p[0] - p[1], p[2] + p[3], p[2] - p[3]
    return jnp.concatenate([s + u, t + v, s - u, t - v], axis=1)


def adam_kernel(tokens_all, recv_ref, first_ref, second_ref, master_ref, signs_ref, nm_ref, nf_ref, ns_ref, new_ref):
    total = jnp.sum(recv_ref[...].astype(F32), axis=0)
    half = total.shape[1]
    root = math.sqrt(2 * half)
    sign = (1 - 2 * signs_ref[...]).astype(F32)
    sign0, sign1 = sign[:, :half], sign[:, half:]
    gap = PAIR_GAP
    spun = hadamard(jnp.concatenate([total[:gap] * sign0, total[gap:] * sign1], axis=0)) * (1.0 / (root * tokens_all))
    q0, q1 = spun[:gap], spun[gap:]
    coded = jnp.concatenate([q0 + q1, q0 - q1], axis=1)
    new_first = beta_first * first_ref[...] + (1.0 - beta_first) * coded
    new_second = beta_second * second_ref[...] + (1.0 - beta_second) * coded * coded
    nf_ref[...] = new_first
    ns_ref[...] = new_second
    first_hat = new_first / (1.0 - beta_first**adam_steps)
    second_hat = new_second / (1.0 - beta_second**adam_steps)
    ratio = first_hat / (jnp.sqrt(second_hat) + adam_eps)
    lower, upper = ratio[:, :half], ratio[:, half:]
    back = hadamard(jnp.concatenate([lower + upper, lower - upper], axis=0)) / root
    update = jnp.concatenate([back[:gap] * sign0, back[gap:] * sign1], axis=0)
    master = master_ref[...]
    new_master = master - learn_rate * (update + weight_decay * master)
    nm_ref[...] = new_master
    new_ref[...] = new_master.astype(BF16)


def ring(n, s):
    return [(i, (i + s) % n) for i in range(n)]


def along_z(shift):
    pairs = []
    for zl in range(ZL):
        for zh in range(ZH):
            for c in range(C):
                z = (zh * ZL + zl + shift(c)) % (ZH * ZL)
                pairs.append(((zl * ZH + zh) * C + c, ((z % ZL) * ZH + z // ZL) * C + c))
    return pairs


def to_all(value, axes, n):
    copies = jnp.broadcast_to(value, (n, *value.shape))
    return lax.all_to_all(copies, axes, 0, 0, tiled=True)


def shards(tokens, norm_gain, key_cotangent, secondary, master, moment_first, moment_second, signs):
    tok_rows, width = tokens.shape
    keys_w = key_cotangent.shape[1]
    c = lax.axis_index("c")
    gain = norm_gain.reshape(1, width)
    node_rows = secondary.shape[0]

    half = lax.dynamic_slice_in_dim(secondary, c * (node_rows // 2), node_rows // 2, 0)
    column = to_all(half, "y", Y).reshape(Y * node_rows // 2, keys_w)
    z_axes = ("zl", "zh", "c")
    from_up = lax.ppermute(column, z_axes, along_z(lambda c: -1))
    from_down = lax.ppermute(column, z_axes, along_z(lambda c: 1))
    from_far = lax.ppermute(column, z_axes, along_z(lambda c: 2 - 4 * c))
    weights = []
    for block in (column, from_up, from_down, from_far):
        weights += [block, lax.ppermute(block, "c", ring(C, 1))]

    part = width // X
    send, inv = kernel_call(
        norm_kernel,
        (shape((X, tok_rows, part + keys_w), BF16), shape((tok_rows, 128), F32)),
        tok_rows * width * 6,
        5 << 20,
        3,
    )(tokens, gain, key_cotangent)
    recv = lax.all_to_all(send, "x", 0, 0, tiled=True).reshape(X * tok_rows, part + keys_w)
    own, sib = kernel_call(
        grad_kernel,
        (shape((part // 2, keys_w), F32), shape((part // 2, keys_w), BF16)),
        2 * X * tok_rows * part * keys_w,
        6 << 20,
        1,
    )(recv)
    sib = lax.ppermute(sib, "c", ring(C, 1))
    summed = (own + sib.astype(F32)).astype(BF16)
    blocks = lax.all_to_all(summed.reshape(Y, -1, keys_w), "y", 0, 0, tiled=True)
    summed = jnp.sum(blocks.astype(F32), axis=0).astype(BF16)
    blocks = lax.all_to_all(summed.reshape(ZL * ZH, ROWS, keys_w), ("zl", "zh"), 0, 0, tiled=True)
    new_master, new_first, new_second, new_rows = kernel_call(
        functools.partial(adam_kernel, tok_rows * math.prod(SIZES)),
        (
            shape(master.shape, F32),
            shape(moment_first.shape, F32),
            shape(moment_second.shape, F32),
            shape(master.shape, BF16),
        ),
        1 << 25,
        1 << 20,
        5,
    )(blocks, moment_first, moment_second, master, signs.reshape(1, -1))

    mine = to_all(new_rows, ("x", "zh"), X * ZH)
    other = lax.ppermute(mine, "c", ring(C, 1))
    even = jnp.where(c == 0, mine, other)
    odd = jnp.where(c == 0, other, mine)
    new_secondary = jnp.stack([even, odd], axis=1).reshape(node_rows, keys_w)

    keys, token_grad = kernel_call(
        out_kernel,
        (shape((tok_rows, keys_w), BF16), shape(tokens.shape, BF16)),
        4 * tok_rows * width * keys_w,
        14 << 20,
        4 + len(weights),
    )(tokens, gain, key_cotangent, inv, *weights)
    return (keys, token_grad, new_master, new_first, new_second, new_secondary)


def solution(mesh):
    fine = Mesh(mesh.devices.reshape(SIZES), AXES)
    split = P(AXES, None)
    return jax.shard_map(
        shards,
        mesh=fine,
        in_specs=(split, P(), split, P(("zl", "y"), None), split, split, split, P()),
        out_specs=(split, split, split, split, split, P(("zl", "y"), None)),
        check_vma=False,
    )
```

time: 314 us -> 165 us (0.53)
  waiting for transfers between devices: 229 us -> 24.4 us
  blocking collectives: 0 us -> 84.2 us
  Pallas kernels: 0 us -> 20.7 us
  matrix products: 19.7 us -> 0 us
  other arithmetic: 18.3 us -> 2.46 us
  starting transfers between devices: 15.2 us -> 31 us
  local copies, waits for them, and re-layouts: 15.2 us -> 0.89 us
  between operations: 14.2 us -> 0.71 us
    all_gather x1 -> x0, waiting for transfers between devices: 99.8 us -> none  [shards(): gathered = lax.all_gather(secondary, 'node', axis=0, tiled=True)]
    reduce_scatter x1 -> x0, waiting for transfers between devices: 98.5 us -> none  [shards(): lax.psum_scatter(joined.reshape(amount, 2 * key_width).astype(jnp.bfloat1...]
    all_to_all x0 -> x4, blocking collectives: none -> 84.2 us  [the longest x1 35.6 us: shards(): lax.all_to_all(send, 'x', 0, 0, tiled=True)]
    all_to_all x2 -> x1, waiting for transfers between devices: 29.5 us -> 0.01 us  [shards(): lax.all_to_all(summed.reshape(Y, -1, keys_w), 'y', 0, 0, tiled=True)]
    ppermute x0 -> x9, starting transfers between devices: none -> 27.5 us  [the longest x4 15.3 us: shards(): weights += [block, lax.ppermute(block, 'c', ring(C, 1))]]
    ppermute x0 -> x9, waiting for transfers between devices: none -> 24.3 us  [the longest x1 23.6 us: shards(): from_far = lax.ppermute(column, z_axes, along_z(lambda c: 2 - 4 * c))]
    pallas_call x0 -> x4, Pallas kernels: none -> 20.7 us  [the longest x1 9.61 us: shards(): kernel_call(out_kernel, (shape((tok_rows, keys_w), BF16), shape(tokens.sh...]
    dot_general x6 -> x0, matrix products: 19.7 us -> none  [the longest x1 6.46 us: shards(): lax.dot_general(key_cotangent, gathered, (((1,), (1,)), ((), ())), prefer...]
  transfers between devices with their start and end apart: 4 -> 10, of which waited for: 4 -> 2; matrix products, arithmetic and copies ran while one was open for 3% -> 1% of each run, Pallas kernels for 0% -> 7%
where the time goes in v1:
time: 165 us; the launch traced here: 164 us
  blocking collectives  84.2 us (51%)
  starting transfers between devices  31 us (19%)
  waiting for transfers between devices  24.4 us (15%)
  Pallas kernels  20.7 us (13%)
  other arithmetic  2.46 us (1%)
    all_to_all x1, blocking collectives, shards(): lax.all_to_all(send, 'x', 0, 0, tiled=True)  35.6 us
    all_to_all x2, blocking collectives, to_all(): return lax.all_to_all(copies, axes, 0, 0, tiled=True)  31.7 us
    ppermute x1, waiting for transfers between devices, shards(): from_far = lax.ppermute(column, z_axes, along_z(lambda c: 2 - 4 * c))  23.6 us
    all_to_all x1, blocking collectives, shards(): lax.all_to_all(summed.reshape(ZL * ZH, ROWS, keys_w), ('zl', 'zh'), 0, 0,...  17 us
    ppermute x4, starting transfers between devices, shards(): weights += [block, lax.ppermute(block, 'c', ring(C, 1))]  15.3 us
    pallas_call x1, Pallas kernels, shards(): kernel_call(out_kernel, (shape((tok_rows, keys_w), BF16), shape(tokens.sh...  9.61 us
    ppermute x1, starting transfers between devices, shards(): from_far = lax.ppermute(column, z_axes, along_z(lambda c: 2 - 4 * c))  5.12 us
    pallas_call x1, Pallas kernels, shards(): kernel_call(grad_kernel, (shape((part // 2, keys_w), F32), shape((part //...  4.71 us
  transfers between devices with their start and end apart: 10, of which 2 were waited for; matrix products, arithmetic and copies ran while one was open for 1% of the time, Pallas kernels for 7%

profile of v1, /device:TPU:33, one launch (start us, length us, event | category | flops | bytes accessed | tf_op | source)
XLA Modules:
  0.0 164.4 jit_solution(13166930538618969115)
XLA Ops:
  0.6 0.0 copy-start
  0.6 4.2 %shard_map.127 = (bf16[4,128,2560]{2,1,0:T(8,128)(2,1)}, f32[128,128]{1,0:T(8,128)}) custom-call(bf16[128,8192]{1,0:T(8,128)(2,1)} %tok_ref.3, f32[1,8192]{1,0:T(1,128)} %bitcast.21, bf16[128,512]{1,0:T(8,128)(2,1)} %cot_ref.3), custom_call_target="tpu_custom_call" | custom-call | flops 6291456 | bytes 5242880 | tf_op jit(solution)/shard_map/pallas_call | solution.py:203
  4.9 35.6 %all_to_all.25 = bf16[4,128,2560]{2,1,0:T(8,128)(2,1)} all-to-all(bf16[4,128,2560]{2,1,0:T(8,128)(2,1)} %get-tuple-element.19), channel_id=1, replica_groups=mesh['zl'=4,'y'=4,'x'=4,'zh'=2,'c'=2] {'x'}, dimensions={0} | all-to-all | bytes 5242880 | tf_op jit(solution)/shard_map/all_to_all | solution.py:210
  40.4 4.7 %shard_map.129 = (f32[1024,512]{1,0:T(8,128)}, bf16[1024,512]{1,0:T(8,128)(2,1)}) custom-call(bf16[512,2560]{1,0:T(8,128)(2,1)} %bitcast.18), custom_call_target="tpu_custom_call" | custom-call | flops 1073741824 | bytes 6291456 | tf_op jit(solution)/shard_map/pallas_call | solution.py:211
  45.2 1.8 %collective-permute-start.7 = (bf16[1024,512]{1,0:T(8,128)(2,1)}, bf16[1024,512]{1,0:T(8,128)(2,1)S(1)}, u32[]{:S(2)}, u32[]{:S(2)}) collective-permute-start(bf16[1024,512]{1,0:T(8,128)(2,1)} %get-tuple-element.21), channel_id=1, source_target_pairs={{0,1},{1,0},{2,3},{3,2},{4,5},{5,4},{6,7},{7,6},{8,9},{9,8},{10,11... | collective-permute-start | bytes 3145736 | tf_op jit(solution)/shard_map/ppermute | solution.py:218
  47.0 0.0 copy-done
  47.0 0.0 copy-start.2
  47.0 0.1 broadcast_in_dim.6
  47.1 19.0 %all_to_all.26 = bf16[4,256,512]{2,1,0:T(8,128)(2,1)S(1)} all-to-all(bf16[4,256,512]{2,1,0:T(8,128)(2,1)S(1)} %broadcast_in_dim.6), channel_id=1, replica_groups=mesh['zl'=4,'y'=4,'x'=4,'zh'=2,'c'=2] {'y'}, dimensions={0} | all-to-all | bytes 2097152 | tf_op jit(solution)/shard_map/all_to_all | solution.py:182
  66.2 0.0 copy-start.1
  66.2 5.1 %collective-permute-start.5 = (bf16[1024,512]{1,0:T(8,128)(2,1)S(1)}, bf16[1024,512]{1,0:T(8,128)(2,1)}, u32[]{:S(2)}, u32[]{:S(2)}) collective-permute-start(bf16[1024,512]{1,0:T(8,128)(2,1)S(1)} %bitcast.13), channel_id=1, source_target_pairs={{0,128},{1,131},{2,130},{3,129},{64,192},{65,195},{66,194},{67,193... | collective-permute-start | bytes 3145736 | tf_op jit(solution)/shard_map/ppermute | solution.py:197
  71.3 0.0 collective-permute-start.3
  71.3 1.5 collective-permute-start.1
  72.7 0.0 collective-permute-done.7
  72.7 0.0 copy-done.2
  72.8 1.3 add_convert_fusion
  74.1 3.5 %all-to-all-start.2 = ((bf16[4,256,512]{2,1,0:T(8,128)(2,1)}), bf16[4,256,512]{2,1,0:T(8,128)(2,1)S(1)}, u32[]{:S(2)}, u32[]{:S(2)}) async-start(bf16[4,256,512]{2,1,0:T(8,128)(2,1)} %bitcast.3), calls=%async_computation.2 | async-start | bytes 2097152 | tf_op jit(solution)/shard_map/all_to_all | solution.py:220
  77.6 0.0 copy-done.1
  77.6 1.0 collective-permute-start
  78.6 23.6 %collective-permute-done.5.refs_6_ = bf16[1024,512]{1,0:T(8,128)(2,1)} collective-permute-done((bf16[1024,512]{1,0:T(8,128)(2,1)S(1)}, bf16[1024,512]{1,0:T(8,128)(2,1)}, u32[]{:S(2)}, u32[]{:S(2)}) %collective-permute-start.5) | collective-permute-done | bytes 1048608 | tf_op jit(solution)/shard_map/ppermute | solution.py:197
  102.3 4.8 %collective-permute-start.6 = (bf16[1024,512]{1,0:T(8,128)(2,1)}, bf16[1024,512]{1,0:T(8,128)(2,1)}, u32[]{:S(2)}, u32[]{:S(2)}) collective-permute-start(bf16[1024,512]{1,0:T(8,128)(2,1)} %collective-permute-done.5.refs_6_), channel_id=1, source_target_pairs={{0,1},{1,0},{2,3},{3,2},{4,5},{5,4},{6,7},{7,6},{8,9},{9,8},{10,11... | collective-permute-start | bytes 3145736 | tf_op jit(solution)/shard_map/ppermute | solution.py:200
  107.1 0.7 collective-permute-done.3.refs_4_
  107.8 9.5 %collective-permute-start.4 = (bf16[1024,512]{1,0:T(8,128)(2,1)}, bf16[1024,512]{1,0:T(8,128)(2,1)}, u32[]{:S(2)}, u32[]{:S(2)}) collective-permute-start(bf16[1024,512]{1,0:T(8,128)(2,1)} %collective-permute-done.3.refs_4_), channel_id=1, source_target_pairs={{0,1},{1,0},{2,3},{3,2},{4,5},{5,4},{6,7},{7,6},{8,9},{9,8},{10,11... | collective-permute-start | bytes 3145736 | tf_op jit(solution)/shard_map/ppermute | solution.py:200
  117.2 0.0 collective-permute-done.1.refs_2_
  117.3 0.0 collective-permute-start.2
  117.3 0.0 all-to-all-done.2
  117.3 0.2 reduce_sum.12
  117.5 17.0 %all_to_all.27.recv_ref = bf16[8,32,512]{2,1,0:T(8,128)(2,1)} all-to-all(bf16[8,32,512]{2,1,0:T(8,128)(2,1)S(1)} %bitcast.19), channel_id=1, replica_groups=mesh['zl'=4,'y'=4,'x'=4,'zh'=2,'c'=2] {'zl','zh'}, dimensions={0} | all-to-all | bytes 524288 | tf_op jit(solution)/shard_map/all_to_all | solution.py:222
  134.5 2.1 %shard_map.130 = (f32[32,512]{1,0:T(8,128)}, f32[16,1024]{1,0:T(8,128)}, f32[16,1024]{1,0:T(8,128)}, bf16[32,512]{1,0:T(8,128)(2,1)}) custom-call(bf16[8,32,512]{2,1,0:T(8,128)(2,1)} %all_to_all.27.recv_ref, f32[16,1024]{1,0:T(8,128)} %first_ref.1, f32[16,1024]{1,0:T(8,128)} %second_ref.1, f32[32,512]{1,0:T(8,128)} %master_ref.1, s32[1,1024]{1,0:T(1,128)} %bitcast.23), custom_call_target="tpu_custom_call" | custom-call | flops 33554432 | bytes 1048576 | tf_op jit(solution)/shard_map/pallas_call | solution.py:223
  136.6 0.8 broadcast_in_dim.7
  137.4 12.7 %all_to_all.28 = bf16[8,32,512]{2,1,0:T(8,128)(2,1)S(1)} all-to-all(bf16[8,32,512]{2,1,0:T(8,128)(2,1)S(1)} %broadcast_in_dim.7), channel_id=1, replica_groups=mesh['zl'=4,'y'=4,'x'=4,'zh'=2,'c'=2] {'x','zh'}, dimensions={0} | all-to-all | bytes 524288 | tf_op jit(solution)/shard_map/all_to_all | solution.py:182
  150.1 3.8 %collective-permute-start.8 = (bf16[8,32,512]{2,1,0:T(8,128)(2,1)S(1)}, bf16[8,32,512]{2,1,0:T(8,128)(2,1)S(1)}, u32[]{:S(2)}, u32[]{:S(2)}) collective-permute-start(bf16[8,32,512]{2,1,0:T(8,128)(2,1)S(1)} %all_to_all.28), channel_id=1, source_target_pairs={{0,1},{1,0},{2,3},{3,2},{4,5},{5,4},{6,7},{7,6},{8,9},{9,8},{10,11... | collective-permute-start | bytes 786440 | tf_op jit(solution)/shard_map/ppermute | solution.py:237
  153.8 0.0 collective-permute-done.refs_1_
  153.8 0.0 collective-permute-done.6.refs_7_
  153.9 0.0 collective-permute-done.4.refs_5_
  153.9 0.0 collective-permute-done.2.refs_3_
  153.9 9.6 %shard_map.128 = (bf16[128,512]{1,0:T(8,128)(2,1)}, bf16[128,8192]{1,0:T(8,128)(2,1)}) custom-call(bf16[128,8192]{1,0:T(8,128)(2,1)} %tok_ref.3, f32[1,8192]{1,0:T(1,128)} %bitcast.22, bf16[128,512]{1,0:T(8,128)(2,1)} %cot_ref.3, f32[128,128]{1,0:T(8,128)} %get-tuple-element.16.inv_ref, bf16[1024,512]{1,0:T(8,128)(2,1)} %bitcast.17, ...), custom_call_target="tpu_custom_call" | custom-call | flops 2147483648 | bytes 14680064 | tf_op jit(solution)/shard_map/pallas_call | solution.py:242
  163.5 0.0 collective-permute-done.8
  163.5 0.8 pad_maximum_fusion
  (2 shorter events, 0.1 us)
Async XLA Ops:
  0.6 46.4 %copy-start = (bf16[512,512]{1,0:T(8,128)(2,1)S(1)}, bf16[512,512]{1,0:T(8,128)(2,1)}, u32[]{:S(2)}) copy-start(bf16[512,512]{1,0:T(8,128)(2,1)} %param.11) | copy-start | bytes 1572868
  45.2 27.6 %collective-permute-start.7 = (bf16[1024,512]{1,0:T(8,128)(2,1)}, bf16[1024,512]{1,0:T(8,128)(2,1)S(1)}, u32[]{:S(2)}, u32[]{:S(2)}) collective-permute-start(bf16[1024,512]{1,0:T(8,128)(2,1)} %get-tuple-element.21), channel_id=1, source_target_pairs={{0,1},{1,0},{2,3},{3,2},{4,5},{5,4},{6,7},{7,6},{8,9},{9,8},{10,11... | collective-permute-start | bytes 3145736 | tf_op jit(solution)/shard_map/ppermute | solution.py:218
  47.0 25.8 %copy-start.2 = (f32[1024,512]{1,0:T(8,128)S(1)}, f32[1024,512]{1,0:T(8,128)}, u32[]{:S(2)}) copy-start(f32[1024,512]{1,0:T(8,128)} %get-tuple-element.20) | copy-start | bytes 6291460
  66.2 11.5 %copy-start.1 = (bf16[4,256,512]{2,1,0:T(8,128)(2,1)}, bf16[4,256,512]{2,1,0:T(8,128)(2,1)S(1)}, u32[]{:S(2)}) copy-start(bf16[4,256,512]{2,1,0:T(8,128)(2,1)S(1)} %all_to_all.26) | copy-start | bytes 3145732
  66.2 36.1 %collective-permute-start.5 = (bf16[1024,512]{1,0:T(8,128)(2,1)S(1)}, bf16[1024,512]{1,0:T(8,128)(2,1)}, u32[]{:S(2)}, u32[]{:S(2)}) collective-permute-start(bf16[1024,512]{1,0:T(8,128)(2,1)S(1)} %bitcast.13), channel_id=1, source_target_pairs={{0,128},{1,131},{2,130},{3,129},{64,192},{65,195},{66,194},{67,193... | collective-permute-start | bytes 3145736 | tf_op jit(solution)/shard_map/ppermute | solution.py:197
  71.3 36.5 %collective-permute-start.3 = (bf16[1024,512]{1,0:T(8,128)(2,1)S(1)}, bf16[1024,512]{1,0:T(8,128)(2,1)}, u32[]{:S(2)}, u32[]{:S(2)}) collective-permute-start(bf16[1024,512]{1,0:T(8,128)(2,1)S(1)} %bitcast.14), channel_id=1, source_target_pairs={{0,64},{1,65},{2,66},{3,67},{64,128},{65,129},{66,130},{67,131},{1... | collective-permute-start | bytes 3145736 | tf_op jit(solution)/shard_map/ppermute | solution.py:196
  71.3 46.0 %collective-permute-start.1 = (bf16[1024,512]{1,0:T(8,128)(2,1)S(1)}, bf16[1024,512]{1,0:T(8,128)(2,1)}, u32[]{:S(2)}, u32[]{:S(2)}) collective-permute-start(bf16[1024,512]{1,0:T(8,128)(2,1)S(1)} %bitcast.15), channel_id=1, source_target_pairs={{0,194},{1,195},{2,192},{3,193},{64,0},{65,1},{66,2},{67,3},{128,6... | collective-permute-start | bytes 3145736 | tf_op jit(solution)/shard_map/ppermute | solution.py:195
  74.1 43.2 %all-to-all-start.2 = ((bf16[4,256,512]{2,1,0:T(8,128)(2,1)}), bf16[4,256,512]{2,1,0:T(8,128)(2,1)S(1)}, u32[]{:S(2)}, u32[]{:S(2)}) async-start(bf16[4,256,512]{2,1,0:T(8,128)(2,1)} %bitcast.3), calls=%async_computation.2 | async-start | bytes 2097152 | tf_op jit(solution)/shard_map/all_to_all | solution.py:220
  77.6 76.2 %collective-permute-start = (bf16[1024,512]{1,0:T(8,128)(2,1)S(1)}, bf16[1024,512]{1,0:T(8,128)(2,1)}, u32[]{:S(2)}, u32[]{:S(2)}) collective-permute-start(bf16[1024,512]{1,0:T(8,128)(2,1)S(1)} %bitcast.16), channel_id=1, source_target_pairs={{0,1},{1,0},{2,3},{3,2},{4,5},{5,4},{6,7},{7,6},{8,9},{9,8},{10,11... | collective-permute-start | bytes 3145736 | tf_op jit(solution)/shard_map/ppermute | solution.py:200
  102.3 51.6 %collective-permute-start.6 = (bf16[1024,512]{1,0:T(8,128)(2,1)}, bf16[1024,512]{1,0:T(8,128)(2,1)}, u32[]{:S(2)}, u32[]{:S(2)}) collective-permute-start(bf16[1024,512]{1,0:T(8,128)(2,1)} %collective-permute-done.5.refs_6_), channel_id=1, source_target_pairs={{0,1},{1,0},{2,3},{3,2},{4,5},{5,4},{6,7},{7,6},{8,9},{9,8},{10,11... | collective-permute-start | bytes 3145736 | tf_op jit(solution)/shard_map/ppermute | solution.py:200
  107.8 46.1 %collective-permute-start.4 = (bf16[1024,512]{1,0:T(8,128)(2,1)}, bf16[1024,512]{1,0:T(8,128)(2,1)}, u32[]{:S(2)}, u32[]{:S(2)}) collective-permute-start(bf16[1024,512]{1,0:T(8,128)(2,1)} %collective-permute-done.3.refs_4_), channel_id=1, source_target_pairs={{0,1},{1,0},{2,3},{3,2},{4,5},{5,4},{6,7},{7,6},{8,9},{9,8},{10,11... | collective-permute-start | bytes 3145736 | tf_op jit(solution)/shard_map/ppermute | solution.py:200
  117.3 36.6 %collective-permute-start.2 = (bf16[1024,512]{1,0:T(8,128)(2,1)}, bf16[1024,512]{1,0:T(8,128)(2,1)}, u32[]{:S(2)}, u32[]{:S(2)}) collective-permute-start(bf16[1024,512]{1,0:T(8,128)(2,1)} %collective-permute-done.1.refs_2_), channel_id=1, source_target_pairs={{0,1},{1,0},{2,3},{3,2},{4,5},{5,4},{6,7},{7,6},{8,9},{9,8},{10,11... | collective-permute-start | bytes 3145736 | tf_op jit(solution)/shard_map/ppermute | solution.py:200
  150.1 13.4 %collective-permute-start.8 = (bf16[8,32,512]{2,1,0:T(8,128)(2,1)S(1)}, bf16[8,32,512]{2,1,0:T(8,128)(2,1)S(1)}, u32[]{:S(2)}, u32[]{:S(2)}) collective-permute-start(bf16[8,32,512]{2,1,0:T(8,128)(2,1)S(1)} %all_to_all.28), channel_id=1, source_target_pairs={{0,1},{1,0},{2,3},{3,2},{4,5},{5,4},{6,7},{7,6},{8,9},{9,8},{10,11... | collective-permute-start | bytes 786440 | tf_op jit(solution)/shard_map/ppermute | solution.py:237

commit v2 on v1

--- a/solution.py
+++ b/solution.py
@@ -81,7 +81,7 @@
 
 def out_kernel(tok_ref, gain_ref, cot_ref, inv_ref, *refs):
     w_refs, (keys_ref, tg_ref) = refs[:-2], refs[-2:]
-    c, zl = lax.axis_index("c"), lax.axis_index("zl")
+    c, zl, y = (lax.axis_index(name) for name in ("c", "zl", "y"))
     rows, width = tok_ref.shape
     step = width // (ZL * Y)
     half = step // 2
@@ -91,11 +91,11 @@
     def places():
         for s, off in enumerate((0, 1, 3, 2)):
             for h in range(2):
-                for y in range(Y):
-                    node = lax.rem(zl + off, ZL) * Y + y
+                for k in range(Y):
+                    node = lax.rem(zl + off, ZL) * Y + lax.rem(y + k, Y)
                     core = c if h == 0 else 1 - c
                     at = pl.multiple_of(node * step + core * half, half)
-                    yield pl.ds(at, half), w_refs[2 * s + h], slice(y * half, (y + 1) * half)
+                    yield pl.ds(at, half), w_refs[2 * s + h], slice(k * half, (k + 1) * half)
 
     keys = jnp.zeros(keys_ref.shape, F32)
     for cols, w_ref, wrows in places():
@@ -190,14 +190,11 @@
     node_rows = secondary.shape[0]
 
     half = lax.dynamic_slice_in_dim(secondary, c * (node_rows // 2), node_rows // 2, 0)
-    column = to_all(half, "y", Y).reshape(Y * node_rows // 2, keys_w)
+    column = [half] + [lax.ppermute(half, "y", ring(Y, -k)) for k in range(1, Y)]
+    column = jnp.concatenate(column, axis=0)
     z_axes = ("zl", "zh", "c")
     from_up = lax.ppermute(column, z_axes, along_z(lambda c: -1))
     from_down = lax.ppermute(column, z_axes, along_z(lambda c: 1))
-    from_far = lax.ppermute(column, z_axes, along_z(lambda c: 2 - 4 * c))
-    weights = []
-    for block in (column, from_up, from_down, from_far):
-        weights += [block, lax.ppermute(block, "c", ring(C, 1))]
 
     part = width // X
     send, inv = kernel_call(
@@ -208,18 +205,27 @@
         3,
     )(tokens, gain, key_cotangent)
     recv = lax.all_to_all(send, "x", 0, 0, tiled=True).reshape(X * tok_rows, part + keys_w)
+    recv, _ = lax.optimization_barrier((recv, column))
     own, sib = kernel_call(
         grad_kernel,
         (shape((part // 2, keys_w), F32), shape((part // 2, keys_w), BF16)),
-        2 * X * tok_rows * part * keys_w,
-        6 << 20,
+        0,
+        1 << 20,
         1,
     )(recv)
+    sib, column, from_up, from_down = lax.optimization_barrier((sib, column, from_up, from_down))
     sib = lax.ppermute(sib, "c", ring(C, 1))
     summed = (own + sib.astype(F32)).astype(BF16)
+    summed, column, from_up, from_down = lax.optimization_barrier((summed, column, from_up, from_down))
+    from_far = lax.ppermute(column, z_axes, along_z(lambda c: 2 - 4 * c))
+    weights = []
+    for block in (column, from_up, from_down):
+        weights += [block, lax.ppermute(block, "c", ring(C, 1))]
     blocks = lax.all_to_all(summed.reshape(Y, -1, keys_w), "y", 0, 0, tiled=True)
     summed = jnp.sum(blocks.astype(F32), axis=0).astype(BF16)
     blocks = lax.all_to_all(summed.reshape(ZL * ZH, ROWS, keys_w), ("zl", "zh"), 0, 0, tiled=True)
+    blocks, from_far = lax.optimization_barrier((blocks, from_far))
+    weights += [from_far, lax.ppermute(from_far, "c", ring(C, 1))]
     new_master, new_first, new_second, new_rows = kernel_call(
         functools.partial(adam_kernel, tok_rows * math.prod(SIZES)),
         (
@@ -232,13 +238,9 @@
         1 << 20,
         5,
     )(blocks, moment_first, moment_second, master, signs.reshape(1, -1))
+    new_rows, inv = lax.optimization_barrier((new_rows, inv))
 
     mine = to_all(new_rows, ("x", "zh"), X * ZH)
-    other = lax.ppermute(mine, "c", ring(C, 1))
-    even = jnp.where(c == 0, mine, other)
-    odd = jnp.where(c == 0, other, mine)
-    new_secondary = jnp.stack([even, odd], axis=1).reshape(node_rows, keys_w)
-
     keys, token_grad = kernel_call(
         out_kernel,
         (shape((tok_rows, keys_w), BF16), shape(tokens.shape, BF16)),
@@ -246,6 +248,11 @@
         14 << 20,
         4 + len(weights),
     )(tokens, gain, key_cotangent, inv, *weights)
+    mine, keys, token_grad = lax.optimization_barrier((mine, keys, token_grad))
+    other = lax.ppermute(mine, "c", ring(C, 1))
+    even = jnp.where(c == 0, mine, other)
+    odd = jnp.where(c == 0, other, mine)
+    new_secondary = jnp.stack([even, odd], axis=1).reshape(node_rows, keys_w)
     return (keys, token_grad, new_master, new_first, new_second, new_secondary)
 
 

time: 165 us -> 130 us (0.79)
  blocking collectives: 84.2 us -> 0 us
  waiting for transfers between devices: 24.4 us -> 64.5 us
  starting transfers between devices: 31 us -> 35.1 us
  other arithmetic: 2.46 us -> 5.77 us
  local copies, waits for them, and re-layouts: 0.89 us -> 3.02 us
    all_to_all x4 -> x0, blocking collectives: 84.2 us -> none  [the longest x1 35.6 us: shards(): lax.all_to_all(send, 'x', 0, 0, tiled=True)]
    ppermute x1, waiting for transfers between devices: 23.6 us -> 0.01 us  [shards(): from_far = lax.ppermute(column, z_axes, along_z(lambda c: 2 - 4 * c))]
    all_to_all x0 -> x3, waiting for transfers between devices: none -> 23.6 us  [the longest x1 10.1 us: shards(): lax.all_to_all(send, 'x', 0, 0, tiled=True)]
    all_to_all x0 -> x3, starting transfers between devices: none -> 15.5 us  [the longest x1 5.96 us: shards(): lax.all_to_all(summed.reshape(ZL * ZH, ROWS, keys_w), ('zl', 'zh'), 0, 0,...]
    ppermute x0 -> x4, waiting for transfers between devices: none -> 14.3 us  [the longest x3 14.3 us: shards(): lax.ppermute(half, 'y', ring(Y, -k))]
    ppermute x4 -> x3, starting transfers between devices: 15.3 us -> 1.99 us  [shards(): weights += [block, lax.ppermute(block, 'c', ring(C, 1))]]
    all_to_all x1, waiting for transfers between devices: 0.01 us -> 12.4 us  [shards(): lax.all_to_all(summed.reshape(Y, -1, keys_w), 'y', 0, 0, tiled=True)]
    ppermute x0 -> x4, starting transfers between devices: none -> 8.06 us  [the longest x1 4.21 us: shards(): weights += [from_far, lax.ppermute(from_far, 'c', ring(C, 1))]]
  transfers between devices with their start and end apart: 10 -> 16, of which waited for: 2 -> 11; matrix products, arithmetic and copies ran while one was open for 1% -> 3% of each run, Pallas kernels for 7% -> 13%
where the time goes in v2:
time: 130 us
  waiting for transfers between devices  64.5 us (50%)
  starting transfers between devices  35.1 us (27%)
  Pallas kernels  20.7 us (16%)
  other arithmetic  5.77 us (4%)
  local copies, waits for them, and re-layouts  3.02 us (2%)
    ppermute x3, waiting for transfers between devices, shards(): lax.ppermute(half, 'y', ring(Y, -k))  14.3 us
    all_to_all x1, waiting for transfers between devices, shards(): lax.all_to_all(summed.reshape(Y, -1, keys_w), 'y', 0, 0, tiled=True)  12.4 us
    all_to_all x1, waiting for transfers between devices, shards(): lax.all_to_all(send, 'x', 0, 0, tiled=True)  10.1 us
    pallas_call x1, Pallas kernels, shards(): kernel_call(out_kernel, (shape((tok_rows, keys_w), BF16), shape(tokens.sh...  9.6 us
    all_to_all x1, waiting for transfers between devices, shards(): lax.all_to_all(summed.reshape(ZL * ZH, ROWS, keys_w), ('zl', 'zh'), 0, 0,...  8.89 us
    ppermute x1, waiting for transfers between devices, shards(): from_up = lax.ppermute(column, z_axes, along_z(lambda c: -1))  6.94 us
    all_to_all x1, starting transfers between devices, shards(): lax.all_to_all(summed.reshape(ZL * ZH, ROWS, keys_w), ('zl', 'zh'), 0, 0,...  5.96 us
    all_to_all x1, starting transfers between devices, to_all(): return lax.all_to_all(copies, axes, 0, 0, tiled=True)  5.48 us
  transfers between devices with their start and end apart: 16, of which 11 were waited for; matrix products, arithmetic and copies ran while one was open for 3% of the time, Pallas kernels for 13%

profile of v2, /device:TPU:33, one launch (start us, length us, event | category | flops | bytes accessed | tf_op | source)
XLA Modules:
  0.0 129.8 jit_solution(17860884188527555777)
XLA Ops:
  0.6 0.0 copy-start
  0.6 4.2 %shard_map.127 = (bf16[4,128,2560]{2,1,0:T(8,128)(2,1)}, f32[128,128]{1,0:T(8,128)}) custom-call(bf16[128,8192]{1,0:T(8,128)(2,1)} %tok_ref.3, f32[1,8192]{1,0:T(1,128)} %bitcast.14, bf16[128,512]{1,0:T(8,128)(2,1)} %cot_ref.3), custom_call_target="tpu_custom_call" | custom-call | flops 6291456 | bytes 5242880 | tf_op jit(solution)/shard_map/pallas_call | solution.py:200
  4.9 4.0 %all-to-all-start = ((bf16[4,128,2560]{2,1,0:T(8,128)(2,1)}), bf16[4,128,2560]{2,1,0:T(8,128)(2,1)S(1)}, u32[]{:S(2)}, u32[]{:S(2)}) async-start(bf16[4,128,2560]{2,1,0:T(8,128)(2,1)} %get-tuple-element.32), calls=%async_computation | async-start | bytes 5242880 | tf_op jit(solution)/shard_map/all_to_all | solution.py:207
  8.9 0.0 copy-done
  8.9 2.8 %collective-permute-start = (bf16[256,512]{1,0:T(8,128)(2,1)S(1)}, bf16[256,512]{1,0:T(8,128)(2,1)S(1)}, u32[]{:S(2)}, u32[]{:S(2)}) collective-permute-start(bf16[256,512]{1,0:T(8,128)(2,1)S(1)} %constant_dynamic-slice_fusion), channel_id=1, source_target_pairs={{0,48},{16,0},{32,16},{48,32},{1,49},{17,1},{33,17},{49,33},{2,50}... | collective-permute-start | bytes 786440 | tf_op jit(solution)/shard_map/ppermute | solution.py:193
  11.7 0.3 collective-permute-start.1
  12.1 0.7 collective-permute-start.2
  12.8 4.7 %collective-permute-done = bf16[256,512]{1,0:T(8,128)(2,1)S(1)} collective-permute-done((bf16[256,512]{1,0:T(8,128)(2,1)S(1)}, bf16[256,512]{1,0:T(8,128)(2,1)S(1)}, u32[]{:S(2)}, u32[]{:S(2)}) %collective-permute-start) | collective-permute-done | bytes 262176 | tf_op jit(solution)/shard_map/ppermute | solution.py:193
  17.4 2.4 %collective-permute-done.1 = bf16[256,512]{1,0:T(8,128)(2,1)S(1)} collective-permute-done((bf16[256,512]{1,0:T(8,128)(2,1)S(1)}, bf16[256,512]{1,0:T(8,128)(2,1)S(1)}, u32[]{:S(2)}, u32[]{:S(2)}) %collective-permute-start.1) | collective-permute-done | bytes 262176 | tf_op jit(solution)/shard_map/ppermute | solution.py:193
  19.8 7.2 %collective-permute-done.2 = bf16[256,512]{1,0:T(8,128)(2,1)S(1)} collective-permute-done((bf16[256,512]{1,0:T(8,128)(2,1)S(1)}, bf16[256,512]{1,0:T(8,128)(2,1)S(1)}, u32[]{:S(2)}, u32[]{:S(2)}) %collective-permute-start.2) | collective-permute-done | bytes 262176 | tf_op jit(solution)/shard_map/ppermute | solution.py:193
  27.1 1.1 pad_maximum_fusion.refs_0_
  28.1 0.0 collective-permute-start.3
  28.2 1.6 %collective-permute-start.4 = (bf16[1024,512]{1,0:T(8,128)(2,1)}, bf16[1024,512]{1,0:T(8,128)(2,1)}, u32[]{:S(2)}, u32[]{:S(2)}) collective-permute-start(bf16[1024,512]{1,0:T(8,128)(2,1)} %pad_maximum_fusion.refs_0_), channel_id=1, source_target_pairs={{0,64},{1,65},{2,66},{3,67},{64,128},{65,129},{66,130},{67,131},{1... | collective-permute-start | bytes 3145736 | tf_op jit(solution)/shard_map/ppermute | solution.py:197
  29.8 10.1 %all-to-all-done = bf16[4,128,2560]{2,1,0:T(8,128)(2,1)S(1)} async-done(((bf16[4,128,2560]{2,1,0:T(8,128)(2,1)}), bf16[4,128,2560]{2,1,0:T(8,128)(2,1)S(1)}, u32[]{:S(2)}, u32[]{:S(2)}) %all-to-all-start) | async-done | bytes 2621472 | tf_op jit(solution)/shard_map/all_to_all | solution.py:207
  39.9 0.0 copy-start.1
  39.9 1.5 %copy-done.1 = bf16[4,128,2560]{2,1,0:T(8,128)(2,1)} copy-done((bf16[4,128,2560]{2,1,0:T(8,128)(2,1)}, bf16[4,128,2560]{2,1,0:T(8,128)(2,1)S(1)}, u32[]{:S(2)}) %copy-start.1) | copy-done | bytes 2621464
  41.4 4.7 %shard_map.128 = (f32[1024,512]{1,0:T(8,128)}, bf16[1024,512]{1,0:T(8,128)(2,1)}) custom-call(bf16[512,2560]{1,0:T(8,128)(2,1)} %bitcast.12), custom_call_target="tpu_custom_call" | custom-call | bytes 1048576 | tf_op jit(solution)/shard_map/pallas_call | solution.py:209
  46.1 6.9 %collective-permute-done.3.refs_2_ = bf16[1024,512]{1,0:T(8,128)(2,1)} collective-permute-done((bf16[1024,512]{1,0:T(8,128)(2,1)}, bf16[1024,512]{1,0:T(8,128)(2,1)}, u32[]{:S(2)}, u32[]{:S(2)}) %collective-permute-start.3) | collective-permute-done | bytes 1048608 | tf_op jit(solution)/shard_map/ppermute | solution.py:196
  53.1 3.6 %collective-permute-done.4.refs_4_ = bf16[1024,512]{1,0:T(8,128)(2,1)} collective-permute-done((bf16[1024,512]{1,0:T(8,128)(2,1)}, bf16[1024,512]{1,0:T(8,128)(2,1)}, u32[]{:S(2)}, u32[]{:S(2)}) %collective-permute-start.4) | collective-permute-done | bytes 1048608 | tf_op jit(solution)/shard_map/ppermute | solution.py:197
  56.7 1.3 %collective-permute-start.5 = (bf16[1024,512]{1,0:T(8,128)(2,1)}, bf16[1024,512]{1,0:T(8,128)(2,1)S(1)}, u32[]{:S(2)}, u32[]{:S(2)}) collective-permute-start(bf16[1024,512]{1,0:T(8,128)(2,1)} %get-tuple-element.36), channel_id=1, source_target_pairs={{0,1},{1,0},{2,3},{3,2},{4,5},{5,4},{6,7},{7,6},{8,9},{9,8},{10,11... | collective-permute-start | bytes 3145736 | tf_op jit(solution)/shard_map/ppermute | solution.py:217
  58.0 2.5 %collective-permute-done.5 = bf16[1024,512]{1,0:T(8,128)(2,1)S(1)} collective-permute-done((bf16[1024,512]{1,0:T(8,128)(2,1)}, bf16[1024,512]{1,0:T(8,128)(2,1)S(1)}, u32[]{:S(2)}, u32[]{:S(2)}) %collective-permute-start.5) | collective-permute-done | bytes 1048608 | tf_op jit(solution)/shard_map/ppermute | solution.py:217
  60.5 2.9 %add_convert_fusion = bf16[1024,512]{1,0:T(8,128)(2,1)} fusion(f32[1024,512]{1,0:T(8,128)} %get-tuple-element.34, bf16[1024,512]{1,0:T(8,128)(2,1)S(1)} %collective-permute-done.5), kind=kLoop, calls=%fused_computation | loop fusion | flops 1572864 | bytes 4194304 | tf_op jit(solution)/shard_map/convert_element_type | solution.py:218
  63.4 3.5 %all-to-all-start.1 = ((bf16[4,256,512]{2,1,0:T(8,128)(2,1)}), bf16[4,256,512]{2,1,0:T(8,128)(2,1)S(1)}, u32[]{:S(2)}, u32[]{:S(2)}) async-start(bf16[4,256,512]{2,1,0:T(8,128)(2,1)} %bitcast.2), calls=%async_computation.1 | async-start | bytes 2097152 | tf_op jit(solution)/shard_map/all_to_all | solution.py:224
  66.9 2.4 %collective-permute-start.6 = (bf16[1024,512]{1,0:T(8,128)(2,1)}, bf16[1024,512]{1,0:T(8,128)(2,1)S(1)}, u32[]{:S(2)}, u32[]{:S(2)}) collective-permute-start(bf16[1024,512]{1,0:T(8,128)(2,1)} %pad_maximum_fusion.refs_0_), channel_id=1, source_target_pairs={{0,128},{1,131},{2,130},{3,129},{64,192},{65,195},{66,194},{67,193... | collective-permute-start | bytes 3145736 | tf_op jit(solution)/shard_map/ppermute | solution.py:220
  69.4 12.4 %all-to-all-done.1 = bf16[4,256,512]{2,1,0:T(8,128)(2,1)S(1)} async-done(((bf16[4,256,512]{2,1,0:T(8,128)(2,1)}), bf16[4,256,512]{2,1,0:T(8,128)(2,1)S(1)}, u32[]{:S(2)}, u32[]{:S(2)}) %all-to-all-start.1) | async-done | bytes 1048608 | tf_op jit(solution)/shard_map/all_to_all | solution.py:224
  81.8 0.9 reduce_sum.12
  82.7 6.0 %all-to-all-start.2 = ((bf16[8,32,512]{2,1,0:T(8,128)(2,1)}), bf16[8,32,512]{2,1,0:T(8,128)(2,1)S(1)}, u32[]{:S(2)}, u32[]{:S(2)}) async-start(bf16[8,32,512]{2,1,0:T(8,128)(2,1)} %bitcast.3), calls=%async_computation.2 | async-start | bytes 524288 | tf_op jit(solution)/shard_map/all_to_all | solution.py:226
  88.6 1.5 %collective-permute-start.7 = (bf16[1024,512]{1,0:T(8,128)(2,1)}, bf16[1024,512]{1,0:T(8,128)(2,1)}, u32[]{:S(2)}, u32[]{:S(2)}) collective-permute-start(bf16[1024,512]{1,0:T(8,128)(2,1)} %pad_maximum_fusion.refs_0_), channel_id=1, source_target_pairs={{0,1},{1,0},{2,3},{3,2},{4,5},{5,4},{6,7},{7,6},{8,9},{9,8},{10,11... | collective-permute-start | bytes 3145736 | tf_op jit(solution)/shard_map/ppermute | solution.py:223
  90.1 0.0 collective-permute-start.8
  90.1 0.5 collective-permute-start.9
  90.6 0.0 collective-permute-done.6.refs_6_
  90.6 0.0 copy-start.3
  90.6 8.9 %all-to-all-done.2.recv_ref = bf16[8,32,512]{2,1,0:T(8,128)(2,1)S(1)} async-done(((bf16[8,32,512]{2,1,0:T(8,128)(2,1)}), bf16[8,32,512]{2,1,0:T(8,128)(2,1)S(1)}, u32[]{:S(2)}, u32[]{:S(2)}) %all-to-all-start.2) | async-done | bytes 262176 | tf_op jit(solution)/shard_map/all_to_all | solution.py:226
  99.5 0.0 copy-start.2
  99.5 4.2 %collective-permute-start.10 = (bf16[1024,512]{1,0:T(8,128)(2,1)S(1)}, bf16[1024,512]{1,0:T(8,128)(2,1)}, u32[]{:S(2)}, u32[]{:S(2)}) collective-permute-start(bf16[1024,512]{1,0:T(8,128)(2,1)S(1)} %collective-permute-done.6.refs_6_), channel_id=1, source_target_pairs={{0,1},{1,0},{2,3},{3,2},{4,5},{5,4},{6,7},{7,6},{8,9},{9,8},{10,11... | collective-permute-start | bytes 3145736 | tf_op jit(solution)/shard_map/ppermute | solution.py:228
  103.7 0.0 copy-done.2
  103.7 2.1 %shard_map.129 = (f32[32,512]{1,0:T(8,128)}, f32[16,1024]{1,0:T(8,128)}, f32[16,1024]{1,0:T(8,128)}, bf16[32,512]{1,0:T(8,128)(2,1)}) custom-call(bf16[8,32,512]{2,1,0:T(8,128)(2,1)} %copy-done.2, f32[16,1024]{1,0:T(8,128)} %first_ref.1, f32[16,1024]{1,0:T(8,128)} %second_ref.1, f32[32,512]{1,0:T(8,128)} %master_ref.1, s32[1,1024]{1,0:T(1,128)} %bitcast.16), custom_call_target="tpu_custom_call" | custom-call | flops 33554432 | bytes 1048576 | tf_op jit(solution)/shard_map/pallas_call | solution.py:229
  105.9 1.5 %broadcast_in_dim.3 = bf16[8,32,512]{2,1,0:T(8,128)(2,1)} broadcast(bf16[32,512]{1,0:T(8,128)(2,1)} %get-tuple-element.45), dimensions={1,2} | broadcast | bytes 294912 | tf_op jit(solution)/shard_map/broadcast_in_dim | solution.py:181
  107.3 5.5 %all-to-all-start.3 = ((bf16[8,32,512]{2,1,0:T(8,128)(2,1)}), bf16[8,32,512]{2,1,0:T(8,128)(2,1)S(1)}, u32[]{:S(2)}, u32[]{:S(2)}) async-start(bf16[8,32,512]{2,1,0:T(8,128)(2,1)} %broadcast_in_dim.3), calls=%async_computation.3 | async-start | bytes 524288 | tf_op jit(solution)/shard_map/all_to_all | solution.py:182
  112.8 0.0 collective-permute-done.7.refs_1_
  112.8 0.0 collective-permute-done.8.refs_3_
  112.8 0.0 collective-permute-done.9.refs_5_
  112.8 0.0 collective-permute-done.10.refs_7_
  112.8 0.0 copy-done.3
  112.9 9.6 %shard_map.130 = (bf16[128,512]{1,0:T(8,128)(2,1)}, bf16[128,8192]{1,0:T(8,128)(2,1)}) custom-call(bf16[128,8192]{1,0:T(8,128)(2,1)} %tok_ref.3, f32[1,8192]{1,0:T(1,128)} %bitcast.15, bf16[128,512]{1,0:T(8,128)(2,1)} %cot_ref.3, f32[128,128]{1,0:T(8,128)} %get-tuple-element.46.inv_ref, bf16[1024,512]{1,0:T(8,128)(2,1)} %pad_maximum_fusion.refs_0_, ...), custom_call_target="tpu_custom_call" | custom-call | flops 2147483648 | bytes 14680064 | tf_op jit(solution)/shard_map/pallas_call | solution.py:244
  122.5 4.6 %all-to-all-done.3 = bf16[8,32,512]{2,1,0:T(8,128)(2,1)S(1)} async-done(((bf16[8,32,512]{2,1,0:T(8,128)(2,1)}), bf16[8,32,512]{2,1,0:T(8,128)(2,1)S(1)}, u32[]{:S(2)}, u32[]{:S(2)}) %all-to-all-start.3) | async-done | bytes 262176 | tf_op jit(solution)/shard_map/all_to_all | solution.py:182
  127.0 0.7 collective-permute-start.11
  127.8 1.2 collective-permute-done.11
  129.0 0.8 pad_maximum_fusion.1
  (2 shorter events, 0.1 us)
Async XLA Ops:
  0.6 8.2 %copy-start = (bf16[512,512]{1,0:T(8,128)(2,1)S(1)}, bf16[512,512]{1,0:T(8,128)(2,1)}, u32[]{:S(2)}) copy-start(bf16[512,512]{1,0:T(8,128)(2,1)} %param.11) | copy-start | bytes 1572868
  4.9 35.1 %all-to-all-start = ((bf16[4,128,2560]{2,1,0:T(8,128)(2,1)}), bf16[4,128,2560]{2,1,0:T(8,128)(2,1)S(1)}, u32[]{:S(2)}, u32[]{:S(2)}) async-start(bf16[4,128,2560]{2,1,0:T(8,128)(2,1)} %get-tuple-element.32), calls=%async_computation | async-start | bytes 5242880 | tf_op jit(solution)/shard_map/all_to_all | solution.py:207
  8.9 8.5 %collective-permute-start = (bf16[256,512]{1,0:T(8,128)(2,1)S(1)}, bf16[256,512]{1,0:T(8,128)(2,1)S(1)}, u32[]{:S(2)}, u32[]{:S(2)}) collective-permute-start(bf16[256,512]{1,0:T(8,128)(2,1)S(1)} %constant_dynamic-slice_fusion), channel_id=1, source_target_pairs={{0,48},{16,0},{32,16},{48,32},{1,49},{17,1},{33,17},{49,33},{2,50}... | collective-permute-start | bytes 786440 | tf_op jit(solution)/shard_map/ppermute | solution.py:193
  11.7 8.1 %collective-permute-start.1 = (bf16[256,512]{1,0:T(8,128)(2,1)S(1)}, bf16[256,512]{1,0:T(8,128)(2,1)S(1)}, u32[]{:S(2)}, u32[]{:S(2)}) collective-permute-start(bf16[256,512]{1,0:T(8,128)(2,1)S(1)} %constant_dynamic-slice_fusion), channel_id=1, source_target_pairs={{0,32},{16,48},{32,0},{48,16},{1,33},{17,49},{33,1},{49,17},{2,34}... | collective-permute-start | bytes 786440 | tf_op jit(solution)/shard_map/ppermute | solution.py:193
  12.1 15.0 %collective-permute-start.2 = (bf16[256,512]{1,0:T(8,128)(2,1)S(1)}, bf16[256,512]{1,0:T(8,128)(2,1)S(1)}, u32[]{:S(2)}, u32[]{:S(2)}) collective-permute-start(bf16[256,512]{1,0:T(8,128)(2,1)S(1)} %constant_dynamic-slice_fusion), channel_id=1, source_target_pairs={{0,16},{16,32},{32,48},{48,0},{1,17},{17,33},{33,49},{49,1},{2,18}... | collective-permute-start | bytes 786440 | tf_op jit(solution)/shard_map/ppermute | solution.py:193
  28.1 24.9 %collective-permute-start.3 = (bf16[1024,512]{1,0:T(8,128)(2,1)}, bf16[1024,512]{1,0:T(8,128)(2,1)}, u32[]{:S(2)}, u32[]{:S(2)}) collective-permute-start(bf16[1024,512]{1,0:T(8,128)(2,1)} %pad_maximum_fusion.refs_0_), channel_id=1, source_target_pairs={{0,194},{1,195},{2,192},{3,193},{64,0},{65,1},{66,2},{67,3},{128,6... | collective-permute-start | bytes 3145736 | tf_op jit(solution)/shard_map/ppermute | solution.py:196
  28.2 28.5 %collective-permute-start.4 = (bf16[1024,512]{1,0:T(8,128)(2,1)}, bf16[1024,512]{1,0:T(8,128)(2,1)}, u32[]{:S(2)}, u32[]{:S(2)}) collective-permute-start(bf16[1024,512]{1,0:T(8,128)(2,1)} %pad_maximum_fusion.refs_0_), channel_id=1, source_target_pairs={{0,64},{1,65},{2,66},{3,67},{64,128},{65,129},{66,130},{67,131},{1... | collective-permute-start | bytes 3145736 | tf_op jit(solution)/shard_map/ppermute | solution.py:197
  39.9 1.5 %copy-start.1 = (bf16[4,128,2560]{2,1,0:T(8,128)(2,1)}, bf16[4,128,2560]{2,1,0:T(8,128)(2,1)S(1)}, u32[]{:S(2)}) copy-start(bf16[4,128,2560]{2,1,0:T(8,128)(2,1)S(1)} %all-to-all-done) | copy-start | bytes 7864324
  56.7 3.8 %collective-permute-start.5 = (bf16[1024,512]{1,0:T(8,128)(2,1)}, bf16[1024,512]{1,0:T(8,128)(2,1)S(1)}, u32[]{:S(2)}, u32[]{:S(2)}) collective-permute-start(bf16[1024,512]{1,0:T(8,128)(2,1)} %get-tuple-element.36), channel_id=1, source_target_pairs={{0,1},{1,0},{2,3},{3,2},{4,5},{5,4},{6,7},{7,6},{8,9},{9,8},{10,11... | collective-permute-start | bytes 3145736 | tf_op jit(solution)/shard_map/ppermute | solution.py:217
  63.4 18.3 %all-to-all-start.1 = ((bf16[4,256,512]{2,1,0:T(8,128)(2,1)}), bf16[4,256,512]{2,1,0:T(8,128)(2,1)S(1)}, u32[]{:S(2)}, u32[]{:S(2)}) async-start(bf16[4,256,512]{2,1,0:T(8,128)(2,1)} %bitcast.2), calls=%async_computation.1 | async-start | bytes 2097152 | tf_op jit(solution)/shard_map/all_to_all | solution.py:224
  66.9 23.7 %collective-permute-start.6 = (bf16[1024,512]{1,0:T(8,128)(2,1)}, bf16[1024,512]{1,0:T(8,128)(2,1)S(1)}, u32[]{:S(2)}, u32[]{:S(2)}) collective-permute-start(bf16[1024,512]{1,0:T(8,128)(2,1)} %pad_maximum_fusion.refs_0_), channel_id=1, source_target_pairs={{0,128},{1,131},{2,130},{3,129},{64,192},{65,195},{66,194},{67,193... | collective-permute-start | bytes 3145736 | tf_op jit(solution)/shard_map/ppermute | solution.py:220
  82.7 16.8 %all-to-all-start.2 = ((bf16[8,32,512]{2,1,0:T(8,128)(2,1)}), bf16[8,32,512]{2,1,0:T(8,128)(2,1)S(1)}, u32[]{:S(2)}, u32[]{:S(2)}) async-start(bf16[8,32,512]{2,1,0:T(8,128)(2,1)} %bitcast.3), calls=%async_computation.2 | async-start | bytes 524288 | tf_op jit(solution)/shard_map/all_to_all | solution.py:226
  88.6 24.2 %collective-permute-start.7 = (bf16[1024,512]{1,0:T(8,128)(2,1)}, bf16[1024,512]{1,0:T(8,128)(2,1)}, u32[]{:S(2)}, u32[]{:S(2)}) collective-permute-start(bf16[1024,512]{1,0:T(8,128)(2,1)} %pad_maximum_fusion.refs_0_), channel_id=1, source_target_pairs={{0,1},{1,0},{2,3},{3,2},{4,5},{5,4},{6,7},{7,6},{8,9},{9,8},{10,11... | collective-permute-start | bytes 3145736 | tf_op jit(solution)/shard_map/ppermute | solution.py:223
  90.1 22.7 %collective-permute-start.8 = (bf16[1024,512]{1,0:T(8,128)(2,1)}, bf16[1024,512]{1,0:T(8,128)(2,1)}, u32[]{:S(2)}, u32[]{:S(2)}) collective-permute-start(bf16[1024,512]{1,0:T(8,128)(2,1)} %collective-permute-done.3.refs_2_), channel_id=1, source_target_pairs={{0,1},{1,0},{2,3},{3,2},{4,5},{5,4},{6,7},{7,6},{8,9},{9,8},{10,11... | collective-permute-start | bytes 3145736 | tf_op jit(solution)/shard_map/ppermute | solution.py:223
  90.1 22.7 %collective-permute-start.9 = (bf16[1024,512]{1,0:T(8,128)(2,1)}, bf16[1024,512]{1,0:T(8,128)(2,1)}, u32[]{:S(2)}, u32[]{:S(2)}) collective-permute-start(bf16[1024,512]{1,0:T(8,128)(2,1)} %collective-permute-done.4.refs_4_), channel_id=1, source_target_pairs={{0,1},{1,0},{2,3},{3,2},{4,5},{5,4},{6,7},{7,6},{8,9},{9,8},{10,11... | collective-permute-start | bytes 3145736 | tf_op jit(solution)/shard_map/ppermute | solution.py:223
  90.6 22.2 %copy-start.3 = (bf16[1024,512]{1,0:T(8,128)(2,1)}, bf16[1024,512]{1,0:T(8,128)(2,1)S(1)}, u32[]{:S(2)}) copy-start(bf16[1024,512]{1,0:T(8,128)(2,1)S(1)} %collective-permute-done.6.refs_6_) | copy-start | bytes 3145732
  99.5 4.2 %copy-start.2 = (bf16[8,32,512]{2,1,0:T(8,128)(2,1)}, bf16[8,32,512]{2,1,0:T(8,128)(2,1)S(1)}, u32[]{:S(2)}) copy-start(bf16[8,32,512]{2,1,0:T(8,128)(2,1)S(1)} %all-to-all-done.2.recv_ref) | copy-start | bytes 786436
  99.5 13.3 %collective-permute-start.10 = (bf16[1024,512]{1,0:T(8,128)(2,1)S(1)}, bf16[1024,512]{1,0:T(8,128)(2,1)}, u32[]{:S(2)}, u32[]{:S(2)}) collective-permute-start(bf16[1024,512]{1,0:T(8,128)(2,1)S(1)} %collective-permute-done.6.refs_6_), channel_id=1, source_target_pairs={{0,1},{1,0},{2,3},{3,2},{4,5},{5,4},{6,7},{7,6},{8,9},{9,8},{10,11... | collective-permute-start | bytes 3145736 | tf_op jit(solution)/shard_map/ppermute | solution.py:228
  107.3 19.7 %all-to-all-start.3 = ((bf16[8,32,512]{2,1,0:T(8,128)(2,1)}), bf16[8,32,512]{2,1,0:T(8,128)(2,1)S(1)}, u32[]{:S(2)}, u32[]{:S(2)}) async-start(bf16[8,32,512]{2,1,0:T(8,128)(2,1)} %broadcast_in_dim.3), calls=%async_computation.3 | async-start | bytes 524288 | tf_op jit(solution)/shard_map/all_to_all | solution.py:182
  127.0 1.9 %collective-permute-start.11 = (bf16[8,32,512]{2,1,0:T(8,128)(2,1)S(1)}, bf16[8,32,512]{2,1,0:T(8,128)(2,1)S(1)}, u32[]{:S(2)}, u32[]{:S(2)}) collective-permute-start(bf16[8,32,512]{2,1,0:T(8,128)(2,1)S(1)} %all-to-all-done.3), channel_id=1, source_target_pairs={{0,1},{1,0},{2,3},{3,2},{4,5},{5,4},{6,7},{7,6},{8,9},{9,8},{10,11... | collective-permute-start | bytes 786440 | tf_op jit(solution)/shard_map/ppermute | solution.py:252

commit v3 on v2

--- a/solution.py
+++ b/solution.py
@@ -31,14 +31,14 @@
     return jax.ShapeDtypeStruct(dims, kind)
 
 
-def kernel_call(body, outs, flops, nbytes, n_in):
+def kernel_call(body, outs, flops, nbytes, n_in, limit=24 << 20):
     return pl.pallas_call(
         body,
         out_shape=outs,
         in_specs=[VMEM] * n_in,
         out_specs=jax.tree.map(lambda _: VMEM, outs),
         cost_estimate=pl.CostEstimate(flops=flops, bytes_accessed=nbytes, transcendentals=0),
-        compiler_params=pltpu.CompilerParams(vmem_limit_bytes=56 << 20),
+        compiler_params=pltpu.CompilerParams(vmem_limit_bytes=limit),
     )
 
 
@@ -62,7 +62,7 @@
         send_ref[x, :, ZL * Y * part :] = cot_ref[...]
 
 
-def grad_kernel(recv_ref, own_ref, sib_ref):
+def grad_kernel(recv_ref, own_ref, sib_a_ref, sib_b_ref):
     c = lax.axis_index("c")
     part = ZH * C * ROWS
     cols = ZL * Y * part
@@ -75,7 +75,8 @@
                 at = y * part + zh * C * ROWS
                 first, second = grad[at : at + ROWS], grad[at + ROWS : at + 2 * ROWS]
                 to = ((y * ZL + zl) * ZH + zh) * ROWS
-                own_ref[to : to + ROWS, :] = jnp.where(c == 0, first, second)
+                own_ref[to : to + ROWS, :] = jnp.where(c == 0, first, second).astype(BF16)
+                sib_ref, to = (sib_a_ref, to) if y < Y // 2 else (sib_b_ref, to - Y // 2 * ZL * ZH * ROWS)
                 sib_ref[to : to + ROWS, :] = jnp.where(c == 0, second, first).astype(BF16)
 
 
@@ -160,7 +161,7 @@
     master = master_ref[...]
     new_master = master - learn_rate * (update + weight_decay * master)
     nm_ref[...] = new_master
-    new_ref[...] = new_master.astype(BF16)
+    new_ref[...] = jnp.broadcast_to(new_master.astype(BF16), new_ref.shape)
 
 
 def ring(n, s):
@@ -177,11 +178,6 @@
     return pairs
 
 
-def to_all(value, axes, n):
-    copies = jnp.broadcast_to(value, (n, *value.shape))
-    return lax.all_to_all(copies, axes, 0, 0, tiled=True)
-
-
 def shards(tokens, norm_gain, key_cotangent, secondary, master, moment_first, moment_second, signs):
     tok_rows, width = tokens.shape
     keys_w = key_cotangent.shape[1]
@@ -197,50 +193,39 @@
     from_down = lax.ppermute(column, z_axes, along_z(lambda c: 1))
 
     part = width // X
-    send, inv = kernel_call(
+    step = 32
+    by_rows = lambda cols: pl.BlockSpec((step, cols), lambda i: (i, 0))
+    send, inv = pl.pallas_call(
         norm_kernel,
-        (shape((X, tok_rows, part + keys_w), BF16), shape((tok_rows, 128), F32)),
-        tok_rows * width * 6,
-        5 << 20,
-        3,
+        out_shape=(shape((X, tok_rows, part + keys_w), BF16), shape((tok_rows, 128), F32)),
+        grid=(tok_rows // step,),
+        in_specs=[by_rows(width), pl.BlockSpec((1, width), lambda i: (0, 0)), by_rows(keys_w)],
+        out_specs=(pl.BlockSpec((X, step, part + keys_w), lambda i: (0, i, 0)), by_rows(128)),
+        cost_estimate=pl.CostEstimate(flops=tok_rows * width * 6, bytes_accessed=5 << 20, transcendentals=0),
+        compiler_params=pltpu.CompilerParams(vmem_limit_bytes=56 << 20),
     )(tokens, gain, key_cotangent)
     recv = lax.all_to_all(send, "x", 0, 0, tiled=True).reshape(X * tok_rows, part + keys_w)
     recv, _ = lax.optimization_barrier((recv, column))
-    own, sib = kernel_call(
+    own, *sib = kernel_call(
         grad_kernel,
-        (shape((part // 2, keys_w), F32), shape((part // 2, keys_w), BF16)),
+        (shape((part // 2, keys_w), BF16),) + (shape((part // 4, keys_w), BF16),) * 2,
         0,
         1 << 20,
         1,
     )(recv)
-    sib, column, from_up, from_down = lax.optimization_barrier((sib, column, from_up, from_down))
-    sib = lax.ppermute(sib, "c", ring(C, 1))
-    summed = (own + sib.astype(F32)).astype(BF16)
+    sib = [lax.ppermute(piece, "c", ring(C, 1)) for piece in sib]
+    summed = (own.astype(F32) + jnp.concatenate(sib, axis=0).astype(F32)).astype(BF16)
     summed, column, from_up, from_down = lax.optimization_barrier((summed, column, from_up, from_down))
-    from_far = lax.ppermute(column, z_axes, along_z(lambda c: 2 - 4 * c))
+    from_far = jnp.where(c == 0, from_up, from_down)
+    from_far = lax.ppermute(from_far, z_axes, along_z(lambda c: 2 * c - 1))
     weights = []
     for block in (column, from_up, from_down):
         weights += [block, lax.ppermute(block, "c", ring(C, 1))]
     blocks = lax.all_to_all(summed.reshape(Y, -1, keys_w), "y", 0, 0, tiled=True)
+    blocks, from_far = lax.optimization_barrier((blocks, from_far))
+    weights += [from_far, lax.ppermute(from_far, "c", ring(C, 1))]
     summed = jnp.sum(blocks.astype(F32), axis=0).astype(BF16)
     blocks = lax.all_to_all(summed.reshape(ZL * ZH, ROWS, keys_w), ("zl", "zh"), 0, 0, tiled=True)
-    blocks, from_far = lax.optimization_barrier((blocks, from_far))
-    weights += [from_far, lax.ppermute(from_far, "c", ring(C, 1))]
-    new_master, new_first, new_second, new_rows = kernel_call(
-        functools.partial(adam_kernel, tok_rows * math.prod(SIZES)),
-        (
-            shape(master.shape, F32),
-            shape(moment_first.shape, F32),
-            shape(moment_second.shape, F32),
-            shape(master.shape, BF16),
-        ),
-        1 << 25,
-        1 << 20,
-        5,
-    )(blocks, moment_first, moment_second, master, signs.reshape(1, -1))
-    new_rows, inv = lax.optimization_barrier((new_rows, inv))
-
-    mine = to_all(new_rows, ("x", "zh"), X * ZH)
     keys, token_grad = kernel_call(
         out_kernel,
         (shape((tok_rows, keys_w), BF16), shape(tokens.shape, BF16)),
@@ -248,7 +233,21 @@
         14 << 20,
         4 + len(weights),
     )(tokens, gain, key_cotangent, inv, *weights)
-    mine, keys, token_grad = lax.optimization_barrier((mine, keys, token_grad))
+    blocks, keys, token_grad = lax.optimization_barrier((blocks, keys, token_grad))
+    new_master, new_first, new_second, new_rows = kernel_call(
+        functools.partial(adam_kernel, tok_rows * math.prod(SIZES)),
+        (
+            shape(master.shape, F32),
+            shape(moment_first.shape, F32),
+            shape(moment_second.shape, F32),
+            shape((X * ZH, *master.shape), BF16),
+        ),
+        1 << 25,
+        1 << 20,
+        5,
+    )(blocks, moment_first, moment_second, master, signs.reshape(1, -1))
+
+    mine = lax.all_to_all(new_rows, ("x", "zh"), 0, 0, tiled=True)
     other = lax.ppermute(mine, "c", ring(C, 1))
     even = jnp.where(c == 0, mine, other)
     odd = jnp.where(c == 0, other, mine)

time: 130 us -> 120 us (0.923)
  waiting for transfers between devices: 64.5 us -> 40.9 us
  blocking collectives: 0 us -> 20.6 us
  starting transfers between devices: 35.1 us -> 30.5 us
  Pallas kernels: 20.7 us -> 16.8 us
  other arithmetic: 5.77 us -> 8.19 us
    all_to_all x0 -> x1, blocking collectives: none -> 20.6 us  [shards(): mine = lax.all_to_all(new_rows, ('x', 'zh'), 0, 0, tiled=True)]
    all_to_all x1, waiting for transfers between devices: 8.89 us -> 1.59 us  [shards(): lax.all_to_all(summed.reshape(ZL * ZH, ROWS, keys_w), ('zl', 'zh'), 0, 0,...]
    ppermute x1, waiting for transfers between devices: 6.94 us -> 0.01 us  [shards(): from_up = lax.ppermute(column, z_axes, along_z(lambda c: -1))]
    all_to_all x1 -> x0, starting transfers between devices: 5.48 us -> none  [to_all(): return lax.all_to_all(copies, axes, 0, 0, tiled=True)]
    all_to_all x1 -> x0, waiting for transfers between devices: 4.58 us -> none  [to_all(): return lax.all_to_all(copies, axes, 0, 0, tiled=True)]
    ppermute x3, waiting for transfers between devices: 14.3 us -> 9.94 us  [shards(): lax.ppermute(half, 'y', ring(Y, -k))]
    ppermute x1, waiting for transfers between devices: 3.61 us -> 0.01 us  [shards(): from_down = lax.ppermute(column, z_axes, along_z(lambda c: 1))]
    all_to_all x1, waiting for transfers between devices: 10.1 us -> 13.3 us  [shards(): lax.all_to_all(send, 'x', 0, 0, tiled=True)]
  transfers between devices with their start and end apart: 16 -> 16, of which waited for: 11 -> 8; matrix products, arithmetic and copies ran while one was open for 3% -> 5% of each run, Pallas kernels for 13% -> 9%
where the time goes in v3:
time: 120 us
  waiting for transfers between devices  40.9 us (34%)
  starting transfers between devices  30.5 us (25%)
  blocking collectives  20.6 us (17%)
  Pallas kernels  16.8 us (14%)
  other arithmetic  8.19 us (7%)
  local copies, waits for them, and re-layouts  1.86 us (2%)
    all_to_all x1, blocking collectives, shards(): mine = lax.all_to_all(new_rows, ('x', 'zh'), 0, 0, tiled=True)  20.6 us
    all_to_all x1, waiting for transfers between devices, shards(): lax.all_to_all(send, 'x', 0, 0, tiled=True)  13.3 us
    all_to_all x1, waiting for transfers between devices, shards(): lax.all_to_all(summed.reshape(Y, -1, keys_w), 'y', 0, 0, tiled=True)  12.4 us
    ppermute x3, waiting for transfers between devices, shards(): lax.ppermute(half, 'y', ring(Y, -k))  9.94 us
    pallas_call x1, Pallas kernels, shards(): kernel_call(out_kernel, (shape((tok_rows, keys_w), BF16), shape(tokens.sh...  8.99 us
    all_to_all x1, starting transfers between devices, shards(): lax.all_to_all(summed.reshape(Y, -1, keys_w), 'y', 0, 0, tiled=True)  5.97 us
    ppermute x3, starting transfers between devices, shards(): lax.ppermute(half, 'y', ring(Y, -k))  5.06 us
    all_to_all x1, starting transfers between devices, shards(): lax.all_to_all(summed.reshape(ZL * ZH, ROWS, keys_w), ('zl', 'zh'), 0, 0,...  4.95 us
  transfers between devices with their start and end apart: 16, of which 8 were waited for; matrix products, arithmetic and copies ran while one was open for 5% of the time, Pallas kernels for 9%

profile of v3, /device:TPU:33, one launch (start us, length us, event | category | flops | bytes accessed | tf_op | source)
XLA Modules:
  0.0 119.6 jit_solution(9446887931363153235)
XLA Ops:
  0.6 0.0 copy-start
  0.6 4.5 %shard_map.127 = (bf16[4,128,2560]{2,1,0:T(8,128)(2,1)}, f32[128,128]{1,0:T(8,128)}) custom-call(bf16[128,8192]{1,0:T(8,128)(2,1)} %tok_ref.3, f32[1,8192]{1,0:T(1,128)} %bitcast.11, bf16[128,512]{1,0:T(8,128)(2,1)} %cot_ref.3), custom_call_target="tpu_custom_call" | custom-call | flops 6291456 | bytes 5242880 | tf_op jit(solution)/shard_map/pallas_call | solution.py:198
  5.1 4.0 %all-to-all-start = ((bf16[4,128,2560]{2,1,0:T(8,128)(2,1)}), bf16[4,128,2560]{2,1,0:T(8,128)(2,1)S(1)}, u32[]{:S(2)}, u32[]{:S(2)}) async-start(bf16[4,128,2560]{2,1,0:T(8,128)(2,1)} %get-tuple-element.27), calls=%async_computation | async-start | bytes 5242880 | tf_op jit(solution)/shard_map/all_to_all | solution.py:207
  9.1 0.0 copy-done
  9.1 1.4 %collective-permute-start.2 = (bf16[256,512]{1,0:T(8,128)(2,1)S(1)}, bf16[256,512]{1,0:T(8,128)(2,1)S(1)}, u32[]{:S(2)}, u32[]{:S(2)}) collective-permute-start(bf16[256,512]{1,0:T(8,128)(2,1)S(1)} %constant_dynamic-slice_fusion), channel_id=1, source_target_pairs={{0,16},{16,32},{32,48},{48,0},{1,17},{17,33},{33,49},{49,1},{2,18}... | collective-permute-start | bytes 786440 | tf_op jit(solution)/shard_map/ppermute | solution.py:189
  10.5 2.6 %collective-permute-start.1 = (bf16[256,512]{1,0:T(8,128)(2,1)S(1)}, bf16[256,512]{1,0:T(8,128)(2,1)S(1)}, u32[]{:S(2)}, u32[]{:S(2)}) collective-permute-start(bf16[256,512]{1,0:T(8,128)(2,1)S(1)} %constant_dynamic-slice_fusion), channel_id=1, source_target_pairs={{0,32},{16,48},{32,0},{48,16},{1,33},{17,49},{33,1},{49,17},{2,34}... | collective-permute-start | bytes 786440 | tf_op jit(solution)/shard_map/ppermute | solution.py:189
  13.1 1.1 collective-permute-start
  14.2 3.2 %collective-permute-done.2 = bf16[256,512]{1,0:T(8,128)(2,1)S(1)} collective-permute-done((bf16[256,512]{1,0:T(8,128)(2,1)S(1)}, bf16[256,512]{1,0:T(8,128)(2,1)S(1)}, u32[]{:S(2)}, u32[]{:S(2)}) %collective-permute-start.2) | collective-permute-done | bytes 262176 | tf_op jit(solution)/shard_map/ppermute | solution.py:189
  17.4 6.7 %collective-permute-done.1 = bf16[256,512]{1,0:T(8,128)(2,1)S(1)} collective-permute-done((bf16[256,512]{1,0:T(8,128)(2,1)S(1)}, bf16[256,512]{1,0:T(8,128)(2,1)S(1)}, u32[]{:S(2)}, u32[]{:S(2)}) %collective-permute-start.1) | collective-permute-done | bytes 262176 | tf_op jit(solution)/shard_map/ppermute | solution.py:189
  24.1 0.0 collective-permute-done
  24.1 1.1 pad_maximum_fusion.refs_0_
  25.2 1.6 %collective-permute-start.6 = (bf16[1024,512]{1,0:T(8,128)(2,1)}, bf16[1024,512]{1,0:T(8,128)(2,1)}, u32[]{:S(2)}, u32[]{:S(2)}) collective-permute-start(bf16[1024,512]{1,0:T(8,128)(2,1)} %pad_maximum_fusion.refs_0_), channel_id=1, source_target_pairs={{0,64},{1,65},{2,66},{3,67},{64,128},{65,129},{66,130},{67,131},{1... | collective-permute-start | bytes 3145736 | tf_op jit(solution)/shard_map/ppermute | solution.py:193
  26.8 0.0 collective-permute-start.5
  26.8 13.3 %all-to-all-done = bf16[4,128,2560]{2,1,0:T(8,128)(2,1)S(1)} async-done(((bf16[4,128,2560]{2,1,0:T(8,128)(2,1)}), bf16[4,128,2560]{2,1,0:T(8,128)(2,1)S(1)}, u32[]{:S(2)}, u32[]{:S(2)}) %all-to-all-start) | async-done | bytes 2621472 | tf_op jit(solution)/shard_map/all_to_all | solution.py:207
  40.2 2.2 %shard_map.128 = (bf16[1024,512]{1,0:T(8,128)(2,1)S(1)}, bf16[512,512]{1,0:T(8,128)(2,1)}, bf16[512,512]{1,0:T(8,128)(2,1)}) custom-call(bf16[512,2560]{1,0:T(8,128)(2,1)S(1)} %bitcast.10), custom_call_target="tpu_custom_call" | custom-call | bytes 1048576 | tf_op jit(solution)/shard_map/pallas_call | solution.py:209
  42.4 0.0 copy-start.2
  42.4 1.0 copy-done.2
  43.3 1.9 %collective-permute-start.3 = (bf16[512,512]{1,0:T(8,128)(2,1)}, bf16[512,512]{1,0:T(8,128)(2,1)S(1)}, u32[]{:S(2)}, u32[]{:S(2)}) collective-permute-start(bf16[512,512]{1,0:T(8,128)(2,1)} %get-tuple-element.30), channel_id=1, source_target_pairs={{0,1},{1,0},{2,3},{3,2},{4,5},{5,4},{6,7},{7,6},{8,9},{9,8},{10,11... | collective-permute-start | bytes 1572872 | tf_op jit(solution)/shard_map/ppermute | solution.py:216
  45.2 0.0 collective-permute-start.4
  45.2 1.7 %collective-permute-done.3 = bf16[512,512]{1,0:T(8,128)(2,1)S(1)} collective-permute-done((bf16[512,512]{1,0:T(8,128)(2,1)}, bf16[512,512]{1,0:T(8,128)(2,1)S(1)}, u32[]{:S(2)}, u32[]{:S(2)}) %collective-permute-start.3) | collective-permute-done | bytes 524320 | tf_op jit(solution)/shard_map/ppermute | solution.py:216
  46.9 0.7 collective-permute-done.4
  47.7 2.6 %add_convert_fusion = bf16[1024,512]{1,0:T(8,128)(2,1)} fusion(bf16[1024,512]{1,0:T(8,128)(2,1)} %copy-done.2, bf16[512,512]{1,0:T(8,128)(2,1)S(1)} %collective-permute-done.4, bf16[512,512]{1,0:T(8,128)(2,1)S(1)} %collective-permute-done.3), kind=kLoop, calls=%fused_computation | loop fusion | flops 3670016 | bytes 3145728 | tf_op jit(solution)/shard_map/convert_element_type | solution.py:217
  50.3 0.0 collective-permute-done.6.refs_4_
  50.3 0.0 collective-permute-done.5.refs_2_
  50.3 2.3 %broadcast_select_fusion = bf16[1024,512]{1,0:T(8,128)(2,1)} fusion(bf16[1024,512]{1,0:T(8,128)(2,1)} %collective-permute-done.5.refs_2_, bf16[1024,512]{1,0:T(8,128)(2,1)} %collective-permute-done.6.refs_4_, pred[]{:T(512)S(6)} %eq.2), kind=kLoop, calls=%fused_computation.2 | loop fusion | flops 524288 | bytes 3145729 | tf_op jit(solution)/shard_map/jit(_where)/select_n | solution.py:219
  52.6 0.0 copy-start.1
  52.6 0.0 copy-start.3
  52.6 0.0 copy-start.4
  52.6 0.0 copy-start.5
  52.6 2.8 %collective-permute-start.7 = (bf16[1024,512]{1,0:T(8,128)(2,1)}, bf16[1024,512]{1,0:T(8,128)(2,1)}, u32[]{:S(2)}, u32[]{:S(2)}) collective-permute-start(bf16[1024,512]{1,0:T(8,128)(2,1)} %broadcast_select_fusion), channel_id=1, source_target_pairs={{0,194},{1,65},{2,192},{3,67},{64,0},{65,129},{66,2},{67,131},{128... | collective-permute-start | bytes 3145736 | tf_op jit(solution)/shard_map/ppermute | solution.py:220
  55.4 6.0 %all-to-all-start.1 = ((bf16[4,256,512]{2,1,0:T(8,128)(2,1)}), bf16[4,256,512]{2,1,0:T(8,128)(2,1)}, u32[]{:S(2)}, u32[]{:S(2)}) async-start(bf16[4,256,512]{2,1,0:T(8,128)(2,1)} %bitcast.14), calls=%async_computation.1 | async-start | bytes 2097152 | tf_op jit(solution)/shard_map/all_to_all | solution.py:224
  61.4 1.2 collective-permute-start.9
  62.5 0.0 collective-permute-start.10
  62.5 0.5 collective-permute-start.8
  63.0 12.4 %all-to-all-done.1 = bf16[4,256,512]{2,1,0:T(8,128)(2,1)} async-done(((bf16[4,256,512]{2,1,0:T(8,128)(2,1)}), bf16[4,256,512]{2,1,0:T(8,128)(2,1)}, u32[]{:S(2)}, u32[]{:S(2)}) %all-to-all-start.1) | async-done | bytes 1048608 | tf_op jit(solution)/shard_map/all_to_all | solution.py:224
  75.4 0.0 collective-permute-done.7.refs_6_
  75.5 2.1 %collective-permute-start.11 = (bf16[1024,512]{1,0:T(8,128)(2,1)}, bf16[1024,512]{1,0:T(8,128)(2,1)}, u32[]{:S(2)}, u32[]{:S(2)}) collective-permute-start(bf16[1024,512]{1,0:T(8,128)(2,1)} %collective-permute-done.7.refs_6_), channel_id=1, source_target_pairs={{0,1},{1,0},{2,3},{3,2},{4,5},{5,4},{6,7},{7,6},{8,9},{9,8},{10,11... | collective-permute-start | bytes 3145736 | tf_op jit(solution)/shard_map/ppermute | solution.py:226
  77.5 2.2 %reduce_sum.12 = bf16[256,512]{1,0:T(8,128)(2,1)} reduce(bf16[4,256,512]{2,1,0:T(8,128)(2,1)} %all-to-all-done.1, bf16[]{:T(256)} %constant.12.clone.1), dimensions={0}, to_apply=%region_0.1 | reduce | flops 393216 | bytes 1310722 | tf_op jit(solution)/shard_map/reduce_sum | solution.py:227
  79.7 4.9 %all-to-all-start.2 = ((bf16[8,32,512]{2,1,0:T(8,128)(2,1)}), bf16[8,32,512]{2,1,0:T(8,128)(2,1)S(1)}, u32[]{:S(2)}, u32[]{:S(2)}) async-start(bf16[8,32,512]{2,1,0:T(8,128)(2,1)} %bitcast.3), calls=%async_computation.2 | async-start | bytes 524288 | tf_op jit(solution)/shard_map/all_to_all | solution.py:228
  84.6 0.0 collective-permute-done.8.refs_1_
  84.6 0.0 collective-permute-done.9.refs_3_
  84.6 0.0 collective-permute-done.10.refs_5_
  84.6 0.0 collective-permute-done.11.refs_7_
  84.7 0.0 copy-done.1
  84.7 0.0 copy-done.3
  84.7 0.0 copy-done.4
  84.7 0.0 copy-done.5
  84.7 0.0 copy-start.6
  84.7 0.0 copy-start.7
  84.7 0.0 copy-start.8
  84.7 0.0 copy-start.9
  84.7 9.0 %shard_map.129 = (bf16[128,512]{1,0:T(8,128)(2,1)}, bf16[128,8192]{1,0:T(8,128)(2,1)}) custom-call(bf16[128,8192]{1,0:T(8,128)(2,1)S(1)} %copy-done.1, f32[1,8192]{1,0:T(1,128)S(1)} %bitcast.12, bf16[128,512]{1,0:T(8,128)(2,1)S(1)} %copy-done.3, f32[128,128]{1,0:T(8,128)S(1)} %copy-done.5, bf16[1024,512]{1,0:T(8,128)(2,1)} %pad_maximum_fusion.refs_0_, ...), custom_call_target="tpu_custom_call" | custom-call | flops 2147483648 | bytes 14680064 | tf_op jit(solution)/shard_map/pallas_call | solution.py:229
  93.7 1.6 %all-to-all-done.2.recv_ref = bf16[8,32,512]{2,1,0:T(8,128)(2,1)S(1)} async-done(((bf16[8,32,512]{2,1,0:T(8,128)(2,1)}), bf16[8,32,512]{2,1,0:T(8,128)(2,1)S(1)}, u32[]{:S(2)}, u32[]{:S(2)}) %all-to-all-start.2) | async-done | bytes 262176 | tf_op jit(solution)/shard_map/all_to_all | solution.py:228
  95.3 0.0 copy-done.6
  95.3 0.0 copy-done.7
  95.3 0.0 copy-done.8
  95.3 0.0 copy-done.9
  95.3 1.1 shard_map.130
  96.5 20.6 %all_to_all.20 = bf16[8,32,512]{2,1,0:T(8,128)(2,1)S(1)} all-to-all(bf16[8,32,512]{2,1,0:T(8,128)(2,1)S(1)} %get-tuple-element.47), channel_id=1, replica_groups=mesh['zl'=4,'y'=4,'x'=4,'zh'=2,'c'=2] {'x','zh'}, dimensions={0} | all-to-all | bytes 524288 | tf_op jit(solution)/shard_map/all_to_all | solution.py:250
  117.0 0.5 collective-permute-start.12
  117.5 1.2 collective-permute-done.12
  118.7 0.1 pad_maximum_fusion.1
  118.8 0.8 copy.14
  (2 shorter events, 0.1 us)
Async XLA Ops:
  0.6 8.5 %copy-start = (bf16[512,512]{1,0:T(8,128)(2,1)S(1)}, bf16[512,512]{1,0:T(8,128)(2,1)}, u32[]{:S(2)}) copy-start(bf16[512,512]{1,0:T(8,128)(2,1)} %param.11) | copy-start | bytes 1572868
  5.1 35.1 %all-to-all-start = ((bf16[4,128,2560]{2,1,0:T(8,128)(2,1)}), bf16[4,128,2560]{2,1,0:T(8,128)(2,1)S(1)}, u32[]{:S(2)}, u32[]{:S(2)}) async-start(bf16[4,128,2560]{2,1,0:T(8,128)(2,1)} %get-tuple-element.27), calls=%async_computation | async-start | bytes 5242880 | tf_op jit(solution)/shard_map/all_to_all | solution.py:207
  9.1 8.3 %collective-permute-start.2 = (bf16[256,512]{1,0:T(8,128)(2,1)S(1)}, bf16[256,512]{1,0:T(8,128)(2,1)S(1)}, u32[]{:S(2)}, u32[]{:S(2)}) collective-permute-start(bf16[256,512]{1,0:T(8,128)(2,1)S(1)} %constant_dynamic-slice_fusion), channel_id=1, source_target_pairs={{0,16},{16,32},{32,48},{48,0},{1,17},{17,33},{33,49},{49,1},{2,18}... | collective-permute-start | bytes 786440 | tf_op jit(solution)/shard_map/ppermute | solution.py:189
  10.5 13.6 %collective-permute-start.1 = (bf16[256,512]{1,0:T(8,128)(2,1)S(1)}, bf16[256,512]{1,0:T(8,128)(2,1)S(1)}, u32[]{:S(2)}, u32[]{:S(2)}) collective-permute-start(bf16[256,512]{1,0:T(8,128)(2,1)S(1)} %constant_dynamic-slice_fusion), channel_id=1, source_target_pairs={{0,32},{16,48},{32,0},{48,16},{1,33},{17,49},{33,1},{49,17},{2,34}... | collective-permute-start | bytes 786440 | tf_op jit(solution)/shard_map/ppermute | solution.py:189
  13.1 11.0 %collective-permute-start = (bf16[256,512]{1,0:T(8,128)(2,1)S(1)}, bf16[256,512]{1,0:T(8,128)(2,1)S(1)}, u32[]{:S(2)}, u32[]{:S(2)}) collective-permute-start(bf16[256,512]{1,0:T(8,128)(2,1)S(1)} %constant_dynamic-slice_fusion), channel_id=1, source_target_pairs={{0,48},{16,0},{32,16},{48,32},{1,49},{17,1},{33,17},{49,33},{2,50}... | collective-permute-start | bytes 786440 | tf_op jit(solution)/shard_map/ppermute | solution.py:189
  25.2 25.1 %collective-permute-start.6 = (bf16[1024,512]{1,0:T(8,128)(2,1)}, bf16[1024,512]{1,0:T(8,128)(2,1)}, u32[]{:S(2)}, u32[]{:S(2)}) collective-permute-start(bf16[1024,512]{1,0:T(8,128)(2,1)} %pad_maximum_fusion.refs_0_), channel_id=1, source_target_pairs={{0,64},{1,65},{2,66},{3,67},{64,128},{65,129},{66,130},{67,131},{1... | collective-permute-start | bytes 3145736 | tf_op jit(solution)/shard_map/ppermute | solution.py:193
  26.8 23.4 %collective-permute-start.5 = (bf16[1024,512]{1,0:T(8,128)(2,1)}, bf16[1024,512]{1,0:T(8,128)(2,1)}, u32[]{:S(2)}, u32[]{:S(2)}) collective-permute-start(bf16[1024,512]{1,0:T(8,128)(2,1)} %pad_maximum_fusion.refs_0_), channel_id=1, source_target_pairs={{0,194},{1,195},{2,192},{3,193},{64,0},{65,1},{66,2},{67,3},{128,6... | collective-permute-start | bytes 3145736 | tf_op jit(solution)/shard_map/ppermute | solution.py:192
  42.4 1.0 copy-start.2
  43.3 3.6 %collective-permute-start.3 = (bf16[512,512]{1,0:T(8,128)(2,1)}, bf16[512,512]{1,0:T(8,128)(2,1)S(1)}, u32[]{:S(2)}, u32[]{:S(2)}) collective-permute-start(bf16[512,512]{1,0:T(8,128)(2,1)} %get-tuple-element.30), channel_id=1, source_target_pairs={{0,1},{1,0},{2,3},{3,2},{4,5},{5,4},{6,7},{7,6},{8,9},{9,8},{10,11... | collective-permute-start | bytes 1572872 | tf_op jit(solution)/shard_map/ppermute | solution.py:216
  45.2 2.5 %collective-permute-start.4 = (bf16[512,512]{1,0:T(8,128)(2,1)}, bf16[512,512]{1,0:T(8,128)(2,1)S(1)}, u32[]{:S(2)}, u32[]{:S(2)}) collective-permute-start(bf16[512,512]{1,0:T(8,128)(2,1)} %get-tuple-element.31), channel_id=1, source_target_pairs={{0,1},{1,0},{2,3},{3,2},{4,5},{5,4},{6,7},{7,6},{8,9},{9,8},{10,11... | collective-permute-start | bytes 1572872 | tf_op jit(solution)/shard_map/ppermute | solution.py:216
  52.6 32.1 %copy-start.1 = (bf16[128,8192]{1,0:T(8,128)(2,1)S(1)}, bf16[128,8192]{1,0:T(8,128)(2,1)}, u32[]{:S(2)}) copy-start(bf16[128,8192]{1,0:T(8,128)(2,1)} %tok_ref.3) | copy-start | bytes 6291460
  52.6 32.1 %copy-start.3 = (bf16[128,512]{1,0:T(8,128)(2,1)S(1)}, bf16[128,512]{1,0:T(8,128)(2,1)}, u32[]{:S(2)}) copy-start(bf16[128,512]{1,0:T(8,128)(2,1)} %cot_ref.3) | copy-start | bytes 393220
  52.6 32.1 %copy-start.4 = (f32[8192]{0:T(1024)S(1)}, f32[8192]{0:T(1024)}, u32[]{:S(2)}) copy-start(f32[8192]{0:T(1024)} %param.9) | copy-start | bytes 98308
  52.6 32.1 %copy-start.5 = (f32[128,128]{1,0:T(8,128)S(1)}, f32[128,128]{1,0:T(8,128)}, u32[]{:S(2)}) copy-start(f32[128,128]{1,0:T(8,128)} %get-tuple-element.36.inv_ref) | copy-start | bytes 196612
  52.6 22.8 %collective-permute-start.7 = (bf16[1024,512]{1,0:T(8,128)(2,1)}, bf16[1024,512]{1,0:T(8,128)(2,1)}, u32[]{:S(2)}, u32[]{:S(2)}) collective-permute-start(bf16[1024,512]{1,0:T(8,128)(2,1)} %broadcast_select_fusion), channel_id=1, source_target_pairs={{0,194},{1,65},{2,192},{3,67},{64,0},{65,129},{66,2},{67,131},{128... | collective-permute-start | bytes 3145736 | tf_op jit(solution)/shard_map/ppermute | solution.py:220
  55.4 20.1 %all-to-all-start.1 = ((bf16[4,256,512]{2,1,0:T(8,128)(2,1)}), bf16[4,256,512]{2,1,0:T(8,128)(2,1)}, u32[]{:S(2)}, u32[]{:S(2)}) async-start(bf16[4,256,512]{2,1,0:T(8,128)(2,1)} %bitcast.14), calls=%async_computation.1 | async-start | bytes 2097152 | tf_op jit(solution)/shard_map/all_to_all | solution.py:224
  61.4 23.3 %collective-permute-start.9 = (bf16[1024,512]{1,0:T(8,128)(2,1)}, bf16[1024,512]{1,0:T(8,128)(2,1)}, u32[]{:S(2)}, u32[]{:S(2)}) collective-permute-start(bf16[1024,512]{1,0:T(8,128)(2,1)} %collective-permute-done.5.refs_2_), channel_id=1, source_target_pairs={{0,1},{1,0},{2,3},{3,2},{4,5},{5,4},{6,7},{7,6},{8,9},{9,8},{10,11... | collective-permute-start | bytes 3145736 | tf_op jit(solution)/shard_map/ppermute | solution.py:223
  62.5 22.1 %collective-permute-start.10 = (bf16[1024,512]{1,0:T(8,128)(2,1)}, bf16[1024,512]{1,0:T(8,128)(2,1)}, u32[]{:S(2)}, u32[]{:S(2)}) collective-permute-start(bf16[1024,512]{1,0:T(8,128)(2,1)} %collective-permute-done.6.refs_4_), channel_id=1, source_target_pairs={{0,1},{1,0},{2,3},{3,2},{4,5},{5,4},{6,7},{7,6},{8,9},{9,8},{10,11... | collective-permute-start | bytes 3145736 | tf_op jit(solution)/shard_map/ppermute | solution.py:223
  62.5 22.1 %collective-permute-start.8 = (bf16[1024,512]{1,0:T(8,128)(2,1)}, bf16[1024,512]{1,0:T(8,128)(2,1)}, u32[]{:S(2)}, u32[]{:S(2)}) collective-permute-start(bf16[1024,512]{1,0:T(8,128)(2,1)} %pad_maximum_fusion.refs_0_), channel_id=1, source_target_pairs={{0,1},{1,0},{2,3},{3,2},{4,5},{5,4},{6,7},{7,6},{8,9},{9,8},{10,11... | collective-permute-start | bytes 3145736 | tf_op jit(solution)/shard_map/ppermute | solution.py:223
  75.5 9.2 %collective-permute-start.11 = (bf16[1024,512]{1,0:T(8,128)(2,1)}, bf16[1024,512]{1,0:T(8,128)(2,1)}, u32[]{:S(2)}, u32[]{:S(2)}) collective-permute-start(bf16[1024,512]{1,0:T(8,128)(2,1)} %collective-permute-done.7.refs_6_), channel_id=1, source_target_pairs={{0,1},{1,0},{2,3},{3,2},{4,5},{5,4},{6,7},{7,6},{8,9},{9,8},{10,11... | collective-permute-start | bytes 3145736 | tf_op jit(solution)/shard_map/ppermute | solution.py:226
  79.7 15.6 %all-to-all-start.2 = ((bf16[8,32,512]{2,1,0:T(8,128)(2,1)}), bf16[8,32,512]{2,1,0:T(8,128)(2,1)S(1)}, u32[]{:S(2)}, u32[]{:S(2)}) async-start(bf16[8,32,512]{2,1,0:T(8,128)(2,1)} %bitcast.3), calls=%async_computation.2 | async-start | bytes 524288 | tf_op jit(solution)/shard_map/all_to_all | solution.py:228
  84.7 10.6 %copy-start.6 = (f32[16,1024]{1,0:T(8,128)S(1)}, f32[16,1024]{1,0:T(8,128)}, u32[]{:S(2)}) copy-start(f32[16,1024]{1,0:T(8,128)} %first_ref.1) | copy-start | bytes 196612
  84.7 10.6 %copy-start.7 = (f32[16,1024]{1,0:T(8,128)S(1)}, f32[16,1024]{1,0:T(8,128)}, u32[]{:S(2)}) copy-start(f32[16,1024]{1,0:T(8,128)} %second_ref.1) | copy-start | bytes 196612
  84.7 10.6 %copy-start.8 = (f32[32,512]{1,0:T(8,128)S(1)}, f32[32,512]{1,0:T(8,128)}, u32[]{:S(2)}) copy-start(f32[32,512]{1,0:T(8,128)} %master_ref.1) | copy-start | bytes 196612
  84.7 10.6 %copy-start.9 = (s32[1024]{0:T(1024)S(1)}, s32[1024]{0:T(1024)}, u32[]{:S(2)}) copy-start(s32[1024]{0:T(1024)} %param.15) | copy-start | bytes 12292
  117.0 1.7 %collective-permute-start.12 = (bf16[8,32,512]{2,1,0:T(8,128)(2,1)S(1)}, bf16[8,32,512]{2,1,0:T(8,128)(2,1)S(1)}, u32[]{:S(2)}, u32[]{:S(2)}) collective-permute-start(bf16[8,32,512]{2,1,0:T(8,128)(2,1)S(1)} %all_to_all.20), channel_id=1, source_target_pairs={{0,1},{1,0},{2,3},{3,2},{4,5},{5,4},{6,7},{7,6},{8,9},{9,8},{10,11... | collective-permute-start | bytes 786440 | tf_op jit(solution)/shard_map/ppermute | solution.py:251

commit v4 on v3

--- a/solution.py
+++ b/solution.py
@@ -43,6 +43,7 @@
 
 
 def norm_kernel(tok_ref, gain_ref, cot_ref, send_ref, inv_ref):
+    c = lax.axis_index("c")
     rows, width = tok_ref.shape
     step = X * ZH * C * ROWS
     acc = jnp.zeros((rows, step), F32)
@@ -53,31 +54,41 @@
     inv = jnp.broadcast_to(inv, inv_ref.shape)
     inv_ref[...] = inv
     part = ZH * C * ROWS
-    for n in range(ZL * Y):
-        for x in range(X):
-            cols = slice(n * step + x * part, n * step + (x + 1) * part)
-            normed = tok_ref[:, cols].astype(F32) * inv
-            send_ref[x, :, n * part : (n + 1) * part] = (normed * gain_ref[:, cols]).astype(BF16)
-    for x in range(X):
-        send_ref[x, :, ZL * Y * part :] = cot_ref[...]
-
-
-def grad_kernel(recv_ref, own_ref, sib_a_ref, sib_b_ref):
-    c = lax.axis_index("c")
+    stride_p, stride_q = jnp.where(c == 0, part, step), jnp.where(c == 0, step, part)
+    for zl in range(ZL):
+        for p in range(X):
+            for q in range(Y):
+                at = pl.multiple_of(zl * Y * step + p * stride_p + q * stride_q, part)
+                cols = pl.ds(at, part)
+                normed = tok_ref[:, cols].astype(F32) * inv
+                to = (zl * Y + q) * part
+                send_ref[p, :, to : to + part] = (normed * gain_ref[:, cols]).astype(BF16)
+    for p in range(X):
+        send_ref[p, :, ZL * Y * part :] = cot_ref[...]
+
+
+def grad_kernel(recv_ref, send_ref):
     part = ZH * C * ROWS
     cols = ZL * Y * part
     cot = recv_ref[:, cols:]
     for zl in range(ZL):
         block = recv_ref[:, zl * Y * part : (zl + 1) * Y * part]
         grad = lax.dot_general(block, cot, (((0,), (0,)), ((), ())), preferred_element_type=F32)
-        for y in range(Y):
+        grad = grad.astype(BF16)
+        for q in range(Y):
             for zh in range(ZH):
-                at = y * part + zh * C * ROWS
-                first, second = grad[at : at + ROWS], grad[at + ROWS : at + 2 * ROWS]
-                to = ((y * ZL + zl) * ZH + zh) * ROWS
-                own_ref[to : to + ROWS, :] = jnp.where(c == 0, first, second).astype(BF16)
-                sib_ref, to = (sib_a_ref, to) if y < Y // 2 else (sib_b_ref, to - Y // 2 * ZL * ZH * ROWS)
-                sib_ref[to : to + ROWS, :] = jnp.where(c == 0, second, first).astype(BF16)
+                for c in range(C):
+                    at = q * part + (zh * C + c) * ROWS
+                    to = ((c * ZL + zl) * ZH + zh) * ROWS
+                    send_ref[q, to : to + ROWS, :] = grad[at : at + ROWS]
+
+
+def sum_kernel(recv_ref, own_ref, sib_ref):
+    c = lax.axis_index("c")
+    rows = own_ref.shape[0]
+    for ref, core in ((sib_ref, 1 - c), (own_ref, c)):
+        part = recv_ref[:, pl.ds(pl.multiple_of(core * rows, rows), rows), :].astype(F32)
+        ref[...] = jnp.sum(part, axis=0).astype(ref.dtype)
 
 
 def out_kernel(tok_ref, gain_ref, cot_ref, inv_ref, *refs):
@@ -178,6 +189,15 @@
     return pairs
 
 
+def mixed(value, first):
+    groups = []
+    for c in range(C):
+        for i in range(X):
+            lines = [((i, j) if (c == 0) == first else (j, i)) for j in range(Y)]
+            groups.append([(y * X + x) * C + c for y, x in lines])
+    return lax.all_to_all(value, ("y", "x", "c"), 0, 0, axis_index_groups=groups, tiled=True)
+
+
 def shards(tokens, norm_gain, key_cotangent, secondary, master, moment_first, moment_second, signs):
     tok_rows, width = tokens.shape
     keys_w = key_cotangent.shape[1]
@@ -189,8 +209,6 @@
     column = [half] + [lax.ppermute(half, "y", ring(Y, -k)) for k in range(1, Y)]
     column = jnp.concatenate(column, axis=0)
     z_axes = ("zl", "zh", "c")
-    from_up = lax.ppermute(column, z_axes, along_z(lambda c: -1))
-    from_down = lax.ppermute(column, z_axes, along_z(lambda c: 1))
 
     part = width // X
     step = 32
@@ -204,36 +222,36 @@
         cost_estimate=pl.CostEstimate(flops=tok_rows * width * 6, bytes_accessed=5 << 20, transcendentals=0),
         compiler_params=pltpu.CompilerParams(vmem_limit_bytes=56 << 20),
     )(tokens, gain, key_cotangent)
-    recv = lax.all_to_all(send, "x", 0, 0, tiled=True).reshape(X * tok_rows, part + keys_w)
-    recv, _ = lax.optimization_barrier((recv, column))
-    own, *sib = kernel_call(
+    recv = mixed(send, True).reshape(X * tok_rows, part + keys_w)
+    from_up = lax.ppermute(column, z_axes, along_z(lambda c: -1))
+    from_down = lax.ppermute(column, z_axes, along_z(lambda c: 1))
+    weights = []
+    for block in (column, from_up, from_down):
+        weights += [block, lax.ppermute(block, "c", ring(C, 1))]
+    send = kernel_call(
         grad_kernel,
-        (shape((part // 2, keys_w), BF16),) + (shape((part // 4, keys_w), BF16),) * 2,
+        shape((Y, part // Y, keys_w), BF16),
         0,
         1 << 20,
         1,
+        40 << 20,
     )(recv)
-    sib = [lax.ppermute(piece, "c", ring(C, 1)) for piece in sib]
-    summed = (own.astype(F32) + jnp.concatenate(sib, axis=0).astype(F32)).astype(BF16)
-    summed, column, from_up, from_down = lax.optimization_barrier((summed, column, from_up, from_down))
-    from_far = jnp.where(c == 0, from_up, from_down)
+    blocks = mixed(send, False)
+    own, sib = kernel_call(
+        sum_kernel,
+        (shape((part // Y // C, keys_w), F32), shape((part // Y // C, keys_w), BF16)),
+        0,
+        1 << 20,
+        1,
+    )(blocks)
+    sib = lax.ppermute(sib, "c", ring(C, 1))
+    summed = (own + sib.astype(F32)).astype(BF16)
+    summed, *weights = lax.optimization_barrier((summed, *weights))
+    from_far = jnp.where(c == 0, weights[2], weights[4])
     from_far = lax.ppermute(from_far, z_axes, along_z(lambda c: 2 * c - 1))
-    weights = []
-    for block in (column, from_up, from_down):
-        weights += [block, lax.ppermute(block, "c", ring(C, 1))]
-    blocks = lax.all_to_all(summed.reshape(Y, -1, keys_w), "y", 0, 0, tiled=True)
+    blocks = lax.all_to_all(summed.reshape(ZL * ZH, ROWS, keys_w), ("zl", "zh"), 0, 0, tiled=True)
     blocks, from_far = lax.optimization_barrier((blocks, from_far))
     weights += [from_far, lax.ppermute(from_far, "c", ring(C, 1))]
-    summed = jnp.sum(blocks.astype(F32), axis=0).astype(BF16)
-    blocks = lax.all_to_all(summed.reshape(ZL * ZH, ROWS, keys_w), ("zl", "zh"), 0, 0, tiled=True)
-    keys, token_grad = kernel_call(
-        out_kernel,
-        (shape((tok_rows, keys_w), BF16), shape(tokens.shape, BF16)),
-        4 * tok_rows * width * keys_w,
-        14 << 20,
-        4 + len(weights),
-    )(tokens, gain, key_cotangent, inv, *weights)
-    blocks, keys, token_grad = lax.optimization_barrier((blocks, keys, token_grad))
     new_master, new_first, new_second, new_rows = kernel_call(
         functools.partial(adam_kernel, tok_rows * math.prod(SIZES)),
         (
@@ -248,6 +266,14 @@
     )(blocks, moment_first, moment_second, master, signs.reshape(1, -1))
 
     mine = lax.all_to_all(new_rows, ("x", "zh"), 0, 0, tiled=True)
+    keys, token_grad = kernel_call(
+        out_kernel,
+        (shape((tok_rows, keys_w), BF16), shape(tokens.shape, BF16)),
+        4 * tok_rows * width * keys_w,
+        14 << 20,
+        4 + len(weights),
+    )(tokens, gain, key_cotangent, inv, *weights)
+    mine, keys, token_grad = lax.optimization_barrier((mine, keys, token_grad))
     other = lax.ppermute(mine, "c", ring(C, 1))
     even = jnp.where(c == 0, mine, other)
     odd = jnp.where(c == 0, other, mine)

time: 120 us -> 121 us (level); the launches traced: 120 us -> 119 us
  waiting for transfers between devices: 40.9 us -> 47.5 us
  other arithmetic: 8.19 us -> 2.73 us
  starting transfers between devices: 30.5 us -> 26.1 us
  blocking collectives: 20.6 us -> 23.6 us
    all_to_all x3, waiting for transfers between devices: 27.3 us -> 7.04 us  [the longest x1 5.15 us: shards(): mine = lax.all_to_all(new_rows, ('x', 'zh'), 0, 0, tiled=True)]
    ppermute x3, waiting for transfers between devices: 9.94 us -> 24.3 us  [shards(): lax.ppermute(half, 'y', ring(Y, -k))]
    ppermute x1, waiting for transfers between devices: 0.01 us -> 11.3 us  [shards(): from_up = lax.ppermute(column, z_axes, along_z(lambda c: -1))]
    all_to_all x1, blocking collectives: 20.6 us -> 23.6 us  [shards(): lax.all_to_all(summed.reshape(ZL * ZH, ROWS, keys_w), ('zl', 'zh'), 0, 0,...]
    convert_element_type x1, other arithmetic: 2.58 us -> 0.07 us  [shards(): summed = (own + sib.astype(F32)).astype(BF16)]
    ppermute x1, waiting for transfers between devices: 0.01 us -> 2.18 us  [shards(): from_down = lax.ppermute(column, z_axes, along_z(lambda c: 1))]
    reduce_sum x1 -> x0, other arithmetic: 2.15 us -> none  [shards(): summed = jnp.sum(blocks.astype(F32), axis=0).astype(BF16)]
    ppermute x2 -> x1, starting transfers between devices: 1.87 us -> 0.09 us  [shards(): sib = lax.ppermute(sib, 'c', ring(C, 1))]
  transfers between devices with their start and end apart: 16 -> 15, of which waited for: 8 -> 8; matrix products, arithmetic and copies ran while one was open for 5% -> 1% of each run, Pallas kernels for 9% -> 10%
where the time goes in v4:
time: 121 us; the launch traced here: 119 us
  waiting for transfers between devices  47.5 us (39%)
  starting transfers between devices  26.1 us (22%)
  blocking collectives  23.6 us (20%)
  Pallas kernels  16.3 us (13%)
  other arithmetic  2.73 us (2%)
  local copies, waits for them, and re-layouts  2.22 us (2%)
    ppermute x3, waiting for transfers between devices, shards(): lax.ppermute(half, 'y', ring(Y, -k))  24.3 us
    all_to_all x1, blocking collectives, shards(): lax.all_to_all(summed.reshape(ZL * ZH, ROWS, keys_w), ('zl', 'zh'), 0, 0,...  23.6 us
    ppermute x1, waiting for transfers between devices, shards(): from_up = lax.ppermute(column, z_axes, along_z(lambda c: -1))  11.3 us
    pallas_call x1, Pallas kernels, shards(): kernel_call(out_kernel, (shape((tok_rows, keys_w), BF16), shape(tokens.sh...  8.93 us
    all_to_all x1, starting transfers between devices, shards(): mine = lax.all_to_all(new_rows, ('x', 'zh'), 0, 0, tiled=True)  8.51 us
    all_to_all x2, starting transfers between devices, mixed(): lax.all_to_all(value, ('y', 'x', 'c'), 0, 0, axis_index_groups=groups, ti...  8.19 us
    all_to_all x1, waiting for transfers between devices, shards(): mine = lax.all_to_all(new_rows, ('x', 'zh'), 0, 0, tiled=True)  5.15 us
    ppermute x3, starting transfers between devices, shards(): lax.ppermute(half, 'y', ring(Y, -k))  5.12 us
  transfers between devices with their start and end apart: 15, of which 8 were waited for; matrix products, arithmetic and copies ran while one was open for 1% of the time, Pallas kernels for 10%

profile of v4, /device:TPU:33, one launch (start us, length us, event | category | flops | bytes accessed | tf_op | source)
XLA Modules:
  0.0 119.4 jit_solution(5066901564091925662)
XLA Ops:
  0.6 0.0 copy-start
  0.6 4.6 %shard_map.127 = (bf16[4,128,2560]{2,1,0:T(8,128)(2,1)}, f32[128,128]{1,0:T(8,128)}) custom-call(bf16[128,8192]{1,0:T(8,128)(2,1)} %tok_ref.3, f32[1,8192]{1,0:T(1,128)} %bitcast.10, bf16[128,512]{1,0:T(8,128)(2,1)} %cot_ref.3), custom_call_target="tpu_custom_call" | custom-call | flops 6291456 | bytes 5242880 | tf_op jit(solution)/shard_map/pallas_call | solution.py:216
  5.3 4.2 %all-to-all-start = ((bf16[4,128,2560]{2,1,0:T(8,128)(2,1)}), bf16[4,128,2560]{2,1,0:T(8,128)(2,1)S(1)}, u32[]{:S(2)}, u32[]{:S(2)}) async-start(bf16[4,128,2560]{2,1,0:T(8,128)(2,1)} %get-tuple-element.28), calls=%async_computation | async-start | bytes 5242880 | tf_op jit(solution)/shard_map/all_to_all | solution.py:198
  9.5 0.0 copy-done
  9.5 1.5 %collective-permute-start.3 = (bf16[256,512]{1,0:T(8,128)(2,1)S(1)}, bf16[256,512]{1,0:T(8,128)(2,1)S(1)}, u32[]{:S(2)}, u32[]{:S(2)}) collective-permute-start(bf16[256,512]{1,0:T(8,128)(2,1)S(1)} %constant_dynamic-slice_fusion), channel_id=1, source_target_pairs={{0,16},{16,32},{32,48},{48,0},{1,17},{17,33},{33,49},{49,1},{2,18}... | collective-permute-start | bytes 786440 | tf_op jit(solution)/shard_map/ppermute | solution.py:209
  11.0 2.4 %collective-permute-start.2 = (bf16[256,512]{1,0:T(8,128)(2,1)S(1)}, bf16[256,512]{1,0:T(8,128)(2,1)S(1)}, u32[]{:S(2)}, u32[]{:S(2)}) collective-permute-start(bf16[256,512]{1,0:T(8,128)(2,1)S(1)} %constant_dynamic-slice_fusion), channel_id=1, source_target_pairs={{0,32},{16,48},{32,0},{48,16},{1,33},{17,49},{33,1},{49,17},{2,34}... | collective-permute-start | bytes 786440 | tf_op jit(solution)/shard_map/ppermute | solution.py:209
  13.4 1.2 collective-permute-start.1
  14.6 21.2 %collective-permute-done.3 = bf16[256,512]{1,0:T(8,128)(2,1)S(1)} collective-permute-done((bf16[256,512]{1,0:T(8,128)(2,1)S(1)}, bf16[256,512]{1,0:T(8,128)(2,1)S(1)}, u32[]{:S(2)}, u32[]{:S(2)}) %collective-permute-start.3) | collective-permute-done | bytes 262176 | tf_op jit(solution)/shard_map/ppermute | solution.py:209
  35.8 3.1 %collective-permute-done.2 = bf16[256,512]{1,0:T(8,128)(2,1)S(1)} collective-permute-done((bf16[256,512]{1,0:T(8,128)(2,1)S(1)}, bf16[256,512]{1,0:T(8,128)(2,1)S(1)}, u32[]{:S(2)}, u32[]{:S(2)}) %collective-permute-start.2) | collective-permute-done | bytes 262176 | tf_op jit(solution)/shard_map/ppermute | solution.py:209
  38.9 0.0 collective-permute-done.1
  38.9 1.0 pad_maximum_fusion.refs_0_
  40.0 0.0 collective-permute-start.5
  40.0 1.6 %collective-permute-start.7 = (bf16[1024,512]{1,0:T(8,128)(2,1)}, bf16[1024,512]{1,0:T(8,128)(2,1)}, u32[]{:S(2)}, u32[]{:S(2)}) collective-permute-start(bf16[1024,512]{1,0:T(8,128)(2,1)} %pad_maximum_fusion.refs_0_), channel_id=1, source_target_pairs={{0,64},{1,65},{2,66},{3,67},{64,128},{65,129},{66,130},{67,131},{1... | collective-permute-start | bytes 3145736 | tf_op jit(solution)/shard_map/ppermute | solution.py:227
  41.6 0.0 all-to-all-done
  41.6 1.3 %shard_map.128 = bf16[4,512,512]{2,1,0:T(8,128)(2,1)S(1)} custom-call(bf16[512,2560]{1,0:T(8,128)(2,1)S(1)} %bitcast.9), custom_call_target="tpu_custom_call" | custom-call | bytes 1048576 | tf_op jit(solution)/shard_map/pallas_call | solution.py:231
  42.9 0.0 copy-start.1
  42.9 1.3 %copy-done.1 = bf16[4,512,512]{2,1,0:T(8,128)(2,1)} copy-done((bf16[4,512,512]{2,1,0:T(8,128)(2,1)}, bf16[4,512,512]{2,1,0:T(8,128)(2,1)S(1)}, u32[]{:S(2)}) %copy-start.1) | copy-done | bytes 2097176
  44.2 4.0 %all-to-all-start.1 = ((bf16[4,512,512]{2,1,0:T(8,128)(2,1)}), bf16[4,512,512]{2,1,0:T(8,128)(2,1)S(1)}, u32[]{:S(2)}, u32[]{:S(2)}) async-start(bf16[4,512,512]{2,1,0:T(8,128)(2,1)} %copy-done.1), calls=%async_computation.1 | async-start | bytes 4194304 | tf_op jit(solution)/shard_map/all_to_all | solution.py:198
  48.2 0.0 collective-permute-start.4
  48.2 11.3 %collective-permute-done.5.refs_2_ = bf16[1024,512]{1,0:T(8,128)(2,1)} collective-permute-done((bf16[1024,512]{1,0:T(8,128)(2,1)}, bf16[1024,512]{1,0:T(8,128)(2,1)}, u32[]{:S(2)}, u32[]{:S(2)}) %collective-permute-start.5) | collective-permute-done | bytes 1048608 | tf_op jit(solution)/shard_map/ppermute | solution.py:226
  59.5 0.0 collective-permute-start.6
  59.5 2.2 %collective-permute-done.7.refs_4_ = bf16[1024,512]{1,0:T(8,128)(2,1)} collective-permute-done((bf16[1024,512]{1,0:T(8,128)(2,1)}, bf16[1024,512]{1,0:T(8,128)(2,1)}, u32[]{:S(2)}, u32[]{:S(2)}) %collective-permute-start.7) | collective-permute-done | bytes 1048608 | tf_op jit(solution)/shard_map/ppermute | solution.py:227
  61.7 0.0 collective-permute-start.8
  61.7 1.9 %all-to-all-done.1.recv_ref = bf16[4,512,512]{2,1,0:T(8,128)(2,1)S(1)} async-done(((bf16[4,512,512]{2,1,0:T(8,128)(2,1)}), bf16[4,512,512]{2,1,0:T(8,128)(2,1)S(1)}, u32[]{:S(2)}, u32[]{:S(2)}) %all-to-all-start.1) | async-done | bytes 2097184 | tf_op jit(solution)/shard_map/all_to_all | solution.py:198
  63.6 0.2 shard_map.129
  63.8 0.1 collective-permute-start
  63.9 1.5 %collective-permute-done = bf16[256,512]{1,0:T(8,128)(2,1)S(1)} collective-permute-done((bf16[256,512]{1,0:T(8,128)(2,1)S(1)}, bf16[256,512]{1,0:T(8,128)(2,1)S(1)}, u32[]{:S(2)}, u32[]{:S(2)}) %collective-permute-start) | collective-permute-done | bytes 262176 | tf_op jit(solution)/shard_map/ppermute | solution.py:247
  65.5 0.1 add_convert_fusion
  65.5 0.0 copy-start.6
  65.6 0.0 copy-start.7
  65.6 0.0 copy-start.8
  65.6 0.0 copy-start.9
  65.6 0.0 copy-start.2
  65.6 0.0 copy-start.3
  65.6 0.0 copy-start.4
  65.6 0.0 copy-start.5
  65.6 0.0 collective-permute-done.4.refs_1_
  65.6 0.0 collective-permute-done.6.refs_3_
  65.7 0.0 collective-permute-done.8.refs_5_
  65.7 1.5 %broadcast_select_fusion = bf16[1024,512]{1,0:T(8,128)(2,1)S(1)} fusion(bf16[1024,512]{1,0:T(8,128)(2,1)} %collective-permute-done.5.refs_2_, bf16[1024,512]{1,0:T(8,128)(2,1)} %collective-permute-done.7.refs_4_, pred[]{:T(512)S(6)} %eq.2), kind=kLoop, calls=%fused_computation.1 | loop fusion | flops 524288 | bytes 3145729 | tf_op jit(solution)/shard_map/jit(_where)/select_n | solution.py:250
  67.2 1.7 %collective-permute-start.9 = (bf16[1024,512]{1,0:T(8,128)(2,1)S(1)}, bf16[1024,512]{1,0:T(8,128)(2,1)}, u32[]{:S(2)}, u32[]{:S(2)}) collective-permute-start(bf16[1024,512]{1,0:T(8,128)(2,1)S(1)} %broadcast_select_fusion), channel_id=1, source_target_pairs={{0,194},{1,65},{2,192},{3,67},{64,0},{65,129},{66,2},{67,131},{128... | collective-permute-start | bytes 3145736 | tf_op jit(solution)/shard_map/ppermute | solution.py:251
  68.9 23.6 %all_to_all.20.recv_ref = bf16[8,32,512]{2,1,0:T(8,128)(2,1)S(1)} all-to-all(bf16[8,32,512]{2,1,0:T(8,128)(2,1)S(1)} %bitcast.13), channel_id=1, replica_groups=mesh['zl'=4,'y'=4,'x'=4,'zh'=2,'c'=2] {'zl','zh'}, dimensions={0} | all-to-all | bytes 524288 | tf_op jit(solution)/shard_map/all_to_all | solution.py:252
  92.5 0.0 collective-permute-done.9.refs_6_
  92.5 0.4 collective-permute-start.10
  92.9 0.0 copy-done.6
  92.9 0.0 copy-done.7
  92.9 0.0 copy-done.8
  92.9 0.0 copy-done.9
  92.9 1.2 %shard_map.130 = (f32[32,512]{1,0:T(8,128)}, f32[16,1024]{1,0:T(8,128)}, f32[16,1024]{1,0:T(8,128)}, bf16[8,32,512]{2,1,0:T(8,128)(2,1)}) custom-call(bf16[8,32,512]{2,1,0:T(8,128)(2,1)S(1)} %all_to_all.20.recv_ref, f32[16,1024]{1,0:T(8,128)S(1)} %copy-done.6, f32[16,1024]{1,0:T(8,128)S(1)} %copy-done.7, f32[32,512]{1,0:T(8,128)S(1)} %copy-done.8, ...), custom_call_target="tpu_custom_call" | custom-call | flops 33554432 | bytes 1048576 | tf_op jit(solution)/shard_map/pallas_call | solution.py:255
  94.2 8.5 %all-to-all-start.3 = ((bf16[8,32,512]{2,1,0:T(8,128)(2,1)}), bf16[8,32,512]{2,1,0:T(8,128)(2,1)S(1)}, u32[]{:S(2)}, u32[]{:S(2)}) async-start(bf16[8,32,512]{2,1,0:T(8,128)(2,1)} %get-tuple-element.35), calls=%async_computation.3 | async-start | bytes 524288 | tf_op jit(solution)/shard_map/all_to_all | solution.py:268
  102.7 0.0 collective-permute-done.10.refs_7_
  102.7 0.0 copy-done.2
  102.7 0.0 copy-done.3
  102.7 0.0 copy-done.4
  102.7 0.0 copy-done.5
  102.7 8.9 %shard_map.131 = (bf16[128,512]{1,0:T(8,128)(2,1)}, bf16[128,8192]{1,0:T(8,128)(2,1)}) custom-call(bf16[128,8192]{1,0:T(8,128)(2,1)S(1)} %copy-done.2, f32[1,8192]{1,0:T(1,128)S(1)} %bitcast.11, bf16[128,512]{1,0:T(8,128)(2,1)S(1)} %copy-done.3, f32[128,128]{1,0:T(8,128)S(1)} %copy-done.5, bf16[1024,512]{1,0:T(8,128)(2,1)} %pad_maximum_fusion.refs_0_, ...), custom_call_target="tpu_custom_call" | custom-call | flops 2147483648 | bytes 14680064 | tf_op jit(solution)/shard_map/pallas_call | solution.py:269
  111.6 5.1 %all-to-all-done.3 = bf16[8,32,512]{2,1,0:T(8,128)(2,1)S(1)} async-done(((bf16[8,32,512]{2,1,0:T(8,128)(2,1)}), bf16[8,32,512]{2,1,0:T(8,128)(2,1)S(1)}, u32[]{:S(2)}, u32[]{:S(2)}) %all-to-all-start.3) | async-done | bytes 262176 | tf_op jit(solution)/shard_map/all_to_all | solution.py:268
  116.8 0.5 collective-permute-start.11
  117.3 1.2 collective-permute-done.11
  118.4 0.1 select_bitcast_fusion.1
  118.5 0.1 pad_maximum_fusion.1
  118.5 0.8 copy.14
  (1 shorter events, 0.0 us)
Async XLA Ops:
  0.6 8.8 %copy-start = (bf16[512,512]{1,0:T(8,128)(2,1)S(1)}, bf16[512,512]{1,0:T(8,128)(2,1)}, u32[]{:S(2)}) copy-start(bf16[512,512]{1,0:T(8,128)(2,1)} %param.11) | copy-start | bytes 1572868
  5.3 36.3 %all-to-all-start = ((bf16[4,128,2560]{2,1,0:T(8,128)(2,1)}), bf16[4,128,2560]{2,1,0:T(8,128)(2,1)S(1)}, u32[]{:S(2)}, u32[]{:S(2)}) async-start(bf16[4,128,2560]{2,1,0:T(8,128)(2,1)} %get-tuple-element.28), calls=%async_computation | async-start | bytes 5242880 | tf_op jit(solution)/shard_map/all_to_all | solution.py:198
  9.5 26.3 %collective-permute-start.3 = (bf16[256,512]{1,0:T(8,128)(2,1)S(1)}, bf16[256,512]{1,0:T(8,128)(2,1)S(1)}, u32[]{:S(2)}, u32[]{:S(2)}) collective-permute-start(bf16[256,512]{1,0:T(8,128)(2,1)S(1)} %constant_dynamic-slice_fusion), channel_id=1, source_target_pairs={{0,16},{16,32},{32,48},{48,0},{1,17},{17,33},{33,49},{49,1},{2,18}... | collective-permute-start | bytes 786440 | tf_op jit(solution)/shard_map/ppermute | solution.py:209
  11.0 27.9 %collective-permute-start.2 = (bf16[256,512]{1,0:T(8,128)(2,1)S(1)}, bf16[256,512]{1,0:T(8,128)(2,1)S(1)}, u32[]{:S(2)}, u32[]{:S(2)}) collective-permute-start(bf16[256,512]{1,0:T(8,128)(2,1)S(1)} %constant_dynamic-slice_fusion), channel_id=1, source_target_pairs={{0,32},{16,48},{32,0},{48,16},{1,33},{17,49},{33,1},{49,17},{2,34}... | collective-permute-start | bytes 786440 | tf_op jit(solution)/shard_map/ppermute | solution.py:209
  13.4 25.5 %collective-permute-start.1 = (bf16[256,512]{1,0:T(8,128)(2,1)S(1)}, bf16[256,512]{1,0:T(8,128)(2,1)S(1)}, u32[]{:S(2)}, u32[]{:S(2)}) collective-permute-start(bf16[256,512]{1,0:T(8,128)(2,1)S(1)} %constant_dynamic-slice_fusion), channel_id=1, source_target_pairs={{0,48},{16,0},{32,16},{48,32},{1,49},{17,1},{33,17},{49,33},{2,50}... | collective-permute-start | bytes 786440 | tf_op jit(solution)/shard_map/ppermute | solution.py:209
  40.0 19.5 %collective-permute-start.5 = (bf16[1024,512]{1,0:T(8,128)(2,1)}, bf16[1024,512]{1,0:T(8,128)(2,1)}, u32[]{:S(2)}, u32[]{:S(2)}) collective-permute-start(bf16[1024,512]{1,0:T(8,128)(2,1)} %pad_maximum_fusion.refs_0_), channel_id=1, source_target_pairs={{0,194},{1,195},{2,192},{3,193},{64,0},{65,1},{66,2},{67,3},{128,6... | collective-permute-start | bytes 3145736 | tf_op jit(solution)/shard_map/ppermute | solution.py:226
  40.0 21.7 %collective-permute-start.7 = (bf16[1024,512]{1,0:T(8,128)(2,1)}, bf16[1024,512]{1,0:T(8,128)(2,1)}, u32[]{:S(2)}, u32[]{:S(2)}) collective-permute-start(bf16[1024,512]{1,0:T(8,128)(2,1)} %pad_maximum_fusion.refs_0_), channel_id=1, source_target_pairs={{0,64},{1,65},{2,66},{3,67},{64,128},{65,129},{66,130},{67,131},{1... | collective-permute-start | bytes 3145736 | tf_op jit(solution)/shard_map/ppermute | solution.py:227
  42.9 1.3 %copy-start.1 = (bf16[4,512,512]{2,1,0:T(8,128)(2,1)}, bf16[4,512,512]{2,1,0:T(8,128)(2,1)S(1)}, u32[]{:S(2)}) copy-start(bf16[4,512,512]{2,1,0:T(8,128)(2,1)S(1)} %shard_map.128) | copy-start | bytes 6291460
  44.2 19.4 %all-to-all-start.1 = ((bf16[4,512,512]{2,1,0:T(8,128)(2,1)}), bf16[4,512,512]{2,1,0:T(8,128)(2,1)S(1)}, u32[]{:S(2)}, u32[]{:S(2)}) async-start(bf16[4,512,512]{2,1,0:T(8,128)(2,1)} %copy-done.1), calls=%async_computation.1 | async-start | bytes 4194304 | tf_op jit(solution)/shard_map/all_to_all | solution.py:198
  48.2 17.4 %collective-permute-start.4 = (bf16[1024,512]{1,0:T(8,128)(2,1)}, bf16[1024,512]{1,0:T(8,128)(2,1)}, u32[]{:S(2)}, u32[]{:S(2)}) collective-permute-start(bf16[1024,512]{1,0:T(8,128)(2,1)} %pad_maximum_fusion.refs_0_), channel_id=1, source_target_pairs={{0,1},{1,0},{2,3},{3,2},{4,5},{5,4},{6,7},{7,6},{8,9},{9,8},{10,11... | collective-permute-start | bytes 3145736 | tf_op jit(solution)/shard_map/ppermute | solution.py:230
  59.5 6.1 %collective-permute-start.6 = (bf16[1024,512]{1,0:T(8,128)(2,1)}, bf16[1024,512]{1,0:T(8,128)(2,1)}, u32[]{:S(2)}, u32[]{:S(2)}) collective-permute-start(bf16[1024,512]{1,0:T(8,128)(2,1)} %collective-permute-done.5.refs_2_), channel_id=1, source_target_pairs={{0,1},{1,0},{2,3},{3,2},{4,5},{5,4},{6,7},{7,6},{8,9},{9,8},{10,11... | collective-permute-start | bytes 3145736 | tf_op jit(solution)/shard_map/ppermute | solution.py:230
  61.7 4.0 %collective-permute-start.8 = (bf16[1024,512]{1,0:T(8,128)(2,1)}, bf16[1024,512]{1,0:T(8,128)(2,1)}, u32[]{:S(2)}, u32[]{:S(2)}) collective-permute-start(bf16[1024,512]{1,0:T(8,128)(2,1)} %collective-permute-done.7.refs_4_), channel_id=1, source_target_pairs={{0,1},{1,0},{2,3},{3,2},{4,5},{5,4},{6,7},{7,6},{8,9},{9,8},{10,11... | collective-permute-start | bytes 3145736 | tf_op jit(solution)/shard_map/ppermute | solution.py:230
  63.8 1.6 %collective-permute-start = (bf16[256,512]{1,0:T(8,128)(2,1)S(1)}, bf16[256,512]{1,0:T(8,128)(2,1)S(1)}, u32[]{:S(2)}, u32[]{:S(2)}) collective-permute-start(bf16[256,512]{1,0:T(8,128)(2,1)S(1)} %get-tuple-element.30), channel_id=1, source_target_pairs={{0,1},{1,0},{2,3},{3,2},{4,5},{5,4},{6,7},{7,6},{8,9},{9,8},{10,11... | collective-permute-start | bytes 786440 | tf_op jit(solution)/shard_map/ppermute | solution.py:247
  65.5 27.4 %copy-start.6 = (f32[16,1024]{1,0:T(8,128)S(1)}, f32[16,1024]{1,0:T(8,128)}, u32[]{:S(2)}) copy-start(f32[16,1024]{1,0:T(8,128)} %first_ref.1) | copy-start | bytes 196612
  65.6 27.4 %copy-start.7 = (f32[16,1024]{1,0:T(8,128)S(1)}, f32[16,1024]{1,0:T(8,128)}, u32[]{:S(2)}) copy-start(f32[16,1024]{1,0:T(8,128)} %second_ref.1) | copy-start | bytes 196612
  65.6 27.4 %copy-start.8 = (f32[32,512]{1,0:T(8,128)S(1)}, f32[32,512]{1,0:T(8,128)}, u32[]{:S(2)}) copy-start(f32[32,512]{1,0:T(8,128)} %master_ref.1) | copy-start | bytes 196612
  65.6 27.4 %copy-start.9 = (s32[1024]{0:T(1024)S(1)}, s32[1024]{0:T(1024)}, u32[]{:S(2)}) copy-start(s32[1024]{0:T(1024)} %param.15) | copy-start | bytes 12292
  65.6 37.1 %copy-start.2 = (bf16[128,8192]{1,0:T(8,128)(2,1)S(1)}, bf16[128,8192]{1,0:T(8,128)(2,1)}, u32[]{:S(2)}) copy-start(bf16[128,8192]{1,0:T(8,128)(2,1)} %tok_ref.3) | copy-start | bytes 6291460
  65.6 37.1 %copy-start.3 = (bf16[128,512]{1,0:T(8,128)(2,1)S(1)}, bf16[128,512]{1,0:T(8,128)(2,1)}, u32[]{:S(2)}) copy-start(bf16[128,512]{1,0:T(8,128)(2,1)} %cot_ref.3) | copy-start | bytes 393220
  65.6 37.1 %copy-start.4 = (f32[8192]{0:T(1024)S(1)}, f32[8192]{0:T(1024)}, u32[]{:S(2)}) copy-start(f32[8192]{0:T(1024)} %param.9) | copy-start | bytes 98308
  65.6 37.1 %copy-start.5 = (f32[128,128]{1,0:T(8,128)S(1)}, f32[128,128]{1,0:T(8,128)}, u32[]{:S(2)}) copy-start(f32[128,128]{1,0:T(8,128)} %get-tuple-element.36.inv_ref) | copy-start | bytes 196612
  67.2 25.4 %collective-permute-start.9 = (bf16[1024,512]{1,0:T(8,128)(2,1)S(1)}, bf16[1024,512]{1,0:T(8,128)(2,1)}, u32[]{:S(2)}, u32[]{:S(2)}) collective-permute-start(bf16[1024,512]{1,0:T(8,128)(2,1)S(1)} %broadcast_select_fusion), channel_id=1, source_target_pairs={{0,194},{1,65},{2,192},{3,67},{64,0},{65,129},{66,2},{67,131},{128... | collective-permute-start | bytes 3145736 | tf_op jit(solution)/shard_map/ppermute | solution.py:251
  92.5 10.1 %collective-permute-start.10 = (bf16[1024,512]{1,0:T(8,128)(2,1)}, bf16[1024,512]{1,0:T(8,128)(2,1)}, u32[]{:S(2)}, u32[]{:S(2)}) collective-permute-start(bf16[1024,512]{1,0:T(8,128)(2,1)} %collective-permute-done.9.refs_6_), channel_id=1, source_target_pairs={{0,1},{1,0},{2,3},{3,2},{4,5},{5,4},{6,7},{7,6},{8,9},{9,8},{10,11... | collective-permute-start | bytes 3145736 | tf_op jit(solution)/shard_map/ppermute | solution.py:254
  94.2 22.6 %all-to-all-start.3 = ((bf16[8,32,512]{2,1,0:T(8,128)(2,1)}), bf16[8,32,512]{2,1,0:T(8,128)(2,1)S(1)}, u32[]{:S(2)}, u32[]{:S(2)}) async-start(bf16[8,32,512]{2,1,0:T(8,128)(2,1)} %get-tuple-element.35), calls=%async_computation.3 | async-start | bytes 524288 | tf_op jit(solution)/shard_map/all_to_all | solution.py:268
  116.8 1.6 %collective-permute-start.11 = (bf16[8,32,512]{2,1,0:T(8,128)(2,1)S(1)}, bf16[8,32,512]{2,1,0:T(8,128)(2,1)S(1)}, u32[]{:S(2)}, u32[]{:S(2)}) collective-permute-start(bf16[8,32,512]{2,1,0:T(8,128)(2,1)S(1)} %all-to-all-done.3), channel_id=1, source_target_pairs={{0,1},{1,0},{2,3},{3,2},{4,5},{5,4},{6,7},{7,6},{8,9},{9,8},{10,11... | collective-permute-start | bytes 786440 | tf_op jit(solution)/shard_map/ppermute | solution.py:277

commit v5 on v4

--- a/solution.py
+++ b/solution.py
@@ -104,8 +104,9 @@
         for s, off in enumerate((0, 1, 3, 2)):
             for h in range(2):
                 for k in range(Y):
-                    node = lax.rem(zl + off, ZL) * Y + lax.rem(y + k, Y)
                     core = c if h == 0 else 1 - c
+                    on_zl, on_y = jnp.where(core == 0, off, k), jnp.where(core == 0, k, off)
+                    node = lax.rem(zl + on_zl, ZL) * Y + lax.rem(y + on_y, Y)
                     at = pl.multiple_of(node * step + core * half, half)
                     yield pl.ds(at, half), w_refs[2 * s + h], slice(k * half, (k + 1) * half)
 
@@ -179,14 +180,29 @@
     return [(i, (i + s) % n) for i in range(n)]
 
 
-def along_z(shift):
+GATHER = ("zl", "y", "zh", "c")
+
+
+def moved(on_z, shift):
     pairs = []
-    for zl in range(ZL):
-        for zh in range(ZH):
-            for c in range(C):
-                z = (zh * ZL + zl + shift(c)) % (ZH * ZL)
-                pairs.append(((zl * ZH + zh) * C + c, ((z % ZL) * ZH + z // ZL) * C + c))
+    for i in range(ZL * Y * ZH * C):
+        zl, y, zh, c = i // (Y * ZH * C), i // (ZH * C) % Y, i // C % ZH, i % C
+        if on_z(c):
+            z = (zh * ZL + zl + shift(zl, True)) % (ZH * ZL)
+            zl, zh = z % ZL, z // ZL
+        else:
+            y = (y + shift(y, False)) % Y
+        pairs.append((i, ((zl * Y + y) * ZH + zh) * C + c))
     return pairs
+
+
+def first_step(value, k):
+    shift = lambda place, on_z: {1: -1, 2: 2 - 4 * (place % 2) if on_z else -2, 3: 1}[k]
+    return lax.ppermute(value, GATHER, moved(lambda c: c == 1, shift))
+
+
+def second_step(value, shift):
+    return lax.ppermute(value, GATHER, moved(lambda c: c == 0, shift))
 
 
 def mixed(value, first):
@@ -206,9 +222,7 @@
     node_rows = secondary.shape[0]
 
     half = lax.dynamic_slice_in_dim(secondary, c * (node_rows // 2), node_rows // 2, 0)
-    column = [half] + [lax.ppermute(half, "y", ring(Y, -k)) for k in range(1, Y)]
-    column = jnp.concatenate(column, axis=0)
-    z_axes = ("zl", "zh", "c")
+    column = jnp.concatenate([half] + [first_step(half, k) for k in range(1, Y)], axis=0)
 
     part = width // X
     step = 32
@@ -223,8 +237,8 @@
         compiler_params=pltpu.CompilerParams(vmem_limit_bytes=56 << 20),
     )(tokens, gain, key_cotangent)
     recv = mixed(send, True).reshape(X * tok_rows, part + keys_w)
-    from_up = lax.ppermute(column, z_axes, along_z(lambda c: -1))
-    from_down = lax.ppermute(column, z_axes, along_z(lambda c: 1))
+    from_up = second_step(column, lambda place, on_z: -1)
+    from_down = second_step(column, lambda place, on_z: 1)
     weights = []
     for block in (column, from_up, from_down):
         weights += [block, lax.ppermute(block, "c", ring(C, 1))]
@@ -247,8 +261,9 @@
     sib = lax.ppermute(sib, "c", ring(C, 1))
     summed = (own + sib.astype(F32)).astype(BF16)
     summed, *weights = lax.optimization_barrier((summed, *weights))
-    from_far = jnp.where(c == 0, weights[2], weights[4])
-    from_far = lax.ppermute(from_far, z_axes, along_z(lambda c: 2 * c - 1))
+    odd = jnp.where(c == 0, lax.axis_index("zl"), lax.axis_index("y")) % 2 == 1
+    from_far = jnp.where(odd, weights[2], weights[4])
+    from_far = second_step(from_far, lambda place, on_z: 1 - 2 * (place % 2))
     blocks = lax.all_to_all(summed.reshape(ZL * ZH, ROWS, keys_w), ("zl", "zh"), 0, 0, tiled=True)
     blocks, from_far = lax.optimization_barrier((blocks, from_far))
     weights += [from_far, lax.ppermute(from_far, "c", ring(C, 1))]

time: 121 us -> 109 us (0.901); the launches traced: 119 us -> 109 us
  waiting for transfers between devices: 47.5 us -> 37.8 us
  blocking collectives: 23.6 us -> 17.3 us
  starting transfers between devices: 26.1 us -> 31.8 us
    ppermute x6, waiting for transfers between devices: 37.8 us -> 15 us  [the longest x3 7.5 us: second_step(): return lax.ppermute(value, GATHER, moved(lambda c: c == 0, shift))]
    all_to_all x2, waiting for transfers between devices: 1.89 us -> 15.2 us  [mixed(): lax.all_to_all(value, ('y', 'x', 'c'), 0, 0, axis_index_groups=groups, ti...]
    ppermute x1, starting transfers between devices: 0.4 us -> 8.04 us  [shards(): weights += [from_far, lax.ppermute(from_far, 'c', ring(C, 1))]]
    all_to_all x1, blocking collectives: 23.6 us -> 17.3 us  [shards(): lax.all_to_all(summed.reshape(ZL * ZH, ROWS, keys_w), ('zl', 'zh'), 0, 0,...]
    all_to_all x1, starting transfers between devices: 8.51 us -> 5.37 us  [shards(): mine = lax.all_to_all(new_rows, ('x', 'zh'), 0, 0, tiled=True)]
  transfers between devices with their start and end apart: 15 -> 15, of which waited for: 8 -> 10; matrix products, arithmetic and copies ran while one was open for 1% -> 1% of each run, Pallas kernels for 10% -> 11%
where the time goes in v5:
time: 109 us
  waiting for transfers between devices  37.8 us (35%)
  starting transfers between devices  31.8 us (29%)
  blocking collectives  17.3 us (16%)
  Pallas kernels  16.3 us (15%)
  other arithmetic  2.73 us (3%)
  local copies, waits for them, and re-layouts  2.22 us (2%)
    all_to_all x1, blocking collectives, shards(): lax.all_to_all(summed.reshape(ZL * ZH, ROWS, keys_w), ('zl', 'zh'), 0, 0,...  17.3 us
    all_to_all x2, waiting for transfers between devices, mixed(): lax.all_to_all(value, ('y', 'x', 'c'), 0, 0, axis_index_groups=groups, ti...  15.2 us
    pallas_call x1, Pallas kernels, shards(): kernel_call(out_kernel, (shape((tok_rows, keys_w), BF16), shape(tokens.sh...  8.96 us
    all_to_all x2, starting transfers between devices, mixed(): lax.all_to_all(value, ('y', 'x', 'c'), 0, 0, axis_index_groups=groups, ti...  8.2 us
    ppermute x1, starting transfers between devices, shards(): weights += [from_far, lax.ppermute(from_far, 'c', ring(C, 1))]  8.04 us
    ppermute x3, waiting for transfers between devices, second_step(): return lax.ppermute(value, GATHER, moved(lambda c: c == 0, shift))  7.5 us
    ppermute x3, waiting for transfers between devices, first_step(): return lax.ppermute(value, GATHER, moved(lambda c: c == 1, shift))  7.49 us
    all_to_all x1, starting transfers between devices, shards(): mine = lax.all_to_all(new_rows, ('x', 'zh'), 0, 0, tiled=True)  5.37 us
  transfers between devices with their start and end apart: 15, of which 10 were waited for; matrix products, arithmetic and copies ran while one was open for 1% of the time, Pallas kernels for 11%

profile of v5, /device:TPU:33, one launch (start us, length us, event | category | flops | bytes accessed | tf_op | source)
XLA Modules:
  0.0 109.0 jit_solution(5750109037589761526)
XLA Ops:
  0.6 0.0 copy-start
  0.6 4.6 %shard_map.127 = (bf16[4,128,2560]{2,1,0:T(8,128)(2,1)}, f32[128,128]{1,0:T(8,128)}) custom-call(bf16[128,8192]{1,0:T(8,128)(2,1)} %tok_ref.3, f32[1,8192]{1,0:T(1,128)} %bitcast.10, bf16[128,512]{1,0:T(8,128)(2,1)} %cot_ref.3), custom_call_target="tpu_custom_call" | custom-call | flops 6291456 | bytes 5242880 | tf_op jit(solution)/shard_map/pallas_call | solution.py:230
  5.3 4.2 %all-to-all-start = ((bf16[4,128,2560]{2,1,0:T(8,128)(2,1)}), bf16[4,128,2560]{2,1,0:T(8,128)(2,1)S(1)}, u32[]{:S(2)}, u32[]{:S(2)}) async-start(bf16[4,128,2560]{2,1,0:T(8,128)(2,1)} %get-tuple-element.28), calls=%async_computation | async-start | bytes 5242880 | tf_op jit(solution)/shard_map/all_to_all | solution.py:214
  9.5 0.0 copy-done
  9.5 1.7 %collective-permute-start.3 = (bf16[256,512]{1,0:T(8,128)(2,1)S(1)}, bf16[256,512]{1,0:T(8,128)(2,1)S(1)}, u32[]{:S(2)}, u32[]{:S(2)}) collective-permute-start(bf16[256,512]{1,0:T(8,128)(2,1)S(1)} %constant_dynamic-slice_fusion), channel_id=1, source_target_pairs={{0,16},{1,65},{2,18},{3,67},{16,32},{17,81},{18,34},{19,83},{32,48... | collective-permute-start | bytes 786440 | tf_op jit(solution)/shard_map/ppermute | solution.py:201
  11.2 3.6 %collective-permute-start.2 = (bf16[256,512]{1,0:T(8,128)(2,1)S(1)}, bf16[256,512]{1,0:T(8,128)(2,1)S(1)}, u32[]{:S(2)}, u32[]{:S(2)}) collective-permute-start(bf16[256,512]{1,0:T(8,128)(2,1)S(1)} %constant_dynamic-slice_fusion), channel_id=1, source_target_pairs={{0,32},{1,129},{2,34},{3,131},{16,48},{17,145},{18,50},{19,147},{3... | collective-permute-start | bytes 786440 | tf_op jit(solution)/shard_map/ppermute | solution.py:201
  14.8 0.0 collective-permute-start.1
  14.8 0.3 collective-permute-done.3
  15.1 4.4 %collective-permute-done.2 = bf16[256,512]{1,0:T(8,128)(2,1)S(1)} collective-permute-done((bf16[256,512]{1,0:T(8,128)(2,1)S(1)}, bf16[256,512]{1,0:T(8,128)(2,1)S(1)}, u32[]{:S(2)}, u32[]{:S(2)}) %collective-permute-start.2) | collective-permute-done | bytes 262176 | tf_op jit(solution)/shard_map/ppermute | solution.py:201
  19.5 2.8 %collective-permute-done.1 = bf16[256,512]{1,0:T(8,128)(2,1)S(1)} collective-permute-done((bf16[256,512]{1,0:T(8,128)(2,1)S(1)}, bf16[256,512]{1,0:T(8,128)(2,1)S(1)}, u32[]{:S(2)}, u32[]{:S(2)}) %collective-permute-start.1) | collective-permute-done | bytes 262176 | tf_op jit(solution)/shard_map/ppermute | solution.py:201
  22.3 1.0 pad_maximum_fusion.refs_0_
  23.3 2.7 %collective-permute-start.5 = (bf16[1024,512]{1,0:T(8,128)(2,1)}, bf16[1024,512]{1,0:T(8,128)(2,1)}, u32[]{:S(2)}, u32[]{:S(2)}) collective-permute-start(bf16[1024,512]{1,0:T(8,128)(2,1)} %pad_maximum_fusion.refs_0_), channel_id=1, source_target_pairs={{0,194},{1,49},{2,192},{3,51},{16,210},{17,1},{18,208},{19,3},{32,... | collective-permute-start | bytes 3145736 | tf_op jit(solution)/shard_map/ppermute | solution.py:205
  26.0 0.0 collective-permute-start.7
  26.0 7.4 %all-to-all-done = bf16[4,128,2560]{2,1,0:T(8,128)(2,1)S(1)} async-done(((bf16[4,128,2560]{2,1,0:T(8,128)(2,1)}), bf16[4,128,2560]{2,1,0:T(8,128)(2,1)S(1)}, u32[]{:S(2)}, u32[]{:S(2)}) %all-to-all-start) | async-done | bytes 2621472 | tf_op jit(solution)/shard_map/all_to_all | solution.py:214
  33.4 1.3 %shard_map.128 = bf16[4,512,512]{2,1,0:T(8,128)(2,1)S(1)} custom-call(bf16[512,2560]{1,0:T(8,128)(2,1)S(1)} %bitcast.9), custom_call_target="tpu_custom_call" | custom-call | bytes 1048576 | tf_op jit(solution)/shard_map/pallas_call | solution.py:245
  34.6 0.0 copy-start.1
  34.7 1.3 %copy-done.1 = bf16[4,512,512]{2,1,0:T(8,128)(2,1)} copy-done((bf16[4,512,512]{2,1,0:T(8,128)(2,1)}, bf16[4,512,512]{2,1,0:T(8,128)(2,1)S(1)}, u32[]{:S(2)}) %copy-start.1) | copy-done | bytes 2097176
  36.0 4.0 %all-to-all-start.1 = ((bf16[4,512,512]{2,1,0:T(8,128)(2,1)}), bf16[4,512,512]{2,1,0:T(8,128)(2,1)S(1)}, u32[]{:S(2)}, u32[]{:S(2)}) async-start(bf16[4,512,512]{2,1,0:T(8,128)(2,1)} %copy-done.1), calls=%async_computation.1 | async-start | bytes 4194304 | tf_op jit(solution)/shard_map/all_to_all | solution.py:214
  40.0 0.0 collective-permute-start.4
  40.0 6.2 %collective-permute-done.5.refs_2_ = bf16[1024,512]{1,0:T(8,128)(2,1)} collective-permute-done((bf16[1024,512]{1,0:T(8,128)(2,1)}, bf16[1024,512]{1,0:T(8,128)(2,1)}, u32[]{:S(2)}, u32[]{:S(2)}) %collective-permute-start.5) | collective-permute-done | bytes 1048608 | tf_op jit(solution)/shard_map/ppermute | solution.py:205
  46.2 0.0 collective-permute-start.6
  46.2 1.2 %collective-permute-done.7.refs_4_ = bf16[1024,512]{1,0:T(8,128)(2,1)} collective-permute-done((bf16[1024,512]{1,0:T(8,128)(2,1)}, bf16[1024,512]{1,0:T(8,128)(2,1)}, u32[]{:S(2)}, u32[]{:S(2)}) %collective-permute-start.7) | collective-permute-done | bytes 1048608 | tf_op jit(solution)/shard_map/ppermute | solution.py:205
  47.5 0.3 collective-permute-start.8
  47.8 7.8 %all-to-all-done.1.recv_ref = bf16[4,512,512]{2,1,0:T(8,128)(2,1)S(1)} async-done(((bf16[4,512,512]{2,1,0:T(8,128)(2,1)}), bf16[4,512,512]{2,1,0:T(8,128)(2,1)S(1)}, u32[]{:S(2)}, u32[]{:S(2)}) %all-to-all-start.1) | async-done | bytes 2097184 | tf_op jit(solution)/shard_map/all_to_all | solution.py:214
  55.6 0.2 shard_map.129
  55.9 0.9 collective-permute-start
  56.8 1.2 %collective-permute-done = bf16[256,512]{1,0:T(8,128)(2,1)S(1)} collective-permute-done((bf16[256,512]{1,0:T(8,128)(2,1)S(1)}, bf16[256,512]{1,0:T(8,128)(2,1)S(1)}, u32[]{:S(2)}, u32[]{:S(2)}) %collective-permute-start) | collective-permute-done | bytes 262176 | tf_op jit(solution)/shard_map/ppermute | solution.py:261
  58.0 0.1 add_convert_fusion
  58.0 0.0 copy-start.6
  58.0 0.0 copy-start.7
  58.1 0.0 copy-start.8
  58.1 0.0 copy-start.9
  58.1 0.0 copy-start.2
  58.1 0.0 copy-start.3
  58.1 0.0 copy-start.4
  58.1 0.0 copy-start.5
  58.1 0.0 collective-permute-done.4.refs_1_
  58.1 0.0 collective-permute-done.6.refs_3_
  58.1 0.0 collective-permute-done.8.refs_5_
  58.2 1.5 %broadcast_select_fusion = bf16[1024,512]{1,0:T(8,128)(2,1)S(1)} fusion(bf16[1024,512]{1,0:T(8,128)(2,1)} %collective-permute-done.5.refs_2_, bf16[1024,512]{1,0:T(8,128)(2,1)} %collective-permute-done.7.refs_4_, pred[]{:T(512)S(6)} %eq.11), kind=kLoop, calls=%fused_computation.1 | loop fusion | flops 524288 | bytes 3145729 | tf_op jit(solution)/shard_map/jit(_where)/select_n | solution.py:265
  59.7 0.4 collective-permute-start.9
  60.0 17.3 %all_to_all.20.recv_ref = bf16[8,32,512]{2,1,0:T(8,128)(2,1)S(1)} all-to-all(bf16[8,32,512]{2,1,0:T(8,128)(2,1)S(1)} %bitcast.13), channel_id=1, replica_groups=mesh['zl'=4,'y'=4,'x'=4,'zh'=2,'c'=2] {'zl','zh'}, dimensions={0} | all-to-all | bytes 524288 | tf_op jit(solution)/shard_map/all_to_all | solution.py:267
  77.3 0.0 collective-permute-done.9.refs_6_
  77.3 8.0 %collective-permute-start.10 = (bf16[1024,512]{1,0:T(8,128)(2,1)}, bf16[1024,512]{1,0:T(8,128)(2,1)}, u32[]{:S(2)}, u32[]{:S(2)}) collective-permute-start(bf16[1024,512]{1,0:T(8,128)(2,1)} %collective-permute-done.9.refs_6_), channel_id=1, source_target_pairs={{0,1},{1,0},{2,3},{3,2},{4,5},{5,4},{6,7},{7,6},{8,9},{9,8},{10,11... | collective-permute-start | bytes 3145736 | tf_op jit(solution)/shard_map/ppermute | solution.py:269
  85.4 0.0 copy-done.6
  85.4 0.0 copy-done.7
  85.4 0.0 copy-done.8
  85.4 0.0 copy-done.9
  85.4 1.2 %shard_map.130 = (f32[32,512]{1,0:T(8,128)}, f32[16,1024]{1,0:T(8,128)}, f32[16,1024]{1,0:T(8,128)}, bf16[8,32,512]{2,1,0:T(8,128)(2,1)}) custom-call(bf16[8,32,512]{2,1,0:T(8,128)(2,1)S(1)} %all_to_all.20.recv_ref, f32[16,1024]{1,0:T(8,128)S(1)} %copy-done.6, f32[16,1024]{1,0:T(8,128)S(1)} %copy-done.7, f32[32,512]{1,0:T(8,128)S(1)} %copy-done.8, ...), custom_call_target="tpu_custom_call" | custom-call | flops 33554432 | bytes 1048576 | tf_op jit(solution)/shard_map/pallas_call | solution.py:270
  86.6 5.4 %all-to-all-start.3 = ((bf16[8,32,512]{2,1,0:T(8,128)(2,1)}), bf16[8,32,512]{2,1,0:T(8,128)(2,1)S(1)}, u32[]{:S(2)}, u32[]{:S(2)}) async-start(bf16[8,32,512]{2,1,0:T(8,128)(2,1)} %get-tuple-element.35), calls=%async_computation.3 | async-start | bytes 524288 | tf_op jit(solution)/shard_map/all_to_all | solution.py:283
  92.0 0.0 collective-permute-done.10.refs_7_
  92.0 0.0 copy-done.2
  92.0 0.0 copy-done.3
  92.0 0.0 copy-done.4
  92.0 0.0 copy-done.5
  92.0 9.0 %shard_map.131 = (bf16[128,512]{1,0:T(8,128)(2,1)}, bf16[128,8192]{1,0:T(8,128)(2,1)}) custom-call(bf16[128,8192]{1,0:T(8,128)(2,1)S(1)} %copy-done.2, f32[1,8192]{1,0:T(1,128)S(1)} %bitcast.11, bf16[128,512]{1,0:T(8,128)(2,1)S(1)} %copy-done.3, f32[128,128]{1,0:T(8,128)S(1)} %copy-done.5, bf16[1024,512]{1,0:T(8,128)(2,1)} %pad_maximum_fusion.refs_0_, ...), custom_call_target="tpu_custom_call" | custom-call | flops 2147483648 | bytes 14680064 | tf_op jit(solution)/shard_map/pallas_call | solution.py:284
  101.0 5.3 %all-to-all-done.3 = bf16[8,32,512]{2,1,0:T(8,128)(2,1)S(1)} async-done(((bf16[8,32,512]{2,1,0:T(8,128)(2,1)}), bf16[8,32,512]{2,1,0:T(8,128)(2,1)S(1)}, u32[]{:S(2)}, u32[]{:S(2)}) %all-to-all-start.3) | async-done | bytes 262176 | tf_op jit(solution)/shard_map/all_to_all | solution.py:283
  106.3 0.6 collective-permute-start.11
  106.9 1.2 %collective-permute-done.11 = bf16[8,32,512]{2,1,0:T(8,128)(2,1)S(1)} collective-permute-done((bf16[8,32,512]{2,1,0:T(8,128)(2,1)S(1)}, bf16[8,32,512]{2,1,0:T(8,128)(2,1)S(1)}, u32[]{:S(2)}, u32[]{:S(2)}) %collective-permute-start.11) | collective-permute-done | bytes 262176 | tf_op jit(solution)/shard_map/ppermute | solution.py:292
  108.1 0.1 select_bitcast_fusion.1
  108.1 0.1 pad_maximum_fusion.1
  108.2 0.8 copy.14
  (1 shorter events, 0.0 us)
Async XLA Ops:
  0.6 8.8 %copy-start = (bf16[512,512]{1,0:T(8,128)(2,1)S(1)}, bf16[512,512]{1,0:T(8,128)(2,1)}, u32[]{:S(2)}) copy-start(bf16[512,512]{1,0:T(8,128)(2,1)} %param.11) | copy-start | bytes 1572868
  5.3 28.1 %all-to-all-start = ((bf16[4,128,2560]{2,1,0:T(8,128)(2,1)}), bf16[4,128,2560]{2,1,0:T(8,128)(2,1)S(1)}, u32[]{:S(2)}, u32[]{:S(2)}) async-start(bf16[4,128,2560]{2,1,0:T(8,128)(2,1)} %get-tuple-element.28), calls=%async_computation | async-start | bytes 5242880 | tf_op jit(solution)/shard_map/all_to_all | solution.py:214
  9.5 5.6 %collective-permute-start.3 = (bf16[256,512]{1,0:T(8,128)(2,1)S(1)}, bf16[256,512]{1,0:T(8,128)(2,1)S(1)}, u32[]{:S(2)}, u32[]{:S(2)}) collective-permute-start(bf16[256,512]{1,0:T(8,128)(2,1)S(1)} %constant_dynamic-slice_fusion), channel_id=1, source_target_pairs={{0,16},{1,65},{2,18},{3,67},{16,32},{17,81},{18,34},{19,83},{32,48... | collective-permute-start | bytes 786440 | tf_op jit(solution)/shard_map/ppermute | solution.py:201
  11.2 8.3 %collective-permute-start.2 = (bf16[256,512]{1,0:T(8,128)(2,1)S(1)}, bf16[256,512]{1,0:T(8,128)(2,1)S(1)}, u32[]{:S(2)}, u32[]{:S(2)}) collective-permute-start(bf16[256,512]{1,0:T(8,128)(2,1)S(1)} %constant_dynamic-slice_fusion), channel_id=1, source_target_pairs={{0,32},{1,129},{2,34},{3,131},{16,48},{17,145},{18,50},{19,147},{3... | collective-permute-start | bytes 786440 | tf_op jit(solution)/shard_map/ppermute | solution.py:201
  14.8 7.5 %collective-permute-start.1 = (bf16[256,512]{1,0:T(8,128)(2,1)S(1)}, bf16[256,512]{1,0:T(8,128)(2,1)S(1)}, u32[]{:S(2)}, u32[]{:S(2)}) collective-permute-start(bf16[256,512]{1,0:T(8,128)(2,1)S(1)} %constant_dynamic-slice_fusion), channel_id=1, source_target_pairs={{0,48},{1,195},{2,50},{3,193},{16,0},{17,211},{18,2},{19,209},{32,... | collective-permute-start | bytes 786440 | tf_op jit(solution)/shard_map/ppermute | solution.py:201
  23.3 22.9 %collective-permute-start.5 = (bf16[1024,512]{1,0:T(8,128)(2,1)}, bf16[1024,512]{1,0:T(8,128)(2,1)}, u32[]{:S(2)}, u32[]{:S(2)}) collective-permute-start(bf16[1024,512]{1,0:T(8,128)(2,1)} %pad_maximum_fusion.refs_0_), channel_id=1, source_target_pairs={{0,194},{1,49},{2,192},{3,51},{16,210},{17,1},{18,208},{19,3},{32,... | collective-permute-start | bytes 3145736 | tf_op jit(solution)/shard_map/ppermute | solution.py:205
  26.0 21.5 %collective-permute-start.7 = (bf16[1024,512]{1,0:T(8,128)(2,1)}, bf16[1024,512]{1,0:T(8,128)(2,1)}, u32[]{:S(2)}, u32[]{:S(2)}) collective-permute-start(bf16[1024,512]{1,0:T(8,128)(2,1)} %pad_maximum_fusion.refs_0_), channel_id=1, source_target_pairs={{0,64},{1,17},{2,66},{3,19},{16,80},{17,33},{18,82},{19,35},{32,96... | collective-permute-start | bytes 3145736 | tf_op jit(solution)/shard_map/ppermute | solution.py:205
  34.6 1.3 %copy-start.1 = (bf16[4,512,512]{2,1,0:T(8,128)(2,1)}, bf16[4,512,512]{2,1,0:T(8,128)(2,1)S(1)}, u32[]{:S(2)}) copy-start(bf16[4,512,512]{2,1,0:T(8,128)(2,1)S(1)} %shard_map.128) | copy-start | bytes 6291460
  36.0 19.7 %all-to-all-start.1 = ((bf16[4,512,512]{2,1,0:T(8,128)(2,1)}), bf16[4,512,512]{2,1,0:T(8,128)(2,1)S(1)}, u32[]{:S(2)}, u32[]{:S(2)}) async-start(bf16[4,512,512]{2,1,0:T(8,128)(2,1)} %copy-done.1), calls=%async_computation.1 | async-start | bytes 4194304 | tf_op jit(solution)/shard_map/all_to_all | solution.py:214
  40.0 18.1 %collective-permute-start.4 = (bf16[1024,512]{1,0:T(8,128)(2,1)}, bf16[1024,512]{1,0:T(8,128)(2,1)}, u32[]{:S(2)}, u32[]{:S(2)}) collective-permute-start(bf16[1024,512]{1,0:T(8,128)(2,1)} %pad_maximum_fusion.refs_0_), channel_id=1, source_target_pairs={{0,1},{1,0},{2,3},{3,2},{4,5},{5,4},{6,7},{7,6},{8,9},{9,8},{10,11... | collective-permute-start | bytes 3145736 | tf_op jit(solution)/shard_map/ppermute | solution.py:244
  46.2 11.9 %collective-permute-start.6 = (bf16[1024,512]{1,0:T(8,128)(2,1)}, bf16[1024,512]{1,0:T(8,128)(2,1)}, u32[]{:S(2)}, u32[]{:S(2)}) collective-permute-start(bf16[1024,512]{1,0:T(8,128)(2,1)} %collective-permute-done.5.refs_2_), channel_id=1, source_target_pairs={{0,1},{1,0},{2,3},{3,2},{4,5},{5,4},{6,7},{7,6},{8,9},{9,8},{10,11... | collective-permute-start | bytes 3145736 | tf_op jit(solution)/shard_map/ppermute | solution.py:244
  47.5 10.7 %collective-permute-start.8 = (bf16[1024,512]{1,0:T(8,128)(2,1)}, bf16[1024,512]{1,0:T(8,128)(2,1)}, u32[]{:S(2)}, u32[]{:S(2)}) collective-permute-start(bf16[1024,512]{1,0:T(8,128)(2,1)} %collective-permute-done.7.refs_4_), channel_id=1, source_target_pairs={{0,1},{1,0},{2,3},{3,2},{4,5},{5,4},{6,7},{7,6},{8,9},{9,8},{10,11... | collective-permute-start | bytes 3145736 | tf_op jit(solution)/shard_map/ppermute | solution.py:244
  55.9 2.1 %collective-permute-start = (bf16[256,512]{1,0:T(8,128)(2,1)S(1)}, bf16[256,512]{1,0:T(8,128)(2,1)S(1)}, u32[]{:S(2)}, u32[]{:S(2)}) collective-permute-start(bf16[256,512]{1,0:T(8,128)(2,1)S(1)} %get-tuple-element.30), channel_id=1, source_target_pairs={{0,1},{1,0},{2,3},{3,2},{4,5},{5,4},{6,7},{7,6},{8,9},{9,8},{10,11... | collective-permute-start | bytes 786440 | tf_op jit(solution)/shard_map/ppermute | solution.py:261
  58.0 27.4 %copy-start.6 = (f32[16,1024]{1,0:T(8,128)S(1)}, f32[16,1024]{1,0:T(8,128)}, u32[]{:S(2)}) copy-start(f32[16,1024]{1,0:T(8,128)} %first_ref.1) | copy-start | bytes 196612
  58.0 27.3 %copy-start.7 = (f32[16,1024]{1,0:T(8,128)S(1)}, f32[16,1024]{1,0:T(8,128)}, u32[]{:S(2)}) copy-start(f32[16,1024]{1,0:T(8,128)} %second_ref.1) | copy-start | bytes 196612
  58.1 27.3 %copy-start.8 = (f32[32,512]{1,0:T(8,128)S(1)}, f32[32,512]{1,0:T(8,128)}, u32[]{:S(2)}) copy-start(f32[32,512]{1,0:T(8,128)} %master_ref.1) | copy-start | bytes 196612
  58.1 27.3 %copy-start.9 = (s32[1024]{0:T(1024)S(1)}, s32[1024]{0:T(1024)}, u32[]{:S(2)}) copy-start(s32[1024]{0:T(1024)} %param.15) | copy-start | bytes 12292
  58.1 33.9 %copy-start.2 = (bf16[128,8192]{1,0:T(8,128)(2,1)S(1)}, bf16[128,8192]{1,0:T(8,128)(2,1)}, u32[]{:S(2)}) copy-start(bf16[128,8192]{1,0:T(8,128)(2,1)} %tok_ref.3) | copy-start | bytes 6291460
  58.1 33.9 %copy-start.3 = (bf16[128,512]{1,0:T(8,128)(2,1)S(1)}, bf16[128,512]{1,0:T(8,128)(2,1)}, u32[]{:S(2)}) copy-start(bf16[128,512]{1,0:T(8,128)(2,1)} %cot_ref.3) | copy-start | bytes 393220
  58.1 33.9 %copy-start.4 = (f32[8192]{0:T(1024)S(1)}, f32[8192]{0:T(1024)}, u32[]{:S(2)}) copy-start(f32[8192]{0:T(1024)} %param.9) | copy-start | bytes 98308
  58.1 33.9 %copy-start.5 = (f32[128,128]{1,0:T(8,128)S(1)}, f32[128,128]{1,0:T(8,128)}, u32[]{:S(2)}) copy-start(f32[128,128]{1,0:T(8,128)} %get-tuple-element.36.inv_ref) | copy-start | bytes 196612
  59.7 17.7 %collective-permute-start.9 = (bf16[1024,512]{1,0:T(8,128)(2,1)S(1)}, bf16[1024,512]{1,0:T(8,128)(2,1)}, u32[]{:S(2)}, u32[]{:S(2)}) collective-permute-start(bf16[1024,512]{1,0:T(8,128)(2,1)S(1)} %broadcast_select_fusion), channel_id=1, source_target_pairs={{0,64},{1,17},{2,66},{3,19},{16,80},{17,1},{18,82},{19,3},{32,96},... | collective-permute-start | bytes 3145736 | tf_op jit(solution)/shard_map/ppermute | solution.py:205
  77.3 14.6 %collective-permute-start.10 = (bf16[1024,512]{1,0:T(8,128)(2,1)}, bf16[1024,512]{1,0:T(8,128)(2,1)}, u32[]{:S(2)}, u32[]{:S(2)}) collective-permute-start(bf16[1024,512]{1,0:T(8,128)(2,1)} %collective-permute-done.9.refs_6_), channel_id=1, source_target_pairs={{0,1},{1,0},{2,3},{3,2},{4,5},{5,4},{6,7},{7,6},{8,9},{9,8},{10,11... | collective-permute-start | bytes 3145736 | tf_op jit(solution)/shard_map/ppermute | solution.py:269
  86.6 19.7 %all-to-all-start.3 = ((bf16[8,32,512]{2,1,0:T(8,128)(2,1)}), bf16[8,32,512]{2,1,0:T(8,128)(2,1)S(1)}, u32[]{:S(2)}, u32[]{:S(2)}) async-start(bf16[8,32,512]{2,1,0:T(8,128)(2,1)} %get-tuple-element.35), calls=%async_computation.3 | async-start | bytes 524288 | tf_op jit(solution)/shard_map/all_to_all | solution.py:283
  106.3 1.8 %collective-permute-start.11 = (bf16[8,32,512]{2,1,0:T(8,128)(2,1)S(1)}, bf16[8,32,512]{2,1,0:T(8,128)(2,1)S(1)}, u32[]{:S(2)}, u32[]{:S(2)}) collective-permute-start(bf16[8,32,512]{2,1,0:T(8,128)(2,1)S(1)} %all-to-all-done.3), channel_id=1, source_target_pairs={{0,1},{1,0},{2,3},{3,2},{4,5},{5,4},{6,7},{7,6},{8,9},{9,8},{10,11... | collective-permute-start | bytes 786440 | tf_op jit(solution)/shard_map/ppermute | solution.py:292

commit v6 on v5

--- a/solution.py
+++ b/solution.py
@@ -91,36 +91,47 @@
         ref[...] = jnp.sum(part, axis=0).astype(ref.dtype)
 
 
-def out_kernel(tok_ref, gain_ref, cot_ref, inv_ref, *refs):
-    w_refs, (keys_ref, tg_ref) = refs[:-2], refs[-2:]
+def places(width, refs):
     c, zl, y = (lax.axis_index(name) for name in ("c", "zl", "y"))
-    rows, width = tok_ref.shape
     step = width // (ZL * Y)
     half = step // 2
-    inv = jnp.concatenate([inv_ref[...]] * (half // inv_ref.shape[1]), axis=1)
-    cot = cot_ref[...]
-
-    def places():
-        for s, off in enumerate((0, 1, 3, 2)):
-            for h in range(2):
-                for k in range(Y):
-                    core = c if h == 0 else 1 - c
-                    on_zl, on_y = jnp.where(core == 0, off, k), jnp.where(core == 0, k, off)
-                    node = lax.rem(zl + on_zl, ZL) * Y + lax.rem(y + on_y, Y)
-                    at = pl.multiple_of(node * step + core * half, half)
-                    yield pl.ds(at, half), w_refs[2 * s + h], slice(k * half, (k + 1) * half)
-
+    for s, off in enumerate((0, 1, 3, 2)):
+        for h in range(C):
+            for k in range(Y):
+                core = c if h == 0 else 1 - c
+                on_zl, on_y = jnp.where(core == 0, off, k), jnp.where(core == 0, k, off)
+                node = lax.rem(zl + on_zl, ZL) * Y + lax.rem(y + on_y, Y)
+                at = pl.multiple_of(node * step + core * half, half)
+                ref, row = (refs[2 * s + h], k) if s < 3 else (refs[2 * (s + k // 2) + h], k % 2)
+                yield pl.ds(at, half), ref[row * half : (row + 1) * half, :]
+
+
+def widened(ref, cols):
+    return jnp.concatenate([ref[...]] * (cols // ref.shape[1]), axis=1)
+
+
+def keys_kernel(tok_ref, gain_ref, cot_ref, inv_ref, *refs):
+    refs, (keys_ref, mean_ref) = refs[:-2], refs[-2:]
+    width = tok_ref.shape[1]
+    inv = widened(inv_ref, width // (ZL * Y * C))
     keys = jnp.zeros(keys_ref.shape, F32)
-    for cols, w_ref, wrows in places():
+    for cols, weights in places(width, refs):
         normed = tok_ref[:, cols].astype(F32) * inv
         hidden = (normed * gain_ref[:, cols]).astype(BF16)
-        keys = keys + jnp.dot(hidden, w_ref[wrows, :], preferred_element_type=F32)
+        keys = keys + jnp.dot(hidden, weights, preferred_element_type=F32)
     keys_ref[...] = keys.astype(BF16)
-    mean = jnp.sum(cot.astype(F32) * keys, axis=-1, keepdims=True) / width
-    for cols, w_ref, wrows in places():
-        hidden_grad = lax.dot_general(
-            cot, w_ref[wrows, :], (((1,), (1,)), ((), ())), preferred_element_type=F32
-        )
+    mean = jnp.sum(cot_ref[...].astype(F32) * keys, axis=-1, keepdims=True) / width
+    mean_ref[...] = jnp.broadcast_to(mean, mean_ref.shape)
+
+
+def token_grad_kernel(tok_ref, gain_ref, cot_ref, inv_ref, mean_ref, *refs):
+    refs, (tg_ref,) = refs[:-1], refs[-1:]
+    width = tok_ref.shape[1]
+    inv = widened(inv_ref, width // (ZL * Y * C))
+    mean = widened(mean_ref, width // (ZL * Y * C))
+    cot = cot_ref[...]
+    for cols, weights in places(width, refs):
+        hidden_grad = lax.dot_general(cot, weights, (((1,), (1,)), ((), ())), preferred_element_type=F32)
         normed = tok_ref[:, cols].astype(F32) * inv
         tg_ref[:, cols] = (inv * (hidden_grad * gain_ref[:, cols] - normed * mean)).astype(BF16)
 
@@ -258,15 +269,26 @@
         1 << 20,
         1,
     )(blocks)
+    from_up, from_down = weights[2], weights[4]
+    rows = from_up.shape[0] // 2
+    far = [
+        second_step(from_up[:rows], lambda place, on_z: -1),
+        second_step(from_down[rows:], lambda place, on_z: 1),
+    ]
+    sib, far, weights = lax.optimization_barrier((sib, far, weights))
     sib = lax.ppermute(sib, "c", ring(C, 1))
     summed = (own + sib.astype(F32)).astype(BF16)
-    summed, *weights = lax.optimization_barrier((summed, *weights))
-    odd = jnp.where(c == 0, lax.axis_index("zl"), lax.axis_index("y")) % 2 == 1
-    from_far = jnp.where(odd, weights[2], weights[4])
-    from_far = second_step(from_far, lambda place, on_z: 1 - 2 * (place % 2))
+    for block in far:
+        weights += [block, lax.ppermute(block, "c", ring(C, 1))]
     blocks = lax.all_to_all(summed.reshape(ZL * ZH, ROWS, keys_w), ("zl", "zh"), 0, 0, tiled=True)
-    blocks, from_far = lax.optimization_barrier((blocks, from_far))
-    weights += [from_far, lax.ppermute(from_far, "c", ring(C, 1))]
+    keys, mean = kernel_call(
+        keys_kernel,
+        (shape((tok_rows, keys_w), BF16), shape((tok_rows, 128), F32)),
+        2 * tok_rows * width * keys_w,
+        11 << 20,
+        4 + len(weights),
+    )(tokens, gain, key_cotangent, inv, *weights)
+    blocks, keys, mean = lax.optimization_barrier((blocks, keys, mean))
     new_master, new_first, new_second, new_rows = kernel_call(
         functools.partial(adam_kernel, tok_rows * math.prod(SIZES)),
         (
@@ -281,14 +303,14 @@
     )(blocks, moment_first, moment_second, master, signs.reshape(1, -1))
 
     mine = lax.all_to_all(new_rows, ("x", "zh"), 0, 0, tiled=True)
-    keys, token_grad = kernel_call(
-        out_kernel,
-        (shape((tok_rows, keys_w), BF16), shape(tokens.shape, BF16)),
-        4 * tok_rows * width * keys_w,
-        14 << 20,
-        4 + len(weights),
-    )(tokens, gain, key_cotangent, inv, *weights)
-    mine, keys, token_grad = lax.optimization_barrier((mine, keys, token_grad))
+    token_grad = kernel_call(
+        token_grad_kernel,
+        shape(tokens.shape, BF16),
+        2 * tok_rows * width * keys_w,
+        13 << 20,
+        5 + len(weights),
+    )(tokens, gain, key_cotangent, inv, mean, *weights)
+    mine, token_grad = lax.optimization_barrier((mine, token_grad))
     other = lax.ppermute(mine, "c", ring(C, 1))
     even = jnp.where(c == 0, mine, other)
     odd = jnp.where(c == 0, other, mine)

time: 109 us -> 110 us (level)
  blocking collectives: 17.3 us -> 0 us
  local copies, waits for them, and re-layouts: 2.22 us -> 13.8 us
  Pallas kernels: 16.3 us -> 21.6 us
    all_to_all x1 -> x0, blocking collectives: 17.3 us -> none  [shards(): lax.all_to_all(summed.reshape(ZL * ZH, ROWS, keys_w), ('zl', 'zh'), 0, 0,...]
    ppermute x1 -> x0, starting transfers between devices: 8.04 us -> none  [shards(): weights += [from_far, lax.ppermute(from_far, 'c', ring(C, 1))]]
    unnamed x20 -> x30, local copies, waits for them, and re-layouts: 1.37 us -> 9.21 us
    all_to_all x0 -> x1, starting transfers between devices: none -> 6.3 us  [shards(): lax.all_to_all(summed.reshape(ZL * ZH, ROWS, keys_w), ('zl', 'zh'), 0, 0,...]
    all_to_all x2, waiting for transfers between devices: 15.2 us -> 9.93 us  [mixed(): lax.all_to_all(value, ('y', 'x', 'c'), 0, 0, axis_index_groups=groups, ti...]
    ppermute x3 -> x4, waiting for transfers between devices: 7.5 us -> 11.8 us  [second_step(): return lax.ppermute(value, GATHER, moved(lambda c: c == 0, shift))]
    pallas_call x1 -> x2, Pallas kernels: 8.96 us -> 12.7 us  [the longest x1 7.5 us: shards(): kernel_call(token_grad_kernel, shape(tokens.shape, BF16), 2 * tok_rows *...]
    slice x0 -> x2, local copies, waits for them, and re-layouts: none -> 3.74 us  [the longest x1 1.87 us: shards(): from_down[rows:]]
  transfers between devices with their start and end apart: 15 -> 18, of which waited for: 10 -> 13; matrix products, arithmetic and copies ran while one was open for 1% -> 5% of each run, Pallas kernels for 11% -> 15%
where the time goes in v6:
time: 110 us; the launch traced here: 109 us
  waiting for transfers between devices  38.7 us (35%)
  starting transfers between devices  32.1 us (29%)
  Pallas kernels  21.6 us (20%)
  local copies, waits for them, and re-layouts  13.8 us (13%)
  other arithmetic  1.93 us (2%)
    ppermute x4, waiting for transfers between devices, second_step(): return lax.ppermute(value, GATHER, moved(lambda c: c == 0, shift))  11.8 us
    all_to_all x2, waiting for transfers between devices, mixed(): lax.all_to_all(value, ('y', 'x', 'c'), 0, 0, axis_index_groups=groups, ti...  9.93 us
    unnamed x30, local copies, waits for them, and re-layouts  9.21 us
    all_to_all x2, starting transfers between devices, mixed(): lax.all_to_all(value, ('y', 'x', 'c'), 0, 0, axis_index_groups=groups, ti...  8.62 us
    pallas_call x1, Pallas kernels, shards(): kernel_call(token_grad_kernel, shape(tokens.shape, BF16), 2 * tok_rows *...  7.5 us
    ppermute x3, waiting for transfers between devices, first_step(): return lax.ppermute(value, GATHER, moved(lambda c: c == 1, shift))  7.49 us
    all_to_all x1, starting transfers between devices, shards(): lax.all_to_all(summed.reshape(ZL * ZH, ROWS, keys_w), ('zl', 'zh'), 0, 0,...  6.3 us
    ppermute x3, starting transfers between devices, first_step(): return lax.ppermute(value, GATHER, moved(lambda c: c == 1, shift))  5.29 us
  transfers between devices with their start and end apart: 18, of which 13 were waited for; matrix products, arithmetic and copies ran while one was open for 5% of the time, Pallas kernels for 15%

profile of v6, /device:TPU:33, one launch (start us, length us, event | category | flops | bytes accessed | tf_op | source)
XLA Modules:
  0.0 108.9 jit_solution(1091862612307448228)
XLA Ops:
  0.6 0.0 copy-start
  0.6 4.6 %shard_map.127 = (bf16[4,128,2560]{2,1,0:T(8,128)(2,1)}, f32[128,128]{1,0:T(8,128)}) custom-call(bf16[128,8192]{1,0:T(8,128)(2,1)} %tok_ref.5, f32[1,8192]{1,0:T(1,128)} %bitcast.10, bf16[128,512]{1,0:T(8,128)(2,1)} %cot_ref.5), custom_call_target="tpu_custom_call" | custom-call | flops 6291456 | bytes 5242880 | tf_op jit(solution)/shard_map/pallas_call | solution.py:241
  5.3 4.2 %all-to-all-start = ((bf16[4,128,2560]{2,1,0:T(8,128)(2,1)}), bf16[4,128,2560]{2,1,0:T(8,128)(2,1)S(1)}, u32[]{:S(2)}, u32[]{:S(2)}) async-start(bf16[4,128,2560]{2,1,0:T(8,128)(2,1)} %get-tuple-element.30), calls=%async_computation | async-start | bytes 5242880 | tf_op jit(solution)/shard_map/all_to_all | solution.py:225
  9.5 0.0 copy-done
  9.5 1.7 %collective-permute-start.2 = (bf16[256,512]{1,0:T(8,128)(2,1)S(1)}, bf16[256,512]{1,0:T(8,128)(2,1)S(1)}, u32[]{:S(2)}, u32[]{:S(2)}) collective-permute-start(bf16[256,512]{1,0:T(8,128)(2,1)S(1)} %constant_dynamic-slice_fusion), channel_id=1, source_target_pairs={{0,16},{1,65},{2,18},{3,67},{16,32},{17,81},{18,34},{19,83},{32,48... | collective-permute-start | bytes 786440 | tf_op jit(solution)/shard_map/ppermute | solution.py:212
  11.2 3.6 %collective-permute-start.1 = (bf16[256,512]{1,0:T(8,128)(2,1)S(1)}, bf16[256,512]{1,0:T(8,128)(2,1)S(1)}, u32[]{:S(2)}, u32[]{:S(2)}) collective-permute-start(bf16[256,512]{1,0:T(8,128)(2,1)S(1)} %constant_dynamic-slice_fusion), channel_id=1, source_target_pairs={{0,32},{1,129},{2,34},{3,131},{16,48},{17,145},{18,50},{19,147},{3... | collective-permute-start | bytes 786440 | tf_op jit(solution)/shard_map/ppermute | solution.py:212
  14.8 0.0 collective-permute-start
  14.8 0.3 collective-permute-done.2
  15.1 4.4 %collective-permute-done.1 = bf16[256,512]{1,0:T(8,128)(2,1)S(1)} collective-permute-done((bf16[256,512]{1,0:T(8,128)(2,1)S(1)}, bf16[256,512]{1,0:T(8,128)(2,1)S(1)}, u32[]{:S(2)}, u32[]{:S(2)}) %collective-permute-start.1) | collective-permute-done | bytes 262176 | tf_op jit(solution)/shard_map/ppermute | solution.py:212
  19.5 2.8 %collective-permute-done = bf16[256,512]{1,0:T(8,128)(2,1)S(1)} collective-permute-done((bf16[256,512]{1,0:T(8,128)(2,1)S(1)}, bf16[256,512]{1,0:T(8,128)(2,1)S(1)}, u32[]{:S(2)}, u32[]{:S(2)}) %collective-permute-start) | collective-permute-done | bytes 262176 | tf_op jit(solution)/shard_map/ppermute | solution.py:212
  22.3 1.1 pad_maximum_fusion.refs_0_
  23.3 2.7 %collective-permute-start.3 = (bf16[1024,512]{1,0:T(8,128)(2,1)}, bf16[1024,512]{1,0:T(8,128)(2,1)}, u32[]{:S(2)}, u32[]{:S(2)}) collective-permute-start(bf16[1024,512]{1,0:T(8,128)(2,1)} %pad_maximum_fusion.refs_0_), channel_id=1, source_target_pairs={{0,194},{1,49},{2,192},{3,51},{16,210},{17,1},{18,208},{19,3},{32,... | collective-permute-start | bytes 3145736 | tf_op jit(solution)/shard_map/ppermute | solution.py:216
  26.0 0.0 collective-permute-start.5
  26.0 7.3 %all-to-all-done = bf16[4,128,2560]{2,1,0:T(8,128)(2,1)S(1)} async-done(((bf16[4,128,2560]{2,1,0:T(8,128)(2,1)}), bf16[4,128,2560]{2,1,0:T(8,128)(2,1)S(1)}, u32[]{:S(2)}, u32[]{:S(2)}) %all-to-all-start) | async-done | bytes 2621472 | tf_op jit(solution)/shard_map/all_to_all | solution.py:225
  33.4 1.3 %shard_map.128 = bf16[4,512,512]{2,1,0:T(8,128)(2,1)S(1)} custom-call(bf16[512,2560]{1,0:T(8,128)(2,1)S(1)} %bitcast.9), custom_call_target="tpu_custom_call" | custom-call | bytes 1048576 | tf_op jit(solution)/shard_map/pallas_call | solution.py:256
  34.7 0.0 copy-start.2
  34.7 1.3 %copy-done.2 = bf16[4,512,512]{2,1,0:T(8,128)(2,1)} copy-done((bf16[4,512,512]{2,1,0:T(8,128)(2,1)}, bf16[4,512,512]{2,1,0:T(8,128)(2,1)S(1)}, u32[]{:S(2)}) %copy-start.2) | copy-done | bytes 2097176
  36.0 4.4 %all-to-all-start.1 = ((bf16[4,512,512]{2,1,0:T(8,128)(2,1)}), bf16[4,512,512]{2,1,0:T(8,128)(2,1)}, u32[]{:S(2)}, u32[]{:S(2)}) async-start(bf16[4,512,512]{2,1,0:T(8,128)(2,1)} %copy-done.2), calls=%async_computation.1 | async-start | bytes 4194304 | tf_op jit(solution)/shard_map/all_to_all | solution.py:225
  40.4 0.1 collective-permute-start.7
  40.5 5.3 %collective-permute-done.3.refs_2_ = bf16[1024,512]{1,0:T(8,128)(2,1)} collective-permute-done((bf16[1024,512]{1,0:T(8,128)(2,1)}, bf16[1024,512]{1,0:T(8,128)(2,1)}, u32[]{:S(2)}, u32[]{:S(2)}) %collective-permute-start.3) | collective-permute-done | bytes 1048608 | tf_op jit(solution)/shard_map/ppermute | solution.py:216
  45.9 0.0 collective-permute-start.8
  45.9 1.4 %collective-permute-done.5.refs_4_ = bf16[1024,512]{1,0:T(8,128)(2,1)} collective-permute-done((bf16[1024,512]{1,0:T(8,128)(2,1)}, bf16[1024,512]{1,0:T(8,128)(2,1)}, u32[]{:S(2)}, u32[]{:S(2)}) %collective-permute-start.5) | collective-permute-done | bytes 1048608 | tf_op jit(solution)/shard_map/ppermute | solution.py:216
  47.2 0.6 collective-permute-start.9
  47.8 1.9 %slice.8 = bf16[512,512]{1,0:T(8,128)(2,1)} slice(bf16[1024,512]{1,0:T(8,128)(2,1)} %collective-permute-done.3.refs_2_), slice={[0:512], [0:512]} | slice | bytes 1048576 | tf_op jit(solution)/shard_map/slice | solution.py:275
  49.7 2.0 %collective-permute-start.4 = (bf16[512,512]{1,0:T(8,128)(2,1)}, bf16[512,512]{1,0:T(8,128)(2,1)S(1)}, u32[]{:S(2)}, u32[]{:S(2)}) collective-permute-start(bf16[512,512]{1,0:T(8,128)(2,1)} %slice.8), channel_id=1, source_target_pairs={{0,194},{1,49},{2,192},{3,51},{16,210},{17,1},{18,208},{19,3},{32,... | collective-permute-start | bytes 1572872 | tf_op jit(solution)/shard_map/ppermute | solution.py:216
  51.7 1.9 %slice.9 = bf16[512,512]{1,0:T(8,128)(2,1)} slice(bf16[1024,512]{1,0:T(8,128)(2,1)} %collective-permute-done.5.refs_4_), slice={[512:1024], [0:512]} | slice | bytes 1048576 | tf_op jit(solution)/shard_map/slice | solution.py:276
  53.5 0.0 collective-permute-start.6
  53.5 2.6 %all-to-all-done.1.recv_ref = bf16[4,512,512]{2,1,0:T(8,128)(2,1)} async-done(((bf16[4,512,512]{2,1,0:T(8,128)(2,1)}), bf16[4,512,512]{2,1,0:T(8,128)(2,1)}, u32[]{:S(2)}, u32[]{:S(2)}) %all-to-all-start.1) | async-done | bytes 2097184 | tf_op jit(solution)/shard_map/all_to_all | solution.py:225
  56.1 1.8 %shard_map.129 = (f32[256,512]{1,0:T(8,128)S(1)}, bf16[256,512]{1,0:T(8,128)(2,1)S(1)}) custom-call(bf16[4,512,512]{2,1,0:T(8,128)(2,1)} %all-to-all-done.1.recv_ref), custom_call_target="tpu_custom_call" | custom-call | bytes 1048576 | tf_op jit(solution)/shard_map/pallas_call | solution.py:265
  58.0 0.0 collective-permute-done.7.refs_1_
  58.0 2.3 %collective-permute-done.4.refs_6_ = bf16[512,512]{1,0:T(8,128)(2,1)S(1)} collective-permute-done((bf16[512,512]{1,0:T(8,128)(2,1)}, bf16[512,512]{1,0:T(8,128)(2,1)S(1)}, u32[]{:S(2)}, u32[]{:S(2)}) %collective-permute-start.4) | collective-permute-done | bytes 524320 | tf_op jit(solution)/shard_map/ppermute | solution.py:216
  60.3 2.8 %collective-permute-done.6.refs_8_ = bf16[512,512]{1,0:T(8,128)(2,1)} collective-permute-done((bf16[512,512]{1,0:T(8,128)(2,1)}, bf16[512,512]{1,0:T(8,128)(2,1)}, u32[]{:S(2)}, u32[]{:S(2)}) %collective-permute-start.6) | collective-permute-done | bytes 524320 | tf_op jit(solution)/shard_map/ppermute | solution.py:216
  63.1 0.0 collective-permute-done.8.refs_3_
  63.1 0.0 collective-permute-done.9.refs_5_
  63.1 1.2 %collective-permute-start.10 = (bf16[256,512]{1,0:T(8,128)(2,1)S(1)}, bf16[256,512]{1,0:T(8,128)(2,1)S(1)}, u32[]{:S(2)}, u32[]{:S(2)}) collective-permute-start(bf16[256,512]{1,0:T(8,128)(2,1)S(1)} %get-tuple-element.33), channel_id=1, source_target_pairs={{0,1},{1,0},{2,3},{3,2},{4,5},{5,4},{6,7},{7,6},{8,9},{9,8},{10,11... | collective-permute-start | bytes 786440 | tf_op jit(solution)/shard_map/ppermute | solution.py:279
  64.3 0.1 collective-permute-start.11
  64.4 0.4 collective-permute-start.12
  64.8 0.7 collective-permute-done.10
  65.5 0.8 add_convert_fusion
  66.2 6.3 %all-to-all-start.2 = ((bf16[8,32,512]{2,1,0:T(8,128)(2,1)}), bf16[8,32,512]{2,1,0:T(8,128)(2,1)S(1)}, u32[]{:S(2)}, u32[]{:S(2)}) async-start(bf16[8,32,512]{2,1,0:T(8,128)(2,1)} %bitcast.14), calls=%async_computation.2 | async-start | bytes 524288 | tf_op jit(solution)/shard_map/all_to_all | solution.py:283
  72.5 0.0 collective-permute-done.11.refs_7_
  72.5 0.0 collective-permute-done.12.refs_9_
  72.5 0.0 copy-done.1
  72.6 0.0 copy-start.4
  72.6 0.7 copy-done.4
  73.3 0.8 copy-done.6
  74.2 5.2 %shard_map.130 = (bf16[128,512]{1,0:T(8,128)(2,1)}, f32[128,128]{1,0:T(8,128)S(1)}) custom-call(bf16[128,8192]{1,0:T(8,128)(2,1)S(1)} %copy-done.1, f32[1,8192]{1,0:T(1,128)S(1)} %bitcast.11, bf16[128,512]{1,0:T(8,128)(2,1)S(1)} %copy-done.3, f32[128,128]{1,0:T(8,128)S(1)} %copy-done.6, bf16[1024,512]{1,0:T(8,128)(2,1)} %pad_maximum_fusion.refs_0_, ...), custom_call_target="tpu_custom_call" | custom-call | flops 1073741824 | bytes 11534336 | tf_op jit(solution)/shard_map/pallas_call | solution.py:284
  79.4 0.6 copy-done.9
  80.0 3.3 %all-to-all-done.2.recv_ref = bf16[8,32,512]{2,1,0:T(8,128)(2,1)S(1)} async-done(((bf16[8,32,512]{2,1,0:T(8,128)(2,1)}), bf16[8,32,512]{2,1,0:T(8,128)(2,1)S(1)}, u32[]{:S(2)}, u32[]{:S(2)}) %all-to-all-start.2) | async-done | bytes 262176 | tf_op jit(solution)/shard_map/all_to_all | solution.py:283
  83.3 0.8 copy-done.11
  84.2 0.8 copy-done.12
  85.0 0.8 copy-done.13
  85.9 1.1 %shard_map.131 = (f32[32,512]{1,0:T(8,128)}, f32[16,1024]{1,0:T(8,128)}, f32[16,1024]{1,0:T(8,128)}, bf16[8,32,512]{2,1,0:T(8,128)(2,1)S(1)}) custom-call(bf16[8,32,512]{2,1,0:T(8,128)(2,1)S(1)} %all-to-all-done.2.recv_ref, f32[16,1024]{1,0:T(8,128)S(1)} %copy-done.11, f32[16,1024]{1,0:T(8,128)S(1)} %copy-done.12, f32[32,512]{1,0:T(8,128)S(1)} %copy-done.13, ...), custom_call_target="tpu_custom_call" | custom-call | flops 33554432 | bytes 1048576 | tf_op jit(solution)/shard_map/pallas_call | solution.py:292
  87.0 0.7 copy-done.8
  87.7 4.3 %all-to-all-start.3 = ((bf16[8,32,512]{2,1,0:T(8,128)(2,1)}), bf16[8,32,512]{2,1,0:T(8,128)(2,1)S(1)}, u32[]{:S(2)}, u32[]{:S(2)}) async-start(bf16[8,32,512]{2,1,0:T(8,128)(2,1)} %copy-done.8), calls=%async_computation.3 | async-start | bytes 524288 | tf_op jit(solution)/shard_map/all_to_all | solution.py:305
  92.0 0.8 copy-done.5
  92.7 0.8 copy-done.7
  93.6 0.8 copy-done.10
  94.4 7.5 %shard_map.132 = bf16[128,8192]{1,0:T(8,128)(2,1)} custom-call(bf16[128,8192]{1,0:T(8,128)(2,1)S(1)} %copy-done.1, f32[1,8192]{1,0:T(1,128)S(1)} %bitcast.12, bf16[128,512]{1,0:T(8,128)(2,1)S(1)} %copy-done.3, f32[128,128]{1,0:T(8,128)S(1)} %copy-done.7, f32[128,128]{1,0:T(8,128)S(1)} %copy-done.10, bf16[1024,512]{1,0:T(8,128)(2,1)} %pad_maximum_fusion.refs_0_, ...), custom_call_target="tpu_custom_call" | custom-call | flops 1073741824 | bytes 13631488 | tf_op jit(solution)/shard_map/pallas_call | solution.py:306
  101.9 4.3 %all-to-all-done.3 = bf16[8,32,512]{2,1,0:T(8,128)(2,1)S(1)} async-done(((bf16[8,32,512]{2,1,0:T(8,128)(2,1)}), bf16[8,32,512]{2,1,0:T(8,128)(2,1)S(1)}, u32[]{:S(2)}, u32[]{:S(2)}) %all-to-all-start.3) | async-done | bytes 262176 | tf_op jit(solution)/shard_map/all_to_all | solution.py:305
  106.2 0.6 collective-permute-start.13
  106.8 1.2 %collective-permute-done.13 = bf16[8,32,512]{2,1,0:T(8,128)(2,1)S(1)} collective-permute-done((bf16[8,32,512]{2,1,0:T(8,128)(2,1)S(1)}, bf16[8,32,512]{2,1,0:T(8,128)(2,1)S(1)}, u32[]{:S(2)}, u32[]{:S(2)}) %collective-permute-start.13) | collective-permute-done | bytes 262176 | tf_op jit(solution)/shard_map/ppermute | solution.py:314
  108.0 0.1 pad_maximum_fusion.1
  108.1 0.8 copy.14
  (16 shorter events, 0.1 us)
Async XLA Ops:
  0.6 8.8 %copy-start = (bf16[512,512]{1,0:T(8,128)(2,1)S(1)}, bf16[512,512]{1,0:T(8,128)(2,1)}, u32[]{:S(2)}) copy-start(bf16[512,512]{1,0:T(8,128)(2,1)} %param.11) | copy-start | bytes 1572868
  5.3 28.1 %all-to-all-start = ((bf16[4,128,2560]{2,1,0:T(8,128)(2,1)}), bf16[4,128,2560]{2,1,0:T(8,128)(2,1)S(1)}, u32[]{:S(2)}, u32[]{:S(2)}) async-start(bf16[4,128,2560]{2,1,0:T(8,128)(2,1)} %get-tuple-element.30), calls=%async_computation | async-start | bytes 5242880 | tf_op jit(solution)/shard_map/all_to_all | solution.py:225
  9.5 5.6 %collective-permute-start.2 = (bf16[256,512]{1,0:T(8,128)(2,1)S(1)}, bf16[256,512]{1,0:T(8,128)(2,1)S(1)}, u32[]{:S(2)}, u32[]{:S(2)}) collective-permute-start(bf16[256,512]{1,0:T(8,128)(2,1)S(1)} %constant_dynamic-slice_fusion), channel_id=1, source_target_pairs={{0,16},{1,65},{2,18},{3,67},{16,32},{17,81},{18,34},{19,83},{32,48... | collective-permute-start | bytes 786440 | tf_op jit(solution)/shard_map/ppermute | solution.py:212
  11.2 8.3 %collective-permute-start.1 = (bf16[256,512]{1,0:T(8,128)(2,1)S(1)}, bf16[256,512]{1,0:T(8,128)(2,1)S(1)}, u32[]{:S(2)}, u32[]{:S(2)}) collective-permute-start(bf16[256,512]{1,0:T(8,128)(2,1)S(1)} %constant_dynamic-slice_fusion), channel_id=1, source_target_pairs={{0,32},{1,129},{2,34},{3,131},{16,48},{17,145},{18,50},{19,147},{3... | collective-permute-start | bytes 786440 | tf_op jit(solution)/shard_map/ppermute | solution.py:212
  14.8 7.5 %collective-permute-start = (bf16[256,512]{1,0:T(8,128)(2,1)S(1)}, bf16[256,512]{1,0:T(8,128)(2,1)S(1)}, u32[]{:S(2)}, u32[]{:S(2)}) collective-permute-start(bf16[256,512]{1,0:T(8,128)(2,1)S(1)} %constant_dynamic-slice_fusion), channel_id=1, source_target_pairs={{0,48},{1,195},{2,50},{3,193},{16,0},{17,211},{18,2},{19,209},{32,... | collective-permute-start | bytes 786440 | tf_op jit(solution)/shard_map/ppermute | solution.py:212
  23.3 22.5 %collective-permute-start.3 = (bf16[1024,512]{1,0:T(8,128)(2,1)}, bf16[1024,512]{1,0:T(8,128)(2,1)}, u32[]{:S(2)}, u32[]{:S(2)}) collective-permute-start(bf16[1024,512]{1,0:T(8,128)(2,1)} %pad_maximum_fusion.refs_0_), channel_id=1, source_target_pairs={{0,194},{1,49},{2,192},{3,51},{16,210},{17,1},{18,208},{19,3},{32,... | collective-permute-start | bytes 3145736 | tf_op jit(solution)/shard_map/ppermute | solution.py:216
  26.0 21.2 %collective-permute-start.5 = (bf16[1024,512]{1,0:T(8,128)(2,1)}, bf16[1024,512]{1,0:T(8,128)(2,1)}, u32[]{:S(2)}, u32[]{:S(2)}) collective-permute-start(bf16[1024,512]{1,0:T(8,128)(2,1)} %pad_maximum_fusion.refs_0_), channel_id=1, source_target_pairs={{0,64},{1,17},{2,66},{3,19},{16,80},{17,33},{18,82},{19,35},{32,96... | collective-permute-start | bytes 3145736 | tf_op jit(solution)/shard_map/ppermute | solution.py:216
  34.7 1.3 %copy-start.2 = (bf16[4,512,512]{2,1,0:T(8,128)(2,1)}, bf16[4,512,512]{2,1,0:T(8,128)(2,1)S(1)}, u32[]{:S(2)}) copy-start(bf16[4,512,512]{2,1,0:T(8,128)(2,1)S(1)} %shard_map.128) | copy-start | bytes 6291460
  36.0 20.2 %all-to-all-start.1 = ((bf16[4,512,512]{2,1,0:T(8,128)(2,1)}), bf16[4,512,512]{2,1,0:T(8,128)(2,1)}, u32[]{:S(2)}, u32[]{:S(2)}) async-start(bf16[4,512,512]{2,1,0:T(8,128)(2,1)} %copy-done.2), calls=%async_computation.1 | async-start | bytes 4194304 | tf_op jit(solution)/shard_map/all_to_all | solution.py:225
  40.4 17.6 %collective-permute-start.7 = (bf16[1024,512]{1,0:T(8,128)(2,1)}, bf16[1024,512]{1,0:T(8,128)(2,1)}, u32[]{:S(2)}, u32[]{:S(2)}) collective-permute-start(bf16[1024,512]{1,0:T(8,128)(2,1)} %pad_maximum_fusion.refs_0_), channel_id=1, source_target_pairs={{0,1},{1,0},{2,3},{3,2},{4,5},{5,4},{6,7},{7,6},{8,9},{9,8},{10,11... | collective-permute-start | bytes 3145736 | tf_op jit(solution)/shard_map/ppermute | solution.py:255
  45.9 17.2 %collective-permute-start.8 = (bf16[1024,512]{1,0:T(8,128)(2,1)}, bf16[1024,512]{1,0:T(8,128)(2,1)}, u32[]{:S(2)}, u32[]{:S(2)}) collective-permute-start(bf16[1024,512]{1,0:T(8,128)(2,1)} %collective-permute-done.3.refs_2_), channel_id=1, source_target_pairs={{0,1},{1,0},{2,3},{3,2},{4,5},{5,4},{6,7},{7,6},{8,9},{9,8},{10,11... | collective-permute-start | bytes 3145736 | tf_op jit(solution)/shard_map/ppermute | solution.py:255
  47.2 15.9 %collective-permute-start.9 = (bf16[1024,512]{1,0:T(8,128)(2,1)}, bf16[1024,512]{1,0:T(8,128)(2,1)}, u32[]{:S(2)}, u32[]{:S(2)}) collective-permute-start(bf16[1024,512]{1,0:T(8,128)(2,1)} %collective-permute-done.5.refs_4_), channel_id=1, source_target_pairs={{0,1},{1,0},{2,3},{3,2},{4,5},{5,4},{6,7},{7,6},{8,9},{9,8},{10,11... | collective-permute-start | bytes 3145736 | tf_op jit(solution)/shard_map/ppermute | solution.py:255
  49.7 10.6 %collective-permute-start.4 = (bf16[512,512]{1,0:T(8,128)(2,1)}, bf16[512,512]{1,0:T(8,128)(2,1)S(1)}, u32[]{:S(2)}, u32[]{:S(2)}) collective-permute-start(bf16[512,512]{1,0:T(8,128)(2,1)} %slice.8), channel_id=1, source_target_pairs={{0,194},{1,49},{2,192},{3,51},{16,210},{17,1},{18,208},{19,3},{32,... | collective-permute-start | bytes 1572872 | tf_op jit(solution)/shard_map/ppermute | solution.py:216
  53.5 19.0 %copy-start.1 = (bf16[128,8192]{1,0:T(8,128)(2,1)S(1)}, bf16[128,8192]{1,0:T(8,128)(2,1)}, u32[]{:S(2)}) copy-start(bf16[128,8192]{1,0:T(8,128)(2,1)} %tok_ref.5) | copy-start | bytes 6291460
  53.5 19.0 %copy-start.3 = (bf16[128,512]{1,0:T(8,128)(2,1)S(1)}, bf16[128,512]{1,0:T(8,128)(2,1)}, u32[]{:S(2)}) copy-start(bf16[128,512]{1,0:T(8,128)(2,1)} %cot_ref.5) | copy-start | bytes 393220
  53.5 9.6 %collective-permute-start.6 = (bf16[512,512]{1,0:T(8,128)(2,1)}, bf16[512,512]{1,0:T(8,128)(2,1)}, u32[]{:S(2)}, u32[]{:S(2)}) collective-permute-start(bf16[512,512]{1,0:T(8,128)(2,1)} %slice.9), channel_id=1, source_target_pairs={{0,64},{1,17},{2,66},{3,19},{16,80},{17,33},{18,82},{19,35},{32,96... | collective-permute-start | bytes 1572872 | tf_op jit(solution)/shard_map/ppermute | solution.py:216
  63.1 2.3 %collective-permute-start.10 = (bf16[256,512]{1,0:T(8,128)(2,1)S(1)}, bf16[256,512]{1,0:T(8,128)(2,1)S(1)}, u32[]{:S(2)}, u32[]{:S(2)}) collective-permute-start(bf16[256,512]{1,0:T(8,128)(2,1)S(1)} %get-tuple-element.33), channel_id=1, source_target_pairs={{0,1},{1,0},{2,3},{3,2},{4,5},{5,4},{6,7},{7,6},{8,9},{9,8},{10,11... | collective-permute-start | bytes 786440 | tf_op jit(solution)/shard_map/ppermute | solution.py:279
  64.3 8.2 %collective-permute-start.11 = (bf16[512,512]{1,0:T(8,128)(2,1)S(1)}, bf16[512,512]{1,0:T(8,128)(2,1)}, u32[]{:S(2)}, u32[]{:S(2)}) collective-permute-start(bf16[512,512]{1,0:T(8,128)(2,1)S(1)} %collective-permute-done.4.refs_6_), channel_id=1, source_target_pairs={{0,1},{1,0},{2,3},{3,2},{4,5},{5,4},{6,7},{7,6},{8,9},{9,8},{10,11... | collective-permute-start | bytes 1572872 | tf_op jit(solution)/shard_map/ppermute | solution.py:282
  64.4 8.2 %collective-permute-start.12 = (bf16[512,512]{1,0:T(8,128)(2,1)}, bf16[512,512]{1,0:T(8,128)(2,1)}, u32[]{:S(2)}, u32[]{:S(2)}) collective-permute-start(bf16[512,512]{1,0:T(8,128)(2,1)} %collective-permute-done.6.refs_8_), channel_id=1, source_target_pairs={{0,1},{1,0},{2,3},{3,2},{4,5},{5,4},{6,7},{7,6},{8,9},{9,8},{10,11... | collective-permute-start | bytes 1572872 | tf_op jit(solution)/shard_map/ppermute | solution.py:282
  66.2 17.1 %all-to-all-start.2 = ((bf16[8,32,512]{2,1,0:T(8,128)(2,1)}), bf16[8,32,512]{2,1,0:T(8,128)(2,1)S(1)}, u32[]{:S(2)}, u32[]{:S(2)}) async-start(bf16[8,32,512]{2,1,0:T(8,128)(2,1)} %bitcast.14), calls=%async_computation.2 | async-start | bytes 524288 | tf_op jit(solution)/shard_map/all_to_all | solution.py:283
  72.6 0.8 copy-start.4
  73.3 0.8 copy-start.6
  74.2 9.2 %copy-start.14 = (s32[1024]{0:T(1024)S(1)}, s32[1024]{0:T(1024)}, u32[]{:S(2)}) copy-start(s32[1024]{0:T(1024)} %param.15) | copy-start | bytes 12292
  79.4 0.6 copy-start.9
  83.3 0.8 copy-start.11
  84.2 0.8 copy-start.12
  85.0 0.8 copy-start.13
  87.0 0.7 copy-start.8
  87.7 18.6 %all-to-all-start.3 = ((bf16[8,32,512]{2,1,0:T(8,128)(2,1)}), bf16[8,32,512]{2,1,0:T(8,128)(2,1)S(1)}, u32[]{:S(2)}, u32[]{:S(2)}) async-start(bf16[8,32,512]{2,1,0:T(8,128)(2,1)} %copy-done.8), calls=%async_computation.3 | async-start | bytes 524288 | tf_op jit(solution)/shard_map/all_to_all | solution.py:305
  92.0 0.8 copy-start.5
  92.7 0.8 copy-start.7
  93.6 0.8 copy-start.10
  106.2 1.8 %collective-permute-start.13 = (bf16[8,32,512]{2,1,0:T(8,128)(2,1)S(1)}, bf16[8,32,512]{2,1,0:T(8,128)(2,1)S(1)}, u32[]{:S(2)}, u32[]{:S(2)}) collective-permute-start(bf16[8,32,512]{2,1,0:T(8,128)(2,1)S(1)} %all-to-all-done.3), channel_id=1, source_target_pairs={{0,1},{1,0},{2,3},{3,2},{4,5},{5,4},{6,7},{7,6},{8,9},{9,8},{10,11... | collective-permute-start | bytes 786440 | tf_op jit(solution)/shard_map/ppermute | solution.py:314

commit v7 on v6

--- a/solution.py
+++ b/solution.py
@@ -236,7 +236,7 @@
     column = jnp.concatenate([half] + [first_step(half, k) for k in range(1, Y)], axis=0)
 
     part = width // X
-    step = 32
+    step = 64
     by_rows = lambda cols: pl.BlockSpec((step, cols), lambda i: (i, 0))
     send, inv = pl.pallas_call(
         norm_kernel,
@@ -275,9 +275,10 @@
         second_step(from_up[:rows], lambda place, on_z: -1),
         second_step(from_down[rows:], lambda place, on_z: 1),
     ]
-    sib, far, weights = lax.optimization_barrier((sib, far, weights))
+    sib, weights = lax.optimization_barrier((sib, weights))
     sib = lax.ppermute(sib, "c", ring(C, 1))
     summed = (own + sib.astype(F32)).astype(BF16)
+    summed, far = lax.optimization_barrier((summed, far))
     for block in far:
         weights += [block, lax.ppermute(block, "c", ring(C, 1))]
     blocks = lax.all_to_all(summed.reshape(ZL * ZH, ROWS, keys_w), ("zl", "zh"), 0, 0, tiled=True)
@@ -287,6 +288,7 @@
         2 * tok_rows * width * keys_w,
         11 << 20,
         4 + len(weights),
+        60 << 20,
     )(tokens, gain, key_cotangent, inv, *weights)
     blocks, keys, mean = lax.optimization_barrier((blocks, keys, mean))
     new_master, new_first, new_second, new_rows = kernel_call(
@@ -300,6 +302,7 @@
         1 << 25,
         1 << 20,
         5,
+        60 << 20,
     )(blocks, moment_first, moment_second, master, signs.reshape(1, -1))
 
     mine = lax.all_to_all(new_rows, ("x", "zh"), 0, 0, tiled=True)
@@ -309,6 +312,7 @@
         2 * tok_rows * width * keys_w,
         13 << 20,
         5 + len(weights),
+        60 << 20,
     )(tokens, gain, key_cotangent, inv, mean, *weights)
     mine, token_grad = lax.optimization_barrier((mine, token_grad))
     other = lax.ppermute(mine, "c", ring(C, 1))

time: 110 us -> 105 us (0.955)
  local copies, waits for them, and re-layouts: 13.8 us -> 7.56 us
    unnamed x30 -> x12, local copies, waits for them, and re-layouts: 9.21 us -> 2.99 us
    pallas_call x1, Pallas kernels: 1.84 us -> 0.25 us  [shards(): kernel_call(sum_kernel, (shape((part // Y // C, keys_w), F32), shape((par...]
    pallas_call x1, Pallas kernels: 1.11 us -> 2.27 us  [shards(): kernel_call(functools.partial(adam_kernel, tok_rows * math.prod(SIZES)),...]
    pallas_call x1, Pallas kernels: 4.64 us -> 3.54 us  [shards(): pl.pallas_call(norm_kernel, out_shape=(shape((X, tok_rows, part + keys_w)...]
where the time goes in v7:
time: 105 us; the launch traced here: 104 us
  waiting for transfers between devices  39.7 us (38%)
  starting transfers between devices  32.7 us (31%)
  Pallas kernels  21.8 us (21%)
  local copies, waits for them, and re-layouts  7.56 us (7%)
  other arithmetic  1.92 us (2%)
    ppermute x4, waiting for transfers between devices, second_step(): return lax.ppermute(value, GATHER, moved(lambda c: c == 0, shift))  12 us
    all_to_all x2, waiting for transfers between devices, mixed(): lax.all_to_all(value, ('y', 'x', 'c'), 0, 0, axis_index_groups=groups, ti...  9.23 us
    pallas_call x1, Pallas kernels, shards(): kernel_call(token_grad_kernel, shape(tokens.shape, BF16), 2 * tok_rows *...  8.36 us
    all_to_all x2, starting transfers between devices, mixed(): lax.all_to_all(value, ('y', 'x', 'c'), 0, 0, axis_index_groups=groups, ti...  8.2 us
    ppermute x3, waiting for transfers between devices, first_step(): return lax.ppermute(value, GATHER, moved(lambda c: c == 1, shift))  7.49 us
    all_to_all x1, starting transfers between devices, shards(): lax.all_to_all(summed.reshape(ZL * ZH, ROWS, keys_w), ('zl', 'zh'), 0, 0,...  6.5 us
    pallas_call x1, Pallas kernels, shards(): kernel_call(keys_kernel, (shape((tok_rows, keys_w), BF16), shape((tok_row...  6.07 us
    ppermute x3, starting transfers between devices, first_step(): return lax.ppermute(value, GATHER, moved(lambda c: c == 1, shift))  5.29 us
  transfers between devices with their start and end apart: 18, of which 13 were waited for; matrix products, arithmetic and copies ran while one was open for 5% of the time, Pallas kernels for 15%

profile of v7, /device:TPU:33, one launch (start us, length us, event | category | flops | bytes accessed | tf_op | source)
XLA Modules:
  0.0 104.4 jit_solution(6406187978213875167)
XLA Ops:
  0.6 0.0 copy-start
  0.6 3.5 %shard_map.127 = (bf16[4,128,2560]{2,1,0:T(8,128)(2,1)}, f32[128,128]{1,0:T(8,128)}) custom-call(bf16[128,8192]{1,0:T(8,128)(2,1)} %tok_ref.5, f32[1,8192]{1,0:T(1,128)} %bitcast.11, bf16[128,512]{1,0:T(8,128)(2,1)} %cot_ref.5), custom_call_target="tpu_custom_call" | custom-call | flops 6291456 | bytes 5242880 | tf_op jit(solution)/shard_map/pallas_call | solution.py:241
  4.2 4.2 %all-to-all-start = ((bf16[4,128,2560]{2,1,0:T(8,128)(2,1)}), bf16[4,128,2560]{2,1,0:T(8,128)(2,1)S(1)}, u32[]{:S(2)}, u32[]{:S(2)}) async-start(bf16[4,128,2560]{2,1,0:T(8,128)(2,1)} %get-tuple-element.31), calls=%async_computation | async-start | bytes 5242880 | tf_op jit(solution)/shard_map/all_to_all | solution.py:225
  8.4 0.0 copy-done
  8.4 1.7 %collective-permute-start.2 = (bf16[256,512]{1,0:T(8,128)(2,1)S(1)}, bf16[256,512]{1,0:T(8,128)(2,1)S(1)}, u32[]{:S(2)}, u32[]{:S(2)}) collective-permute-start(bf16[256,512]{1,0:T(8,128)(2,1)S(1)} %constant_dynamic-slice_fusion), channel_id=1, source_target_pairs={{0,16},{1,65},{2,18},{3,67},{16,32},{17,81},{18,34},{19,83},{32,48... | collective-permute-start | bytes 786440 | tf_op jit(solution)/shard_map/ppermute | solution.py:212
  10.1 3.6 %collective-permute-start.1 = (bf16[256,512]{1,0:T(8,128)(2,1)S(1)}, bf16[256,512]{1,0:T(8,128)(2,1)S(1)}, u32[]{:S(2)}, u32[]{:S(2)}) collective-permute-start(bf16[256,512]{1,0:T(8,128)(2,1)S(1)} %constant_dynamic-slice_fusion), channel_id=1, source_target_pairs={{0,32},{1,129},{2,34},{3,131},{16,48},{17,145},{18,50},{19,147},{3... | collective-permute-start | bytes 786440 | tf_op jit(solution)/shard_map/ppermute | solution.py:212
  13.7 0.0 collective-permute-start
  13.7 0.3 collective-permute-done.2
  14.0 4.4 %collective-permute-done.1 = bf16[256,512]{1,0:T(8,128)(2,1)S(1)} collective-permute-done((bf16[256,512]{1,0:T(8,128)(2,1)S(1)}, bf16[256,512]{1,0:T(8,128)(2,1)S(1)}, u32[]{:S(2)}, u32[]{:S(2)}) %collective-permute-start.1) | collective-permute-done | bytes 262176 | tf_op jit(solution)/shard_map/ppermute | solution.py:212
  18.4 2.8 %collective-permute-done = bf16[256,512]{1,0:T(8,128)(2,1)S(1)} collective-permute-done((bf16[256,512]{1,0:T(8,128)(2,1)S(1)}, bf16[256,512]{1,0:T(8,128)(2,1)S(1)}, u32[]{:S(2)}, u32[]{:S(2)}) %collective-permute-start) | collective-permute-done | bytes 262176 | tf_op jit(solution)/shard_map/ppermute | solution.py:212
  21.2 1.1 %pad_maximum_fusion.refs_0_ = bf16[1024,512]{1,0:T(8,128)(2,1)} fusion(bf16[256,512]{1,0:T(8,128)(2,1)S(1)} %collective-permute-done.2, bf16[256,512]{1,0:T(8,128)(2,1)S(1)} %collective-permute-done.1, bf16[256,512]{1,0:T(8,128)(2,1)S(1)} %collective-permute-done, bf16[256,512]{1,0:T(8,128)(2,1)S(1)} %constant_dynamic-slice_fusion), kind=kLoop, calls=%fused_computation | loop fusion | flops 4194304 | bytes 2097152 | tf_op jit(solution)/shard_map/concatenate | solution.py:236
  22.2 2.7 %collective-permute-start.4 = (bf16[1024,512]{1,0:T(8,128)(2,1)}, bf16[1024,512]{1,0:T(8,128)(2,1)}, u32[]{:S(2)}, u32[]{:S(2)}) collective-permute-start(bf16[1024,512]{1,0:T(8,128)(2,1)} %pad_maximum_fusion.refs_0_), channel_id=1, source_target_pairs={{0,194},{1,49},{2,192},{3,51},{16,210},{17,1},{18,208},{19,3},{32,... | collective-permute-start | bytes 3145736 | tf_op jit(solution)/shard_map/ppermute | solution.py:216
  24.9 0.0 collective-permute-start.6
  24.9 7.4 %all-to-all-done = bf16[4,128,2560]{2,1,0:T(8,128)(2,1)S(1)} async-done(((bf16[4,128,2560]{2,1,0:T(8,128)(2,1)}), bf16[4,128,2560]{2,1,0:T(8,128)(2,1)S(1)}, u32[]{:S(2)}, u32[]{:S(2)}) %all-to-all-start) | async-done | bytes 2621472 | tf_op jit(solution)/shard_map/all_to_all | solution.py:225
  32.3 1.3 %shard_map.128 = bf16[4,512,512]{2,1,0:T(8,128)(2,1)S(1)} custom-call(bf16[512,2560]{1,0:T(8,128)(2,1)S(1)} %bitcast.9), custom_call_target="tpu_custom_call" | custom-call | bytes 1048576 | tf_op jit(solution)/shard_map/pallas_call | solution.py:256
  33.5 0.0 copy-start.1
  33.6 1.3 %copy-done.1 = bf16[4,512,512]{2,1,0:T(8,128)(2,1)} copy-done((bf16[4,512,512]{2,1,0:T(8,128)(2,1)}, bf16[4,512,512]{2,1,0:T(8,128)(2,1)S(1)}, u32[]{:S(2)}) %copy-start.1) | copy-done | bytes 2097176
  34.9 4.0 %all-to-all-start.1 = ((bf16[4,512,512]{2,1,0:T(8,128)(2,1)}), bf16[4,512,512]{2,1,0:T(8,128)(2,1)S(1)}, u32[]{:S(2)}, u32[]{:S(2)}) async-start(bf16[4,512,512]{2,1,0:T(8,128)(2,1)} %copy-done.1), calls=%async_computation.1 | async-start | bytes 4194304 | tf_op jit(solution)/shard_map/all_to_all | solution.py:225
  38.9 0.0 collective-permute-start.3
  38.9 6.2 %collective-permute-done.4.refs_2_ = bf16[1024,512]{1,0:T(8,128)(2,1)} collective-permute-done((bf16[1024,512]{1,0:T(8,128)(2,1)}, bf16[1024,512]{1,0:T(8,128)(2,1)}, u32[]{:S(2)}, u32[]{:S(2)}) %collective-permute-start.4) | collective-permute-done | bytes 1048608 | tf_op jit(solution)/shard_map/ppermute | solution.py:216
  45.1 0.0 collective-permute-start.5
  45.1 1.2 %collective-permute-done.6.refs_4_ = bf16[1024,512]{1,0:T(8,128)(2,1)} collective-permute-done((bf16[1024,512]{1,0:T(8,128)(2,1)}, bf16[1024,512]{1,0:T(8,128)(2,1)}, u32[]{:S(2)}, u32[]{:S(2)}) %collective-permute-start.6) | collective-permute-done | bytes 1048608 | tf_op jit(solution)/shard_map/ppermute | solution.py:216
  46.4 0.3 collective-permute-start.7
  46.7 1.9 %slice.8 = bf16[512,512]{1,0:T(8,128)(2,1)} slice(bf16[1024,512]{1,0:T(8,128)(2,1)} %collective-permute-done.4.refs_2_), slice={[0:512], [0:512]} | slice | bytes 1048576 | tf_op jit(solution)/shard_map/slice | solution.py:275
  48.6 2.2 %collective-permute-start.9 = (bf16[512,512]{1,0:T(8,128)(2,1)}, bf16[512,512]{1,0:T(8,128)(2,1)S(1)}, u32[]{:S(2)}, u32[]{:S(2)}) collective-permute-start(bf16[512,512]{1,0:T(8,128)(2,1)} %slice.8), channel_id=1, source_target_pairs={{0,194},{1,49},{2,192},{3,51},{16,210},{17,1},{18,208},{19,3},{32,... | collective-permute-start | bytes 1572872 | tf_op jit(solution)/shard_map/ppermute | solution.py:216
  50.8 1.9 %slice.9 = bf16[512,512]{1,0:T(8,128)(2,1)} slice(bf16[1024,512]{1,0:T(8,128)(2,1)} %collective-permute-done.6.refs_4_), slice={[512:1024], [0:512]} | slice | bytes 1048576 | tf_op jit(solution)/shard_map/slice | solution.py:276
  52.7 0.0 collective-permute-start.10
  52.7 1.9 %all-to-all-done.1.recv_ref = bf16[4,512,512]{2,1,0:T(8,128)(2,1)S(1)} async-done(((bf16[4,512,512]{2,1,0:T(8,128)(2,1)}), bf16[4,512,512]{2,1,0:T(8,128)(2,1)S(1)}, u32[]{:S(2)}, u32[]{:S(2)}) %all-to-all-start.1) | async-done | bytes 2097184 | tf_op jit(solution)/shard_map/all_to_all | solution.py:225
  54.5 0.2 shard_map.129
  54.8 0.0 collective-permute-done.3.refs_1_
  54.8 0.0 collective-permute-done.5.refs_3_
  54.8 0.0 collective-permute-done.7.refs_5_
  54.8 0.9 collective-permute-start.8
  55.7 1.2 %collective-permute-done.8 = bf16[256,512]{1,0:T(8,128)(2,1)S(1)} collective-permute-done((bf16[256,512]{1,0:T(8,128)(2,1)S(1)}, bf16[256,512]{1,0:T(8,128)(2,1)S(1)}, u32[]{:S(2)}, u32[]{:S(2)}) %collective-permute-start.8) | collective-permute-done | bytes 262176 | tf_op jit(solution)/shard_map/ppermute | solution.py:279
  56.9 0.8 add_convert_fusion
  57.7 1.5 %collective-permute-done.9.refs_6_ = bf16[512,512]{1,0:T(8,128)(2,1)S(1)} collective-permute-done((bf16[512,512]{1,0:T(8,128)(2,1)}, bf16[512,512]{1,0:T(8,128)(2,1)S(1)}, u32[]{:S(2)}, u32[]{:S(2)}) %collective-permute-start.9) | collective-permute-done | bytes 524320 | tf_op jit(solution)/shard_map/ppermute | solution.py:216
  59.2 0.0 copy-start.2
  59.2 3.0 %collective-permute-done.10.refs_8_ = bf16[512,512]{1,0:T(8,128)(2,1)} collective-permute-done((bf16[512,512]{1,0:T(8,128)(2,1)}, bf16[512,512]{1,0:T(8,128)(2,1)}, u32[]{:S(2)}, u32[]{:S(2)}) %collective-permute-start.10) | collective-permute-done | bytes 524320 | tf_op jit(solution)/shard_map/ppermute | solution.py:216
  62.2 0.9 collective-permute-start.11
  63.1 0.0 collective-permute-start.12
  63.1 6.5 %all-to-all-start.2 = ((bf16[8,32,512]{2,1,0:T(8,128)(2,1)}), bf16[8,32,512]{2,1,0:T(8,128)(2,1)S(1)}, u32[]{:S(2)}, u32[]{:S(2)}) async-start(bf16[8,32,512]{2,1,0:T(8,128)(2,1)} %bitcast.2), calls=%async_computation.2 | async-start | bytes 524288 | tf_op jit(solution)/shard_map/all_to_all | solution.py:284
  69.6 0.0 collective-permute-done.11.refs_7_
  69.7 0.0 copy-start.3
  69.7 0.0 collective-permute-done.12.refs_9_
  69.7 0.0 copy-start.4
  69.7 0.0 copy-done.2
  69.7 0.7 copy-done.3
  70.4 0.2 copy-done.4
  70.6 6.1 %shard_map.130 = (bf16[128,512]{1,0:T(8,128)(2,1)}, f32[128,128]{1,0:T(8,128)}) custom-call(bf16[128,8192]{1,0:T(8,128)(2,1)} %tok_ref.5, f32[1,8192]{1,0:T(1,128)} %bitcast.12, bf16[128,512]{1,0:T(8,128)(2,1)} %cot_ref.5, f32[128,128]{1,0:T(8,128)} %get-tuple-element.36.inv_ref, bf16[1024,512]{1,0:T(8,128)(2,1)} %pad_maximum_fusion.refs_0_, ...), custom_call_target="tpu_custom_call" | custom-call | flops 1073741824 | bytes 11534336 | tf_op jit(solution)/shard_map/pallas_call | solution.py:285
  76.7 3.7 %all-to-all-done.2.recv_ref = bf16[8,32,512]{2,1,0:T(8,128)(2,1)S(1)} async-done(((bf16[8,32,512]{2,1,0:T(8,128)(2,1)}), bf16[8,32,512]{2,1,0:T(8,128)(2,1)S(1)}, u32[]{:S(2)}, u32[]{:S(2)}) %all-to-all-start.2) | async-done | bytes 262176 | tf_op jit(solution)/shard_map/all_to_all | solution.py:284
  80.5 0.0 copy-start.5
  80.5 0.7 copy-done.5
  81.2 2.3 %shard_map.131 = (f32[32,512]{1,0:T(8,128)}, f32[16,1024]{1,0:T(8,128)}, f32[16,1024]{1,0:T(8,128)}, bf16[8,32,512]{2,1,0:T(8,128)(2,1)}) custom-call(bf16[8,32,512]{2,1,0:T(8,128)(2,1)} %copy-done.5, f32[16,1024]{1,0:T(8,128)} %first_ref.1, f32[16,1024]{1,0:T(8,128)} %second_ref.1, f32[32,512]{1,0:T(8,128)} %master_ref.1, s32[1,1024]{1,0:T(1,128)} %bitcast.14), custom_call_target="tpu_custom_call" | custom-call | flops 33554432 | bytes 1048576 | tf_op jit(solution)/shard_map/pallas_call | solution.py:294
  83.4 4.5 %all-to-all-start.3 = ((bf16[8,32,512]{2,1,0:T(8,128)(2,1)}), bf16[8,32,512]{2,1,0:T(8,128)(2,1)S(1)}, u32[]{:S(2)}, u32[]{:S(2)}) async-start(bf16[8,32,512]{2,1,0:T(8,128)(2,1)} %get-tuple-element.49), calls=%async_computation.3 | async-start | bytes 524288 | tf_op jit(solution)/shard_map/all_to_all | solution.py:308
  87.9 8.4 %shard_map.132 = bf16[128,8192]{1,0:T(8,128)(2,1)} custom-call(bf16[128,8192]{1,0:T(8,128)(2,1)} %tok_ref.5, f32[1,8192]{1,0:T(1,128)} %bitcast.13, bf16[128,512]{1,0:T(8,128)(2,1)} %cot_ref.5, f32[128,128]{1,0:T(8,128)} %get-tuple-element.36.inv_ref, f32[128,128]{1,0:T(8,128)} %get-tuple-element.50.mean_ref, bf16[1024,512]{1,0:T(8,128)(2,1)} %pad_maximum_fusion.refs_0_, ...), custom_call_target="tpu_custom_call" | custom-call | flops 1073741824 | bytes 13631488 | tf_op jit(solution)/shard_map/pallas_call | solution.py:309
  96.3 4.9 %all-to-all-done.3 = bf16[8,32,512]{2,1,0:T(8,128)(2,1)S(1)} async-done(((bf16[8,32,512]{2,1,0:T(8,128)(2,1)}), bf16[8,32,512]{2,1,0:T(8,128)(2,1)S(1)}, u32[]{:S(2)}, u32[]{:S(2)}) %all-to-all-start.3) | async-done | bytes 262176 | tf_op jit(solution)/shard_map/all_to_all | solution.py:308
  101.1 1.1 %collective-permute-start.13 = (bf16[8,32,512]{2,1,0:T(8,128)(2,1)S(1)}, bf16[8,32,512]{2,1,0:T(8,128)(2,1)S(1)}, u32[]{:S(2)}, u32[]{:S(2)}) collective-permute-start(bf16[8,32,512]{2,1,0:T(8,128)(2,1)S(1)} %all-to-all-done.3), channel_id=1, source_target_pairs={{0,1},{1,0},{2,3},{3,2},{4,5},{5,4},{6,7},{7,6},{8,9},{9,8},{10,11... | collective-permute-start | bytes 786440 | tf_op jit(solution)/shard_map/ppermute | solution.py:318
  102.3 1.2 %collective-permute-done.13 = bf16[8,32,512]{2,1,0:T(8,128)(2,1)S(1)} collective-permute-done((bf16[8,32,512]{2,1,0:T(8,128)(2,1)S(1)}, bf16[8,32,512]{2,1,0:T(8,128)(2,1)S(1)}, u32[]{:S(2)}, u32[]{:S(2)}) %collective-permute-start.13) | collective-permute-done | bytes 262176 | tf_op jit(solution)/shard_map/ppermute | solution.py:318
  103.5 0.1 pad_maximum_fusion.1
  103.5 0.8 copy.14
  (2 shorter events, 0.1 us)
Async XLA Ops:
  0.6 7.7 %copy-start = (bf16[512,512]{1,0:T(8,128)(2,1)S(1)}, bf16[512,512]{1,0:T(8,128)(2,1)}, u32[]{:S(2)}) copy-start(bf16[512,512]{1,0:T(8,128)(2,1)} %param.11) | copy-start | bytes 1572868
  4.2 28.1 %all-to-all-start = ((bf16[4,128,2560]{2,1,0:T(8,128)(2,1)}), bf16[4,128,2560]{2,1,0:T(8,128)(2,1)S(1)}, u32[]{:S(2)}, u32[]{:S(2)}) async-start(bf16[4,128,2560]{2,1,0:T(8,128)(2,1)} %get-tuple-element.31), calls=%async_computation | async-start | bytes 5242880 | tf_op jit(solution)/shard_map/all_to_all | solution.py:225
  8.4 5.6 %collective-permute-start.2 = (bf16[256,512]{1,0:T(8,128)(2,1)S(1)}, bf16[256,512]{1,0:T(8,128)(2,1)S(1)}, u32[]{:S(2)}, u32[]{:S(2)}) collective-permute-start(bf16[256,512]{1,0:T(8,128)(2,1)S(1)} %constant_dynamic-slice_fusion), channel_id=1, source_target_pairs={{0,16},{1,65},{2,18},{3,67},{16,32},{17,81},{18,34},{19,83},{32,48... | collective-permute-start | bytes 786440 | tf_op jit(solution)/shard_map/ppermute | solution.py:212
  10.1 8.3 %collective-permute-start.1 = (bf16[256,512]{1,0:T(8,128)(2,1)S(1)}, bf16[256,512]{1,0:T(8,128)(2,1)S(1)}, u32[]{:S(2)}, u32[]{:S(2)}) collective-permute-start(bf16[256,512]{1,0:T(8,128)(2,1)S(1)} %constant_dynamic-slice_fusion), channel_id=1, source_target_pairs={{0,32},{1,129},{2,34},{3,131},{16,48},{17,145},{18,50},{19,147},{3... | collective-permute-start | bytes 786440 | tf_op jit(solution)/shard_map/ppermute | solution.py:212
  13.7 7.5 %collective-permute-start = (bf16[256,512]{1,0:T(8,128)(2,1)S(1)}, bf16[256,512]{1,0:T(8,128)(2,1)S(1)}, u32[]{:S(2)}, u32[]{:S(2)}) collective-permute-start(bf16[256,512]{1,0:T(8,128)(2,1)S(1)} %constant_dynamic-slice_fusion), channel_id=1, source_target_pairs={{0,48},{1,195},{2,50},{3,193},{16,0},{17,211},{18,2},{19,209},{32,... | collective-permute-start | bytes 786440 | tf_op jit(solution)/shard_map/ppermute | solution.py:212
  22.2 22.9 %collective-permute-start.4 = (bf16[1024,512]{1,0:T(8,128)(2,1)}, bf16[1024,512]{1,0:T(8,128)(2,1)}, u32[]{:S(2)}, u32[]{:S(2)}) collective-permute-start(bf16[1024,512]{1,0:T(8,128)(2,1)} %pad_maximum_fusion.refs_0_), channel_id=1, source_target_pairs={{0,194},{1,49},{2,192},{3,51},{16,210},{17,1},{18,208},{19,3},{32,... | collective-permute-start | bytes 3145736 | tf_op jit(solution)/shard_map/ppermute | solution.py:216
  24.9 21.5 %collective-permute-start.6 = (bf16[1024,512]{1,0:T(8,128)(2,1)}, bf16[1024,512]{1,0:T(8,128)(2,1)}, u32[]{:S(2)}, u32[]{:S(2)}) collective-permute-start(bf16[1024,512]{1,0:T(8,128)(2,1)} %pad_maximum_fusion.refs_0_), channel_id=1, source_target_pairs={{0,64},{1,17},{2,66},{3,19},{16,80},{17,33},{18,82},{19,35},{32,96... | collective-permute-start | bytes 3145736 | tf_op jit(solution)/shard_map/ppermute | solution.py:216
  33.5 1.3 %copy-start.1 = (bf16[4,512,512]{2,1,0:T(8,128)(2,1)}, bf16[4,512,512]{2,1,0:T(8,128)(2,1)S(1)}, u32[]{:S(2)}) copy-start(bf16[4,512,512]{2,1,0:T(8,128)(2,1)S(1)} %shard_map.128) | copy-start | bytes 6291460
  34.9 19.7 %all-to-all-start.1 = ((bf16[4,512,512]{2,1,0:T(8,128)(2,1)}), bf16[4,512,512]{2,1,0:T(8,128)(2,1)S(1)}, u32[]{:S(2)}, u32[]{:S(2)}) async-start(bf16[4,512,512]{2,1,0:T(8,128)(2,1)} %copy-done.1), calls=%async_computation.1 | async-start | bytes 4194304 | tf_op jit(solution)/shard_map/all_to_all | solution.py:225
  38.9 15.9 %collective-permute-start.3 = (bf16[1024,512]{1,0:T(8,128)(2,1)}, bf16[1024,512]{1,0:T(8,128)(2,1)}, u32[]{:S(2)}, u32[]{:S(2)}) collective-permute-start(bf16[1024,512]{1,0:T(8,128)(2,1)} %pad_maximum_fusion.refs_0_), channel_id=1, source_target_pairs={{0,1},{1,0},{2,3},{3,2},{4,5},{5,4},{6,7},{7,6},{8,9},{9,8},{10,11... | collective-permute-start | bytes 3145736 | tf_op jit(solution)/shard_map/ppermute | solution.py:255
  45.1 9.7 %collective-permute-start.5 = (bf16[1024,512]{1,0:T(8,128)(2,1)}, bf16[1024,512]{1,0:T(8,128)(2,1)}, u32[]{:S(2)}, u32[]{:S(2)}) collective-permute-start(bf16[1024,512]{1,0:T(8,128)(2,1)} %collective-permute-done.4.refs_2_), channel_id=1, source_target_pairs={{0,1},{1,0},{2,3},{3,2},{4,5},{5,4},{6,7},{7,6},{8,9},{9,8},{10,11... | collective-permute-start | bytes 3145736 | tf_op jit(solution)/shard_map/ppermute | solution.py:255
  46.4 8.4 %collective-permute-start.7 = (bf16[1024,512]{1,0:T(8,128)(2,1)}, bf16[1024,512]{1,0:T(8,128)(2,1)}, u32[]{:S(2)}, u32[]{:S(2)}) collective-permute-start(bf16[1024,512]{1,0:T(8,128)(2,1)} %collective-permute-done.6.refs_4_), channel_id=1, source_target_pairs={{0,1},{1,0},{2,3},{3,2},{4,5},{5,4},{6,7},{7,6},{8,9},{9,8},{10,11... | collective-permute-start | bytes 3145736 | tf_op jit(solution)/shard_map/ppermute | solution.py:255
  48.6 10.6 %collective-permute-start.9 = (bf16[512,512]{1,0:T(8,128)(2,1)}, bf16[512,512]{1,0:T(8,128)(2,1)S(1)}, u32[]{:S(2)}, u32[]{:S(2)}) collective-permute-start(bf16[512,512]{1,0:T(8,128)(2,1)} %slice.8), channel_id=1, source_target_pairs={{0,194},{1,49},{2,192},{3,51},{16,210},{17,1},{18,208},{19,3},{32,... | collective-permute-start | bytes 1572872 | tf_op jit(solution)/shard_map/ppermute | solution.py:216
  52.7 9.6 %collective-permute-start.10 = (bf16[512,512]{1,0:T(8,128)(2,1)}, bf16[512,512]{1,0:T(8,128)(2,1)}, u32[]{:S(2)}, u32[]{:S(2)}) collective-permute-start(bf16[512,512]{1,0:T(8,128)(2,1)} %slice.9), channel_id=1, source_target_pairs={{0,64},{1,17},{2,66},{3,19},{16,80},{17,33},{18,82},{19,35},{32,96... | collective-permute-start | bytes 1572872 | tf_op jit(solution)/shard_map/ppermute | solution.py:216
  54.8 2.1 %collective-permute-start.8 = (bf16[256,512]{1,0:T(8,128)(2,1)S(1)}, bf16[256,512]{1,0:T(8,128)(2,1)S(1)}, u32[]{:S(2)}, u32[]{:S(2)}) collective-permute-start(bf16[256,512]{1,0:T(8,128)(2,1)S(1)} %get-tuple-element.34), channel_id=1, source_target_pairs={{0,1},{1,0},{2,3},{3,2},{4,5},{5,4},{6,7},{7,6},{8,9},{9,8},{10,11... | collective-permute-start | bytes 786440 | tf_op jit(solution)/shard_map/ppermute | solution.py:279
  59.2 10.5 %copy-start.2 = (bf16[512,512]{1,0:T(8,128)(2,1)}, bf16[512,512]{1,0:T(8,128)(2,1)S(1)}, u32[]{:S(2)}) copy-start(bf16[512,512]{1,0:T(8,128)(2,1)S(1)} %collective-permute-done.9.refs_6_) | copy-start | bytes 1572868
  62.2 7.4 %collective-permute-start.11 = (bf16[512,512]{1,0:T(8,128)(2,1)S(1)}, bf16[512,512]{1,0:T(8,128)(2,1)S(1)}, u32[]{:S(2)}, u32[]{:S(2)}) collective-permute-start(bf16[512,512]{1,0:T(8,128)(2,1)S(1)} %collective-permute-done.9.refs_6_), channel_id=1, source_target_pairs={{0,1},{1,0},{2,3},{3,2},{4,5},{5,4},{6,7},{7,6},{8,9},{9,8},{10,11... | collective-permute-start | bytes 1572872 | tf_op jit(solution)/shard_map/ppermute | solution.py:283
  63.1 6.5 %collective-permute-start.12 = (bf16[512,512]{1,0:T(8,128)(2,1)}, bf16[512,512]{1,0:T(8,128)(2,1)S(1)}, u32[]{:S(2)}, u32[]{:S(2)}) collective-permute-start(bf16[512,512]{1,0:T(8,128)(2,1)} %collective-permute-done.10.refs_8_), channel_id=1, source_target_pairs={{0,1},{1,0},{2,3},{3,2},{4,5},{5,4},{6,7},{7,6},{8,9},{9,8},{10,11... | collective-permute-start | bytes 1572872 | tf_op jit(solution)/shard_map/ppermute | solution.py:283
  63.1 17.3 %all-to-all-start.2 = ((bf16[8,32,512]{2,1,0:T(8,128)(2,1)}), bf16[8,32,512]{2,1,0:T(8,128)(2,1)S(1)}, u32[]{:S(2)}, u32[]{:S(2)}) async-start(bf16[8,32,512]{2,1,0:T(8,128)(2,1)} %bitcast.2), calls=%async_computation.2 | async-start | bytes 524288 | tf_op jit(solution)/shard_map/all_to_all | solution.py:284
  69.7 0.8 copy-start.3
  69.7 1.0 copy-start.4
  80.5 0.7 copy-start.5
  83.4 17.7 %all-to-all-start.3 = ((bf16[8,32,512]{2,1,0:T(8,128)(2,1)}), bf16[8,32,512]{2,1,0:T(8,128)(2,1)S(1)}, u32[]{:S(2)}, u32[]{:S(2)}) async-start(bf16[8,32,512]{2,1,0:T(8,128)(2,1)} %get-tuple-element.49), calls=%async_computation.3 | async-start | bytes 524288 | tf_op jit(solution)/shard_map/all_to_all | solution.py:308
  101.1 2.3 %collective-permute-start.13 = (bf16[8,32,512]{2,1,0:T(8,128)(2,1)S(1)}, bf16[8,32,512]{2,1,0:T(8,128)(2,1)S(1)}, u32[]{:S(2)}, u32[]{:S(2)}) collective-permute-start(bf16[8,32,512]{2,1,0:T(8,128)(2,1)S(1)} %all-to-all-done.3), channel_id=1, source_target_pairs={{0,1},{1,0},{2,3},{3,2},{4,5},{5,4},{6,7},{7,6},{8,9},{9,8},{10,11... | collective-permute-start | bytes 786440 | tf_op jit(solution)/shard_map/ppermute | solution.py:318

commit v8 on v7

--- a/solution.py
+++ b/solution.py
@@ -23,6 +23,7 @@
 ZL, Y, X, ZH, C = SIZES
 ROWS = 32
 VMEM = pl.BlockSpec(memory_space=pltpu.VMEM)
+HBM = pl.BlockSpec(memory_space=pltpu.HBM)
 BF16 = jnp.bfloat16
 F32 = jnp.float32
 
@@ -31,12 +32,13 @@
     return jax.ShapeDtypeStruct(dims, kind)
 
 
-def kernel_call(body, outs, flops, nbytes, n_in, limit=24 << 20):
+def kernel_call(body, outs, flops, nbytes, in_specs, limit=24 << 20, out_specs=None, scratch=()):
     return pl.pallas_call(
         body,
         out_shape=outs,
-        in_specs=[VMEM] * n_in,
-        out_specs=jax.tree.map(lambda _: VMEM, outs),
+        in_specs=[VMEM] * in_specs if isinstance(in_specs, int) else in_specs,
+        out_specs=jax.tree.map(lambda _: VMEM, outs) if out_specs is None else out_specs,
+        scratch_shapes=list(scratch),
         cost_estimate=pl.CostEstimate(flops=flops, bytes_accessed=nbytes, transcendentals=0),
         compiler_params=pltpu.CompilerParams(vmem_limit_bytes=limit),
     )
@@ -67,10 +69,11 @@
         send_ref[p, :, ZL * Y * part :] = cot_ref[...]
 
 
-def grad_kernel(recv_ref, send_ref):
+def grad_kernel(recv_ref, send_ref, buf_ref, sem):
     part = ZH * C * ROWS
     cols = ZL * Y * part
     cot = recv_ref[:, cols:]
+    copies = []
     for zl in range(ZL):
         block = recv_ref[:, zl * Y * part : (zl + 1) * Y * part]
         grad = lax.dot_general(block, cot, (((0,), (0,)), ((), ())), preferred_element_type=F32)
@@ -79,43 +82,67 @@
             for zh in range(ZH):
                 for c in range(C):
                     at = q * part + (zh * C + c) * ROWS
-                    to = ((c * ZL + zl) * ZH + zh) * ROWS
-                    send_ref[q, to : to + ROWS, :] = grad[at : at + ROWS]
+                    to = (c * ZH + zh) * ROWS
+                    buf_ref[zl, q, to : to + ROWS, :] = grad[at : at + ROWS]
+        rows = slice(zl * part, (zl + 1) * part)
+        copy = pltpu.make_async_copy(buf_ref.at[zl], send_ref.at[:, rows, :], sem.at[zl])
+        copy.start()
+        copies.append(copy)
+    for copy in copies:
+        copy.wait()
 
 
 def sum_kernel(recv_ref, own_ref, sib_ref):
     c = lax.axis_index("c")
-    rows = own_ref.shape[0]
+    rows = ZH * ROWS
     for ref, core in ((sib_ref, 1 - c), (own_ref, c)):
-        part = recv_ref[:, pl.ds(pl.multiple_of(core * rows, rows), rows), :].astype(F32)
-        ref[...] = jnp.sum(part, axis=0).astype(ref.dtype)
-
-
-def places(width, refs):
+        for zl in range(ZL):
+            at = pl.multiple_of(zl * C * rows + core * rows, rows)
+            part = recv_ref[:, pl.ds(at, rows), :].astype(F32)
+            ref[zl * rows : (zl + 1) * rows, :] = jnp.sum(part, axis=0).astype(ref.dtype)
+
+
+def halves_kernel(up_ref, down_ref, a_ref, b_ref, sem):
+    rows = a_ref.shape[0]
+    copies = (
+        pltpu.make_async_copy(up_ref.at[0:rows, :], a_ref, sem.at[0]),
+        pltpu.make_async_copy(down_ref.at[rows : 2 * rows, :], b_ref, sem.at[1]),
+    )
+    for copy in copies:
+        copy.start()
+    for copy in copies:
+        copy.wait()
+
+
+def places(width, refs, bufs, sem):
     c, zl, y = (lax.axis_index(name) for name in ("c", "zl", "y"))
     step = width // (ZL * Y)
     half = step // 2
-    for s, off in enumerate((0, 1, 3, 2)):
-        for h in range(C):
-            for k in range(Y):
-                core = c if h == 0 else 1 - c
-                on_zl, on_y = jnp.where(core == 0, off, k), jnp.where(core == 0, k, off)
-                node = lax.rem(zl + on_zl, ZL) * Y + lax.rem(y + on_y, Y)
-                at = pl.multiple_of(node * step + core * half, half)
-                ref, row = (refs[2 * s + h], k) if s < 3 else (refs[2 * (s + k // 2) + h], k % 2)
-                yield pl.ds(at, half), ref[row * half : (row + 1) * half, :]
+    copies = [pltpu.make_async_copy(ref, buf, sem.at[i]) for i, (ref, buf) in enumerate(zip(refs, bufs))]
+    for copy in copies:
+        copy.start()
+    for i, buf in enumerate(bufs):
+        copies[i].wait()
+        off = (0, 1, 3)[i // 2] if i < 6 else 2
+        core = c if i % 2 == 0 else 1 - c
+        for row in range(buf.shape[0] // half):
+            k = row if i < 6 else row + 2 * ((i - 6) // 2)
+            on_zl, on_y = jnp.where(core == 0, off, k), jnp.where(core == 0, k, off)
+            node = lax.rem(zl + on_zl, ZL) * Y + lax.rem(y + on_y, Y)
+            at = pl.multiple_of(node * step + core * half, half)
+            yield pl.ds(at, half), buf[row * half : (row + 1) * half, :]
 
 
 def widened(ref, cols):
     return jnp.concatenate([ref[...]] * (cols // ref.shape[1]), axis=1)
 
 
-def keys_kernel(tok_ref, gain_ref, cot_ref, inv_ref, *refs):
-    refs, (keys_ref, mean_ref) = refs[:-2], refs[-2:]
+def keys_kernel(blocks, tok_ref, gain_ref, cot_ref, inv_ref, *refs):
+    w_refs, (keys_ref, mean_ref), bufs, sem = refs[:blocks], refs[blocks : blocks + 2], refs[blocks + 2 : -1], refs[-1]
     width = tok_ref.shape[1]
     inv = widened(inv_ref, width // (ZL * Y * C))
     keys = jnp.zeros(keys_ref.shape, F32)
-    for cols, weights in places(width, refs):
+    for cols, weights in places(width, w_refs, bufs, sem):
         normed = tok_ref[:, cols].astype(F32) * inv
         hidden = (normed * gain_ref[:, cols]).astype(BF16)
         keys = keys + jnp.dot(hidden, weights, preferred_element_type=F32)
@@ -124,13 +151,13 @@
     mean_ref[...] = jnp.broadcast_to(mean, mean_ref.shape)
 
 
-def token_grad_kernel(tok_ref, gain_ref, cot_ref, inv_ref, mean_ref, *refs):
-    refs, (tg_ref,) = refs[:-1], refs[-1:]
+def token_grad_kernel(blocks, tok_ref, gain_ref, cot_ref, inv_ref, mean_ref, *refs):
+    w_refs, tg_ref, bufs, sem = refs[:blocks], refs[blocks], refs[blocks + 1 : -1], refs[-1]
     width = tok_ref.shape[1]
     inv = widened(inv_ref, width // (ZL * Y * C))
     mean = widened(mean_ref, width // (ZL * Y * C))
     cot = cot_ref[...]
-    for cols, weights in places(width, refs):
+    for cols, weights in places(width, w_refs, bufs, sem):
         hidden_grad = lax.dot_general(cot, weights, (((1,), (1,)), ((), ())), preferred_element_type=F32)
         normed = tok_ref[:, cols].astype(F32) * inv
         tg_ref[:, cols] = (inv * (hidden_grad * gain_ref[:, cols] - normed * mean)).astype(BF16)
@@ -255,11 +282,13 @@
         weights += [block, lax.ppermute(block, "c", ring(C, 1))]
     send = kernel_call(
         grad_kernel,
-        shape((Y, part // Y, keys_w), BF16),
+        pltpu.HBM((Y, part // Y, keys_w), BF16),
         0,
         1 << 20,
         1,
         40 << 20,
+        HBM,
+        (pltpu.VMEM((ZL, Y, ZH * C * ROWS, keys_w), BF16), pltpu.SemaphoreType.DMA((ZL,))),
     )(recv)
     blocks = mixed(send, False)
     own, sib = kernel_call(
@@ -271,9 +300,19 @@
     )(blocks)
     from_up, from_down = weights[2], weights[4]
     rows = from_up.shape[0] // 2
+    far_a, far_b = kernel_call(
+        halves_kernel,
+        (shape((rows, keys_w), BF16),) * 2,
+        0,
+        1 << 20,
+        [HBM, HBM],
+        60 << 20,
+        (HBM, HBM),
+        (pltpu.SemaphoreType.DMA((2,)),),
+    )(from_up, from_down)
     far = [
-        second_step(from_up[:rows], lambda place, on_z: -1),
-        second_step(from_down[rows:], lambda place, on_z: 1),
+        second_step(far_a, lambda place, on_z: -1),
+        second_step(far_b, lambda place, on_z: 1),
     ]
     sib, weights = lax.optimization_barrier((sib, weights))
     sib = lax.ppermute(sib, "c", ring(C, 1))
@@ -282,13 +321,16 @@
     for block in far:
         weights += [block, lax.ppermute(block, "c", ring(C, 1))]
     blocks = lax.all_to_all(summed.reshape(ZL * ZH, ROWS, keys_w), ("zl", "zh"), 0, 0, tiled=True)
+    count = len(weights)
+    scratch = [pltpu.VMEM(block.shape, BF16) for block in weights] + [pltpu.SemaphoreType.DMA((count,))]
     keys, mean = kernel_call(
-        keys_kernel,
+        functools.partial(keys_kernel, count),
         (shape((tok_rows, keys_w), BF16), shape((tok_rows, 128), F32)),
         2 * tok_rows * width * keys_w,
         11 << 20,
-        4 + len(weights),
+        [VMEM] * 4 + [HBM] * count,
         60 << 20,
+        scratch=scratch,
     )(tokens, gain, key_cotangent, inv, *weights)
     blocks, keys, mean = lax.optimization_barrier((blocks, keys, mean))
     new_master, new_first, new_second, new_rows = kernel_call(
@@ -307,12 +349,13 @@
 
     mine = lax.all_to_all(new_rows, ("x", "zh"), 0, 0, tiled=True)
     token_grad = kernel_call(
-        token_grad_kernel,
+        functools.partial(token_grad_kernel, count),
         shape(tokens.shape, BF16),
         2 * tok_rows * width * keys_w,
         13 << 20,
-        5 + len(weights),
+        [VMEM] * 5 + [HBM] * count,
         60 << 20,
+        scratch=scratch,
     )(tokens, gain, key_cotangent, inv, mean, *weights)
     mine, token_grad = lax.optimization_barrier((mine, token_grad))
     other = lax.ppermute(mine, "c", ring(C, 1))

time: 105 us -> 134 us (1.28)
  Pallas kernels: 21.8 us -> 55.6 us
  local copies, waits for them, and re-layouts: 7.56 us -> 2.52 us
    pallas_call x3 -> x4, Pallas kernels: 15.7 us -> 49.6 us  [the longest x1 32.9 us: shards(): kernel_call(halves_kernel, (shape((rows, keys_w), BF16),) * 2, 0, 1 << 20...]
    slice x2 -> x0, local copies, waits for them, and re-layouts: 3.73 us -> none  [the longest x1 1.87 us: shards(): from_up[:rows]]
    ppermute x4, waiting for transfers between devices: 12 us -> 15.2 us  [second_step(): return lax.ppermute(value, GATHER, moved(lambda c: c == 0, shift))]
    all_to_all x2, waiting for transfers between devices: 9.23 us -> 7.36 us  [mixed(): lax.all_to_all(value, ('y', 'x', 'c'), 0, 0, axis_index_groups=groups, ti...]
    unnamed x12 -> x10, local copies, waits for them, and re-layouts: 2.99 us -> 1.68 us
  transfers between devices with their start and end apart: 18 -> 18, of which waited for: 13 -> 12; matrix products, arithmetic and copies ran while one was open for 5% -> 1% of each run, Pallas kernels for 15% -> 37%
where the time goes in v8:
time: 134 us
  Pallas kernels  55.6 us (41%)
  waiting for transfers between devices  40.6 us (30%)
  starting transfers between devices  32.2 us (24%)
  local copies, waits for them, and re-layouts  2.52 us (2%)
  other arithmetic  1.92 us (1%)
    pallas_call x1, Pallas kernels, shards(): kernel_call(halves_kernel, (shape((rows, keys_w), BF16),) * 2, 0, 1 << 20...  32.9 us
    ppermute x4, waiting for transfers between devices, second_step(): return lax.ppermute(value, GATHER, moved(lambda c: c == 0, shift))  15.2 us
    pallas_call x1, Pallas kernels, shards(): kernel_call(functools.partial(token_grad_kernel, count), shape(tokens.sha...  8.56 us
    all_to_all x2, starting transfers between devices, mixed(): lax.all_to_all(value, ('y', 'x', 'c'), 0, 0, axis_index_groups=groups, ti...  8.21 us
    ppermute x3, waiting for transfers between devices, first_step(): return lax.ppermute(value, GATHER, moved(lambda c: c == 1, shift))  7.49 us
    all_to_all x2, waiting for transfers between devices, mixed(): lax.all_to_all(value, ('y', 'x', 'c'), 0, 0, axis_index_groups=groups, ti...  7.36 us
    all_to_all x1, starting transfers between devices, shards(): lax.all_to_all(summed.reshape(ZL * ZH, ROWS, keys_w), ('zl', 'zh'), 0, 0,...  6.8 us
    pallas_call x1, Pallas kernels, shards(): kernel_call(functools.partial(keys_kernel, count), (shape((tok_rows, keys...  6.03 us
  transfers between devices with their start and end apart: 18, of which 12 were waited for; matrix products, arithmetic and copies ran while one was open for 1% of the time, Pallas kernels for 37%

profile of v8, /device:TPU:33, one launch (start us, length us, event | category | flops | bytes accessed | tf_op | source)
XLA Modules:
  0.0 133.6 jit_solution(2155408114339271956)
XLA Ops:
  0.6 0.0 copy-start
  0.6 3.5 %shard_map.127 = (bf16[4,128,2560]{2,1,0:T(8,128)(2,1)}, f32[128,128]{1,0:T(8,128)}) custom-call(bf16[128,8192]{1,0:T(8,128)(2,1)} %tok_ref.5, f32[1,8192]{1,0:T(1,128)} %bitcast.11, bf16[128,512]{1,0:T(8,128)(2,1)} %cot_ref.5), custom_call_target="tpu_custom_call" | custom-call | flops 6291456 | bytes 5242880 | tf_op jit(solution)/shard_map/pallas_call | solution.py:268
  4.2 4.2 %all-to-all-start = ((bf16[4,128,2560]{2,1,0:T(8,128)(2,1)}), bf16[4,128,2560]{2,1,0:T(8,128)(2,1)S(1)}, u32[]{:S(2)}, u32[]{:S(2)}) async-start(bf16[4,128,2560]{2,1,0:T(8,128)(2,1)} %get-tuple-element.33), calls=%async_computation | async-start | bytes 5242880 | tf_op jit(solution)/shard_map/all_to_all | solution.py:252
  8.4 0.0 copy-done
  8.4 1.7 %collective-permute-start.2 = (bf16[256,512]{1,0:T(8,128)(2,1)S(1)}, bf16[256,512]{1,0:T(8,128)(2,1)S(1)}, u32[]{:S(2)}, u32[]{:S(2)}) collective-permute-start(bf16[256,512]{1,0:T(8,128)(2,1)S(1)} %constant_dynamic-slice_fusion), channel_id=1, source_target_pairs={{0,16},{1,65},{2,18},{3,67},{16,32},{17,81},{18,34},{19,83},{32,48... | collective-permute-start | bytes 786440 | tf_op jit(solution)/shard_map/ppermute | solution.py:239
  10.1 3.6 %collective-permute-start.1 = (bf16[256,512]{1,0:T(8,128)(2,1)S(1)}, bf16[256,512]{1,0:T(8,128)(2,1)S(1)}, u32[]{:S(2)}, u32[]{:S(2)}) collective-permute-start(bf16[256,512]{1,0:T(8,128)(2,1)S(1)} %constant_dynamic-slice_fusion), channel_id=1, source_target_pairs={{0,32},{1,129},{2,34},{3,131},{16,48},{17,145},{18,50},{19,147},{3... | collective-permute-start | bytes 786440 | tf_op jit(solution)/shard_map/ppermute | solution.py:239
  13.7 0.0 collective-permute-start
  13.7 0.3 collective-permute-done.2
  14.0 4.4 %collective-permute-done.1 = bf16[256,512]{1,0:T(8,128)(2,1)S(1)} collective-permute-done((bf16[256,512]{1,0:T(8,128)(2,1)S(1)}, bf16[256,512]{1,0:T(8,128)(2,1)S(1)}, u32[]{:S(2)}, u32[]{:S(2)}) %collective-permute-start.1) | collective-permute-done | bytes 262176 | tf_op jit(solution)/shard_map/ppermute | solution.py:239
  18.4 2.8 %collective-permute-done = bf16[256,512]{1,0:T(8,128)(2,1)S(1)} collective-permute-done((bf16[256,512]{1,0:T(8,128)(2,1)S(1)}, bf16[256,512]{1,0:T(8,128)(2,1)S(1)}, u32[]{:S(2)}, u32[]{:S(2)}) %collective-permute-start) | collective-permute-done | bytes 262176 | tf_op jit(solution)/shard_map/ppermute | solution.py:239
  21.2 1.1 pad_maximum_fusion.refs_0_
  22.2 2.7 %collective-permute-start.4 = (bf16[1024,512]{1,0:T(8,128)(2,1)}, bf16[1024,512]{1,0:T(8,128)(2,1)}, u32[]{:S(2)}, u32[]{:S(2)}) collective-permute-start(bf16[1024,512]{1,0:T(8,128)(2,1)} %pad_maximum_fusion.refs_0_), channel_id=1, source_target_pairs={{0,194},{1,49},{2,192},{3,51},{16,210},{17,1},{18,208},{19,3},{32,... | collective-permute-start | bytes 3145736 | tf_op jit(solution)/shard_map/ppermute | solution.py:243
  24.9 0.0 collective-permute-start.6
  24.9 7.4 %all-to-all-done = bf16[4,128,2560]{2,1,0:T(8,128)(2,1)S(1)} async-done(((bf16[4,128,2560]{2,1,0:T(8,128)(2,1)}), bf16[4,128,2560]{2,1,0:T(8,128)(2,1)S(1)}, u32[]{:S(2)}, u32[]{:S(2)}) %all-to-all-start) | async-done | bytes 2621472 | tf_op jit(solution)/shard_map/all_to_all | solution.py:252
  32.3 2.1 %shard_map.128 = bf16[4,512,512]{2,1,0:T(8,128)(2,1)} custom-call(bf16[512,2560]{1,0:T(8,128)(2,1)S(1)} %bitcast.9), custom_call_target="tpu_custom_call" | custom-call | bytes 1048576 | tf_op jit(solution)/shard_map/pallas_call | solution.py:283
  34.4 4.0 %all-to-all-start.1 = ((bf16[4,512,512]{2,1,0:T(8,128)(2,1)}), bf16[4,512,512]{2,1,0:T(8,128)(2,1)S(1)}, u32[]{:S(2)}, u32[]{:S(2)}) async-start(bf16[4,512,512]{2,1,0:T(8,128)(2,1)} %shard_map.128), calls=%async_computation.1 | async-start | bytes 4194304 | tf_op jit(solution)/shard_map/all_to_all | solution.py:252
  38.4 0.0 collective-permute-start.3
  38.4 7.2 %collective-permute-done.4.up_ref.refs_2_ = bf16[1024,512]{1,0:T(8,128)(2,1)} collective-permute-done((bf16[1024,512]{1,0:T(8,128)(2,1)}, bf16[1024,512]{1,0:T(8,128)(2,1)}, u32[]{:S(2)}, u32[]{:S(2)}) %collective-permute-start.4) | collective-permute-done | bytes 1048608 | tf_op jit(solution)/shard_map/ppermute | solution.py:243
  45.6 0.0 collective-permute-start.5
  45.6 1.2 collective-permute-done.6.down_ref.refs_4_
  46.8 0.0 collective-permute-start.7
  46.8 32.9 %shard_map.130 = (bf16[512,512]{1,0:T(8,128)(2,1)}, bf16[512,512]{1,0:T(8,128)(2,1)}) custom-call(bf16[1024,512]{1,0:T(8,128)(2,1)} %collective-permute-done.4.up_ref.refs_2_, bf16[1024,512]{1,0:T(8,128)(2,1)} %collective-permute-done.6.down_ref.refs_4_), custom_call_target="tpu_custom_call" | custom-call | bytes 1048576 | tf_op jit(solution)/shard_map/pallas_call | solution.py:303
  79.7 2.6 %collective-permute-start.9 = (bf16[512,512]{1,0:T(8,128)(2,1)}, bf16[512,512]{1,0:T(8,128)(2,1)S(1)}, u32[]{:S(2)}, u32[]{:S(2)}) collective-permute-start(bf16[512,512]{1,0:T(8,128)(2,1)} %get-tuple-element.37), channel_id=1, source_target_pairs={{0,194},{1,49},{2,192},{3,51},{16,210},{17,1},{18,208},{19,3},{32,... | collective-permute-start | bytes 1572872 | tf_op jit(solution)/shard_map/ppermute | solution.py:243
  82.4 0.0 collective-permute-start.10
  82.4 0.0 all-to-all-done.1.recv_ref
  82.4 0.2 shard_map.129
  82.6 0.0 collective-permute-done.3.refs_1_
  82.6 0.0 collective-permute-done.5.refs_3_
  82.7 0.0 collective-permute-done.7.refs_5_
  82.7 0.6 collective-permute-start.8
  83.3 1.2 collective-permute-done.8
  84.4 0.8 add_convert_fusion
  85.2 3.6 %collective-permute-done.9.refs_6_ = bf16[512,512]{1,0:T(8,128)(2,1)S(1)} collective-permute-done((bf16[512,512]{1,0:T(8,128)(2,1)}, bf16[512,512]{1,0:T(8,128)(2,1)S(1)}, u32[]{:S(2)}, u32[]{:S(2)}) %collective-permute-start.9) | collective-permute-done | bytes 524320 | tf_op jit(solution)/shard_map/ppermute | solution.py:243
  88.8 0.0 copy-start.1
  88.8 3.1 %collective-permute-done.10.refs_8_ = bf16[512,512]{1,0:T(8,128)(2,1)} collective-permute-done((bf16[512,512]{1,0:T(8,128)(2,1)}, bf16[512,512]{1,0:T(8,128)(2,1)}, u32[]{:S(2)}, u32[]{:S(2)}) %collective-permute-start.10) | collective-permute-done | bytes 524320 | tf_op jit(solution)/shard_map/ppermute | solution.py:243
  91.9 0.6 collective-permute-start.11
  92.6 0.0 collective-permute-start.12
  92.6 6.8 %all-to-all-start.2 = ((bf16[8,32,512]{2,1,0:T(8,128)(2,1)}), bf16[8,32,512]{2,1,0:T(8,128)(2,1)S(1)}, u32[]{:S(2)}, u32[]{:S(2)}) async-start(bf16[8,32,512]{2,1,0:T(8,128)(2,1)} %bitcast.2), calls=%async_computation.2 | async-start | bytes 524288 | tf_op jit(solution)/shard_map/all_to_all | solution.py:323
  99.4 0.0 collective-permute-done.11.refs_7_
  99.4 0.0 copy-start.2
  99.4 0.0 collective-permute-done.12.refs_9_
  99.4 0.0 copy-start.3
  99.4 0.0 copy-done.1
  99.4 0.7 copy-done.2
  100.2 0.2 copy-done.3
  100.4 6.0 %shard_map.131 = (bf16[128,512]{1,0:T(8,128)(2,1)}, f32[128,128]{1,0:T(8,128)}) custom-call(bf16[128,8192]{1,0:T(8,128)(2,1)} %tok_ref.5, f32[1,8192]{1,0:T(1,128)} %bitcast.12, bf16[128,512]{1,0:T(8,128)(2,1)} %cot_ref.5, f32[128,128]{1,0:T(8,128)} %get-tuple-element.40.inv_ref, bf16[1024,512]{1,0:T(8,128)(2,1)} %pad_maximum_fusion.refs_0_, ...), custom_call_target="tpu_custom_call" | custom-call | flops 1073741824 | bytes 11534336 | tf_op jit(solution)/shard_map/pallas_call | solution.py:326
  106.4 3.8 %all-to-all-done.2.recv_ref = bf16[8,32,512]{2,1,0:T(8,128)(2,1)S(1)} async-done(((bf16[8,32,512]{2,1,0:T(8,128)(2,1)}), bf16[8,32,512]{2,1,0:T(8,128)(2,1)S(1)}, u32[]{:S(2)}, u32[]{:S(2)}) %all-to-all-start.2) | async-done | bytes 262176 | tf_op jit(solution)/shard_map/all_to_all | solution.py:323
  110.2 0.0 copy-start.4
  110.2 0.7 copy-done.4
  110.9 2.3 %shard_map.132 = (f32[32,512]{1,0:T(8,128)}, f32[16,1024]{1,0:T(8,128)}, f32[16,1024]{1,0:T(8,128)}, bf16[8,32,512]{2,1,0:T(8,128)(2,1)}) custom-call(bf16[8,32,512]{2,1,0:T(8,128)(2,1)} %copy-done.4, f32[16,1024]{1,0:T(8,128)} %first_ref.1, f32[16,1024]{1,0:T(8,128)} %second_ref.1, f32[32,512]{1,0:T(8,128)} %master_ref.1, s32[1,1024]{1,0:T(1,128)} %bitcast.14), custom_call_target="tpu_custom_call" | custom-call | flops 33554432 | bytes 1048576 | tf_op jit(solution)/shard_map/pallas_call | solution.py:336
  113.1 3.7 %all-to-all-start.3 = ((bf16[8,32,512]{2,1,0:T(8,128)(2,1)}), bf16[8,32,512]{2,1,0:T(8,128)(2,1)S(1)}, u32[]{:S(2)}, u32[]{:S(2)}) async-start(bf16[8,32,512]{2,1,0:T(8,128)(2,1)} %get-tuple-element.53), calls=%async_computation.3 | async-start | bytes 524288 | tf_op jit(solution)/shard_map/all_to_all | solution.py:350
  116.8 8.6 %shard_map.133 = bf16[128,8192]{1,0:T(8,128)(2,1)} custom-call(bf16[128,8192]{1,0:T(8,128)(2,1)} %tok_ref.5, f32[1,8192]{1,0:T(1,128)} %bitcast.13, bf16[128,512]{1,0:T(8,128)(2,1)} %cot_ref.5, f32[128,128]{1,0:T(8,128)} %get-tuple-element.40.inv_ref, f32[128,128]{1,0:T(8,128)} %get-tuple-element.54.mean_ref, bf16[1024,512]{1,0:T(8,128)(2,1)} %pad_maximum_fusion.refs_0_, ...), custom_call_target="tpu_custom_call" | custom-call | flops 1073741824 | bytes 13631488 | tf_op jit(solution)/shard_map/pallas_call | solution.py:351
  125.4 4.5 %all-to-all-done.3 = bf16[8,32,512]{2,1,0:T(8,128)(2,1)S(1)} async-done(((bf16[8,32,512]{2,1,0:T(8,128)(2,1)}), bf16[8,32,512]{2,1,0:T(8,128)(2,1)S(1)}, u32[]{:S(2)}, u32[]{:S(2)}) %all-to-all-start.3) | async-done | bytes 262176 | tf_op jit(solution)/shard_map/all_to_all | solution.py:350
  129.9 1.6 %collective-permute-start.13 = (bf16[8,32,512]{2,1,0:T(8,128)(2,1)S(1)}, bf16[8,32,512]{2,1,0:T(8,128)(2,1)S(1)}, u32[]{:S(2)}, u32[]{:S(2)}) collective-permute-start(bf16[8,32,512]{2,1,0:T(8,128)(2,1)S(1)} %all-to-all-done.3), channel_id=1, source_target_pairs={{0,1},{1,0},{2,3},{3,2},{4,5},{5,4},{6,7},{7,6},{8,9},{9,8},{10,11... | collective-permute-start | bytes 786440 | tf_op jit(solution)/shard_map/ppermute | solution.py:361
  131.5 1.2 collective-permute-done.13
  132.7 0.1 pad_maximum_fusion.1
  132.8 0.8 copy.14
  (2 shorter events, 0.1 us)
Async XLA Ops:
  0.6 7.7 %copy-start = (bf16[512,512]{1,0:T(8,128)(2,1)S(1)}, bf16[512,512]{1,0:T(8,128)(2,1)}, u32[]{:S(2)}) copy-start(bf16[512,512]{1,0:T(8,128)(2,1)} %param.11) | copy-start | bytes 1572868
  4.2 28.1 %all-to-all-start = ((bf16[4,128,2560]{2,1,0:T(8,128)(2,1)}), bf16[4,128,2560]{2,1,0:T(8,128)(2,1)S(1)}, u32[]{:S(2)}, u32[]{:S(2)}) async-start(bf16[4,128,2560]{2,1,0:T(8,128)(2,1)} %get-tuple-element.33), calls=%async_computation | async-start | bytes 5242880 | tf_op jit(solution)/shard_map/all_to_all | solution.py:252
  8.4 5.6 %collective-permute-start.2 = (bf16[256,512]{1,0:T(8,128)(2,1)S(1)}, bf16[256,512]{1,0:T(8,128)(2,1)S(1)}, u32[]{:S(2)}, u32[]{:S(2)}) collective-permute-start(bf16[256,512]{1,0:T(8,128)(2,1)S(1)} %constant_dynamic-slice_fusion), channel_id=1, source_target_pairs={{0,16},{1,65},{2,18},{3,67},{16,32},{17,81},{18,34},{19,83},{32,48... | collective-permute-start | bytes 786440 | tf_op jit(solution)/shard_map/ppermute | solution.py:239
  10.1 8.3 %collective-permute-start.1 = (bf16[256,512]{1,0:T(8,128)(2,1)S(1)}, bf16[256,512]{1,0:T(8,128)(2,1)S(1)}, u32[]{:S(2)}, u32[]{:S(2)}) collective-permute-start(bf16[256,512]{1,0:T(8,128)(2,1)S(1)} %constant_dynamic-slice_fusion), channel_id=1, source_target_pairs={{0,32},{1,129},{2,34},{3,131},{16,48},{17,145},{18,50},{19,147},{3... | collective-permute-start | bytes 786440 | tf_op jit(solution)/shard_map/ppermute | solution.py:239
  13.7 7.5 %collective-permute-start = (bf16[256,512]{1,0:T(8,128)(2,1)S(1)}, bf16[256,512]{1,0:T(8,128)(2,1)S(1)}, u32[]{:S(2)}, u32[]{:S(2)}) collective-permute-start(bf16[256,512]{1,0:T(8,128)(2,1)S(1)} %constant_dynamic-slice_fusion), channel_id=1, source_target_pairs={{0,48},{1,195},{2,50},{3,193},{16,0},{17,211},{18,2},{19,209},{32,... | collective-permute-start | bytes 786440 | tf_op jit(solution)/shard_map/ppermute | solution.py:239
  22.2 23.4 %collective-permute-start.4 = (bf16[1024,512]{1,0:T(8,128)(2,1)}, bf16[1024,512]{1,0:T(8,128)(2,1)}, u32[]{:S(2)}, u32[]{:S(2)}) collective-permute-start(bf16[1024,512]{1,0:T(8,128)(2,1)} %pad_maximum_fusion.refs_0_), channel_id=1, source_target_pairs={{0,194},{1,49},{2,192},{3,51},{16,210},{17,1},{18,208},{19,3},{32,... | collective-permute-start | bytes 3145736 | tf_op jit(solution)/shard_map/ppermute | solution.py:243
  24.9 21.9 %collective-permute-start.6 = (bf16[1024,512]{1,0:T(8,128)(2,1)}, bf16[1024,512]{1,0:T(8,128)(2,1)}, u32[]{:S(2)}, u32[]{:S(2)}) collective-permute-start(bf16[1024,512]{1,0:T(8,128)(2,1)} %pad_maximum_fusion.refs_0_), channel_id=1, source_target_pairs={{0,64},{1,17},{2,66},{3,19},{16,80},{17,33},{18,82},{19,35},{32,96... | collective-permute-start | bytes 3145736 | tf_op jit(solution)/shard_map/ppermute | solution.py:243
  34.4 48.0 %all-to-all-start.1 = ((bf16[4,512,512]{2,1,0:T(8,128)(2,1)}), bf16[4,512,512]{2,1,0:T(8,128)(2,1)S(1)}, u32[]{:S(2)}, u32[]{:S(2)}) async-start(bf16[4,512,512]{2,1,0:T(8,128)(2,1)} %shard_map.128), calls=%async_computation.1 | async-start | bytes 4194304 | tf_op jit(solution)/shard_map/all_to_all | solution.py:252
  38.4 44.2 %collective-permute-start.3 = (bf16[1024,512]{1,0:T(8,128)(2,1)}, bf16[1024,512]{1,0:T(8,128)(2,1)}, u32[]{:S(2)}, u32[]{:S(2)}) collective-permute-start(bf16[1024,512]{1,0:T(8,128)(2,1)} %pad_maximum_fusion.refs_0_), channel_id=1, source_target_pairs={{0,1},{1,0},{2,3},{3,2},{4,5},{5,4},{6,7},{7,6},{8,9},{9,8},{10,11... | collective-permute-start | bytes 3145736 | tf_op jit(solution)/shard_map/ppermute | solution.py:282
  45.6 37.1 %collective-permute-start.5 = (bf16[1024,512]{1,0:T(8,128)(2,1)}, bf16[1024,512]{1,0:T(8,128)(2,1)}, u32[]{:S(2)}, u32[]{:S(2)}) collective-permute-start(bf16[1024,512]{1,0:T(8,128)(2,1)} %collective-permute-done.4.up_ref.refs_2_), channel_id=1, source_target_pairs={{0,1},{1,0},{2,3},{3,2},{4,5},{5,4},{6,7},{7,6},{8,9},{9,8},{10,11... | collective-permute-start | bytes 3145736 | tf_op jit(solution)/shard_map/ppermute | solution.py:282
  46.8 35.8 %collective-permute-start.7 = (bf16[1024,512]{1,0:T(8,128)(2,1)}, bf16[1024,512]{1,0:T(8,128)(2,1)}, u32[]{:S(2)}, u32[]{:S(2)}) collective-permute-start(bf16[1024,512]{1,0:T(8,128)(2,1)} %collective-permute-done.6.down_ref.refs_4_), channel_id=1, source_target_pairs={{0,1},{1,0},{2,3},{3,2},{4,5},{5,4},{6,7},{7,6},{8,9},{9,8},{10,11... | collective-permute-start | bytes 3145736 | tf_op jit(solution)/shard_map/ppermute | solution.py:282
  79.7 9.1 %collective-permute-start.9 = (bf16[512,512]{1,0:T(8,128)(2,1)}, bf16[512,512]{1,0:T(8,128)(2,1)S(1)}, u32[]{:S(2)}, u32[]{:S(2)}) collective-permute-start(bf16[512,512]{1,0:T(8,128)(2,1)} %get-tuple-element.37), channel_id=1, source_target_pairs={{0,194},{1,49},{2,192},{3,51},{16,210},{17,1},{18,208},{19,3},{32,... | collective-permute-start | bytes 1572872 | tf_op jit(solution)/shard_map/ppermute | solution.py:243
  82.4 9.6 %collective-permute-start.10 = (bf16[512,512]{1,0:T(8,128)(2,1)}, bf16[512,512]{1,0:T(8,128)(2,1)}, u32[]{:S(2)}, u32[]{:S(2)}) collective-permute-start(bf16[512,512]{1,0:T(8,128)(2,1)} %get-tuple-element.38), channel_id=1, source_target_pairs={{0,64},{1,17},{2,66},{3,19},{16,80},{17,33},{18,82},{19,35},{32,96... | collective-permute-start | bytes 1572872 | tf_op jit(solution)/shard_map/ppermute | solution.py:243
  82.7 1.8 %collective-permute-start.8 = (bf16[256,512]{1,0:T(8,128)(2,1)S(1)}, bf16[256,512]{1,0:T(8,128)(2,1)S(1)}, u32[]{:S(2)}, u32[]{:S(2)}) collective-permute-start(bf16[256,512]{1,0:T(8,128)(2,1)S(1)} %get-tuple-element.36), channel_id=1, source_target_pairs={{0,1},{1,0},{2,3},{3,2},{4,5},{5,4},{6,7},{7,6},{8,9},{9,8},{10,11... | collective-permute-start | bytes 786440 | tf_op jit(solution)/shard_map/ppermute | solution.py:318
  88.8 10.6 %copy-start.1 = (bf16[512,512]{1,0:T(8,128)(2,1)}, bf16[512,512]{1,0:T(8,128)(2,1)S(1)}, u32[]{:S(2)}) copy-start(bf16[512,512]{1,0:T(8,128)(2,1)S(1)} %collective-permute-done.9.refs_6_) | copy-start | bytes 1572868
  91.9 7.4 %collective-permute-start.11 = (bf16[512,512]{1,0:T(8,128)(2,1)S(1)}, bf16[512,512]{1,0:T(8,128)(2,1)S(1)}, u32[]{:S(2)}, u32[]{:S(2)}) collective-permute-start(bf16[512,512]{1,0:T(8,128)(2,1)S(1)} %collective-permute-done.9.refs_6_), channel_id=1, source_target_pairs={{0,1},{1,0},{2,3},{3,2},{4,5},{5,4},{6,7},{7,6},{8,9},{9,8},{10,11... | collective-permute-start | bytes 1572872 | tf_op jit(solution)/shard_map/ppermute | solution.py:322
  92.6 6.8 %collective-permute-start.12 = (bf16[512,512]{1,0:T(8,128)(2,1)}, bf16[512,512]{1,0:T(8,128)(2,1)S(1)}, u32[]{:S(2)}, u32[]{:S(2)}) collective-permute-start(bf16[512,512]{1,0:T(8,128)(2,1)} %collective-permute-done.10.refs_8_), channel_id=1, source_target_pairs={{0,1},{1,0},{2,3},{3,2},{4,5},{5,4},{6,7},{7,6},{8,9},{9,8},{10,11... | collective-permute-start | bytes 1572872 | tf_op jit(solution)/shard_map/ppermute | solution.py:322
  92.6 17.6 %all-to-all-start.2 = ((bf16[8,32,512]{2,1,0:T(8,128)(2,1)}), bf16[8,32,512]{2,1,0:T(8,128)(2,1)S(1)}, u32[]{:S(2)}, u32[]{:S(2)}) async-start(bf16[8,32,512]{2,1,0:T(8,128)(2,1)} %bitcast.2), calls=%async_computation.2 | async-start | bytes 524288 | tf_op jit(solution)/shard_map/all_to_all | solution.py:323
  99.4 0.8 copy-start.2
  99.4 1.0 copy-start.3
  110.2 0.7 copy-start.4
  113.1 16.7 %all-to-all-start.3 = ((bf16[8,32,512]{2,1,0:T(8,128)(2,1)}), bf16[8,32,512]{2,1,0:T(8,128)(2,1)S(1)}, u32[]{:S(2)}, u32[]{:S(2)}) async-start(bf16[8,32,512]{2,1,0:T(8,128)(2,1)} %get-tuple-element.53), calls=%async_computation.3 | async-start | bytes 524288 | tf_op jit(solution)/shard_map/all_to_all | solution.py:350
  129.9 2.8 %collective-permute-start.13 = (bf16[8,32,512]{2,1,0:T(8,128)(2,1)S(1)}, bf16[8,32,512]{2,1,0:T(8,128)(2,1)S(1)}, u32[]{:S(2)}, u32[]{:S(2)}) collective-permute-start(bf16[8,32,512]{2,1,0:T(8,128)(2,1)S(1)} %all-to-all-done.3), channel_id=1, source_target_pairs={{0,1},{1,0},{2,3},{3,2},{4,5},{5,4},{6,7},{7,6},{8,9},{9,8},{10,11... | collective-permute-start | bytes 786440 | tf_op jit(solution)/shard_map/ppermute | solution.py:361

commit v9 on v8

--- a/solution.py
+++ b/solution.py
@@ -302,13 +302,12 @@
     rows = from_up.shape[0] // 2
     far_a, far_b = kernel_call(
         halves_kernel,
-        (shape((rows, keys_w), BF16),) * 2,
+        (pltpu.VMEM((rows, keys_w), BF16),) * 2,
         0,
         1 << 20,
         [HBM, HBM],
-        60 << 20,
-        (HBM, HBM),
-        (pltpu.SemaphoreType.DMA((2,)),),
+        24 << 20,
+        scratch=(pltpu.SemaphoreType.DMA((2,)),),
     )(from_up, from_down)
     far = [
         second_step(far_a, lambda place, on_z: -1),

time: 134 us -> 105 us (0.78)
  Pallas kernels: 55.6 us -> 24.7 us
  starting transfers between devices: 32.2 us -> 35.5 us
  waiting for transfers between devices: 40.6 us -> 39 us
    pallas_call x1, Pallas kernels: 32.9 us -> 2.01 us  [shards(): kernel_call(halves_kernel, (pltpu.VMEM((rows, keys_w), BF16),) * 2, 0, 1...]
    ppermute x4, waiting for transfers between devices: 15.2 us -> 11 us  [second_step(): return lax.ppermute(value, GATHER, moved(lambda c: c == 0, shift))]
    all_to_all x2, waiting for transfers between devices: 7.36 us -> 9.91 us  [mixed(): lax.all_to_all(value, ('y', 'x', 'c'), 0, 0, axis_index_groups=groups, ti...]
    ppermute x1, starting transfers between devices: 0.59 us -> 2.24 us  [shards(): sib = lax.ppermute(sib, 'c', ring(C, 1))]
  transfers between devices with their start and end apart: 18 -> 18, of which waited for: 12 -> 13; matrix products, arithmetic and copies ran while one was open for 1% -> 2% of each run, Pallas kernels for 37% -> 18%
where the time goes in v9:
time: 105 us; the launch traced here: 104 us
  waiting for transfers between devices  39 us (37%)
  starting transfers between devices  35.5 us (34%)
  Pallas kernels  24.7 us (24%)
  local copies, waits for them, and re-layouts  2.52 us (2%)
  other arithmetic  1.92 us (2%)
    ppermute x4, waiting for transfers between devices, second_step(): return lax.ppermute(value, GATHER, moved(lambda c: c == 0, shift))  11 us
    all_to_all x2, waiting for transfers between devices, mixed(): lax.all_to_all(value, ('y', 'x', 'c'), 0, 0, axis_index_groups=groups, ti...  9.91 us
    pallas_call x1, Pallas kernels, shards(): kernel_call(functools.partial(token_grad_kernel, count), shape(tokens.sha...  8.56 us
    all_to_all x2, starting transfers between devices, mixed(): lax.all_to_all(value, ('y', 'x', 'c'), 0, 0, axis_index_groups=groups, ti...  8.21 us
    all_to_all x1, starting transfers between devices, shards(): lax.all_to_all(summed.reshape(ZL * ZH, ROWS, keys_w), ('zl', 'zh'), 0, 0,...  8.02 us
    ppermute x3, waiting for transfers between devices, first_step(): return lax.ppermute(value, GATHER, moved(lambda c: c == 1, shift))  7.49 us
    pallas_call x1, Pallas kernels, shards(): kernel_call(functools.partial(keys_kernel, count), (shape((tok_rows, keys...  6.01 us
    ppermute x4, starting transfers between devices, second_step(): return lax.ppermute(value, GATHER, moved(lambda c: c == 0, shift))  5.32 us
  transfers between devices with their start and end apart: 18, of which 13 were waited for; matrix products, arithmetic and copies ran while one was open for 2% of the time, Pallas kernels for 18%

profile of v9, /device:TPU:33, one launch (start us, length us, event | category | flops | bytes accessed | tf_op | source)
XLA Modules:
  0.0 104.3 jit_solution(7016831063044830052)
XLA Ops:
  0.6 0.0 copy-start
  0.6 3.5 %shard_map.127 = (bf16[4,128,2560]{2,1,0:T(8,128)(2,1)}, f32[128,128]{1,0:T(8,128)}) custom-call(bf16[128,8192]{1,0:T(8,128)(2,1)} %tok_ref.5, f32[1,8192]{1,0:T(1,128)} %bitcast.11, bf16[128,512]{1,0:T(8,128)(2,1)} %cot_ref.5), custom_call_target="tpu_custom_call" | custom-call | flops 6291456 | bytes 5242880 | tf_op jit(solution)/shard_map/pallas_call | solution.py:268
  4.2 4.2 %all-to-all-start = ((bf16[4,128,2560]{2,1,0:T(8,128)(2,1)}), bf16[4,128,2560]{2,1,0:T(8,128)(2,1)S(1)}, u32[]{:S(2)}, u32[]{:S(2)}) async-start(bf16[4,128,2560]{2,1,0:T(8,128)(2,1)} %get-tuple-element.33), calls=%async_computation | async-start | bytes 5242880 | tf_op jit(solution)/shard_map/all_to_all | solution.py:252
  8.4 0.0 copy-done
  8.4 1.7 %collective-permute-start.2 = (bf16[256,512]{1,0:T(8,128)(2,1)S(1)}, bf16[256,512]{1,0:T(8,128)(2,1)S(1)}, u32[]{:S(2)}, u32[]{:S(2)}) collective-permute-start(bf16[256,512]{1,0:T(8,128)(2,1)S(1)} %constant_dynamic-slice_fusion), channel_id=1, source_target_pairs={{0,16},{1,65},{2,18},{3,67},{16,32},{17,81},{18,34},{19,83},{32,48... | collective-permute-start | bytes 786440 | tf_op jit(solution)/shard_map/ppermute | solution.py:239
  10.1 3.6 %collective-permute-start.1 = (bf16[256,512]{1,0:T(8,128)(2,1)S(1)}, bf16[256,512]{1,0:T(8,128)(2,1)S(1)}, u32[]{:S(2)}, u32[]{:S(2)}) collective-permute-start(bf16[256,512]{1,0:T(8,128)(2,1)S(1)} %constant_dynamic-slice_fusion), channel_id=1, source_target_pairs={{0,32},{1,129},{2,34},{3,131},{16,48},{17,145},{18,50},{19,147},{3... | collective-permute-start | bytes 786440 | tf_op jit(solution)/shard_map/ppermute | solution.py:239
  13.7 0.0 collective-permute-start
  13.7 0.3 collective-permute-done.2
  14.0 4.4 %collective-permute-done.1 = bf16[256,512]{1,0:T(8,128)(2,1)S(1)} collective-permute-done((bf16[256,512]{1,0:T(8,128)(2,1)S(1)}, bf16[256,512]{1,0:T(8,128)(2,1)S(1)}, u32[]{:S(2)}, u32[]{:S(2)}) %collective-permute-start.1) | collective-permute-done | bytes 262176 | tf_op jit(solution)/shard_map/ppermute | solution.py:239
  18.4 2.8 %collective-permute-done = bf16[256,512]{1,0:T(8,128)(2,1)S(1)} collective-permute-done((bf16[256,512]{1,0:T(8,128)(2,1)S(1)}, bf16[256,512]{1,0:T(8,128)(2,1)S(1)}, u32[]{:S(2)}, u32[]{:S(2)}) %collective-permute-start) | collective-permute-done | bytes 262176 | tf_op jit(solution)/shard_map/ppermute | solution.py:239
  21.2 1.0 %pad_maximum_fusion.refs_0_ = bf16[1024,512]{1,0:T(8,128)(2,1)} fusion(bf16[256,512]{1,0:T(8,128)(2,1)S(1)} %collective-permute-done.2, bf16[256,512]{1,0:T(8,128)(2,1)S(1)} %collective-permute-done.1, bf16[256,512]{1,0:T(8,128)(2,1)S(1)} %collective-permute-done, bf16[256,512]{1,0:T(8,128)(2,1)S(1)} %constant_dynamic-slice_fusion), kind=kLoop, calls=%fused_computation | loop fusion | flops 4194304 | bytes 2097152 | tf_op jit(solution)/shard_map/concatenate | solution.py:263
  22.2 2.7 %collective-permute-start.4 = (bf16[1024,512]{1,0:T(8,128)(2,1)}, bf16[1024,512]{1,0:T(8,128)(2,1)}, u32[]{:S(2)}, u32[]{:S(2)}) collective-permute-start(bf16[1024,512]{1,0:T(8,128)(2,1)} %pad_maximum_fusion.refs_0_), channel_id=1, source_target_pairs={{0,194},{1,49},{2,192},{3,51},{16,210},{17,1},{18,208},{19,3},{32,... | collective-permute-start | bytes 3145736 | tf_op jit(solution)/shard_map/ppermute | solution.py:243
  24.9 0.0 collective-permute-start.6
  24.9 7.4 %all-to-all-done = bf16[4,128,2560]{2,1,0:T(8,128)(2,1)S(1)} async-done(((bf16[4,128,2560]{2,1,0:T(8,128)(2,1)}), bf16[4,128,2560]{2,1,0:T(8,128)(2,1)S(1)}, u32[]{:S(2)}, u32[]{:S(2)}) %all-to-all-start) | async-done | bytes 2621472 | tf_op jit(solution)/shard_map/all_to_all | solution.py:252
  32.2 2.1 %shard_map.128 = bf16[4,512,512]{2,1,0:T(8,128)(2,1)} custom-call(bf16[512,2560]{1,0:T(8,128)(2,1)S(1)} %bitcast.9), custom_call_target="tpu_custom_call" | custom-call | bytes 1048576 | tf_op jit(solution)/shard_map/pallas_call | solution.py:283
  34.4 4.0 %all-to-all-start.1 = ((bf16[4,512,512]{2,1,0:T(8,128)(2,1)}), bf16[4,512,512]{2,1,0:T(8,128)(2,1)S(1)}, u32[]{:S(2)}, u32[]{:S(2)}) async-start(bf16[4,512,512]{2,1,0:T(8,128)(2,1)} %shard_map.128), calls=%async_computation.1 | async-start | bytes 4194304 | tf_op jit(solution)/shard_map/all_to_all | solution.py:252
  38.4 0.0 collective-permute-start.3
  38.4 7.2 %collective-permute-done.4.up_ref.refs_2_ = bf16[1024,512]{1,0:T(8,128)(2,1)} collective-permute-done((bf16[1024,512]{1,0:T(8,128)(2,1)}, bf16[1024,512]{1,0:T(8,128)(2,1)}, u32[]{:S(2)}, u32[]{:S(2)}) %collective-permute-start.4) | collective-permute-done | bytes 1048608 | tf_op jit(solution)/shard_map/ppermute | solution.py:243
  45.6 0.0 collective-permute-start.5
  45.6 1.2 %collective-permute-done.6.down_ref.refs_4_ = bf16[1024,512]{1,0:T(8,128)(2,1)} collective-permute-done((bf16[1024,512]{1,0:T(8,128)(2,1)}, bf16[1024,512]{1,0:T(8,128)(2,1)}, u32[]{:S(2)}, u32[]{:S(2)}) %collective-permute-start.6) | collective-permute-done | bytes 1048608 | tf_op jit(solution)/shard_map/ppermute | solution.py:243
  46.8 0.0 collective-permute-start.7
  46.8 2.0 %shard_map.130 = (bf16[512,512]{1,0:T(8,128)(2,1)}, bf16[512,512]{1,0:T(8,128)(2,1)S(1)}) custom-call(bf16[1024,512]{1,0:T(8,128)(2,1)} %collective-permute-done.4.up_ref.refs_2_, bf16[1024,512]{1,0:T(8,128)(2,1)} %collective-permute-done.6.down_ref.refs_4_), custom_call_target="tpu_custom_call" | custom-call | bytes 1048576 | tf_op jit(solution)/shard_map/pallas_call | solution.py:303
  48.9 2.6 %collective-permute-start.9 = (bf16[512,512]{1,0:T(8,128)(2,1)}, bf16[512,512]{1,0:T(8,128)(2,1)}, u32[]{:S(2)}, u32[]{:S(2)}) collective-permute-start(bf16[512,512]{1,0:T(8,128)(2,1)} %get-tuple-element.37), channel_id=1, source_target_pairs={{0,194},{1,49},{2,192},{3,51},{16,210},{17,1},{18,208},{19,3},{32,... | collective-permute-start | bytes 1572872 | tf_op jit(solution)/shard_map/ppermute | solution.py:243
  51.5 0.0 collective-permute-start.10
  51.5 2.6 %all-to-all-done.1.recv_ref = bf16[4,512,512]{2,1,0:T(8,128)(2,1)S(1)} async-done(((bf16[4,512,512]{2,1,0:T(8,128)(2,1)}), bf16[4,512,512]{2,1,0:T(8,128)(2,1)S(1)}, u32[]{:S(2)}, u32[]{:S(2)}) %all-to-all-start.1) | async-done | bytes 2097184 | tf_op jit(solution)/shard_map/all_to_all | solution.py:252
  54.1 0.2 shard_map.129
  54.3 0.0 collective-permute-done.3.refs_1_
  54.3 0.0 collective-permute-done.5.refs_3_
  54.3 0.0 collective-permute-done.7.refs_5_
  54.3 2.2 %collective-permute-start.8 = (bf16[256,512]{1,0:T(8,128)(2,1)S(1)}, bf16[256,512]{1,0:T(8,128)(2,1)S(1)}, u32[]{:S(2)}, u32[]{:S(2)}) collective-permute-start(bf16[256,512]{1,0:T(8,128)(2,1)S(1)} %get-tuple-element.36), channel_id=1, source_target_pairs={{0,1},{1,0},{2,3},{3,2},{4,5},{5,4},{6,7},{7,6},{8,9},{9,8},{10,11... | collective-permute-start | bytes 786440 | tf_op jit(solution)/shard_map/ppermute | solution.py:317
  56.6 1.2 %collective-permute-done.8 = bf16[256,512]{1,0:T(8,128)(2,1)S(1)} collective-permute-done((bf16[256,512]{1,0:T(8,128)(2,1)S(1)}, bf16[256,512]{1,0:T(8,128)(2,1)S(1)}, u32[]{:S(2)}, u32[]{:S(2)}) %collective-permute-start.8) | collective-permute-done | bytes 262176 | tf_op jit(solution)/shard_map/ppermute | solution.py:317
  57.7 0.8 add_convert_fusion
  58.5 0.7 collective-permute-done.9.refs_6_
  59.2 1.9 %collective-permute-done.10.refs_8_ = bf16[512,512]{1,0:T(8,128)(2,1)} collective-permute-done((bf16[512,512]{1,0:T(8,128)(2,1)S(1)}, bf16[512,512]{1,0:T(8,128)(2,1)}, u32[]{:S(2)}, u32[]{:S(2)}) %collective-permute-start.10) | collective-permute-done | bytes 524320 | tf_op jit(solution)/shard_map/ppermute | solution.py:243
  61.0 0.4 collective-permute-start.11
  61.5 0.1 collective-permute-start.12
  61.6 8.0 %all-to-all-start.2 = ((bf16[8,32,512]{2,1,0:T(8,128)(2,1)}), bf16[8,32,512]{2,1,0:T(8,128)(2,1)S(1)}, u32[]{:S(2)}, u32[]{:S(2)}) async-start(bf16[8,32,512]{2,1,0:T(8,128)(2,1)} %bitcast.2), calls=%async_computation.2 | async-start | bytes 524288 | tf_op jit(solution)/shard_map/all_to_all | solution.py:322
  69.6 0.0 collective-permute-done.11.refs_7_
  69.6 0.0 copy-start.1
  69.6 0.0 collective-permute-done.12.refs_9_
  69.6 0.0 copy-start.2
  69.6 0.8 copy-done.1
  70.4 0.2 copy-done.2
  70.6 6.0 %shard_map.131 = (bf16[128,512]{1,0:T(8,128)(2,1)}, f32[128,128]{1,0:T(8,128)}) custom-call(bf16[128,8192]{1,0:T(8,128)(2,1)} %tok_ref.5, f32[1,8192]{1,0:T(1,128)} %bitcast.12, bf16[128,512]{1,0:T(8,128)(2,1)} %cot_ref.5, f32[128,128]{1,0:T(8,128)} %get-tuple-element.40.inv_ref, bf16[1024,512]{1,0:T(8,128)(2,1)} %pad_maximum_fusion.refs_0_, ...), custom_call_target="tpu_custom_call" | custom-call | flops 1073741824 | bytes 11534336 | tf_op jit(solution)/shard_map/pallas_call | solution.py:325
  76.6 3.7 %all-to-all-done.2.recv_ref = bf16[8,32,512]{2,1,0:T(8,128)(2,1)S(1)} async-done(((bf16[8,32,512]{2,1,0:T(8,128)(2,1)}), bf16[8,32,512]{2,1,0:T(8,128)(2,1)S(1)}, u32[]{:S(2)}, u32[]{:S(2)}) %all-to-all-start.2) | async-done | bytes 262176 | tf_op jit(solution)/shard_map/all_to_all | solution.py:322
  80.3 0.0 copy-start.3
  80.3 0.7 copy-done.3
  81.0 2.2 %shard_map.132 = (f32[32,512]{1,0:T(8,128)}, f32[16,1024]{1,0:T(8,128)}, f32[16,1024]{1,0:T(8,128)}, bf16[8,32,512]{2,1,0:T(8,128)(2,1)}) custom-call(bf16[8,32,512]{2,1,0:T(8,128)(2,1)} %copy-done.3, f32[16,1024]{1,0:T(8,128)} %first_ref.1, f32[16,1024]{1,0:T(8,128)} %second_ref.1, f32[32,512]{1,0:T(8,128)} %master_ref.1, s32[1,1024]{1,0:T(1,128)} %bitcast.14), custom_call_target="tpu_custom_call" | custom-call | flops 33554432 | bytes 1048576 | tf_op jit(solution)/shard_map/pallas_call | solution.py:335
  83.2 4.7 %all-to-all-start.3 = ((bf16[8,32,512]{2,1,0:T(8,128)(2,1)}), bf16[8,32,512]{2,1,0:T(8,128)(2,1)S(1)}, u32[]{:S(2)}, u32[]{:S(2)}) async-start(bf16[8,32,512]{2,1,0:T(8,128)(2,1)} %get-tuple-element.53), calls=%async_computation.3 | async-start | bytes 524288 | tf_op jit(solution)/shard_map/all_to_all | solution.py:349
  87.9 8.6 %shard_map.133 = bf16[128,8192]{1,0:T(8,128)(2,1)} custom-call(bf16[128,8192]{1,0:T(8,128)(2,1)} %tok_ref.5, f32[1,8192]{1,0:T(1,128)} %bitcast.13, bf16[128,512]{1,0:T(8,128)(2,1)} %cot_ref.5, f32[128,128]{1,0:T(8,128)} %get-tuple-element.40.inv_ref, f32[128,128]{1,0:T(8,128)} %get-tuple-element.54.mean_ref, bf16[1024,512]{1,0:T(8,128)(2,1)} %pad_maximum_fusion.refs_0_, ...), custom_call_target="tpu_custom_call" | custom-call | flops 1073741824 | bytes 13631488 | tf_op jit(solution)/shard_map/pallas_call | solution.py:350
  96.5 4.6 %all-to-all-done.3 = bf16[8,32,512]{2,1,0:T(8,128)(2,1)S(1)} async-done(((bf16[8,32,512]{2,1,0:T(8,128)(2,1)}), bf16[8,32,512]{2,1,0:T(8,128)(2,1)S(1)}, u32[]{:S(2)}, u32[]{:S(2)}) %all-to-all-start.3) | async-done | bytes 262176 | tf_op jit(solution)/shard_map/all_to_all | solution.py:349
  101.1 1.2 %collective-permute-start.13 = (bf16[8,32,512]{2,1,0:T(8,128)(2,1)S(1)}, bf16[8,32,512]{2,1,0:T(8,128)(2,1)S(1)}, u32[]{:S(2)}, u32[]{:S(2)}) collective-permute-start(bf16[8,32,512]{2,1,0:T(8,128)(2,1)S(1)} %all-to-all-done.3), channel_id=1, source_target_pairs={{0,1},{1,0},{2,3},{3,2},{4,5},{5,4},{6,7},{7,6},{8,9},{9,8},{10,11... | collective-permute-start | bytes 786440 | tf_op jit(solution)/shard_map/ppermute | solution.py:360
  102.2 1.2 %collective-permute-done.13 = bf16[8,32,512]{2,1,0:T(8,128)(2,1)S(1)} collective-permute-done((bf16[8,32,512]{2,1,0:T(8,128)(2,1)S(1)}, bf16[8,32,512]{2,1,0:T(8,128)(2,1)S(1)}, u32[]{:S(2)}, u32[]{:S(2)}) %collective-permute-start.13) | collective-permute-done | bytes 262176 | tf_op jit(solution)/shard_map/ppermute | solution.py:360
  103.5 0.1 pad_maximum_fusion.1
  103.5 0.8 copy.14
  (2 shorter events, 0.1 us)
Async XLA Ops:
  0.6 7.7 %copy-start = (bf16[512,512]{1,0:T(8,128)(2,1)S(1)}, bf16[512,512]{1,0:T(8,128)(2,1)}, u32[]{:S(2)}) copy-start(bf16[512,512]{1,0:T(8,128)(2,1)} %param.11) | copy-start | bytes 1572868
  4.2 28.1 %all-to-all-start = ((bf16[4,128,2560]{2,1,0:T(8,128)(2,1)}), bf16[4,128,2560]{2,1,0:T(8,128)(2,1)S(1)}, u32[]{:S(2)}, u32[]{:S(2)}) async-start(bf16[4,128,2560]{2,1,0:T(8,128)(2,1)} %get-tuple-element.33), calls=%async_computation | async-start | bytes 5242880 | tf_op jit(solution)/shard_map/all_to_all | solution.py:252
  8.4 5.6 %collective-permute-start.2 = (bf16[256,512]{1,0:T(8,128)(2,1)S(1)}, bf16[256,512]{1,0:T(8,128)(2,1)S(1)}, u32[]{:S(2)}, u32[]{:S(2)}) collective-permute-start(bf16[256,512]{1,0:T(8,128)(2,1)S(1)} %constant_dynamic-slice_fusion), channel_id=1, source_target_pairs={{0,16},{1,65},{2,18},{3,67},{16,32},{17,81},{18,34},{19,83},{32,48... | collective-permute-start | bytes 786440 | tf_op jit(solution)/shard_map/ppermute | solution.py:239
  10.1 8.3 %collective-permute-start.1 = (bf16[256,512]{1,0:T(8,128)(2,1)S(1)}, bf16[256,512]{1,0:T(8,128)(2,1)S(1)}, u32[]{:S(2)}, u32[]{:S(2)}) collective-permute-start(bf16[256,512]{1,0:T(8,128)(2,1)S(1)} %constant_dynamic-slice_fusion), channel_id=1, source_target_pairs={{0,32},{1,129},{2,34},{3,131},{16,48},{17,145},{18,50},{19,147},{3... | collective-permute-start | bytes 786440 | tf_op jit(solution)/shard_map/ppermute | solution.py:239
  13.7 7.5 %collective-permute-start = (bf16[256,512]{1,0:T(8,128)(2,1)S(1)}, bf16[256,512]{1,0:T(8,128)(2,1)S(1)}, u32[]{:S(2)}, u32[]{:S(2)}) collective-permute-start(bf16[256,512]{1,0:T(8,128)(2,1)S(1)} %constant_dynamic-slice_fusion), channel_id=1, source_target_pairs={{0,48},{1,195},{2,50},{3,193},{16,0},{17,211},{18,2},{19,209},{32,... | collective-permute-start | bytes 786440 | tf_op jit(solution)/shard_map/ppermute | solution.py:239
  22.2 23.4 %collective-permute-start.4 = (bf16[1024,512]{1,0:T(8,128)(2,1)}, bf16[1024,512]{1,0:T(8,128)(2,1)}, u32[]{:S(2)}, u32[]{:S(2)}) collective-permute-start(bf16[1024,512]{1,0:T(8,128)(2,1)} %pad_maximum_fusion.refs_0_), channel_id=1, source_target_pairs={{0,194},{1,49},{2,192},{3,51},{16,210},{17,1},{18,208},{19,3},{32,... | collective-permute-start | bytes 3145736 | tf_op jit(solution)/shard_map/ppermute | solution.py:243
  24.9 21.9 %collective-permute-start.6 = (bf16[1024,512]{1,0:T(8,128)(2,1)}, bf16[1024,512]{1,0:T(8,128)(2,1)}, u32[]{:S(2)}, u32[]{:S(2)}) collective-permute-start(bf16[1024,512]{1,0:T(8,128)(2,1)} %pad_maximum_fusion.refs_0_), channel_id=1, source_target_pairs={{0,64},{1,17},{2,66},{3,19},{16,80},{17,33},{18,82},{19,35},{32,96... | collective-permute-start | bytes 3145736 | tf_op jit(solution)/shard_map/ppermute | solution.py:243
  34.4 19.7 %all-to-all-start.1 = ((bf16[4,512,512]{2,1,0:T(8,128)(2,1)}), bf16[4,512,512]{2,1,0:T(8,128)(2,1)S(1)}, u32[]{:S(2)}, u32[]{:S(2)}) async-start(bf16[4,512,512]{2,1,0:T(8,128)(2,1)} %shard_map.128), calls=%async_computation.1 | async-start | bytes 4194304 | tf_op jit(solution)/shard_map/all_to_all | solution.py:252
  38.4 15.9 %collective-permute-start.3 = (bf16[1024,512]{1,0:T(8,128)(2,1)}, bf16[1024,512]{1,0:T(8,128)(2,1)}, u32[]{:S(2)}, u32[]{:S(2)}) collective-permute-start(bf16[1024,512]{1,0:T(8,128)(2,1)} %pad_maximum_fusion.refs_0_), channel_id=1, source_target_pairs={{0,1},{1,0},{2,3},{3,2},{4,5},{5,4},{6,7},{7,6},{8,9},{9,8},{10,11... | collective-permute-start | bytes 3145736 | tf_op jit(solution)/shard_map/ppermute | solution.py:282
  45.6 8.7 %collective-permute-start.5 = (bf16[1024,512]{1,0:T(8,128)(2,1)}, bf16[1024,512]{1,0:T(8,128)(2,1)}, u32[]{:S(2)}, u32[]{:S(2)}) collective-permute-start(bf16[1024,512]{1,0:T(8,128)(2,1)} %collective-permute-done.4.up_ref.refs_2_), channel_id=1, source_target_pairs={{0,1},{1,0},{2,3},{3,2},{4,5},{5,4},{6,7},{7,6},{8,9},{9,8},{10,11... | collective-permute-start | bytes 3145736 | tf_op jit(solution)/shard_map/ppermute | solution.py:282
  46.8 7.5 %collective-permute-start.7 = (bf16[1024,512]{1,0:T(8,128)(2,1)}, bf16[1024,512]{1,0:T(8,128)(2,1)}, u32[]{:S(2)}, u32[]{:S(2)}) collective-permute-start(bf16[1024,512]{1,0:T(8,128)(2,1)} %collective-permute-done.6.down_ref.refs_4_), channel_id=1, source_target_pairs={{0,1},{1,0},{2,3},{3,2},{4,5},{5,4},{6,7},{7,6},{8,9},{9,8},{10,11... | collective-permute-start | bytes 3145736 | tf_op jit(solution)/shard_map/ppermute | solution.py:282
  48.9 10.3 %collective-permute-start.9 = (bf16[512,512]{1,0:T(8,128)(2,1)}, bf16[512,512]{1,0:T(8,128)(2,1)}, u32[]{:S(2)}, u32[]{:S(2)}) collective-permute-start(bf16[512,512]{1,0:T(8,128)(2,1)} %get-tuple-element.37), channel_id=1, source_target_pairs={{0,194},{1,49},{2,192},{3,51},{16,210},{17,1},{18,208},{19,3},{32,... | collective-permute-start | bytes 1572872 | tf_op jit(solution)/shard_map/ppermute | solution.py:243
  51.5 9.5 %collective-permute-start.10 = (bf16[512,512]{1,0:T(8,128)(2,1)S(1)}, bf16[512,512]{1,0:T(8,128)(2,1)}, u32[]{:S(2)}, u32[]{:S(2)}) collective-permute-start(bf16[512,512]{1,0:T(8,128)(2,1)S(1)} %get-tuple-element.38), channel_id=1, source_target_pairs={{0,64},{1,17},{2,66},{3,19},{16,80},{17,33},{18,82},{19,35},{32,96... | collective-permute-start | bytes 1572872 | tf_op jit(solution)/shard_map/ppermute | solution.py:243
  54.3 3.4 %collective-permute-start.8 = (bf16[256,512]{1,0:T(8,128)(2,1)S(1)}, bf16[256,512]{1,0:T(8,128)(2,1)S(1)}, u32[]{:S(2)}, u32[]{:S(2)}) collective-permute-start(bf16[256,512]{1,0:T(8,128)(2,1)S(1)} %get-tuple-element.36), channel_id=1, source_target_pairs={{0,1},{1,0},{2,3},{3,2},{4,5},{5,4},{6,7},{7,6},{8,9},{9,8},{10,11... | collective-permute-start | bytes 786440 | tf_op jit(solution)/shard_map/ppermute | solution.py:317
  61.0 8.5 %collective-permute-start.11 = (bf16[512,512]{1,0:T(8,128)(2,1)}, bf16[512,512]{1,0:T(8,128)(2,1)S(1)}, u32[]{:S(2)}, u32[]{:S(2)}) collective-permute-start(bf16[512,512]{1,0:T(8,128)(2,1)} %collective-permute-done.9.refs_6_), channel_id=1, source_target_pairs={{0,1},{1,0},{2,3},{3,2},{4,5},{5,4},{6,7},{7,6},{8,9},{9,8},{10,11... | collective-permute-start | bytes 1572872 | tf_op jit(solution)/shard_map/ppermute | solution.py:321
  61.5 8.1 %collective-permute-start.12 = (bf16[512,512]{1,0:T(8,128)(2,1)}, bf16[512,512]{1,0:T(8,128)(2,1)S(1)}, u32[]{:S(2)}, u32[]{:S(2)}) collective-permute-start(bf16[512,512]{1,0:T(8,128)(2,1)} %collective-permute-done.10.refs_8_), channel_id=1, source_target_pairs={{0,1},{1,0},{2,3},{3,2},{4,5},{5,4},{6,7},{7,6},{8,9},{9,8},{10,11... | collective-permute-start | bytes 1572872 | tf_op jit(solution)/shard_map/ppermute | solution.py:321
  61.6 18.7 %all-to-all-start.2 = ((bf16[8,32,512]{2,1,0:T(8,128)(2,1)}), bf16[8,32,512]{2,1,0:T(8,128)(2,1)S(1)}, u32[]{:S(2)}, u32[]{:S(2)}) async-start(bf16[8,32,512]{2,1,0:T(8,128)(2,1)} %bitcast.2), calls=%async_computation.2 | async-start | bytes 524288 | tf_op jit(solution)/shard_map/all_to_all | solution.py:322
  69.6 0.8 copy-start.1
  69.6 1.0 copy-start.2
  80.3 0.7 copy-start.3
  83.2 17.9 %all-to-all-start.3 = ((bf16[8,32,512]{2,1,0:T(8,128)(2,1)}), bf16[8,32,512]{2,1,0:T(8,128)(2,1)S(1)}, u32[]{:S(2)}, u32[]{:S(2)}) async-start(bf16[8,32,512]{2,1,0:T(8,128)(2,1)} %get-tuple-element.53), calls=%async_computation.3 | async-start | bytes 524288 | tf_op jit(solution)/shard_map/all_to_all | solution.py:349
  101.1 2.3 %collective-permute-start.13 = (bf16[8,32,512]{2,1,0:T(8,128)(2,1)S(1)}, bf16[8,32,512]{2,1,0:T(8,128)(2,1)S(1)}, u32[]{:S(2)}, u32[]{:S(2)}) collective-permute-start(bf16[8,32,512]{2,1,0:T(8,128)(2,1)S(1)} %all-to-all-done.3), channel_id=1, source_target_pairs={{0,1},{1,0},{2,3},{3,2},{4,5},{5,4},{6,7},{7,6},{8,9},{9,8},{10,11... | collective-permute-start | bytes 786440 | tf_op jit(solution)/shard_map/ppermute | solution.py:360

commit v10 on v9

--- a/solution.py
+++ b/solution.py
@@ -30,6 +30,14 @@
 
 def shape(dims, kind):
     return jax.ShapeDtypeStruct(dims, kind)
+
+
+def in_hbm(*values):
+    return [pltpu.with_memory_space_constraint(value, pltpu.HBM) for value in values]
+
+
+def in_vmem(*values):
+    return [pltpu.with_memory_space_constraint(value, pltpu.VMEM) for value in values]
 
 
 def kernel_call(body, outs, flops, nbytes, in_specs, limit=24 << 20, out_specs=None, scratch=()):
@@ -114,35 +122,31 @@
         copy.wait()
 
 
-def places(width, refs, bufs, sem):
+def places(width, refs):
     c, zl, y = (lax.axis_index(name) for name in ("c", "zl", "y"))
     step = width // (ZL * Y)
     half = step // 2
-    copies = [pltpu.make_async_copy(ref, buf, sem.at[i]) for i, (ref, buf) in enumerate(zip(refs, bufs))]
-    for copy in copies:
-        copy.start()
-    for i, buf in enumerate(bufs):
-        copies[i].wait()
+    for i, ref in enumerate(refs):
         off = (0, 1, 3)[i // 2] if i < 6 else 2
         core = c if i % 2 == 0 else 1 - c
-        for row in range(buf.shape[0] // half):
+        for row in range(ref.shape[0] // half):
             k = row if i < 6 else row + 2 * ((i - 6) // 2)
             on_zl, on_y = jnp.where(core == 0, off, k), jnp.where(core == 0, k, off)
             node = lax.rem(zl + on_zl, ZL) * Y + lax.rem(y + on_y, Y)
             at = pl.multiple_of(node * step + core * half, half)
-            yield pl.ds(at, half), buf[row * half : (row + 1) * half, :]
+            yield pl.ds(at, half), ref[row * half : (row + 1) * half, :]
 
 
 def widened(ref, cols):
     return jnp.concatenate([ref[...]] * (cols // ref.shape[1]), axis=1)
 
 
-def keys_kernel(blocks, tok_ref, gain_ref, cot_ref, inv_ref, *refs):
-    w_refs, (keys_ref, mean_ref), bufs, sem = refs[:blocks], refs[blocks : blocks + 2], refs[blocks + 2 : -1], refs[-1]
+def keys_kernel(tok_ref, gain_ref, cot_ref, inv_ref, *refs):
+    w_refs, (keys_ref, mean_ref) = refs[:-2], refs[-2:]
     width = tok_ref.shape[1]
     inv = widened(inv_ref, width // (ZL * Y * C))
     keys = jnp.zeros(keys_ref.shape, F32)
-    for cols, weights in places(width, w_refs, bufs, sem):
+    for cols, weights in places(width, w_refs):
         normed = tok_ref[:, cols].astype(F32) * inv
         hidden = (normed * gain_ref[:, cols]).astype(BF16)
         keys = keys + jnp.dot(hidden, weights, preferred_element_type=F32)
@@ -151,13 +155,13 @@
     mean_ref[...] = jnp.broadcast_to(mean, mean_ref.shape)
 
 
-def token_grad_kernel(blocks, tok_ref, gain_ref, cot_ref, inv_ref, mean_ref, *refs):
-    w_refs, tg_ref, bufs, sem = refs[:blocks], refs[blocks], refs[blocks + 1 : -1], refs[-1]
+def token_grad_kernel(tok_ref, gain_ref, cot_ref, inv_ref, mean_ref, *refs):
+    w_refs, tg_ref = refs[:-1], refs[-1]
     width = tok_ref.shape[1]
     inv = widened(inv_ref, width // (ZL * Y * C))
     mean = widened(mean_ref, width // (ZL * Y * C))
     cot = cot_ref[...]
-    for cols, weights in places(width, w_refs, bufs, sem):
+    for cols, weights in places(width, w_refs):
         hidden_grad = lax.dot_general(cot, weights, (((1,), (1,)), ((), ())), preferred_element_type=F32)
         normed = tok_ref[:, cols].astype(F32) * inv
         tg_ref[:, cols] = (inv * (hidden_grad * gain_ref[:, cols] - normed * mean)).astype(BF16)
@@ -267,13 +271,13 @@
     by_rows = lambda cols: pl.BlockSpec((step, cols), lambda i: (i, 0))
     send, inv = pl.pallas_call(
         norm_kernel,
-        out_shape=(shape((X, tok_rows, part + keys_w), BF16), shape((tok_rows, 128), F32)),
+        out_shape=(pltpu.HBM((X, tok_rows, part + keys_w), BF16), pltpu.HBM((tok_rows, 128), F32)),
         grid=(tok_rows // step,),
         in_specs=[by_rows(width), pl.BlockSpec((1, width), lambda i: (0, 0)), by_rows(keys_w)],
         out_specs=(pl.BlockSpec((X, step, part + keys_w), lambda i: (0, i, 0)), by_rows(128)),
         cost_estimate=pl.CostEstimate(flops=tok_rows * width * 6, bytes_accessed=5 << 20, transcendentals=0),
-        compiler_params=pltpu.CompilerParams(vmem_limit_bytes=56 << 20),
-    )(tokens, gain, key_cotangent)
+        compiler_params=pltpu.CompilerParams(vmem_limit_bytes=24 << 20),
+    )(*in_hbm(tokens, gain, key_cotangent))
     recv = mixed(send, True).reshape(X * tok_rows, part + keys_w)
     from_up = second_step(column, lambda place, on_z: -1)
     from_down = second_step(column, lambda place, on_z: 1)
@@ -286,7 +290,7 @@
         0,
         1 << 20,
         1,
-        40 << 20,
+        24 << 20,
         HBM,
         (pltpu.VMEM((ZL, Y, ZH * C * ROWS, keys_w), BF16), pltpu.SemaphoreType.DMA((ZL,))),
     )(recv)
@@ -320,42 +324,35 @@
     for block in far:
         weights += [block, lax.ppermute(block, "c", ring(C, 1))]
     blocks = lax.all_to_all(summed.reshape(ZL * ZH, ROWS, keys_w), ("zl", "zh"), 0, 0, tiled=True)
-    count = len(weights)
-    scratch = [pltpu.VMEM(block.shape, BF16) for block in weights] + [pltpu.SemaphoreType.DMA((count,))]
     keys, mean = kernel_call(
-        functools.partial(keys_kernel, count),
-        (shape((tok_rows, keys_w), BF16), shape((tok_rows, 128), F32)),
+        keys_kernel,
+        (pltpu.HBM((tok_rows, keys_w), BF16), pltpu.HBM((tok_rows, 128), F32)),
         2 * tok_rows * width * keys_w,
-        11 << 20,
-        [VMEM] * 4 + [HBM] * count,
-        60 << 20,
-        scratch=scratch,
-    )(tokens, gain, key_cotangent, inv, *weights)
+        3 << 20,
+        4 + len(weights),
+    )(*in_hbm(tokens, gain, key_cotangent, inv), *in_vmem(*weights))
     blocks, keys, mean = lax.optimization_barrier((blocks, keys, mean))
     new_master, new_first, new_second, new_rows = kernel_call(
         functools.partial(adam_kernel, tok_rows * math.prod(SIZES)),
         (
-            shape(master.shape, F32),
-            shape(moment_first.shape, F32),
-            shape(moment_second.shape, F32),
-            shape((X * ZH, *master.shape), BF16),
+            pltpu.HBM(master.shape, F32),
+            pltpu.HBM(moment_first.shape, F32),
+            pltpu.HBM(moment_second.shape, F32),
+            pltpu.HBM((X * ZH, *master.shape), BF16),
         ),
         1 << 25,
         1 << 20,
         5,
-        60 << 20,
-    )(blocks, moment_first, moment_second, master, signs.reshape(1, -1))
+    )(blocks, *in_hbm(moment_first, moment_second, master, signs.reshape(1, -1)))
 
     mine = lax.all_to_all(new_rows, ("x", "zh"), 0, 0, tiled=True)
     token_grad = kernel_call(
-        functools.partial(token_grad_kernel, count),
-        shape(tokens.shape, BF16),
+        token_grad_kernel,
+        pltpu.HBM(tokens.shape, BF16),
         2 * tok_rows * width * keys_w,
-        13 << 20,
-        [VMEM] * 5 + [HBM] * count,
-        60 << 20,
-        scratch=scratch,
-    )(tokens, gain, key_cotangent, inv, mean, *weights)
+        5 << 20,
+        5 + len(weights),
+    )(*in_hbm(tokens, gain, key_cotangent, inv, mean), *in_vmem(*weights))
     mine, token_grad = lax.optimization_barrier((mine, token_grad))
     other = lax.ppermute(mine, "c", ring(C, 1))
     even = jnp.where(c == 0, mine, other)

time: 105 us -> 104 us (level)
  local copies, waits for them, and re-layouts: 2.52 us -> 0.86 us
    unnamed x8 -> x2, local copies, waits for them, and re-layouts: 1.67 us -> 0.01 us
    all_to_all x1, waiting for transfers between devices: 3.69 us -> 5.03 us  [shards(): lax.all_to_all(summed.reshape(ZL * ZH, ROWS, keys_w), ('zl', 'zh'), 0, 0,...]
where the time goes in v10:
time: 104 us; the launch traced here: 103 us
  waiting for transfers between devices  40 us (38%)
  starting transfers between devices  35.7 us (34%)
  Pallas kernels  23.7 us (23%)
  other arithmetic  1.92 us (2%)
    ppermute x4, waiting for transfers between devices, second_step(): return lax.ppermute(value, GATHER, moved(lambda c: c == 0, shift))  11.5 us
    all_to_all x2, waiting for transfers between devices, mixed(): lax.all_to_all(value, ('y', 'x', 'c'), 0, 0, axis_index_groups=groups, ti...  9.73 us
    all_to_all x2, starting transfers between devices, mixed(): lax.all_to_all(value, ('y', 'x', 'c'), 0, 0, axis_index_groups=groups, ti...  8.21 us
    pallas_call x1, Pallas kernels, shards(): kernel_call(token_grad_kernel, pltpu.HBM(tokens.shape, BF16), 2 * tok_row...  7.9 us
    all_to_all x1, starting transfers between devices, shards(): lax.all_to_all(summed.reshape(ZL * ZH, ROWS, keys_w), ('zl', 'zh'), 0, 0,...  7.71 us
    ppermute x3, waiting for transfers between devices, first_step(): return lax.ppermute(value, GATHER, moved(lambda c: c == 1, shift))  7.49 us
    pallas_call x1, Pallas kernels, shards(): kernel_call(keys_kernel, (pltpu.HBM((tok_rows, keys_w), BF16), pltpu.HBM(...  5.65 us
    ppermute x4, starting transfers between devices, second_step(): return lax.ppermute(value, GATHER, moved(lambda c: c == 0, shift))  5.32 us
  transfers between devices with their start and end apart: 18, of which 13 were waited for; matrix products, arithmetic and copies ran while one was open for 2% of the time, Pallas kernels for 18%

profile of v10, /device:TPU:33, one launch (start us, length us, event | category | flops | bytes accessed | tf_op | source)
XLA Modules:
  0.0 103.0 jit_solution(3842896408600859081)
XLA Ops:
  0.6 0.0 copy-start
  0.6 3.5 %shard_map.127 = (bf16[4,128,2560]{2,1,0:T(8,128)(2,1)}, f32[128,128]{1,0:T(8,128)}) custom-call(bf16[128,8192]{1,0:T(8,128)(2,1)} %tok_ref.5, f32[1,8192]{1,0:T(1,128)} %bitcast.11, bf16[128,512]{1,0:T(8,128)(2,1)} %cot_ref.5), custom_call_target="tpu_custom_call" | custom-call | flops 6291456 | bytes 5242880 | tf_op jit(solution)/shard_map/pallas_call | solution.py:272
  4.2 4.2 %all-to-all-start = ((bf16[4,128,2560]{2,1,0:T(8,128)(2,1)}), bf16[4,128,2560]{2,1,0:T(8,128)(2,1)S(1)}, u32[]{:S(2)}, u32[]{:S(2)}) async-start(bf16[4,128,2560]{2,1,0:T(8,128)(2,1)} %get-tuple-element.33), calls=%async_computation | async-start | bytes 5242880 | tf_op jit(solution)/shard_map/all_to_all | solution.py:256
  8.4 0.0 copy-done
  8.4 1.7 %collective-permute-start.2 = (bf16[256,512]{1,0:T(8,128)(2,1)S(1)}, bf16[256,512]{1,0:T(8,128)(2,1)S(1)}, u32[]{:S(2)}, u32[]{:S(2)}) collective-permute-start(bf16[256,512]{1,0:T(8,128)(2,1)S(1)} %constant_dynamic-slice_fusion), channel_id=1, source_target_pairs={{0,16},{1,65},{2,18},{3,67},{16,32},{17,81},{18,34},{19,83},{32,48... | collective-permute-start | bytes 786440 | tf_op jit(solution)/shard_map/ppermute | solution.py:243
  10.1 3.6 %collective-permute-start.1 = (bf16[256,512]{1,0:T(8,128)(2,1)S(1)}, bf16[256,512]{1,0:T(8,128)(2,1)S(1)}, u32[]{:S(2)}, u32[]{:S(2)}) collective-permute-start(bf16[256,512]{1,0:T(8,128)(2,1)S(1)} %constant_dynamic-slice_fusion), channel_id=1, source_target_pairs={{0,32},{1,129},{2,34},{3,131},{16,48},{17,145},{18,50},{19,147},{3... | collective-permute-start | bytes 786440 | tf_op jit(solution)/shard_map/ppermute | solution.py:243
  13.7 0.0 collective-permute-start
  13.7 0.3 collective-permute-done.2
  14.0 4.4 %collective-permute-done.1 = bf16[256,512]{1,0:T(8,128)(2,1)S(1)} collective-permute-done((bf16[256,512]{1,0:T(8,128)(2,1)S(1)}, bf16[256,512]{1,0:T(8,128)(2,1)S(1)}, u32[]{:S(2)}, u32[]{:S(2)}) %collective-permute-start.1) | collective-permute-done | bytes 262176 | tf_op jit(solution)/shard_map/ppermute | solution.py:243
  18.4 2.8 %collective-permute-done = bf16[256,512]{1,0:T(8,128)(2,1)S(1)} collective-permute-done((bf16[256,512]{1,0:T(8,128)(2,1)S(1)}, bf16[256,512]{1,0:T(8,128)(2,1)S(1)}, u32[]{:S(2)}, u32[]{:S(2)}) %collective-permute-start) | collective-permute-done | bytes 262176 | tf_op jit(solution)/shard_map/ppermute | solution.py:243
  21.2 1.0 %pad_maximum_fusion.refs_0_ = bf16[1024,512]{1,0:T(8,128)(2,1)} fusion(bf16[256,512]{1,0:T(8,128)(2,1)S(1)} %collective-permute-done.2, bf16[256,512]{1,0:T(8,128)(2,1)S(1)} %collective-permute-done.1, bf16[256,512]{1,0:T(8,128)(2,1)S(1)} %collective-permute-done, bf16[256,512]{1,0:T(8,128)(2,1)S(1)} %constant_dynamic-slice_fusion), kind=kLoop, calls=%fused_computation | loop fusion | flops 4194304 | bytes 2097152 | tf_op jit(solution)/shard_map/concatenate | solution.py:267
  22.2 2.7 %collective-permute-start.4 = (bf16[1024,512]{1,0:T(8,128)(2,1)}, bf16[1024,512]{1,0:T(8,128)(2,1)}, u32[]{:S(2)}, u32[]{:S(2)}) collective-permute-start(bf16[1024,512]{1,0:T(8,128)(2,1)} %pad_maximum_fusion.refs_0_), channel_id=1, source_target_pairs={{0,194},{1,49},{2,192},{3,51},{16,210},{17,1},{18,208},{19,3},{32,... | collective-permute-start | bytes 3145736 | tf_op jit(solution)/shard_map/ppermute | solution.py:247
  24.9 0.0 collective-permute-start.6
  24.9 7.4 %all-to-all-done = bf16[4,128,2560]{2,1,0:T(8,128)(2,1)S(1)} async-done(((bf16[4,128,2560]{2,1,0:T(8,128)(2,1)}), bf16[4,128,2560]{2,1,0:T(8,128)(2,1)S(1)}, u32[]{:S(2)}, u32[]{:S(2)}) %all-to-all-start) | async-done | bytes 2621472 | tf_op jit(solution)/shard_map/all_to_all | solution.py:256
  32.3 2.1 %shard_map.128 = bf16[4,512,512]{2,1,0:T(8,128)(2,1)} custom-call(bf16[512,2560]{1,0:T(8,128)(2,1)S(1)} %bitcast.9), custom_call_target="tpu_custom_call" | custom-call | bytes 1048576 | tf_op jit(solution)/shard_map/pallas_call | solution.py:287
  34.4 4.0 %all-to-all-start.1 = ((bf16[4,512,512]{2,1,0:T(8,128)(2,1)}), bf16[4,512,512]{2,1,0:T(8,128)(2,1)S(1)}, u32[]{:S(2)}, u32[]{:S(2)}) async-start(bf16[4,512,512]{2,1,0:T(8,128)(2,1)} %shard_map.128), calls=%async_computation.1 | async-start | bytes 4194304 | tf_op jit(solution)/shard_map/all_to_all | solution.py:256
  38.4 0.0 collective-permute-start.3
  38.4 7.2 %collective-permute-done.4.up_ref.refs_2_ = bf16[1024,512]{1,0:T(8,128)(2,1)} collective-permute-done((bf16[1024,512]{1,0:T(8,128)(2,1)}, bf16[1024,512]{1,0:T(8,128)(2,1)}, u32[]{:S(2)}, u32[]{:S(2)}) %collective-permute-start.4) | collective-permute-done | bytes 1048608 | tf_op jit(solution)/shard_map/ppermute | solution.py:247
  45.6 0.0 collective-permute-start.5
  45.6 1.3 %collective-permute-done.6.down_ref.refs_4_ = bf16[1024,512]{1,0:T(8,128)(2,1)} collective-permute-done((bf16[1024,512]{1,0:T(8,128)(2,1)}, bf16[1024,512]{1,0:T(8,128)(2,1)}, u32[]{:S(2)}, u32[]{:S(2)}) %collective-permute-start.6) | collective-permute-done | bytes 1048608 | tf_op jit(solution)/shard_map/ppermute | solution.py:247
  46.8 0.0 collective-permute-start.7
  46.9 2.2 %shard_map.130 = (bf16[512,512]{1,0:T(8,128)(2,1)}, bf16[512,512]{1,0:T(8,128)(2,1)}) custom-call(bf16[1024,512]{1,0:T(8,128)(2,1)} %collective-permute-done.4.up_ref.refs_2_, bf16[1024,512]{1,0:T(8,128)(2,1)} %collective-permute-done.6.down_ref.refs_4_), custom_call_target="tpu_custom_call" | custom-call | bytes 1048576 | tf_op jit(solution)/shard_map/pallas_call | solution.py:307
  49.1 2.6 %collective-permute-start.9 = (bf16[512,512]{1,0:T(8,128)(2,1)}, bf16[512,512]{1,0:T(8,128)(2,1)S(1)}, u32[]{:S(2)}, u32[]{:S(2)}) collective-permute-start(bf16[512,512]{1,0:T(8,128)(2,1)} %get-tuple-element.37), channel_id=1, source_target_pairs={{0,194},{1,49},{2,192},{3,51},{16,210},{17,1},{18,208},{19,3},{32,... | collective-permute-start | bytes 1572872 | tf_op jit(solution)/shard_map/ppermute | solution.py:247
  51.7 0.0 collective-permute-start.10
  51.7 2.4 %all-to-all-done.1.recv_ref = bf16[4,512,512]{2,1,0:T(8,128)(2,1)S(1)} async-done(((bf16[4,512,512]{2,1,0:T(8,128)(2,1)}), bf16[4,512,512]{2,1,0:T(8,128)(2,1)S(1)}, u32[]{:S(2)}, u32[]{:S(2)}) %all-to-all-start.1) | async-done | bytes 2097184 | tf_op jit(solution)/shard_map/all_to_all | solution.py:256
  54.1 0.2 shard_map.129
  54.3 0.0 collective-permute-done.3.refs_1_
  54.3 0.0 collective-permute-done.5.refs_3_
  54.3 0.0 collective-permute-done.7.refs_5_
  54.3 1.8 %collective-permute-start.8 = (bf16[256,512]{1,0:T(8,128)(2,1)S(1)}, bf16[256,512]{1,0:T(8,128)(2,1)S(1)}, u32[]{:S(2)}, u32[]{:S(2)}) collective-permute-start(bf16[256,512]{1,0:T(8,128)(2,1)S(1)} %get-tuple-element.36), channel_id=1, source_target_pairs={{0,1},{1,0},{2,3},{3,2},{4,5},{5,4},{6,7},{7,6},{8,9},{9,8},{10,11... | collective-permute-start | bytes 786440 | tf_op jit(solution)/shard_map/ppermute | solution.py:321
  56.2 1.2 %collective-permute-done.8 = bf16[256,512]{1,0:T(8,128)(2,1)S(1)} collective-permute-done((bf16[256,512]{1,0:T(8,128)(2,1)S(1)}, bf16[256,512]{1,0:T(8,128)(2,1)S(1)}, u32[]{:S(2)}, u32[]{:S(2)}) %collective-permute-start.8) | collective-permute-done | bytes 262176 | tf_op jit(solution)/shard_map/ppermute | solution.py:321
  57.4 0.8 add_convert_fusion
  58.1 1.0 %collective-permute-done.9.refs_6_ = bf16[512,512]{1,0:T(8,128)(2,1)S(1)} collective-permute-done((bf16[512,512]{1,0:T(8,128)(2,1)}, bf16[512,512]{1,0:T(8,128)(2,1)S(1)}, u32[]{:S(2)}, u32[]{:S(2)}) %collective-permute-start.9) | collective-permute-done | bytes 524320 | tf_op jit(solution)/shard_map/ppermute | solution.py:247
  59.2 2.1 %collective-permute-done.10.refs_8_ = bf16[512,512]{1,0:T(8,128)(2,1)} collective-permute-done((bf16[512,512]{1,0:T(8,128)(2,1)}, bf16[512,512]{1,0:T(8,128)(2,1)}, u32[]{:S(2)}, u32[]{:S(2)}) %collective-permute-start.10) | collective-permute-done | bytes 524320 | tf_op jit(solution)/shard_map/ppermute | solution.py:247
  61.2 0.6 collective-permute-start.11
  61.9 0.0 collective-permute-start.12
  61.9 7.7 %all-to-all-start.2 = ((bf16[8,32,512]{2,1,0:T(8,128)(2,1)}), bf16[8,32,512]{2,1,0:T(8,128)(2,1)S(1)}, u32[]{:S(2)}, u32[]{:S(2)}) async-start(bf16[8,32,512]{2,1,0:T(8,128)(2,1)} %bitcast.2), calls=%async_computation.2 | async-start | bytes 524288 | tf_op jit(solution)/shard_map/all_to_all | solution.py:326
  69.6 0.0 collective-permute-done.11.refs_7_
  69.6 0.0 collective-permute-done.12.refs_9_
  69.6 5.7 %shard_map.131 = (bf16[128,512]{1,0:T(8,128)(2,1)}, f32[128,128]{1,0:T(8,128)}) custom-call(bf16[128,8192]{1,0:T(8,128)(2,1)} %tok_ref.5, f32[1,8192]{1,0:T(1,128)} %bitcast.12, bf16[128,512]{1,0:T(8,128)(2,1)} %cot_ref.5, f32[128,128]{1,0:T(8,128)} %get-tuple-element.40.inv_ref, bf16[1024,512]{1,0:T(8,128)(2,1)} %pad_maximum_fusion.refs_0_, ...), custom_call_target="tpu_custom_call" | custom-call | flops 1073741824 | bytes 3145728 | tf_op jit(solution)/shard_map/pallas_call | solution.py:327
  75.2 5.0 %all-to-all-done.2.recv_ref = bf16[8,32,512]{2,1,0:T(8,128)(2,1)S(1)} async-done(((bf16[8,32,512]{2,1,0:T(8,128)(2,1)}), bf16[8,32,512]{2,1,0:T(8,128)(2,1)S(1)}, u32[]{:S(2)}, u32[]{:S(2)}) %all-to-all-start.2) | async-done | bytes 262176 | tf_op jit(solution)/shard_map/all_to_all | solution.py:326
  80.3 2.1 %shard_map.132 = (f32[32,512]{1,0:T(8,128)}, f32[16,1024]{1,0:T(8,128)}, f32[16,1024]{1,0:T(8,128)}, bf16[8,32,512]{2,1,0:T(8,128)(2,1)}) custom-call(bf16[8,32,512]{2,1,0:T(8,128)(2,1)S(1)} %all-to-all-done.2.recv_ref, f32[16,1024]{1,0:T(8,128)} %first_ref.1, f32[16,1024]{1,0:T(8,128)} %second_ref.1, f32[32,512]{1,0:T(8,128)} %master_ref.1, s32[1,1024]{1,0:T(1,128)} %bitcast.14), custom_call_target="tpu_custom_call" | custom-call | flops 33554432 | bytes 1048576 | tf_op jit(solution)/shard_map/pallas_call | solution.py:335
  82.4 4.7 %all-to-all-start.3 = ((bf16[8,32,512]{2,1,0:T(8,128)(2,1)}), bf16[8,32,512]{2,1,0:T(8,128)(2,1)S(1)}, u32[]{:S(2)}, u32[]{:S(2)}) async-start(bf16[8,32,512]{2,1,0:T(8,128)(2,1)} %get-tuple-element.53), calls=%async_computation.3 | async-start | bytes 524288 | tf_op jit(solution)/shard_map/all_to_all | solution.py:348
  87.1 7.9 %shard_map.133 = bf16[128,8192]{1,0:T(8,128)(2,1)} custom-call(bf16[128,8192]{1,0:T(8,128)(2,1)} %tok_ref.5, f32[1,8192]{1,0:T(1,128)} %bitcast.13, bf16[128,512]{1,0:T(8,128)(2,1)} %cot_ref.5, f32[128,128]{1,0:T(8,128)} %get-tuple-element.40.inv_ref, f32[128,128]{1,0:T(8,128)} %get-tuple-element.54.mean_ref, bf16[1024,512]{1,0:T(8,128)(2,1)} %pad_maximum_fusion.refs_0_, ...), custom_call_target="tpu_custom_call" | custom-call | flops 1073741824 | bytes 5242880 | tf_op jit(solution)/shard_map/pallas_call | solution.py:349
  95.0 3.8 %all-to-all-done.3 = bf16[8,32,512]{2,1,0:T(8,128)(2,1)S(1)} async-done(((bf16[8,32,512]{2,1,0:T(8,128)(2,1)}), bf16[8,32,512]{2,1,0:T(8,128)(2,1)S(1)}, u32[]{:S(2)}, u32[]{:S(2)}) %all-to-all-start.3) | async-done | bytes 262176 | tf_op jit(solution)/shard_map/all_to_all | solution.py:348
  98.8 2.0 %collective-permute-start.13 = (bf16[8,32,512]{2,1,0:T(8,128)(2,1)S(1)}, bf16[8,32,512]{2,1,0:T(8,128)(2,1)S(1)}, u32[]{:S(2)}, u32[]{:S(2)}) collective-permute-start(bf16[8,32,512]{2,1,0:T(8,128)(2,1)S(1)} %all-to-all-done.3), channel_id=1, source_target_pairs={{0,1},{1,0},{2,3},{3,2},{4,5},{5,4},{6,7},{7,6},{8,9},{9,8},{10,11... | collective-permute-start | bytes 786440 | tf_op jit(solution)/shard_map/ppermute | solution.py:357
  100.9 1.2 %collective-permute-done.13 = bf16[8,32,512]{2,1,0:T(8,128)(2,1)S(1)} collective-permute-done((bf16[8,32,512]{2,1,0:T(8,128)(2,1)S(1)}, bf16[8,32,512]{2,1,0:T(8,128)(2,1)S(1)}, u32[]{:S(2)}, u32[]{:S(2)}) %collective-permute-start.13) | collective-permute-done | bytes 262176 | tf_op jit(solution)/shard_map/ppermute | solution.py:357
  102.1 0.1 pad_maximum_fusion.1
  102.1 0.8 copy.14
  (2 shorter events, 0.1 us)
Async XLA Ops:
  0.6 7.7 %copy-start = (bf16[512,512]{1,0:T(8,128)(2,1)S(1)}, bf16[512,512]{1,0:T(8,128)(2,1)}, u32[]{:S(2)}) copy-start(bf16[512,512]{1,0:T(8,128)(2,1)} %param.11) | copy-start | bytes 1572868
  4.2 28.1 %all-to-all-start = ((bf16[4,128,2560]{2,1,0:T(8,128)(2,1)}), bf16[4,128,2560]{2,1,0:T(8,128)(2,1)S(1)}, u32[]{:S(2)}, u32[]{:S(2)}) async-start(bf16[4,128,2560]{2,1,0:T(8,128)(2,1)} %get-tuple-element.33), calls=%async_computation | async-start | bytes 5242880 | tf_op jit(solution)/shard_map/all_to_all | solution.py:256
  8.4 5.6 %collective-permute-start.2 = (bf16[256,512]{1,0:T(8,128)(2,1)S(1)}, bf16[256,512]{1,0:T(8,128)(2,1)S(1)}, u32[]{:S(2)}, u32[]{:S(2)}) collective-permute-start(bf16[256,512]{1,0:T(8,128)(2,1)S(1)} %constant_dynamic-slice_fusion), channel_id=1, source_target_pairs={{0,16},{1,65},{2,18},{3,67},{16,32},{17,81},{18,34},{19,83},{32,48... | collective-permute-start | bytes 786440 | tf_op jit(solution)/shard_map/ppermute | solution.py:243
  10.1 8.3 %collective-permute-start.1 = (bf16[256,512]{1,0:T(8,128)(2,1)S(1)}, bf16[256,512]{1,0:T(8,128)(2,1)S(1)}, u32[]{:S(2)}, u32[]{:S(2)}) collective-permute-start(bf16[256,512]{1,0:T(8,128)(2,1)S(1)} %constant_dynamic-slice_fusion), channel_id=1, source_target_pairs={{0,32},{1,129},{2,34},{3,131},{16,48},{17,145},{18,50},{19,147},{3... | collective-permute-start | bytes 786440 | tf_op jit(solution)/shard_map/ppermute | solution.py:243
  13.7 7.5 %collective-permute-start = (bf16[256,512]{1,0:T(8,128)(2,1)S(1)}, bf16[256,512]{1,0:T(8,128)(2,1)S(1)}, u32[]{:S(2)}, u32[]{:S(2)}) collective-permute-start(bf16[256,512]{1,0:T(8,128)(2,1)S(1)} %constant_dynamic-slice_fusion), channel_id=1, source_target_pairs={{0,48},{1,195},{2,50},{3,193},{16,0},{17,211},{18,2},{19,209},{32,... | collective-permute-start | bytes 786440 | tf_op jit(solution)/shard_map/ppermute | solution.py:243
  22.2 23.4 %collective-permute-start.4 = (bf16[1024,512]{1,0:T(8,128)(2,1)}, bf16[1024,512]{1,0:T(8,128)(2,1)}, u32[]{:S(2)}, u32[]{:S(2)}) collective-permute-start(bf16[1024,512]{1,0:T(8,128)(2,1)} %pad_maximum_fusion.refs_0_), channel_id=1, source_target_pairs={{0,194},{1,49},{2,192},{3,51},{16,210},{17,1},{18,208},{19,3},{32,... | collective-permute-start | bytes 3145736 | tf_op jit(solution)/shard_map/ppermute | solution.py:247
  24.9 22.0 %collective-permute-start.6 = (bf16[1024,512]{1,0:T(8,128)(2,1)}, bf16[1024,512]{1,0:T(8,128)(2,1)}, u32[]{:S(2)}, u32[]{:S(2)}) collective-permute-start(bf16[1024,512]{1,0:T(8,128)(2,1)} %pad_maximum_fusion.refs_0_), channel_id=1, source_target_pairs={{0,64},{1,17},{2,66},{3,19},{16,80},{17,33},{18,82},{19,35},{32,96... | collective-permute-start | bytes 3145736 | tf_op jit(solution)/shard_map/ppermute | solution.py:247
  34.4 19.7 %all-to-all-start.1 = ((bf16[4,512,512]{2,1,0:T(8,128)(2,1)}), bf16[4,512,512]{2,1,0:T(8,128)(2,1)S(1)}, u32[]{:S(2)}, u32[]{:S(2)}) async-start(bf16[4,512,512]{2,1,0:T(8,128)(2,1)} %shard_map.128), calls=%async_computation.1 | async-start | bytes 4194304 | tf_op jit(solution)/shard_map/all_to_all | solution.py:256
  38.4 15.9 %collective-permute-start.3 = (bf16[1024,512]{1,0:T(8,128)(2,1)}, bf16[1024,512]{1,0:T(8,128)(2,1)}, u32[]{:S(2)}, u32[]{:S(2)}) collective-permute-start(bf16[1024,512]{1,0:T(8,128)(2,1)} %pad_maximum_fusion.refs_0_), channel_id=1, source_target_pairs={{0,1},{1,0},{2,3},{3,2},{4,5},{5,4},{6,7},{7,6},{8,9},{9,8},{10,11... | collective-permute-start | bytes 3145736 | tf_op jit(solution)/shard_map/ppermute | solution.py:286
  45.6 8.7 %collective-permute-start.5 = (bf16[1024,512]{1,0:T(8,128)(2,1)}, bf16[1024,512]{1,0:T(8,128)(2,1)}, u32[]{:S(2)}, u32[]{:S(2)}) collective-permute-start(bf16[1024,512]{1,0:T(8,128)(2,1)} %collective-permute-done.4.up_ref.refs_2_), channel_id=1, source_target_pairs={{0,1},{1,0},{2,3},{3,2},{4,5},{5,4},{6,7},{7,6},{8,9},{9,8},{10,11... | collective-permute-start | bytes 3145736 | tf_op jit(solution)/shard_map/ppermute | solution.py:286
  46.8 7.5 %collective-permute-start.7 = (bf16[1024,512]{1,0:T(8,128)(2,1)}, bf16[1024,512]{1,0:T(8,128)(2,1)}, u32[]{:S(2)}, u32[]{:S(2)}) collective-permute-start(bf16[1024,512]{1,0:T(8,128)(2,1)} %collective-permute-done.6.down_ref.refs_4_), channel_id=1, source_target_pairs={{0,1},{1,0},{2,3},{3,2},{4,5},{5,4},{6,7},{7,6},{8,9},{9,8},{10,11... | collective-permute-start | bytes 3145736 | tf_op jit(solution)/shard_map/ppermute | solution.py:286
  49.1 10.1 %collective-permute-start.9 = (bf16[512,512]{1,0:T(8,128)(2,1)}, bf16[512,512]{1,0:T(8,128)(2,1)S(1)}, u32[]{:S(2)}, u32[]{:S(2)}) collective-permute-start(bf16[512,512]{1,0:T(8,128)(2,1)} %get-tuple-element.37), channel_id=1, source_target_pairs={{0,194},{1,49},{2,192},{3,51},{16,210},{17,1},{18,208},{19,3},{32,... | collective-permute-start | bytes 1572872 | tf_op jit(solution)/shard_map/ppermute | solution.py:247
  51.7 9.6 %collective-permute-start.10 = (bf16[512,512]{1,0:T(8,128)(2,1)}, bf16[512,512]{1,0:T(8,128)(2,1)}, u32[]{:S(2)}, u32[]{:S(2)}) collective-permute-start(bf16[512,512]{1,0:T(8,128)(2,1)} %get-tuple-element.38), channel_id=1, source_target_pairs={{0,64},{1,17},{2,66},{3,19},{16,80},{17,33},{18,82},{19,35},{32,96... | collective-permute-start | bytes 1572872 | tf_op jit(solution)/shard_map/ppermute | solution.py:247
  54.3 3.0 %collective-permute-start.8 = (bf16[256,512]{1,0:T(8,128)(2,1)S(1)}, bf16[256,512]{1,0:T(8,128)(2,1)S(1)}, u32[]{:S(2)}, u32[]{:S(2)}) collective-permute-start(bf16[256,512]{1,0:T(8,128)(2,1)S(1)} %get-tuple-element.36), channel_id=1, source_target_pairs={{0,1},{1,0},{2,3},{3,2},{4,5},{5,4},{6,7},{7,6},{8,9},{9,8},{10,11... | collective-permute-start | bytes 786440 | tf_op jit(solution)/shard_map/ppermute | solution.py:321
  61.2 8.3 %collective-permute-start.11 = (bf16[512,512]{1,0:T(8,128)(2,1)S(1)}, bf16[512,512]{1,0:T(8,128)(2,1)S(1)}, u32[]{:S(2)}, u32[]{:S(2)}) collective-permute-start(bf16[512,512]{1,0:T(8,128)(2,1)S(1)} %collective-permute-done.9.refs_6_), channel_id=1, source_target_pairs={{0,1},{1,0},{2,3},{3,2},{4,5},{5,4},{6,7},{7,6},{8,9},{9,8},{10,11... | collective-permute-start | bytes 1572872 | tf_op jit(solution)/shard_map/ppermute | solution.py:325
  61.9 7.7 %collective-permute-start.12 = (bf16[512,512]{1,0:T(8,128)(2,1)}, bf16[512,512]{1,0:T(8,128)(2,1)S(1)}, u32[]{:S(2)}, u32[]{:S(2)}) collective-permute-start(bf16[512,512]{1,0:T(8,128)(2,1)} %collective-permute-done.10.refs_8_), channel_id=1, source_target_pairs={{0,1},{1,0},{2,3},{3,2},{4,5},{5,4},{6,7},{7,6},{8,9},{9,8},{10,11... | collective-permute-start | bytes 1572872 | tf_op jit(solution)/shard_map/ppermute | solution.py:325
  61.9 18.4 %all-to-all-start.2 = ((bf16[8,32,512]{2,1,0:T(8,128)(2,1)}), bf16[8,32,512]{2,1,0:T(8,128)(2,1)S(1)}, u32[]{:S(2)}, u32[]{:S(2)}) async-start(bf16[8,32,512]{2,1,0:T(8,128)(2,1)} %bitcast.2), calls=%async_computation.2 | async-start | bytes 524288 | tf_op jit(solution)/shard_map/all_to_all | solution.py:326
  82.4 16.5 %all-to-all-start.3 = ((bf16[8,32,512]{2,1,0:T(8,128)(2,1)}), bf16[8,32,512]{2,1,0:T(8,128)(2,1)S(1)}, u32[]{:S(2)}, u32[]{:S(2)}) async-start(bf16[8,32,512]{2,1,0:T(8,128)(2,1)} %get-tuple-element.53), calls=%async_computation.3 | async-start | bytes 524288 | tf_op jit(solution)/shard_map/all_to_all | solution.py:348
  98.8 3.2 %collective-permute-start.13 = (bf16[8,32,512]{2,1,0:T(8,128)(2,1)S(1)}, bf16[8,32,512]{2,1,0:T(8,128)(2,1)S(1)}, u32[]{:S(2)}, u32[]{:S(2)}) collective-permute-start(bf16[8,32,512]{2,1,0:T(8,128)(2,1)S(1)} %all-to-all-done.3), channel_id=1, source_target_pairs={{0,1},{1,0},{2,3},{3,2},{4,5},{5,4},{6,7},{7,6},{8,9},{9,8},{10,11... | collective-permute-start | bytes 786440 | tf_op jit(solution)/shard_map/ppermute | solution.py:357

commit v11 on v10

--- a/solution.py
+++ b/solution.py
@@ -238,8 +238,7 @@
     return pairs
 
 
-def first_step(value, k):
-    shift = lambda place, on_z: {1: -1, 2: 2 - 4 * (place % 2) if on_z else -2, 3: 1}[k]
+def first_step(value, shift):
     return lax.ppermute(value, GATHER, moved(lambda c: c == 1, shift))
 
 
@@ -264,7 +263,11 @@
     node_rows = secondary.shape[0]
 
     half = lax.dynamic_slice_in_dim(secondary, c * (node_rows // 2), node_rows // 2, 0)
-    column = jnp.concatenate([half] + [first_step(half, k) for k in range(1, Y)], axis=0)
+    up = first_step(half, lambda place, on_z: -1)
+    down = first_step(half, lambda place, on_z: 1)
+    odd = jnp.where(c == 0, lax.axis_index("y"), lax.axis_index("zl")) % 2 == 1
+    far = first_step(jnp.where(odd, up, down), lambda place, on_z: 1 - 2 * (place % 2))
+    column = jnp.concatenate([half, up, far, down], axis=0)
 
     part = width // X
     step = 64

time: 104 us -> 108 us (1.038)
  starting transfers between devices: 35.7 us -> 43.4 us
  waiting for transfers between devices: 40 us -> 34.5 us
  other arithmetic: 1.92 us -> 3.95 us
    ppermute x5, starting transfers between devices: 0.63 us -> 12.6 us  [shards(): weights += [block, lax.ppermute(block, 'c', ring(C, 1))]]
    all_to_all x2, waiting for transfers between devices: 9.73 us -> 4.33 us  [mixed(): lax.all_to_all(value, ('y', 'x', 'c'), 0, 0, axis_index_groups=groups, ti...]
    ppermute x4, waiting for transfers between devices: 11.5 us -> 7.73 us  [second_step(): return lax.ppermute(value, GATHER, moved(lambda c: c == 0, shift))]
    ppermute x3, waiting for transfers between devices: 7.49 us -> 9.85 us  [first_step(): return lax.ppermute(value, GATHER, moved(lambda c: c == 1, shift))]
    all_to_all x1, waiting for transfers between devices: 3.84 us -> 5.51 us  [shards(): mine = lax.all_to_all(new_rows, ('x', 'zh'), 0, 0, tiled=True)]
    all_to_all x1, starting transfers between devices: 7.71 us -> 6.19 us  [shards(): lax.all_to_all(summed.reshape(ZL * ZH, ROWS, keys_w), ('zl', 'zh'), 0, 0,...]
    ppermute x3, starting transfers between devices: 5.29 us -> 3.94 us  [first_step(): return lax.ppermute(value, GATHER, moved(lambda c: c == 1, shift))]
  transfers between devices with their start and end apart: 18 -> 18, of which waited for: 13 -> 11; matrix products, arithmetic and copies ran while one was open for 2% -> 4% of each run, Pallas kernels for 18% -> 17%
where the time goes in v11:
time: 108 us; the launch traced here: 107 us
  starting transfers between devices  43.4 us (40%)
  waiting for transfers between devices  34.5 us (32%)
  Pallas kernels  23.8 us (22%)
  other arithmetic  3.95 us (4%)
    ppermute x5, starting transfers between devices, shards(): weights += [block, lax.ppermute(block, 'c', ring(C, 1))]  12.6 us
    ppermute x3, waiting for transfers between devices, first_step(): return lax.ppermute(value, GATHER, moved(lambda c: c == 1, shift))  9.85 us
    all_to_all x2, starting transfers between devices, mixed(): lax.all_to_all(value, ('y', 'x', 'c'), 0, 0, axis_index_groups=groups, ti...  8.09 us
    pallas_call x1, Pallas kernels, shards(): kernel_call(token_grad_kernel, pltpu.HBM(tokens.shape, BF16), 2 * tok_row...  7.9 us
    ppermute x4, waiting for transfers between devices, second_step(): return lax.ppermute(value, GATHER, moved(lambda c: c == 0, shift))  7.73 us
    all_to_all x1, starting transfers between devices, shards(): lax.all_to_all(summed.reshape(ZL * ZH, ROWS, keys_w), ('zl', 'zh'), 0, 0,...  6.19 us
    pallas_call x1, Pallas kernels, shards(): kernel_call(keys_kernel, (pltpu.HBM((tok_rows, keys_w), BF16), pltpu.HBM(...  5.66 us
    all_to_all x1, waiting for transfers between devices, shards(): mine = lax.all_to_all(new_rows, ('x', 'zh'), 0, 0, tiled=True)  5.51 us
  transfers between devices with their start and end apart: 18, of which 11 were waited for; matrix products, arithmetic and copies ran while one was open for 4% of the time, Pallas kernels for 17%

profile of v11, /device:TPU:33, one launch (start us, length us, event | category | flops | bytes accessed | tf_op | source)
XLA Modules:
  0.0 107.2 jit_solution(13471579605105800034)
XLA Ops:
  0.6 0.0 copy-start
  0.6 3.5 %shard_map.127 = (bf16[4,128,2560]{2,1,0:T(8,128)(2,1)}, f32[128,128]{1,0:T(8,128)}) custom-call(bf16[128,8192]{1,0:T(8,128)(2,1)} %tok_ref.5, f32[1,8192]{1,0:T(1,128)} %bitcast.11, bf16[128,512]{1,0:T(8,128)(2,1)} %cot_ref.5), custom_call_target="tpu_custom_call" | custom-call | flops 6291456 | bytes 5242880 | tf_op jit(solution)/shard_map/pallas_call | solution.py:275
  4.2 4.2 %all-to-all-start = ((bf16[4,128,2560]{2,1,0:T(8,128)(2,1)}), bf16[4,128,2560]{2,1,0:T(8,128)(2,1)S(1)}, u32[]{:S(2)}, u32[]{:S(2)}) async-start(bf16[4,128,2560]{2,1,0:T(8,128)(2,1)} %get-tuple-element.33), calls=%async_computation | async-start | bytes 5242880 | tf_op jit(solution)/shard_map/all_to_all | solution.py:255
  8.4 0.0 copy-done
  8.4 1.7 %collective-permute-start.1 = (bf16[256,512]{1,0:T(8,128)(2,1)S(1)}, bf16[256,512]{1,0:T(8,128)(2,1)}, u32[]{:S(2)}, u32[]{:S(2)}) collective-permute-start(bf16[256,512]{1,0:T(8,128)(2,1)S(1)} %constant_dynamic-slice_fusion), channel_id=1, source_target_pairs={{0,16},{1,65},{2,18},{3,67},{16,32},{17,81},{18,34},{19,83},{32,48... | collective-permute-start | bytes 786440 | tf_op jit(solution)/shard_map/ppermute | solution.py:242
  10.1 0.0 collective-permute-start
  10.1 4.0 %collective-permute-done.1 = bf16[256,512]{1,0:T(8,128)(2,1)} collective-permute-done((bf16[256,512]{1,0:T(8,128)(2,1)S(1)}, bf16[256,512]{1,0:T(8,128)(2,1)}, u32[]{:S(2)}, u32[]{:S(2)}) %collective-permute-start.1) | collective-permute-done | bytes 262176 | tf_op jit(solution)/shard_map/ppermute | solution.py:242
  14.1 1.8 %collective-permute-done = bf16[256,512]{1,0:T(8,128)(2,1)} collective-permute-done((bf16[256,512]{1,0:T(8,128)(2,1)S(1)}, bf16[256,512]{1,0:T(8,128)(2,1)}, u32[]{:S(2)}, u32[]{:S(2)}) %collective-permute-start) | collective-permute-done | bytes 262176 | tf_op jit(solution)/shard_map/ppermute | solution.py:242
  15.9 1.0 broadcast_select_fusion
  16.9 2.2 %collective-permute-start.2 = (bf16[256,512]{1,0:T(8,128)(2,1)S(1)}, bf16[256,512]{1,0:T(8,128)(2,1)S(1)}, u32[]{:S(2)}, u32[]{:S(2)}) collective-permute-start(bf16[256,512]{1,0:T(8,128)(2,1)S(1)} %broadcast_select_fusion), channel_id=1, source_target_pairs={{0,16},{1,65},{2,18},{3,67},{16,0},{17,81},{18,2},{19,83},{32,48},... | collective-permute-start | bytes 786440 | tf_op jit(solution)/shard_map/ppermute | solution.py:242
  19.1 4.1 %collective-permute-done.2 = bf16[256,512]{1,0:T(8,128)(2,1)S(1)} collective-permute-done((bf16[256,512]{1,0:T(8,128)(2,1)S(1)}, bf16[256,512]{1,0:T(8,128)(2,1)S(1)}, u32[]{:S(2)}, u32[]{:S(2)}) %collective-permute-start.2) | collective-permute-done | bytes 262176 | tf_op jit(solution)/shard_map/ppermute | solution.py:242
  23.2 2.1 %pad_maximum_fusion.refs_0_ = bf16[1024,512]{1,0:T(8,128)(2,1)} fusion(bf16[256,512]{1,0:T(8,128)(2,1)} %collective-permute-done.1, bf16[256,512]{1,0:T(8,128)(2,1)S(1)} %collective-permute-done.2, bf16[256,512]{1,0:T(8,128)(2,1)} %collective-permute-done, bf16[256,512]{1,0:T(8,128)(2,1)S(1)} %constant_dynamic-slice_fusion), kind=kLoop, calls=%fused_computation | loop fusion | flops 4194304 | bytes 2097152 | tf_op jit(solution)/shard_map/concatenate | solution.py:270
  25.2 2.7 %collective-permute-start.4 = (bf16[1024,512]{1,0:T(8,128)(2,1)}, bf16[1024,512]{1,0:T(8,128)(2,1)}, u32[]{:S(2)}, u32[]{:S(2)}) collective-permute-start(bf16[1024,512]{1,0:T(8,128)(2,1)} %pad_maximum_fusion.refs_0_), channel_id=1, source_target_pairs={{0,194},{1,49},{2,192},{3,51},{16,210},{17,1},{18,208},{19,3},{32,... | collective-permute-start | bytes 3145736 | tf_op jit(solution)/shard_map/ppermute | solution.py:246
  27.9 0.0 collective-permute-start.6
  27.9 4.3 %all-to-all-done = bf16[4,128,2560]{2,1,0:T(8,128)(2,1)S(1)} async-done(((bf16[4,128,2560]{2,1,0:T(8,128)(2,1)}), bf16[4,128,2560]{2,1,0:T(8,128)(2,1)S(1)}, u32[]{:S(2)}, u32[]{:S(2)}) %all-to-all-start) | async-done | bytes 2621472 | tf_op jit(solution)/shard_map/all_to_all | solution.py:255
  32.3 2.1 %shard_map.128 = bf16[4,512,512]{2,1,0:T(8,128)(2,1)} custom-call(bf16[512,2560]{1,0:T(8,128)(2,1)S(1)} %bitcast.9), custom_call_target="tpu_custom_call" | custom-call | bytes 1048576 | tf_op jit(solution)/shard_map/pallas_call | solution.py:290
  34.4 3.9 %all-to-all-start.1 = ((bf16[4,512,512]{2,1,0:T(8,128)(2,1)}), bf16[4,512,512]{2,1,0:T(8,128)(2,1)S(1)}, u32[]{:S(2)}, u32[]{:S(2)}) async-start(bf16[4,512,512]{2,1,0:T(8,128)(2,1)} %shard_map.128), calls=%async_computation.1 | async-start | bytes 4194304 | tf_op jit(solution)/shard_map/all_to_all | solution.py:255
  38.3 2.6 %collective-permute-start.3 = (bf16[1024,512]{1,0:T(8,128)(2,1)}, bf16[1024,512]{1,0:T(8,128)(2,1)}, u32[]{:S(2)}, u32[]{:S(2)}) collective-permute-start(bf16[1024,512]{1,0:T(8,128)(2,1)} %pad_maximum_fusion.refs_0_), channel_id=1, source_target_pairs={{0,1},{1,0},{2,3},{3,2},{4,5},{5,4},{6,7},{7,6},{8,9},{9,8},{10,11... | collective-permute-start | bytes 3145736 | tf_op jit(solution)/shard_map/ppermute | solution.py:289
  40.9 1.4 %collective-permute-done.4.up_ref.refs_2_ = bf16[1024,512]{1,0:T(8,128)(2,1)} collective-permute-done((bf16[1024,512]{1,0:T(8,128)(2,1)}, bf16[1024,512]{1,0:T(8,128)(2,1)}, u32[]{:S(2)}, u32[]{:S(2)}) %collective-permute-start.4) | collective-permute-done | bytes 1048608 | tf_op jit(solution)/shard_map/ppermute | solution.py:246
  42.3 5.4 %collective-permute-start.5 = (bf16[1024,512]{1,0:T(8,128)(2,1)}, bf16[1024,512]{1,0:T(8,128)(2,1)}, u32[]{:S(2)}, u32[]{:S(2)}) collective-permute-start(bf16[1024,512]{1,0:T(8,128)(2,1)} %collective-permute-done.4.up_ref.refs_2_), channel_id=1, source_target_pairs={{0,1},{1,0},{2,3},{3,2},{4,5},{5,4},{6,7},{7,6},{8,9},{9,8},{10,11... | collective-permute-start | bytes 3145736 | tf_op jit(solution)/shard_map/ppermute | solution.py:289
  47.7 0.0 collective-permute-done.6.down_ref.refs_4_
  47.7 4.0 %collective-permute-start.7 = (bf16[1024,512]{1,0:T(8,128)(2,1)}, bf16[1024,512]{1,0:T(8,128)(2,1)}, u32[]{:S(2)}, u32[]{:S(2)}) collective-permute-start(bf16[1024,512]{1,0:T(8,128)(2,1)} %collective-permute-done.6.down_ref.refs_4_), channel_id=1, source_target_pairs={{0,1},{1,0},{2,3},{3,2},{4,5},{5,4},{6,7},{7,6},{8,9},{9,8},{10,11... | collective-permute-start | bytes 3145736 | tf_op jit(solution)/shard_map/ppermute | solution.py:289
  51.7 2.2 %shard_map.130 = (bf16[512,512]{1,0:T(8,128)(2,1)}, bf16[512,512]{1,0:T(8,128)(2,1)}) custom-call(bf16[1024,512]{1,0:T(8,128)(2,1)} %collective-permute-done.4.up_ref.refs_2_, bf16[1024,512]{1,0:T(8,128)(2,1)} %collective-permute-done.6.down_ref.refs_4_), custom_call_target="tpu_custom_call" | custom-call | bytes 1048576 | tf_op jit(solution)/shard_map/pallas_call | solution.py:310
  53.9 2.7 %collective-permute-start.9 = (bf16[512,512]{1,0:T(8,128)(2,1)}, bf16[512,512]{1,0:T(8,128)(2,1)S(1)}, u32[]{:S(2)}, u32[]{:S(2)}) collective-permute-start(bf16[512,512]{1,0:T(8,128)(2,1)} %get-tuple-element.37), channel_id=1, source_target_pairs={{0,194},{1,49},{2,192},{3,51},{16,210},{17,1},{18,208},{19,3},{32,... | collective-permute-start | bytes 1572872 | tf_op jit(solution)/shard_map/ppermute | solution.py:246
  56.5 0.0 collective-permute-start.10
  56.5 0.0 all-to-all-done.1.recv_ref
  56.5 0.2 shard_map.129
  56.8 0.0 collective-permute-done.3.refs_1_
  56.8 0.0 collective-permute-done.5.refs_3_
  56.8 0.0 collective-permute-done.7.refs_5_
  56.8 1.0 collective-permute-start.8
  57.8 1.2 %collective-permute-done.8 = bf16[256,512]{1,0:T(8,128)(2,1)S(1)} collective-permute-done((bf16[256,512]{1,0:T(8,128)(2,1)S(1)}, bf16[256,512]{1,0:T(8,128)(2,1)S(1)}, u32[]{:S(2)}, u32[]{:S(2)}) %collective-permute-start.8) | collective-permute-done | bytes 262176 | tf_op jit(solution)/shard_map/ppermute | solution.py:324
  59.0 0.8 add_convert_fusion
  59.7 3.2 %collective-permute-done.9.refs_6_ = bf16[512,512]{1,0:T(8,128)(2,1)S(1)} collective-permute-done((bf16[512,512]{1,0:T(8,128)(2,1)}, bf16[512,512]{1,0:T(8,128)(2,1)S(1)}, u32[]{:S(2)}, u32[]{:S(2)}) %collective-permute-start.9) | collective-permute-done | bytes 524320 | tf_op jit(solution)/shard_map/ppermute | solution.py:246
  63.0 3.1 %collective-permute-done.10.refs_8_ = bf16[512,512]{1,0:T(8,128)(2,1)} collective-permute-done((bf16[512,512]{1,0:T(8,128)(2,1)}, bf16[512,512]{1,0:T(8,128)(2,1)}, u32[]{:S(2)}, u32[]{:S(2)}) %collective-permute-start.10) | collective-permute-done | bytes 524320 | tf_op jit(solution)/shard_map/ppermute | solution.py:246
  66.1 0.6 collective-permute-start.11
  66.6 0.0 collective-permute-start.12
  66.6 6.2 %all-to-all-start.2 = ((bf16[8,32,512]{2,1,0:T(8,128)(2,1)}), bf16[8,32,512]{2,1,0:T(8,128)(2,1)S(1)}, u32[]{:S(2)}, u32[]{:S(2)}) async-start(bf16[8,32,512]{2,1,0:T(8,128)(2,1)} %bitcast.2), calls=%async_computation.2 | async-start | bytes 524288 | tf_op jit(solution)/shard_map/all_to_all | solution.py:329
  72.8 0.0 collective-permute-done.11.refs_7_
  72.8 0.0 collective-permute-done.12.refs_9_
  72.8 5.7 %shard_map.131 = (bf16[128,512]{1,0:T(8,128)(2,1)}, f32[128,128]{1,0:T(8,128)}) custom-call(bf16[128,8192]{1,0:T(8,128)(2,1)} %tok_ref.5, f32[1,8192]{1,0:T(1,128)} %bitcast.12, bf16[128,512]{1,0:T(8,128)(2,1)} %cot_ref.5, f32[128,128]{1,0:T(8,128)} %get-tuple-element.40.inv_ref, bf16[1024,512]{1,0:T(8,128)(2,1)} %pad_maximum_fusion.refs_0_, ...), custom_call_target="tpu_custom_call" | custom-call | flops 1073741824 | bytes 3145728 | tf_op jit(solution)/shard_map/pallas_call | solution.py:330
  78.5 4.8 %all-to-all-done.2.recv_ref = bf16[8,32,512]{2,1,0:T(8,128)(2,1)S(1)} async-done(((bf16[8,32,512]{2,1,0:T(8,128)(2,1)}), bf16[8,32,512]{2,1,0:T(8,128)(2,1)S(1)}, u32[]{:S(2)}, u32[]{:S(2)}) %all-to-all-start.2) | async-done | bytes 262176 | tf_op jit(solution)/shard_map/all_to_all | solution.py:329
  83.3 2.1 %shard_map.132 = (f32[32,512]{1,0:T(8,128)}, f32[16,1024]{1,0:T(8,128)}, f32[16,1024]{1,0:T(8,128)}, bf16[8,32,512]{2,1,0:T(8,128)(2,1)}) custom-call(bf16[8,32,512]{2,1,0:T(8,128)(2,1)S(1)} %all-to-all-done.2.recv_ref, f32[16,1024]{1,0:T(8,128)} %first_ref.1, f32[16,1024]{1,0:T(8,128)} %second_ref.1, f32[32,512]{1,0:T(8,128)} %master_ref.1, s32[1,1024]{1,0:T(1,128)} %bitcast.14), custom_call_target="tpu_custom_call" | custom-call | flops 33554432 | bytes 1048576 | tf_op jit(solution)/shard_map/pallas_call | solution.py:338
  85.4 5.3 %all-to-all-start.3 = ((bf16[8,32,512]{2,1,0:T(8,128)(2,1)}), bf16[8,32,512]{2,1,0:T(8,128)(2,1)S(1)}, u32[]{:S(2)}, u32[]{:S(2)}) async-start(bf16[8,32,512]{2,1,0:T(8,128)(2,1)} %get-tuple-element.53), calls=%async_computation.3 | async-start | bytes 524288 | tf_op jit(solution)/shard_map/all_to_all | solution.py:351
  90.7 7.9 %shard_map.133 = bf16[128,8192]{1,0:T(8,128)(2,1)} custom-call(bf16[128,8192]{1,0:T(8,128)(2,1)} %tok_ref.5, f32[1,8192]{1,0:T(1,128)} %bitcast.13, bf16[128,512]{1,0:T(8,128)(2,1)} %cot_ref.5, f32[128,128]{1,0:T(8,128)} %get-tuple-element.40.inv_ref, f32[128,128]{1,0:T(8,128)} %get-tuple-element.54.mean_ref, bf16[1024,512]{1,0:T(8,128)(2,1)} %pad_maximum_fusion.refs_0_, ...), custom_call_target="tpu_custom_call" | custom-call | flops 1073741824 | bytes 5242880 | tf_op jit(solution)/shard_map/pallas_call | solution.py:352
  98.6 5.5 %all-to-all-done.3 = bf16[8,32,512]{2,1,0:T(8,128)(2,1)S(1)} async-done(((bf16[8,32,512]{2,1,0:T(8,128)(2,1)}), bf16[8,32,512]{2,1,0:T(8,128)(2,1)S(1)}, u32[]{:S(2)}, u32[]{:S(2)}) %all-to-all-start.3) | async-done | bytes 262176 | tf_op jit(solution)/shard_map/all_to_all | solution.py:351
  104.1 1.0 collective-permute-start.13
  105.1 1.2 %collective-permute-done.13 = bf16[8,32,512]{2,1,0:T(8,128)(2,1)S(1)} collective-permute-done((bf16[8,32,512]{2,1,0:T(8,128)(2,1)S(1)}, bf16[8,32,512]{2,1,0:T(8,128)(2,1)S(1)}, u32[]{:S(2)}, u32[]{:S(2)}) %collective-permute-start.13) | collective-permute-done | bytes 262176 | tf_op jit(solution)/shard_map/ppermute | solution.py:360
  106.2 0.1 select_bitcast_fusion.1
  106.3 0.1 pad_maximum_fusion.1
  106.3 0.8 copy.14
  (1 shorter events, 0.0 us)
Async XLA Ops:
  0.6 7.7 %copy-start = (bf16[512,512]{1,0:T(8,128)(2,1)S(1)}, bf16[512,512]{1,0:T(8,128)(2,1)}, u32[]{:S(2)}) copy-start(bf16[512,512]{1,0:T(8,128)(2,1)} %param.11) | copy-start | bytes 1572868
  4.2 28.1 %all-to-all-start = ((bf16[4,128,2560]{2,1,0:T(8,128)(2,1)}), bf16[4,128,2560]{2,1,0:T(8,128)(2,1)S(1)}, u32[]{:S(2)}, u32[]{:S(2)}) async-start(bf16[4,128,2560]{2,1,0:T(8,128)(2,1)} %get-tuple-element.33), calls=%async_computation | async-start | bytes 5242880 | tf_op jit(solution)/shard_map/all_to_all | solution.py:255
  8.4 5.7 %collective-permute-start.1 = (bf16[256,512]{1,0:T(8,128)(2,1)S(1)}, bf16[256,512]{1,0:T(8,128)(2,1)}, u32[]{:S(2)}, u32[]{:S(2)}) collective-permute-start(bf16[256,512]{1,0:T(8,128)(2,1)S(1)} %constant_dynamic-slice_fusion), channel_id=1, source_target_pairs={{0,16},{1,65},{2,18},{3,67},{16,32},{17,81},{18,34},{19,83},{32,48... | collective-permute-start | bytes 786440 | tf_op jit(solution)/shard_map/ppermute | solution.py:242
  10.1 5.8 %collective-permute-start = (bf16[256,512]{1,0:T(8,128)(2,1)S(1)}, bf16[256,512]{1,0:T(8,128)(2,1)}, u32[]{:S(2)}, u32[]{:S(2)}) collective-permute-start(bf16[256,512]{1,0:T(8,128)(2,1)S(1)} %constant_dynamic-slice_fusion), channel_id=1, source_target_pairs={{0,48},{1,195},{2,50},{3,193},{16,0},{17,211},{18,2},{19,209},{32,... | collective-permute-start | bytes 786440 | tf_op jit(solution)/shard_map/ppermute | solution.py:242
  16.9 6.3 %collective-permute-start.2 = (bf16[256,512]{1,0:T(8,128)(2,1)S(1)}, bf16[256,512]{1,0:T(8,128)(2,1)S(1)}, u32[]{:S(2)}, u32[]{:S(2)}) collective-permute-start(bf16[256,512]{1,0:T(8,128)(2,1)S(1)} %broadcast_select_fusion), channel_id=1, source_target_pairs={{0,16},{1,65},{2,18},{3,67},{16,0},{17,81},{18,2},{19,83},{32,48},... | collective-permute-start | bytes 786440 | tf_op jit(solution)/shard_map/ppermute | solution.py:242
  25.2 17.0 %collective-permute-start.4 = (bf16[1024,512]{1,0:T(8,128)(2,1)}, bf16[1024,512]{1,0:T(8,128)(2,1)}, u32[]{:S(2)}, u32[]{:S(2)}) collective-permute-start(bf16[1024,512]{1,0:T(8,128)(2,1)} %pad_maximum_fusion.refs_0_), channel_id=1, source_target_pairs={{0,194},{1,49},{2,192},{3,51},{16,210},{17,1},{18,208},{19,3},{32,... | collective-permute-start | bytes 3145736 | tf_op jit(solution)/shard_map/ppermute | solution.py:246
  27.9 19.8 %collective-permute-start.6 = (bf16[1024,512]{1,0:T(8,128)(2,1)}, bf16[1024,512]{1,0:T(8,128)(2,1)}, u32[]{:S(2)}, u32[]{:S(2)}) collective-permute-start(bf16[1024,512]{1,0:T(8,128)(2,1)} %pad_maximum_fusion.refs_0_), channel_id=1, source_target_pairs={{0,64},{1,17},{2,66},{3,19},{16,80},{17,33},{18,82},{19,35},{32,96... | collective-permute-start | bytes 3145736 | tf_op jit(solution)/shard_map/ppermute | solution.py:246
  34.4 22.2 %all-to-all-start.1 = ((bf16[4,512,512]{2,1,0:T(8,128)(2,1)}), bf16[4,512,512]{2,1,0:T(8,128)(2,1)S(1)}, u32[]{:S(2)}, u32[]{:S(2)}) async-start(bf16[4,512,512]{2,1,0:T(8,128)(2,1)} %shard_map.128), calls=%async_computation.1 | async-start | bytes 4194304 | tf_op jit(solution)/shard_map/all_to_all | solution.py:255
  38.3 18.5 %collective-permute-start.3 = (bf16[1024,512]{1,0:T(8,128)(2,1)}, bf16[1024,512]{1,0:T(8,128)(2,1)}, u32[]{:S(2)}, u32[]{:S(2)}) collective-permute-start(bf16[1024,512]{1,0:T(8,128)(2,1)} %pad_maximum_fusion.refs_0_), channel_id=1, source_target_pairs={{0,1},{1,0},{2,3},{3,2},{4,5},{5,4},{6,7},{7,6},{8,9},{9,8},{10,11... | collective-permute-start | bytes 3145736 | tf_op jit(solution)/shard_map/ppermute | solution.py:289
  42.3 14.5 %collective-permute-start.5 = (bf16[1024,512]{1,0:T(8,128)(2,1)}, bf16[1024,512]{1,0:T(8,128)(2,1)}, u32[]{:S(2)}, u32[]{:S(2)}) collective-permute-start(bf16[1024,512]{1,0:T(8,128)(2,1)} %collective-permute-done.4.up_ref.refs_2_), channel_id=1, source_target_pairs={{0,1},{1,0},{2,3},{3,2},{4,5},{5,4},{6,7},{7,6},{8,9},{9,8},{10,11... | collective-permute-start | bytes 3145736 | tf_op jit(solution)/shard_map/ppermute | solution.py:289
  47.7 9.1 %collective-permute-start.7 = (bf16[1024,512]{1,0:T(8,128)(2,1)}, bf16[1024,512]{1,0:T(8,128)(2,1)}, u32[]{:S(2)}, u32[]{:S(2)}) collective-permute-start(bf16[1024,512]{1,0:T(8,128)(2,1)} %collective-permute-done.6.down_ref.refs_4_), channel_id=1, source_target_pairs={{0,1},{1,0},{2,3},{3,2},{4,5},{5,4},{6,7},{7,6},{8,9},{9,8},{10,11... | collective-permute-start | bytes 3145736 | tf_op jit(solution)/shard_map/ppermute | solution.py:289
  53.9 9.1 %collective-permute-start.9 = (bf16[512,512]{1,0:T(8,128)(2,1)}, bf16[512,512]{1,0:T(8,128)(2,1)S(1)}, u32[]{:S(2)}, u32[]{:S(2)}) collective-permute-start(bf16[512,512]{1,0:T(8,128)(2,1)} %get-tuple-element.37), channel_id=1, source_target_pairs={{0,194},{1,49},{2,192},{3,51},{16,210},{17,1},{18,208},{19,3},{32,... | collective-permute-start | bytes 1572872 | tf_op jit(solution)/shard_map/ppermute | solution.py:246
  56.5 9.6 %collective-permute-start.10 = (bf16[512,512]{1,0:T(8,128)(2,1)}, bf16[512,512]{1,0:T(8,128)(2,1)}, u32[]{:S(2)}, u32[]{:S(2)}) collective-permute-start(bf16[512,512]{1,0:T(8,128)(2,1)} %get-tuple-element.38), channel_id=1, source_target_pairs={{0,64},{1,17},{2,66},{3,19},{16,80},{17,33},{18,82},{19,35},{32,96... | collective-permute-start | bytes 1572872 | tf_op jit(solution)/shard_map/ppermute | solution.py:246
  56.8 2.1 %collective-permute-start.8 = (bf16[256,512]{1,0:T(8,128)(2,1)S(1)}, bf16[256,512]{1,0:T(8,128)(2,1)S(1)}, u32[]{:S(2)}, u32[]{:S(2)}) collective-permute-start(bf16[256,512]{1,0:T(8,128)(2,1)S(1)} %get-tuple-element.36), channel_id=1, source_target_pairs={{0,1},{1,0},{2,3},{3,2},{4,5},{5,4},{6,7},{7,6},{8,9},{9,8},{10,11... | collective-permute-start | bytes 786440 | tf_op jit(solution)/shard_map/ppermute | solution.py:324
  66.1 6.8 %collective-permute-start.11 = (bf16[512,512]{1,0:T(8,128)(2,1)S(1)}, bf16[512,512]{1,0:T(8,128)(2,1)S(1)}, u32[]{:S(2)}, u32[]{:S(2)}) collective-permute-start(bf16[512,512]{1,0:T(8,128)(2,1)S(1)} %collective-permute-done.9.refs_6_), channel_id=1, source_target_pairs={{0,1},{1,0},{2,3},{3,2},{4,5},{5,4},{6,7},{7,6},{8,9},{9,8},{10,11... | collective-permute-start | bytes 1572872 | tf_op jit(solution)/shard_map/ppermute | solution.py:328
  66.6 6.2 %collective-permute-start.12 = (bf16[512,512]{1,0:T(8,128)(2,1)}, bf16[512,512]{1,0:T(8,128)(2,1)S(1)}, u32[]{:S(2)}, u32[]{:S(2)}) collective-permute-start(bf16[512,512]{1,0:T(8,128)(2,1)} %collective-permute-done.10.refs_8_), channel_id=1, source_target_pairs={{0,1},{1,0},{2,3},{3,2},{4,5},{5,4},{6,7},{7,6},{8,9},{9,8},{10,11... | collective-permute-start | bytes 1572872 | tf_op jit(solution)/shard_map/ppermute | solution.py:328
  66.6 16.6 %all-to-all-start.2 = ((bf16[8,32,512]{2,1,0:T(8,128)(2,1)}), bf16[8,32,512]{2,1,0:T(8,128)(2,1)S(1)}, u32[]{:S(2)}, u32[]{:S(2)}) async-start(bf16[8,32,512]{2,1,0:T(8,128)(2,1)} %bitcast.2), calls=%async_computation.2 | async-start | bytes 524288 | tf_op jit(solution)/shard_map/all_to_all | solution.py:329
  85.4 18.7 %all-to-all-start.3 = ((bf16[8,32,512]{2,1,0:T(8,128)(2,1)}), bf16[8,32,512]{2,1,0:T(8,128)(2,1)S(1)}, u32[]{:S(2)}, u32[]{:S(2)}) async-start(bf16[8,32,512]{2,1,0:T(8,128)(2,1)} %get-tuple-element.53), calls=%async_computation.3 | async-start | bytes 524288 | tf_op jit(solution)/shard_map/all_to_all | solution.py:351
  104.1 2.1 %collective-permute-start.13 = (bf16[8,32,512]{2,1,0:T(8,128)(2,1)S(1)}, bf16[8,32,512]{2,1,0:T(8,128)(2,1)S(1)}, u32[]{:S(2)}, u32[]{:S(2)}) collective-permute-start(bf16[8,32,512]{2,1,0:T(8,128)(2,1)S(1)} %all-to-all-done.3), channel_id=1, source_target_pairs={{0,1},{1,0},{2,3},{3,2},{4,5},{5,4},{6,7},{7,6},{8,9},{9,8},{10,11... | collective-permute-start | bytes 786440 | tf_op jit(solution)/shard_map/ppermute | solution.py:360

commit v12 on v10

--- a/solution.py
+++ b/solution.py
@@ -131,7 +131,7 @@
         core = c if i % 2 == 0 else 1 - c
         for row in range(ref.shape[0] // half):
             k = row if i < 6 else row + 2 * ((i - 6) // 2)
-            on_zl, on_y = jnp.where(core == 0, off, k), jnp.where(core == 0, k, off)
+            on_zl, on_y = jnp.where(core == 0, k, off), jnp.where(core == 0, off, k)
             node = lax.rem(zl + on_zl, ZL) * Y + lax.rem(y + on_y, Y)
             at = pl.multiple_of(node * step + core * half, half)
             yield pl.ds(at, half), ref[row * half : (row + 1) * half, :]
@@ -240,11 +240,11 @@
 
 def first_step(value, k):
     shift = lambda place, on_z: {1: -1, 2: 2 - 4 * (place % 2) if on_z else -2, 3: 1}[k]
+    return lax.ppermute(value, GATHER, moved(lambda c: c == 0, shift))
+
+
+def second_step(value, shift):
     return lax.ppermute(value, GATHER, moved(lambda c: c == 1, shift))
-
-
-def second_step(value, shift):
-    return lax.ppermute(value, GATHER, moved(lambda c: c == 0, shift))
 
 
 def mixed(value, first):

time: 104 us -> 109 us (1.048)
  waiting for transfers between devices: 40 us -> 48.4 us
  starting transfers between devices: 35.7 us -> 32.7 us
    ppermute x7, waiting for transfers between devices: 19 us -> 38.2 us  [the longest x3 21.3 us: first_step(): return lax.ppermute(value, GATHER, moved(lambda c: c == 0, shift))]
    all_to_all x2, waiting for transfers between devices: 9.73 us -> 0.01 us  [mixed(): lax.all_to_all(value, ('y', 'x', 'c'), 0, 0, axis_index_groups=groups, ti...]
    all_to_all x1, starting transfers between devices: 7.71 us -> 5.79 us  [shards(): lax.all_to_all(summed.reshape(ZL * ZH, ROWS, keys_w), ('zl', 'zh'), 0, 0,...]
    ppermute x1, starting transfers between devices: 1.85 us -> 0.09 us  [shards(): sib = lax.ppermute(sib, 'c', ring(C, 1))]
    ppermute x1, starting transfers between devices: 2.02 us -> 3.65 us  [shards(): other = lax.ppermute(mine, 'c', ring(C, 1))]
    all_to_all x1, waiting for transfers between devices: 3.84 us -> 2.35 us  [shards(): mine = lax.all_to_all(new_rows, ('x', 'zh'), 0, 0, tiled=True)]
  transfers between devices with their start and end apart: 18 -> 18, of which waited for: 13 -> 11; matrix products, arithmetic and copies ran while one was open for 2% -> 2% of each run, Pallas kernels for 18% -> 17%
where the time goes in v12:
time: 109 us; the launch traced here: 108 us
  waiting for transfers between devices  48.4 us (44%)
  starting transfers between devices  32.7 us (30%)
  Pallas kernels  23.7 us (22%)
  other arithmetic  1.92 us (2%)
    ppermute x3, waiting for transfers between devices, first_step(): return lax.ppermute(value, GATHER, moved(lambda c: c == 0, shift))  21.3 us
    ppermute x4, waiting for transfers between devices, second_step(): return lax.ppermute(value, GATHER, moved(lambda c: c == 1, shift))  17 us
    pallas_call x1, Pallas kernels, shards(): kernel_call(token_grad_kernel, pltpu.HBM(tokens.shape, BF16), 2 * tok_row...  7.88 us
    all_to_all x2, starting transfers between devices, mixed(): lax.all_to_all(value, ('y', 'x', 'c'), 0, 0, axis_index_groups=groups, ti...  7.8 us
    all_to_all x1, starting transfers between devices, shards(): lax.all_to_all(summed.reshape(ZL * ZH, ROWS, keys_w), ('zl', 'zh'), 0, 0,...  5.79 us
    ppermute x4, starting transfers between devices, second_step(): return lax.ppermute(value, GATHER, moved(lambda c: c == 1, shift))  5.69 us
    pallas_call x1, Pallas kernels, shards(): kernel_call(keys_kernel, (pltpu.HBM((tok_rows, keys_w), BF16), pltpu.HBM(...  5.65 us
    all_to_all x1, waiting for transfers between devices, shards(): lax.all_to_all(summed.reshape(ZL * ZH, ROWS, keys_w), ('zl', 'zh'), 0, 0,...  5.13 us
  transfers between devices with their start and end apart: 18, of which 11 were waited for; matrix products, arithmetic and copies ran while one was open for 2% of the time, Pallas kernels for 17%

profile of v12, /device:TPU:33, one launch (start us, length us, event | category | flops | bytes accessed | tf_op | source)
XLA Modules:
  0.0 108.4 jit_solution(13992655685091310353)
XLA Ops:
  0.6 0.0 copy-start
  0.6 3.5 %shard_map.127 = (bf16[4,128,2560]{2,1,0:T(8,128)(2,1)}, f32[128,128]{1,0:T(8,128)}) custom-call(bf16[128,8192]{1,0:T(8,128)(2,1)} %tok_ref.5, f32[1,8192]{1,0:T(1,128)} %bitcast.11, bf16[128,512]{1,0:T(8,128)(2,1)} %cot_ref.5), custom_call_target="tpu_custom_call" | custom-call | flops 6291456 | bytes 5242880 | tf_op jit(solution)/shard_map/pallas_call | solution.py:272
  4.2 4.2 %all-to-all-start = ((bf16[4,128,2560]{2,1,0:T(8,128)(2,1)}), bf16[4,128,2560]{2,1,0:T(8,128)(2,1)S(1)}, u32[]{:S(2)}, u32[]{:S(2)}) async-start(bf16[4,128,2560]{2,1,0:T(8,128)(2,1)} %get-tuple-element.33), calls=%async_computation | async-start | bytes 5242880 | tf_op jit(solution)/shard_map/all_to_all | solution.py:256
  8.4 0.0 copy-done
  8.4 1.5 %collective-permute-start.2 = (bf16[256,512]{1,0:T(8,128)(2,1)S(1)}, bf16[256,512]{1,0:T(8,128)(2,1)S(1)}, u32[]{:S(2)}, u32[]{:S(2)}) collective-permute-start(bf16[256,512]{1,0:T(8,128)(2,1)S(1)} %constant_dynamic-slice_fusion), channel_id=1, source_target_pairs={{0,64},{1,17},{2,66},{3,19},{16,80},{17,33},{18,82},{19,35},{32,96... | collective-permute-start | bytes 786440 | tf_op jit(solution)/shard_map/ppermute | solution.py:243
  9.9 2.4 %collective-permute-start.1 = (bf16[256,512]{1,0:T(8,128)(2,1)S(1)}, bf16[256,512]{1,0:T(8,128)(2,1)S(1)}, u32[]{:S(2)}, u32[]{:S(2)}) collective-permute-start(bf16[256,512]{1,0:T(8,128)(2,1)S(1)} %constant_dynamic-slice_fusion), channel_id=1, source_target_pairs={{0,128},{1,33},{2,130},{3,35},{16,144},{17,49},{18,146},{19,51},{3... | collective-permute-start | bytes 786440 | tf_op jit(solution)/shard_map/ppermute | solution.py:243
  12.3 1.2 %collective-permute-start = (bf16[256,512]{1,0:T(8,128)(2,1)S(1)}, bf16[256,512]{1,0:T(8,128)(2,1)S(1)}, u32[]{:S(2)}, u32[]{:S(2)}) collective-permute-start(bf16[256,512]{1,0:T(8,128)(2,1)S(1)} %constant_dynamic-slice_fusion), channel_id=1, source_target_pairs={{0,194},{1,49},{2,192},{3,51},{16,210},{17,1},{18,208},{19,3},{32,... | collective-permute-start | bytes 786440 | tf_op jit(solution)/shard_map/ppermute | solution.py:243
  13.5 15.5 %collective-permute-done.2 = bf16[256,512]{1,0:T(8,128)(2,1)S(1)} collective-permute-done((bf16[256,512]{1,0:T(8,128)(2,1)S(1)}, bf16[256,512]{1,0:T(8,128)(2,1)S(1)}, u32[]{:S(2)}, u32[]{:S(2)}) %collective-permute-start.2) | collective-permute-done | bytes 262176 | tf_op jit(solution)/shard_map/ppermute | solution.py:243
  29.1 5.1 %collective-permute-done.1 = bf16[256,512]{1,0:T(8,128)(2,1)S(1)} collective-permute-done((bf16[256,512]{1,0:T(8,128)(2,1)S(1)}, bf16[256,512]{1,0:T(8,128)(2,1)S(1)}, u32[]{:S(2)}, u32[]{:S(2)}) %collective-permute-start.1) | collective-permute-done | bytes 262176 | tf_op jit(solution)/shard_map/ppermute | solution.py:243
  34.2 0.6 collective-permute-done
  34.8 1.0 pad_maximum_fusion.refs_0_
  35.8 0.0 collective-permute-start.4
  35.8 3.0 %collective-permute-start.6 = (bf16[1024,512]{1,0:T(8,128)(2,1)}, bf16[1024,512]{1,0:T(8,128)(2,1)}, u32[]{:S(2)}, u32[]{:S(2)}) collective-permute-start(bf16[1024,512]{1,0:T(8,128)(2,1)} %pad_maximum_fusion.refs_0_), channel_id=1, source_target_pairs={{0,16},{1,65},{2,18},{3,67},{16,32},{17,81},{18,34},{19,83},{32,48... | collective-permute-start | bytes 3145736 | tf_op jit(solution)/shard_map/ppermute | solution.py:247
  38.8 0.0 all-to-all-done
  38.8 2.1 %shard_map.128 = bf16[4,512,512]{2,1,0:T(8,128)(2,1)} custom-call(bf16[512,2560]{1,0:T(8,128)(2,1)S(1)} %bitcast.9), custom_call_target="tpu_custom_call" | custom-call | bytes 1048576 | tf_op jit(solution)/shard_map/pallas_call | solution.py:287
  40.9 3.6 %all-to-all-start.1 = ((bf16[4,512,512]{2,1,0:T(8,128)(2,1)}), bf16[4,512,512]{2,1,0:T(8,128)(2,1)S(1)}, u32[]{:S(2)}, u32[]{:S(2)}) async-start(bf16[4,512,512]{2,1,0:T(8,128)(2,1)} %shard_map.128), calls=%async_computation.1 | async-start | bytes 4194304 | tf_op jit(solution)/shard_map/all_to_all | solution.py:256
  44.5 0.1 collective-permute-start.3
  44.6 6.8 %collective-permute-done.4.up_ref.refs_2_ = bf16[1024,512]{1,0:T(8,128)(2,1)} collective-permute-done((bf16[1024,512]{1,0:T(8,128)(2,1)}, bf16[1024,512]{1,0:T(8,128)(2,1)}, u32[]{:S(2)}, u32[]{:S(2)}) %collective-permute-start.4) | collective-permute-done | bytes 1048608 | tf_op jit(solution)/shard_map/ppermute | solution.py:247
  51.5 0.0 collective-permute-start.5
  51.5 4.5 %collective-permute-done.6.down_ref.refs_4_ = bf16[1024,512]{1,0:T(8,128)(2,1)} collective-permute-done((bf16[1024,512]{1,0:T(8,128)(2,1)}, bf16[1024,512]{1,0:T(8,128)(2,1)}, u32[]{:S(2)}, u32[]{:S(2)}) %collective-permute-start.6) | collective-permute-done | bytes 1048608 | tf_op jit(solution)/shard_map/ppermute | solution.py:247
  55.9 0.0 collective-permute-start.7
  55.9 2.2 %shard_map.130 = (bf16[512,512]{1,0:T(8,128)(2,1)}, bf16[512,512]{1,0:T(8,128)(2,1)}) custom-call(bf16[1024,512]{1,0:T(8,128)(2,1)} %collective-permute-done.4.up_ref.refs_2_, bf16[1024,512]{1,0:T(8,128)(2,1)} %collective-permute-done.6.down_ref.refs_4_), custom_call_target="tpu_custom_call" | custom-call | bytes 1048576 | tf_op jit(solution)/shard_map/pallas_call | solution.py:307
  58.1 2.7 %collective-permute-start.9 = (bf16[512,512]{1,0:T(8,128)(2,1)}, bf16[512,512]{1,0:T(8,128)(2,1)S(1)}, u32[]{:S(2)}, u32[]{:S(2)}) collective-permute-start(bf16[512,512]{1,0:T(8,128)(2,1)} %get-tuple-element.37), channel_id=1, source_target_pairs={{0,48},{1,195},{2,50},{3,193},{16,0},{17,211},{18,2},{19,209},{32,... | collective-permute-start | bytes 1572872 | tf_op jit(solution)/shard_map/ppermute | solution.py:247
  60.9 0.0 collective-permute-start.10
  60.9 0.0 all-to-all-done.1.recv_ref
  60.9 0.2 shard_map.129
  61.1 0.0 collective-permute-done.3.refs_1_
  61.1 0.0 collective-permute-done.5.refs_3_
  61.1 0.0 collective-permute-done.7.refs_5_
  61.1 0.1 collective-permute-start.8
  61.2 1.5 %collective-permute-done.8 = bf16[256,512]{1,0:T(8,128)(2,1)S(1)} collective-permute-done((bf16[256,512]{1,0:T(8,128)(2,1)S(1)}, bf16[256,512]{1,0:T(8,128)(2,1)S(1)}, u32[]{:S(2)}, u32[]{:S(2)}) %collective-permute-start.8) | collective-permute-done | bytes 262176 | tf_op jit(solution)/shard_map/ppermute | solution.py:321
  62.8 0.8 add_convert_fusion
  63.6 3.7 %collective-permute-done.9.refs_6_ = bf16[512,512]{1,0:T(8,128)(2,1)S(1)} collective-permute-done((bf16[512,512]{1,0:T(8,128)(2,1)}, bf16[512,512]{1,0:T(8,128)(2,1)S(1)}, u32[]{:S(2)}, u32[]{:S(2)}) %collective-permute-start.9) | collective-permute-done | bytes 524320 | tf_op jit(solution)/shard_map/ppermute | solution.py:247
  67.3 1.9 %collective-permute-done.10.refs_8_ = bf16[512,512]{1,0:T(8,128)(2,1)} collective-permute-done((bf16[512,512]{1,0:T(8,128)(2,1)}, bf16[512,512]{1,0:T(8,128)(2,1)}, u32[]{:S(2)}, u32[]{:S(2)}) %collective-permute-start.10) | collective-permute-done | bytes 524320 | tf_op jit(solution)/shard_map/ppermute | solution.py:247
  69.2 0.4 collective-permute-start.11
  69.6 0.1 collective-permute-start.12
  69.7 5.8 %all-to-all-start.2 = ((bf16[8,32,512]{2,1,0:T(8,128)(2,1)}), bf16[8,32,512]{2,1,0:T(8,128)(2,1)S(1)}, u32[]{:S(2)}, u32[]{:S(2)}) async-start(bf16[8,32,512]{2,1,0:T(8,128)(2,1)} %bitcast.2), calls=%async_computation.2 | async-start | bytes 524288 | tf_op jit(solution)/shard_map/all_to_all | solution.py:326
  75.5 0.0 collective-permute-done.11.refs_7_
  75.5 0.0 collective-permute-done.12.refs_9_
  75.5 5.6 %shard_map.131 = (bf16[128,512]{1,0:T(8,128)(2,1)}, f32[128,128]{1,0:T(8,128)}) custom-call(bf16[128,8192]{1,0:T(8,128)(2,1)} %tok_ref.5, f32[1,8192]{1,0:T(1,128)} %bitcast.12, bf16[128,512]{1,0:T(8,128)(2,1)} %cot_ref.5, f32[128,128]{1,0:T(8,128)} %get-tuple-element.40.inv_ref, bf16[1024,512]{1,0:T(8,128)(2,1)} %pad_maximum_fusion.refs_0_, ...), custom_call_target="tpu_custom_call" | custom-call | flops 1073741824 | bytes 3145728 | tf_op jit(solution)/shard_map/pallas_call | solution.py:327
  81.2 5.1 %all-to-all-done.2.recv_ref = bf16[8,32,512]{2,1,0:T(8,128)(2,1)S(1)} async-done(((bf16[8,32,512]{2,1,0:T(8,128)(2,1)}), bf16[8,32,512]{2,1,0:T(8,128)(2,1)S(1)}, u32[]{:S(2)}, u32[]{:S(2)}) %all-to-all-start.2) | async-done | bytes 262176 | tf_op jit(solution)/shard_map/all_to_all | solution.py:326
  86.3 2.1 %shard_map.132 = (f32[32,512]{1,0:T(8,128)}, f32[16,1024]{1,0:T(8,128)}, f32[16,1024]{1,0:T(8,128)}, bf16[8,32,512]{2,1,0:T(8,128)(2,1)}) custom-call(bf16[8,32,512]{2,1,0:T(8,128)(2,1)S(1)} %all-to-all-done.2.recv_ref, f32[16,1024]{1,0:T(8,128)} %first_ref.1, f32[16,1024]{1,0:T(8,128)} %second_ref.1, f32[32,512]{1,0:T(8,128)} %master_ref.1, s32[1,1024]{1,0:T(1,128)} %bitcast.14), custom_call_target="tpu_custom_call" | custom-call | flops 33554432 | bytes 1048576 | tf_op jit(solution)/shard_map/pallas_call | solution.py:335
  88.4 3.9 %all-to-all-start.3 = ((bf16[8,32,512]{2,1,0:T(8,128)(2,1)}), bf16[8,32,512]{2,1,0:T(8,128)(2,1)S(1)}, u32[]{:S(2)}, u32[]{:S(2)}) async-start(bf16[8,32,512]{2,1,0:T(8,128)(2,1)} %get-tuple-element.53), calls=%async_computation.3 | async-start | bytes 524288 | tf_op jit(solution)/shard_map/all_to_all | solution.py:348
  92.4 7.9 %shard_map.133 = bf16[128,8192]{1,0:T(8,128)(2,1)} custom-call(bf16[128,8192]{1,0:T(8,128)(2,1)} %tok_ref.5, f32[1,8192]{1,0:T(1,128)} %bitcast.13, bf16[128,512]{1,0:T(8,128)(2,1)} %cot_ref.5, f32[128,128]{1,0:T(8,128)} %get-tuple-element.40.inv_ref, f32[128,128]{1,0:T(8,128)} %get-tuple-element.54.mean_ref, bf16[1024,512]{1,0:T(8,128)(2,1)} %pad_maximum_fusion.refs_0_, ...), custom_call_target="tpu_custom_call" | custom-call | flops 1073741824 | bytes 5242880 | tf_op jit(solution)/shard_map/pallas_call | solution.py:349
  100.3 2.3 %all-to-all-done.3 = bf16[8,32,512]{2,1,0:T(8,128)(2,1)S(1)} async-done(((bf16[8,32,512]{2,1,0:T(8,128)(2,1)}), bf16[8,32,512]{2,1,0:T(8,128)(2,1)S(1)}, u32[]{:S(2)}, u32[]{:S(2)}) %all-to-all-start.3) | async-done | bytes 262176 | tf_op jit(solution)/shard_map/all_to_all | solution.py:348
  102.6 3.7 %collective-permute-start.13 = (bf16[8,32,512]{2,1,0:T(8,128)(2,1)S(1)}, bf16[8,32,512]{2,1,0:T(8,128)(2,1)S(1)}, u32[]{:S(2)}, u32[]{:S(2)}) collective-permute-start(bf16[8,32,512]{2,1,0:T(8,128)(2,1)S(1)} %all-to-all-done.3), channel_id=1, source_target_pairs={{0,1},{1,0},{2,3},{3,2},{4,5},{5,4},{6,7},{7,6},{8,9},{9,8},{10,11... | collective-permute-start | bytes 786440 | tf_op jit(solution)/shard_map/ppermute | solution.py:357
  106.3 1.2 %collective-permute-done.13 = bf16[8,32,512]{2,1,0:T(8,128)(2,1)S(1)} collective-permute-done((bf16[8,32,512]{2,1,0:T(8,128)(2,1)S(1)}, bf16[8,32,512]{2,1,0:T(8,128)(2,1)S(1)}, u32[]{:S(2)}, u32[]{:S(2)}) %collective-permute-start.13) | collective-permute-done | bytes 262176 | tf_op jit(solution)/shard_map/ppermute | solution.py:357
  107.5 0.1 pad_maximum_fusion.1
  107.5 0.8 copy.14
  (2 shorter events, 0.1 us)
Async XLA Ops:
  0.6 7.7 %copy-start = (bf16[512,512]{1,0:T(8,128)(2,1)S(1)}, bf16[512,512]{1,0:T(8,128)(2,1)}, u32[]{:S(2)}) copy-start(bf16[512,512]{1,0:T(8,128)(2,1)} %param.11) | copy-start | bytes 1572868
  4.2 34.6 %all-to-all-start = ((bf16[4,128,2560]{2,1,0:T(8,128)(2,1)}), bf16[4,128,2560]{2,1,0:T(8,128)(2,1)S(1)}, u32[]{:S(2)}, u32[]{:S(2)}) async-start(bf16[4,128,2560]{2,1,0:T(8,128)(2,1)} %get-tuple-element.33), calls=%async_computation | async-start | bytes 5242880 | tf_op jit(solution)/shard_map/all_to_all | solution.py:256
  8.4 20.7 %collective-permute-start.2 = (bf16[256,512]{1,0:T(8,128)(2,1)S(1)}, bf16[256,512]{1,0:T(8,128)(2,1)S(1)}, u32[]{:S(2)}, u32[]{:S(2)}) collective-permute-start(bf16[256,512]{1,0:T(8,128)(2,1)S(1)} %constant_dynamic-slice_fusion), channel_id=1, source_target_pairs={{0,64},{1,17},{2,66},{3,19},{16,80},{17,33},{18,82},{19,35},{32,96... | collective-permute-start | bytes 786440 | tf_op jit(solution)/shard_map/ppermute | solution.py:243
  9.9 24.3 %collective-permute-start.1 = (bf16[256,512]{1,0:T(8,128)(2,1)S(1)}, bf16[256,512]{1,0:T(8,128)(2,1)S(1)}, u32[]{:S(2)}, u32[]{:S(2)}) collective-permute-start(bf16[256,512]{1,0:T(8,128)(2,1)S(1)} %constant_dynamic-slice_fusion), channel_id=1, source_target_pairs={{0,128},{1,33},{2,130},{3,35},{16,144},{17,49},{18,146},{19,51},{3... | collective-permute-start | bytes 786440 | tf_op jit(solution)/shard_map/ppermute | solution.py:243
  12.3 22.4 %collective-permute-start = (bf16[256,512]{1,0:T(8,128)(2,1)S(1)}, bf16[256,512]{1,0:T(8,128)(2,1)S(1)}, u32[]{:S(2)}, u32[]{:S(2)}) collective-permute-start(bf16[256,512]{1,0:T(8,128)(2,1)S(1)} %constant_dynamic-slice_fusion), channel_id=1, source_target_pairs={{0,194},{1,49},{2,192},{3,51},{16,210},{17,1},{18,208},{19,3},{32,... | collective-permute-start | bytes 786440 | tf_op jit(solution)/shard_map/ppermute | solution.py:243
  35.8 15.7 %collective-permute-start.4 = (bf16[1024,512]{1,0:T(8,128)(2,1)}, bf16[1024,512]{1,0:T(8,128)(2,1)}, u32[]{:S(2)}, u32[]{:S(2)}) collective-permute-start(bf16[1024,512]{1,0:T(8,128)(2,1)} %pad_maximum_fusion.refs_0_), channel_id=1, source_target_pairs={{0,48},{1,195},{2,50},{3,193},{16,0},{17,211},{18,2},{19,209},{32,... | collective-permute-start | bytes 3145736 | tf_op jit(solution)/shard_map/ppermute | solution.py:247
  35.8 20.1 %collective-permute-start.6 = (bf16[1024,512]{1,0:T(8,128)(2,1)}, bf16[1024,512]{1,0:T(8,128)(2,1)}, u32[]{:S(2)}, u32[]{:S(2)}) collective-permute-start(bf16[1024,512]{1,0:T(8,128)(2,1)} %pad_maximum_fusion.refs_0_), channel_id=1, source_target_pairs={{0,16},{1,65},{2,18},{3,67},{16,32},{17,81},{18,34},{19,83},{32,48... | collective-permute-start | bytes 3145736 | tf_op jit(solution)/shard_map/ppermute | solution.py:247
  40.9 20.0 %all-to-all-start.1 = ((bf16[4,512,512]{2,1,0:T(8,128)(2,1)}), bf16[4,512,512]{2,1,0:T(8,128)(2,1)S(1)}, u32[]{:S(2)}, u32[]{:S(2)}) async-start(bf16[4,512,512]{2,1,0:T(8,128)(2,1)} %shard_map.128), calls=%async_computation.1 | async-start | bytes 4194304 | tf_op jit(solution)/shard_map/all_to_all | solution.py:256
  44.5 16.6 %collective-permute-start.3 = (bf16[1024,512]{1,0:T(8,128)(2,1)}, bf16[1024,512]{1,0:T(8,128)(2,1)}, u32[]{:S(2)}, u32[]{:S(2)}) collective-permute-start(bf16[1024,512]{1,0:T(8,128)(2,1)} %pad_maximum_fusion.refs_0_), channel_id=1, source_target_pairs={{0,1},{1,0},{2,3},{3,2},{4,5},{5,4},{6,7},{7,6},{8,9},{9,8},{10,11... | collective-permute-start | bytes 3145736 | tf_op jit(solution)/shard_map/ppermute | solution.py:286
  51.5 9.7 %collective-permute-start.5 = (bf16[1024,512]{1,0:T(8,128)(2,1)}, bf16[1024,512]{1,0:T(8,128)(2,1)}, u32[]{:S(2)}, u32[]{:S(2)}) collective-permute-start(bf16[1024,512]{1,0:T(8,128)(2,1)} %collective-permute-done.4.up_ref.refs_2_), channel_id=1, source_target_pairs={{0,1},{1,0},{2,3},{3,2},{4,5},{5,4},{6,7},{7,6},{8,9},{9,8},{10,11... | collective-permute-start | bytes 3145736 | tf_op jit(solution)/shard_map/ppermute | solution.py:286
  55.9 5.2 %collective-permute-start.7 = (bf16[1024,512]{1,0:T(8,128)(2,1)}, bf16[1024,512]{1,0:T(8,128)(2,1)}, u32[]{:S(2)}, u32[]{:S(2)}) collective-permute-start(bf16[1024,512]{1,0:T(8,128)(2,1)} %collective-permute-done.6.down_ref.refs_4_), channel_id=1, source_target_pairs={{0,1},{1,0},{2,3},{3,2},{4,5},{5,4},{6,7},{7,6},{8,9},{9,8},{10,11... | collective-permute-start | bytes 3145736 | tf_op jit(solution)/shard_map/ppermute | solution.py:286
  58.1 9.2 %collective-permute-start.9 = (bf16[512,512]{1,0:T(8,128)(2,1)}, bf16[512,512]{1,0:T(8,128)(2,1)S(1)}, u32[]{:S(2)}, u32[]{:S(2)}) collective-permute-start(bf16[512,512]{1,0:T(8,128)(2,1)} %get-tuple-element.37), channel_id=1, source_target_pairs={{0,48},{1,195},{2,50},{3,193},{16,0},{17,211},{18,2},{19,209},{32,... | collective-permute-start | bytes 1572872 | tf_op jit(solution)/shard_map/ppermute | solution.py:247
  60.9 8.4 %collective-permute-start.10 = (bf16[512,512]{1,0:T(8,128)(2,1)}, bf16[512,512]{1,0:T(8,128)(2,1)}, u32[]{:S(2)}, u32[]{:S(2)}) collective-permute-start(bf16[512,512]{1,0:T(8,128)(2,1)} %get-tuple-element.38), channel_id=1, source_target_pairs={{0,16},{1,65},{2,18},{3,67},{16,32},{17,81},{18,34},{19,83},{32,48... | collective-permute-start | bytes 1572872 | tf_op jit(solution)/shard_map/ppermute | solution.py:247
  61.1 1.6 %collective-permute-start.8 = (bf16[256,512]{1,0:T(8,128)(2,1)S(1)}, bf16[256,512]{1,0:T(8,128)(2,1)S(1)}, u32[]{:S(2)}, u32[]{:S(2)}) collective-permute-start(bf16[256,512]{1,0:T(8,128)(2,1)S(1)} %get-tuple-element.36), channel_id=1, source_target_pairs={{0,1},{1,0},{2,3},{3,2},{4,5},{5,4},{6,7},{7,6},{8,9},{9,8},{10,11... | collective-permute-start | bytes 786440 | tf_op jit(solution)/shard_map/ppermute | solution.py:321
  69.2 6.3 %collective-permute-start.11 = (bf16[512,512]{1,0:T(8,128)(2,1)S(1)}, bf16[512,512]{1,0:T(8,128)(2,1)S(1)}, u32[]{:S(2)}, u32[]{:S(2)}) collective-permute-start(bf16[512,512]{1,0:T(8,128)(2,1)S(1)} %collective-permute-done.9.refs_6_), channel_id=1, source_target_pairs={{0,1},{1,0},{2,3},{3,2},{4,5},{5,4},{6,7},{7,6},{8,9},{9,8},{10,11... | collective-permute-start | bytes 1572872 | tf_op jit(solution)/shard_map/ppermute | solution.py:325
  69.6 5.9 %collective-permute-start.12 = (bf16[512,512]{1,0:T(8,128)(2,1)}, bf16[512,512]{1,0:T(8,128)(2,1)S(1)}, u32[]{:S(2)}, u32[]{:S(2)}) collective-permute-start(bf16[512,512]{1,0:T(8,128)(2,1)} %collective-permute-done.10.refs_8_), channel_id=1, source_target_pairs={{0,1},{1,0},{2,3},{3,2},{4,5},{5,4},{6,7},{7,6},{8,9},{9,8},{10,11... | collective-permute-start | bytes 1572872 | tf_op jit(solution)/shard_map/ppermute | solution.py:325
  69.7 16.6 %all-to-all-start.2 = ((bf16[8,32,512]{2,1,0:T(8,128)(2,1)}), bf16[8,32,512]{2,1,0:T(8,128)(2,1)S(1)}, u32[]{:S(2)}, u32[]{:S(2)}) async-start(bf16[8,32,512]{2,1,0:T(8,128)(2,1)} %bitcast.2), calls=%async_computation.2 | async-start | bytes 524288 | tf_op jit(solution)/shard_map/all_to_all | solution.py:326
  88.4 14.2 %all-to-all-start.3 = ((bf16[8,32,512]{2,1,0:T(8,128)(2,1)}), bf16[8,32,512]{2,1,0:T(8,128)(2,1)S(1)}, u32[]{:S(2)}, u32[]{:S(2)}) async-start(bf16[8,32,512]{2,1,0:T(8,128)(2,1)} %get-tuple-element.53), calls=%async_computation.3 | async-start | bytes 524288 | tf_op jit(solution)/shard_map/all_to_all | solution.py:348
  102.6 4.8 %collective-permute-start.13 = (bf16[8,32,512]{2,1,0:T(8,128)(2,1)S(1)}, bf16[8,32,512]{2,1,0:T(8,128)(2,1)S(1)}, u32[]{:S(2)}, u32[]{:S(2)}) collective-permute-start(bf16[8,32,512]{2,1,0:T(8,128)(2,1)S(1)} %all-to-all-done.3), channel_id=1, source_target_pairs={{0,1},{1,0},{2,3},{3,2},{4,5},{5,4},{6,7},{7,6},{8,9},{9,8},{10,11... | collective-permute-start | bytes 786440 | tf_op jit(solution)/shard_map/ppermute | solution.py:357

commit v13 on v10

--- a/solution.py
+++ b/solution.py
@@ -281,9 +281,6 @@
     recv = mixed(send, True).reshape(X * tok_rows, part + keys_w)
     from_up = second_step(column, lambda place, on_z: -1)
     from_down = second_step(column, lambda place, on_z: 1)
-    weights = []
-    for block in (column, from_up, from_down):
-        weights += [block, lax.ppermute(block, "c", ring(C, 1))]
     send = kernel_call(
         grad_kernel,
         pltpu.HBM((Y, part // Y, keys_w), BF16),
@@ -302,7 +299,6 @@
         1 << 20,
         1,
     )(blocks)
-    from_up, from_down = weights[2], weights[4]
     rows = from_up.shape[0] // 2
     far_a, far_b = kernel_call(
         halves_kernel,
@@ -317,10 +313,14 @@
         second_step(far_a, lambda place, on_z: -1),
         second_step(far_b, lambda place, on_z: 1),
     ]
-    sib, weights = lax.optimization_barrier((sib, weights))
+    column, from_up, from_down, far_a, far_b = lax.optimization_barrier((column, from_up, from_down, far_a, far_b))
+    weights = []
+    for block in (column, from_up, from_down):
+        weights += [block, lax.ppermute(block, "c", ring(C, 1))]
+    sib, far = lax.optimization_barrier((sib, far))
     sib = lax.ppermute(sib, "c", ring(C, 1))
     summed = (own + sib.astype(F32)).astype(BF16)
-    summed, far = lax.optimization_barrier((summed, far))
+    summed, weights = lax.optimization_barrier((summed, weights))
     for block in far:
         weights += [block, lax.ppermute(block, "c", ring(C, 1))]
     blocks = lax.all_to_all(summed.reshape(ZL * ZH, ROWS, keys_w), ("zl", "zh"), 0, 0, tiled=True)

time: 104 us -> 105 us (level)
  waiting for transfers between devices: 40 us -> 42.2 us
    ppermute x4, waiting for transfers between devices: 11.5 us -> 15.5 us  [second_step(): return lax.ppermute(value, GATHER, moved(lambda c: c == 0, shift))]
    ppermute x1, starting transfers between devices: 2.02 us -> 3.98 us  [shards(): other = lax.ppermute(mine, 'c', ring(C, 1))]
    all_to_all x1, waiting for transfers between devices: 3.84 us -> 2.15 us  [shards(): mine = lax.all_to_all(new_rows, ('x', 'zh'), 0, 0, tiled=True)]
  transfers between devices with their start and end apart: 18 -> 18, of which waited for: 13 -> 13; matrix products, arithmetic and copies ran while one was open for 2% -> 2% of each run, Pallas kernels for 18% -> 17%
where the time goes in v13:
time: 105 us
  waiting for transfers between devices  42.2 us (40%)
  starting transfers between devices  35.4 us (34%)
  Pallas kernels  23.7 us (23%)
  other arithmetic  1.92 us (2%)
    ppermute x4, waiting for transfers between devices, second_step(): return lax.ppermute(value, GATHER, moved(lambda c: c == 0, shift))  15.5 us
    all_to_all x2, waiting for transfers between devices, mixed(): lax.all_to_all(value, ('y', 'x', 'c'), 0, 0, axis_index_groups=groups, ti...  9.62 us
    all_to_all x2, starting transfers between devices, mixed(): lax.all_to_all(value, ('y', 'x', 'c'), 0, 0, axis_index_groups=groups, ti...  8.21 us
    pallas_call x1, Pallas kernels, shards(): kernel_call(token_grad_kernel, pltpu.HBM(tokens.shape, BF16), 2 * tok_row...  7.89 us
    ppermute x3, waiting for transfers between devices, first_step(): return lax.ppermute(value, GATHER, moved(lambda c: c == 1, shift))  7.49 us
    all_to_all x1, starting transfers between devices, shards(): lax.all_to_all(summed.reshape(ZL * ZH, ROWS, keys_w), ('zl', 'zh'), 0, 0,...  6.86 us
    pallas_call x1, Pallas kernels, shards(): kernel_call(keys_kernel, (pltpu.HBM((tok_rows, keys_w), BF16), pltpu.HBM(...  5.65 us
    ppermute x3, starting transfers between devices, first_step(): return lax.ppermute(value, GATHER, moved(lambda c: c == 1, shift))  5.29 us
  transfers between devices with their start and end apart: 18, of which 13 were waited for; matrix products, arithmetic and copies ran while one was open for 2% of the time, Pallas kernels for 17%

profile of v13, /device:TPU:33, one launch (start us, length us, event | category | flops | bytes accessed | tf_op | source)
XLA Modules:
  0.0 104.9 jit_solution(4416101351599752393)
XLA Ops:
  0.6 0.0 copy-start
  0.6 3.5 %shard_map.127 = (bf16[4,128,2560]{2,1,0:T(8,128)(2,1)}, f32[128,128]{1,0:T(8,128)}) custom-call(bf16[128,8192]{1,0:T(8,128)(2,1)} %tok_ref.5, f32[1,8192]{1,0:T(1,128)} %bitcast.11, bf16[128,512]{1,0:T(8,128)(2,1)} %cot_ref.5), custom_call_target="tpu_custom_call" | custom-call | flops 6291456 | bytes 5242880 | tf_op jit(solution)/shard_map/pallas_call | solution.py:272
  4.2 4.2 %all-to-all-start = ((bf16[4,128,2560]{2,1,0:T(8,128)(2,1)}), bf16[4,128,2560]{2,1,0:T(8,128)(2,1)S(1)}, u32[]{:S(2)}, u32[]{:S(2)}) async-start(bf16[4,128,2560]{2,1,0:T(8,128)(2,1)} %get-tuple-element.36), calls=%async_computation | async-start | bytes 5242880 | tf_op jit(solution)/shard_map/all_to_all | solution.py:256
  8.4 0.0 copy-done
  8.4 1.7 %collective-permute-start.2 = (bf16[256,512]{1,0:T(8,128)(2,1)S(1)}, bf16[256,512]{1,0:T(8,128)(2,1)S(1)}, u32[]{:S(2)}, u32[]{:S(2)}) collective-permute-start(bf16[256,512]{1,0:T(8,128)(2,1)S(1)} %constant_dynamic-slice_fusion), channel_id=1, source_target_pairs={{0,16},{1,65},{2,18},{3,67},{16,32},{17,81},{18,34},{19,83},{32,48... | collective-permute-start | bytes 786440 | tf_op jit(solution)/shard_map/ppermute | solution.py:243
  10.1 3.6 %collective-permute-start.1 = (bf16[256,512]{1,0:T(8,128)(2,1)S(1)}, bf16[256,512]{1,0:T(8,128)(2,1)S(1)}, u32[]{:S(2)}, u32[]{:S(2)}) collective-permute-start(bf16[256,512]{1,0:T(8,128)(2,1)S(1)} %constant_dynamic-slice_fusion), channel_id=1, source_target_pairs={{0,32},{1,129},{2,34},{3,131},{16,48},{17,145},{18,50},{19,147},{3... | collective-permute-start | bytes 786440 | tf_op jit(solution)/shard_map/ppermute | solution.py:243
  13.7 0.0 collective-permute-start
  13.7 0.3 collective-permute-done.2
  14.0 4.4 %collective-permute-done.1 = bf16[256,512]{1,0:T(8,128)(2,1)S(1)} collective-permute-done((bf16[256,512]{1,0:T(8,128)(2,1)S(1)}, bf16[256,512]{1,0:T(8,128)(2,1)S(1)}, u32[]{:S(2)}, u32[]{:S(2)}) %collective-permute-start.1) | collective-permute-done | bytes 262176 | tf_op jit(solution)/shard_map/ppermute | solution.py:243
  18.4 2.8 %collective-permute-done = bf16[256,512]{1,0:T(8,128)(2,1)S(1)} collective-permute-done((bf16[256,512]{1,0:T(8,128)(2,1)S(1)}, bf16[256,512]{1,0:T(8,128)(2,1)S(1)}, u32[]{:S(2)}, u32[]{:S(2)}) %collective-permute-start) | collective-permute-done | bytes 262176 | tf_op jit(solution)/shard_map/ppermute | solution.py:243
  21.2 1.0 pad_maximum_fusion.refs_0_
  22.2 2.7 %collective-permute-start.3 = (bf16[1024,512]{1,0:T(8,128)(2,1)}, bf16[1024,512]{1,0:T(8,128)(2,1)}, u32[]{:S(2)}, u32[]{:S(2)}) collective-permute-start(bf16[1024,512]{1,0:T(8,128)(2,1)} %pad_maximum_fusion.refs_0_), channel_id=1, source_target_pairs={{0,194},{1,49},{2,192},{3,51},{16,210},{17,1},{18,208},{19,3},{32,... | collective-permute-start | bytes 3145736 | tf_op jit(solution)/shard_map/ppermute | solution.py:247
  24.9 0.0 collective-permute-start.4
  24.9 7.4 %all-to-all-done = bf16[4,128,2560]{2,1,0:T(8,128)(2,1)S(1)} async-done(((bf16[4,128,2560]{2,1,0:T(8,128)(2,1)}), bf16[4,128,2560]{2,1,0:T(8,128)(2,1)S(1)}, u32[]{:S(2)}, u32[]{:S(2)}) %all-to-all-start) | async-done | bytes 2621472 | tf_op jit(solution)/shard_map/all_to_all | solution.py:256
  32.3 2.1 %shard_map.128 = bf16[4,512,512]{2,1,0:T(8,128)(2,1)} custom-call(bf16[512,2560]{1,0:T(8,128)(2,1)S(1)} %bitcast.9), custom_call_target="tpu_custom_call" | custom-call | bytes 1048576 | tf_op jit(solution)/shard_map/pallas_call | solution.py:284
  34.4 4.0 %all-to-all-start.1 = ((bf16[4,512,512]{2,1,0:T(8,128)(2,1)}), bf16[4,512,512]{2,1,0:T(8,128)(2,1)S(1)}, u32[]{:S(2)}, u32[]{:S(2)}) async-start(bf16[4,512,512]{2,1,0:T(8,128)(2,1)} %shard_map.128), calls=%async_computation.1 | async-start | bytes 4194304 | tf_op jit(solution)/shard_map/all_to_all | solution.py:256
  38.4 7.2 %collective-permute-done.3.up_ref.refs_2_ = bf16[1024,512]{1,0:T(8,128)(2,1)} collective-permute-done((bf16[1024,512]{1,0:T(8,128)(2,1)}, bf16[1024,512]{1,0:T(8,128)(2,1)}, u32[]{:S(2)}, u32[]{:S(2)}) %collective-permute-start.3) | collective-permute-done | bytes 1048608 | tf_op jit(solution)/shard_map/ppermute | solution.py:247
  45.6 1.3 %collective-permute-done.4.down_ref.refs_4_ = bf16[1024,512]{1,0:T(8,128)(2,1)} collective-permute-done((bf16[1024,512]{1,0:T(8,128)(2,1)}, bf16[1024,512]{1,0:T(8,128)(2,1)}, u32[]{:S(2)}, u32[]{:S(2)}) %collective-permute-start.4) | collective-permute-done | bytes 1048608 | tf_op jit(solution)/shard_map/ppermute | solution.py:247
  46.8 2.2 %shard_map.130 = (bf16[512,512]{1,0:T(8,128)(2,1)}, bf16[512,512]{1,0:T(8,128)(2,1)}) custom-call(bf16[1024,512]{1,0:T(8,128)(2,1)} %collective-permute-done.3.up_ref.refs_2_, bf16[1024,512]{1,0:T(8,128)(2,1)} %collective-permute-done.4.down_ref.refs_4_), custom_call_target="tpu_custom_call" | custom-call | bytes 1048576 | tf_op jit(solution)/shard_map/pallas_call | solution.py:303
  49.0 0.1 collective-permute-start.8
  49.1 0.5 collective-permute-start.9
  49.6 0.1 collective-permute-start.10
  49.7 2.1 %collective-permute-start.5 = (bf16[512,512]{1,0:T(8,128)(2,1)}, bf16[512,512]{1,0:T(8,128)(2,1)S(1)}, u32[]{:S(2)}, u32[]{:S(2)}) collective-permute-start(bf16[512,512]{1,0:T(8,128)(2,1)} %get-tuple-element.39), channel_id=1, source_target_pairs={{0,194},{1,49},{2,192},{3,51},{16,210},{17,1},{18,208},{19,3},{32,... | collective-permute-start | bytes 1572872 | tf_op jit(solution)/shard_map/ppermute | solution.py:247
  51.8 0.0 collective-permute-start.6
  51.8 2.3 %all-to-all-done.1.recv_ref = bf16[4,512,512]{2,1,0:T(8,128)(2,1)S(1)} async-done(((bf16[4,512,512]{2,1,0:T(8,128)(2,1)}), bf16[4,512,512]{2,1,0:T(8,128)(2,1)S(1)}, u32[]{:S(2)}, u32[]{:S(2)}) %all-to-all-start.1) | async-done | bytes 2097184 | tf_op jit(solution)/shard_map/all_to_all | solution.py:256
  54.1 0.2 shard_map.129
  54.3 4.9 %collective-permute-done.5.refs_6_ = bf16[512,512]{1,0:T(8,128)(2,1)S(1)} collective-permute-done((bf16[512,512]{1,0:T(8,128)(2,1)}, bf16[512,512]{1,0:T(8,128)(2,1)S(1)}, u32[]{:S(2)}, u32[]{:S(2)}) %collective-permute-start.5) | collective-permute-done | bytes 524320 | tf_op jit(solution)/shard_map/ppermute | solution.py:247
  59.2 2.2 %collective-permute-done.6.refs_8_ = bf16[512,512]{1,0:T(8,128)(2,1)} collective-permute-done((bf16[512,512]{1,0:T(8,128)(2,1)}, bf16[512,512]{1,0:T(8,128)(2,1)}, u32[]{:S(2)}, u32[]{:S(2)}) %collective-permute-start.6) | collective-permute-done | bytes 524320 | tf_op jit(solution)/shard_map/ppermute | solution.py:247
  61.4 1.0 collective-permute-start.7
  62.4 0.0 collective-permute-start.11
  62.4 1.2 %collective-permute-done.7 = bf16[256,512]{1,0:T(8,128)(2,1)S(1)} collective-permute-done((bf16[256,512]{1,0:T(8,128)(2,1)S(1)}, bf16[256,512]{1,0:T(8,128)(2,1)S(1)}, u32[]{:S(2)}, u32[]{:S(2)}) %collective-permute-start.7) | collective-permute-done | bytes 262176 | tf_op jit(solution)/shard_map/ppermute | solution.py:321
  63.6 0.4 collective-permute-start.12
  63.9 0.8 add_convert_fusion
  64.7 0.0 collective-permute-done.8.refs_1_
  64.7 0.0 collective-permute-done.9.refs_3_
  64.7 0.0 collective-permute-done.10.refs_5_
  64.7 6.9 %all-to-all-start.2 = ((bf16[8,32,512]{2,1,0:T(8,128)(2,1)}), bf16[8,32,512]{2,1,0:T(8,128)(2,1)S(1)}, u32[]{:S(2)}, u32[]{:S(2)}) async-start(bf16[8,32,512]{2,1,0:T(8,128)(2,1)} %bitcast.2), calls=%async_computation.2 | async-start | bytes 524288 | tf_op jit(solution)/shard_map/all_to_all | solution.py:326
  71.6 0.0 collective-permute-done.11.refs_7_
  71.6 0.0 collective-permute-done.12.refs_9_
  71.6 5.7 %shard_map.131 = (bf16[128,512]{1,0:T(8,128)(2,1)}, f32[128,128]{1,0:T(8,128)}) custom-call(bf16[128,8192]{1,0:T(8,128)(2,1)} %tok_ref.5, f32[1,8192]{1,0:T(1,128)} %bitcast.12, bf16[128,512]{1,0:T(8,128)(2,1)} %cot_ref.5, f32[128,128]{1,0:T(8,128)} %get-tuple-element.46.inv_ref, bf16[1024,512]{1,0:T(8,128)(2,1)} %pad_maximum_fusion.refs_0_, ...), custom_call_target="tpu_custom_call" | custom-call | flops 1073741824 | bytes 3145728 | tf_op jit(solution)/shard_map/pallas_call | solution.py:327
  77.2 5.1 %all-to-all-done.2.recv_ref = bf16[8,32,512]{2,1,0:T(8,128)(2,1)S(1)} async-done(((bf16[8,32,512]{2,1,0:T(8,128)(2,1)}), bf16[8,32,512]{2,1,0:T(8,128)(2,1)S(1)}, u32[]{:S(2)}, u32[]{:S(2)}) %all-to-all-start.2) | async-done | bytes 262176 | tf_op jit(solution)/shard_map/all_to_all | solution.py:326
  82.4 2.1 %shard_map.132 = (f32[32,512]{1,0:T(8,128)}, f32[16,1024]{1,0:T(8,128)}, f32[16,1024]{1,0:T(8,128)}, bf16[8,32,512]{2,1,0:T(8,128)(2,1)}) custom-call(bf16[8,32,512]{2,1,0:T(8,128)(2,1)S(1)} %all-to-all-done.2.recv_ref, f32[16,1024]{1,0:T(8,128)} %first_ref.1, f32[16,1024]{1,0:T(8,128)} %second_ref.1, f32[32,512]{1,0:T(8,128)} %master_ref.1, s32[1,1024]{1,0:T(1,128)} %bitcast.14), custom_call_target="tpu_custom_call" | custom-call | flops 33554432 | bytes 1048576 | tf_op jit(solution)/shard_map/pallas_call | solution.py:335
  84.5 4.3 %all-to-all-start.3 = ((bf16[8,32,512]{2,1,0:T(8,128)(2,1)}), bf16[8,32,512]{2,1,0:T(8,128)(2,1)S(1)}, u32[]{:S(2)}, u32[]{:S(2)}) async-start(bf16[8,32,512]{2,1,0:T(8,128)(2,1)} %get-tuple-element.59), calls=%async_computation.3 | async-start | bytes 524288 | tf_op jit(solution)/shard_map/all_to_all | solution.py:348
  88.7 7.9 %shard_map.133 = bf16[128,8192]{1,0:T(8,128)(2,1)} custom-call(bf16[128,8192]{1,0:T(8,128)(2,1)} %tok_ref.5, f32[1,8192]{1,0:T(1,128)} %bitcast.13, bf16[128,512]{1,0:T(8,128)(2,1)} %cot_ref.5, f32[128,128]{1,0:T(8,128)} %get-tuple-element.46.inv_ref, f32[128,128]{1,0:T(8,128)} %get-tuple-element.60.mean_ref, bf16[1024,512]{1,0:T(8,128)(2,1)} %pad_maximum_fusion.refs_0_, ...), custom_call_target="tpu_custom_call" | custom-call | flops 1073741824 | bytes 5242880 | tf_op jit(solution)/shard_map/pallas_call | solution.py:349
  96.6 2.1 %all-to-all-done.3 = bf16[8,32,512]{2,1,0:T(8,128)(2,1)S(1)} async-done(((bf16[8,32,512]{2,1,0:T(8,128)(2,1)}), bf16[8,32,512]{2,1,0:T(8,128)(2,1)S(1)}, u32[]{:S(2)}, u32[]{:S(2)}) %all-to-all-start.3) | async-done | bytes 262176 | tf_op jit(solution)/shard_map/all_to_all | solution.py:348
  98.8 4.0 %collective-permute-start.13 = (bf16[8,32,512]{2,1,0:T(8,128)(2,1)S(1)}, bf16[8,32,512]{2,1,0:T(8,128)(2,1)S(1)}, u32[]{:S(2)}, u32[]{:S(2)}) collective-permute-start(bf16[8,32,512]{2,1,0:T(8,128)(2,1)S(1)} %all-to-all-done.3), channel_id=1, source_target_pairs={{0,1},{1,0},{2,3},{3,2},{4,5},{5,4},{6,7},{7,6},{8,9},{9,8},{10,11... | collective-permute-start | bytes 786440 | tf_op jit(solution)/shard_map/ppermute | solution.py:357
  102.8 1.2 %collective-permute-done.13 = bf16[8,32,512]{2,1,0:T(8,128)(2,1)S(1)} collective-permute-done((bf16[8,32,512]{2,1,0:T(8,128)(2,1)S(1)}, bf16[8,32,512]{2,1,0:T(8,128)(2,1)S(1)}, u32[]{:S(2)}, u32[]{:S(2)}) %collective-permute-start.13) | collective-permute-done | bytes 262176 | tf_op jit(solution)/shard_map/ppermute | solution.py:357
  104.0 0.1 pad_maximum_fusion.1
  104.0 0.8 copy.14
  (2 shorter events, 0.1 us)
Async XLA Ops:
  0.6 7.7 %copy-start = (bf16[512,512]{1,0:T(8,128)(2,1)S(1)}, bf16[512,512]{1,0:T(8,128)(2,1)}, u32[]{:S(2)}) copy-start(bf16[512,512]{1,0:T(8,128)(2,1)} %param.11) | copy-start | bytes 1572868
  4.2 28.1 %all-to-all-start = ((bf16[4,128,2560]{2,1,0:T(8,128)(2,1)}), bf16[4,128,2560]{2,1,0:T(8,128)(2,1)S(1)}, u32[]{:S(2)}, u32[]{:S(2)}) async-start(bf16[4,128,2560]{2,1,0:T(8,128)(2,1)} %get-tuple-element.36), calls=%async_computation | async-start | bytes 5242880 | tf_op jit(solution)/shard_map/all_to_all | solution.py:256
  8.4 5.6 %collective-permute-start.2 = (bf16[256,512]{1,0:T(8,128)(2,1)S(1)}, bf16[256,512]{1,0:T(8,128)(2,1)S(1)}, u32[]{:S(2)}, u32[]{:S(2)}) collective-permute-start(bf16[256,512]{1,0:T(8,128)(2,1)S(1)} %constant_dynamic-slice_fusion), channel_id=1, source_target_pairs={{0,16},{1,65},{2,18},{3,67},{16,32},{17,81},{18,34},{19,83},{32,48... | collective-permute-start | bytes 786440 | tf_op jit(solution)/shard_map/ppermute | solution.py:243
  10.1 8.3 %collective-permute-start.1 = (bf16[256,512]{1,0:T(8,128)(2,1)S(1)}, bf16[256,512]{1,0:T(8,128)(2,1)S(1)}, u32[]{:S(2)}, u32[]{:S(2)}) collective-permute-start(bf16[256,512]{1,0:T(8,128)(2,1)S(1)} %constant_dynamic-slice_fusion), channel_id=1, source_target_pairs={{0,32},{1,129},{2,34},{3,131},{16,48},{17,145},{18,50},{19,147},{3... | collective-permute-start | bytes 786440 | tf_op jit(solution)/shard_map/ppermute | solution.py:243
  13.7 7.5 %collective-permute-start = (bf16[256,512]{1,0:T(8,128)(2,1)S(1)}, bf16[256,512]{1,0:T(8,128)(2,1)S(1)}, u32[]{:S(2)}, u32[]{:S(2)}) collective-permute-start(bf16[256,512]{1,0:T(8,128)(2,1)S(1)} %constant_dynamic-slice_fusion), channel_id=1, source_target_pairs={{0,48},{1,195},{2,50},{3,193},{16,0},{17,211},{18,2},{19,209},{32,... | collective-permute-start | bytes 786440 | tf_op jit(solution)/shard_map/ppermute | solution.py:243
  22.2 23.4 %collective-permute-start.3 = (bf16[1024,512]{1,0:T(8,128)(2,1)}, bf16[1024,512]{1,0:T(8,128)(2,1)}, u32[]{:S(2)}, u32[]{:S(2)}) collective-permute-start(bf16[1024,512]{1,0:T(8,128)(2,1)} %pad_maximum_fusion.refs_0_), channel_id=1, source_target_pairs={{0,194},{1,49},{2,192},{3,51},{16,210},{17,1},{18,208},{19,3},{32,... | collective-permute-start | bytes 3145736 | tf_op jit(solution)/shard_map/ppermute | solution.py:247
  24.9 22.0 %collective-permute-start.4 = (bf16[1024,512]{1,0:T(8,128)(2,1)}, bf16[1024,512]{1,0:T(8,128)(2,1)}, u32[]{:S(2)}, u32[]{:S(2)}) collective-permute-start(bf16[1024,512]{1,0:T(8,128)(2,1)} %pad_maximum_fusion.refs_0_), channel_id=1, source_target_pairs={{0,64},{1,17},{2,66},{3,19},{16,80},{17,33},{18,82},{19,35},{32,96... | collective-permute-start | bytes 3145736 | tf_op jit(solution)/shard_map/ppermute | solution.py:247
  34.4 19.7 %all-to-all-start.1 = ((bf16[4,512,512]{2,1,0:T(8,128)(2,1)}), bf16[4,512,512]{2,1,0:T(8,128)(2,1)S(1)}, u32[]{:S(2)}, u32[]{:S(2)}) async-start(bf16[4,512,512]{2,1,0:T(8,128)(2,1)} %shard_map.128), calls=%async_computation.1 | async-start | bytes 4194304 | tf_op jit(solution)/shard_map/all_to_all | solution.py:256
  49.0 15.7 %collective-permute-start.8 = (bf16[1024,512]{1,0:T(8,128)(2,1)}, bf16[1024,512]{1,0:T(8,128)(2,1)}, u32[]{:S(2)}, u32[]{:S(2)}) collective-permute-start(bf16[1024,512]{1,0:T(8,128)(2,1)} %pad_maximum_fusion.refs_0_), channel_id=1, source_target_pairs={{0,1},{1,0},{2,3},{3,2},{4,5},{5,4},{6,7},{7,6},{8,9},{9,8},{10,11... | collective-permute-start | bytes 3145736 | tf_op jit(solution)/shard_map/ppermute | solution.py:319
  49.1 15.6 %collective-permute-start.9 = (bf16[1024,512]{1,0:T(8,128)(2,1)}, bf16[1024,512]{1,0:T(8,128)(2,1)}, u32[]{:S(2)}, u32[]{:S(2)}) collective-permute-start(bf16[1024,512]{1,0:T(8,128)(2,1)} %collective-permute-done.3.up_ref.refs_2_), channel_id=1, source_target_pairs={{0,1},{1,0},{2,3},{3,2},{4,5},{5,4},{6,7},{7,6},{8,9},{9,8},{10,11... | collective-permute-start | bytes 3145736 | tf_op jit(solution)/shard_map/ppermute | solution.py:319
  49.6 15.1 %collective-permute-start.10 = (bf16[1024,512]{1,0:T(8,128)(2,1)}, bf16[1024,512]{1,0:T(8,128)(2,1)}, u32[]{:S(2)}, u32[]{:S(2)}) collective-permute-start(bf16[1024,512]{1,0:T(8,128)(2,1)} %collective-permute-done.4.down_ref.refs_4_), channel_id=1, source_target_pairs={{0,1},{1,0},{2,3},{3,2},{4,5},{5,4},{6,7},{7,6},{8,9},{9,8},{10,11... | collective-permute-start | bytes 3145736 | tf_op jit(solution)/shard_map/ppermute | solution.py:319
  49.7 9.4 %collective-permute-start.5 = (bf16[512,512]{1,0:T(8,128)(2,1)}, bf16[512,512]{1,0:T(8,128)(2,1)S(1)}, u32[]{:S(2)}, u32[]{:S(2)}) collective-permute-start(bf16[512,512]{1,0:T(8,128)(2,1)} %get-tuple-element.39), channel_id=1, source_target_pairs={{0,194},{1,49},{2,192},{3,51},{16,210},{17,1},{18,208},{19,3},{32,... | collective-permute-start | bytes 1572872 | tf_op jit(solution)/shard_map/ppermute | solution.py:247
  51.8 9.6 %collective-permute-start.6 = (bf16[512,512]{1,0:T(8,128)(2,1)}, bf16[512,512]{1,0:T(8,128)(2,1)}, u32[]{:S(2)}, u32[]{:S(2)}) collective-permute-start(bf16[512,512]{1,0:T(8,128)(2,1)} %get-tuple-element.40), channel_id=1, source_target_pairs={{0,64},{1,17},{2,66},{3,19},{16,80},{17,33},{18,82},{19,35},{32,96... | collective-permute-start | bytes 1572872 | tf_op jit(solution)/shard_map/ppermute | solution.py:247
  61.4 2.2 %collective-permute-start.7 = (bf16[256,512]{1,0:T(8,128)(2,1)S(1)}, bf16[256,512]{1,0:T(8,128)(2,1)S(1)}, u32[]{:S(2)}, u32[]{:S(2)}) collective-permute-start(bf16[256,512]{1,0:T(8,128)(2,1)S(1)} %get-tuple-element.41), channel_id=1, source_target_pairs={{0,1},{1,0},{2,3},{3,2},{4,5},{5,4},{6,7},{7,6},{8,9},{9,8},{10,11... | collective-permute-start | bytes 786440 | tf_op jit(solution)/shard_map/ppermute | solution.py:321
  62.4 9.2 %collective-permute-start.11 = (bf16[512,512]{1,0:T(8,128)(2,1)S(1)}, bf16[512,512]{1,0:T(8,128)(2,1)S(1)}, u32[]{:S(2)}, u32[]{:S(2)}) collective-permute-start(bf16[512,512]{1,0:T(8,128)(2,1)S(1)} %collective-permute-done.5.refs_6_), channel_id=1, source_target_pairs={{0,1},{1,0},{2,3},{3,2},{4,5},{5,4},{6,7},{7,6},{8,9},{9,8},{10,11... | collective-permute-start | bytes 1572872 | tf_op jit(solution)/shard_map/ppermute | solution.py:325
  63.6 8.0 %collective-permute-start.12 = (bf16[512,512]{1,0:T(8,128)(2,1)}, bf16[512,512]{1,0:T(8,128)(2,1)S(1)}, u32[]{:S(2)}, u32[]{:S(2)}) collective-permute-start(bf16[512,512]{1,0:T(8,128)(2,1)} %collective-permute-done.6.refs_8_), channel_id=1, source_target_pairs={{0,1},{1,0},{2,3},{3,2},{4,5},{5,4},{6,7},{7,6},{8,9},{9,8},{10,11... | collective-permute-start | bytes 1572872 | tf_op jit(solution)/shard_map/ppermute | solution.py:325
  64.7 17.7 %all-to-all-start.2 = ((bf16[8,32,512]{2,1,0:T(8,128)(2,1)}), bf16[8,32,512]{2,1,0:T(8,128)(2,1)S(1)}, u32[]{:S(2)}, u32[]{:S(2)}) async-start(bf16[8,32,512]{2,1,0:T(8,128)(2,1)} %bitcast.2), calls=%async_computation.2 | async-start | bytes 524288 | tf_op jit(solution)/shard_map/all_to_all | solution.py:326
  84.5 14.3 %all-to-all-start.3 = ((bf16[8,32,512]{2,1,0:T(8,128)(2,1)}), bf16[8,32,512]{2,1,0:T(8,128)(2,1)S(1)}, u32[]{:S(2)}, u32[]{:S(2)}) async-start(bf16[8,32,512]{2,1,0:T(8,128)(2,1)} %get-tuple-element.59), calls=%async_computation.3 | async-start | bytes 524288 | tf_op jit(solution)/shard_map/all_to_all | solution.py:348
  98.8 5.1 %collective-permute-start.13 = (bf16[8,32,512]{2,1,0:T(8,128)(2,1)S(1)}, bf16[8,32,512]{2,1,0:T(8,128)(2,1)S(1)}, u32[]{:S(2)}, u32[]{:S(2)}) collective-permute-start(bf16[8,32,512]{2,1,0:T(8,128)(2,1)S(1)} %all-to-all-done.3), channel_id=1, source_target_pairs={{0,1},{1,0},{2,3},{3,2},{4,5},{5,4},{6,7},{7,6},{8,9},{9,8},{10,11... | collective-permute-start | bytes 786440 | tf_op jit(solution)/shard_map/ppermute | solution.py:357
